TPU v7x, 32 devices: a whole 2x2x4 slice. The times are simulated.
32 devices in a mesh: dp: 8 (over z, core), tensor: 4 (over y, x).
Axes of the slice: x: 2, y: 2, z: 4, core: 2. Of those that a mesh axis runs over, the one named last changes fastest.
Arguments:
- hidden: bfloat16 [8192, 2048], P('dp'), may hold values from -6 to 6
- lengths: int32 [8], P('dp'), may hold values from 256 to 1024, as said below
- routes: int32 [8192, 6], P('dp'), may hold values from 0 to 15, all different within a row; in each aligned block of 1024 rows (0 to 1023, 1024 to 2047, ...) at most 512 rows name the same one
- attn_gain: bfloat16 [2048], P('dp'), may hold values from 0.5 to 1.5
- w_query: bfloat16 [2048, 3072], P('dp', 'tensor'), may hold values from -0.125 to 0.125
- w_kv_down: bfloat16 [2048, 576], P('dp'), may hold values from -0.125 to 0.125
- kv_gain: bfloat16 [512], P('dp'), may hold values from 0.5 to 1.5
- w_kv_up: bfloat16 [512, 4096], P('dp', 'tensor'), may hold values from -0.25 to 0.25
- w_out: bfloat16 [2048, 2048], P('tensor', 'dp'), may hold values from -2 to 2
- ffn_gain: bfloat16 [2048], P('dp'), may hold values from 0.5 to 1.5
- w_router: bfloat16 [2048, 16], P('dp'), may hold values from -0.0625 to 0.0625
- w_expert_in: bfloat16 [16, 2, 2048, 1408], P(None, None, 'dp', 'tensor'), may hold values from -0.125 to 0.125
- w_expert_out: bfloat16 [16, 1408, 2048], P(None, 'tensor', 'dp'), may hold values from -1.75 to 1.75
- w_shared_in: bfloat16 [2, 2048, 2816], P(None, 'dp', 'tensor'), may hold values from -0.125 to 0.125
- w_shared_out: bfloat16 [2816, 2048], P('tensor', 'dp'), may hold values from -0.1875 to 0.1875
- cotangent: bfloat16 [8192, 2048], P('dp'), may hold values from -6 to 6
Outputs:
- output: bfloat16 [8192, 2048], P('dp')
- grad_hidden: bfloat16 [8192, 2048], P('dp')
- grad_attn_gain: float32 [2048], P('dp')
- grad_w_query: float32 [2048, 3072], P('dp', 'tensor')
- grad_w_kv_down: float32 [2048, 576], P('dp')
- grad_kv_gain: float32 [512], P('dp')
- grad_w_kv_up: float32 [512, 4096], P('dp', 'tensor')
- grad_w_out: float32 [2048, 2048], P('tensor', 'dp')
- grad_ffn_gain: float32 [2048], P('dp')
- grad_w_router: float32 [2048, 16], P('dp')
- grad_w_expert_in: float32 [16, 2, 2048, 1408], P(None, None, 'dp', 'tensor')
- grad_w_expert_out: float32 [16, 1408, 2048], P(None, 'tensor', 'dp')
- grad_w_shared_in: float32 [2, 2048, 2816], P(None, 'dp', 'tensor')
- grad_w_shared_out: float32 [2816, 2048], P('tensor', 'dp')
Inputs may be any that keep to these rules, and one draw needn't show every extreme that they name: `lengths`: valid tokens of a slot; at least one slot is full. `routes`: each row names 6 different experts; among the 1024 rows of one slot no expert is named more than 512 times, a bound that some block reaches.
All inputs are finite; a program needn't handle non-finite values.
Results may differ from a plain program's by a relative error of at most 0.028.
Values may be sent and summed in bfloat16 or wider, within the bound.
No kernel may reach another device: no remote copies, remote signals or barrier semaphores. Data moves between devices by JAX's collectives and lax.ppermute only.
A program may use at most 448 MiB of HBM per device.

v0:
```python
import math

import jax
import jax.numpy as jnp
from jax import lax
from jax.sharding import PartitionSpec as P

NOPE = 128
ROPE = 64
VDIM = 128
LATENT = 512
TOP = 6
EXPERTS = 16
CAP = 512


EPSILON = 1e-06
NEGATIVE = -1e30


def rotate(values, cosine, sine):
    half = values.shape[-1] // 2
    first = values[..., :half]
    second = values[..., half:]
    return jnp.concatenate([first * cosine - second * sine, second * cosine + first * sine], -1)


def rotate_back(grads, cosine, sine):
    half = grads.shape[-1] // 2
    first = grads[..., :half]
    second = grads[..., half:]
    return jnp.concatenate([first * cosine + second * sine, second * cosine - first * sine], -1)


def angle_tables(rows_count):
    positions = jnp.arange(rows_count, dtype=jnp.float32)
    freqs = jnp.exp(jnp.arange(ROPE // 2, dtype=jnp.float32) * (-2.0 * math.log(10000.0) / ROPE))
    angles = positions[:, None] * freqs[None, :]
    return (jnp.cos(angles), jnp.sin(angles))


def slot_table(route_ids, rows_count):
    flat = route_ids.reshape(-1)
    onehot = (flat[:, None] == jnp.arange(EXPERTS, dtype=jnp.int32)[None, :]).astype(jnp.int32)
    before = jnp.cumsum(onehot, axis=0) - onehot
    position = jnp.sum(before * onehot, axis=1)
    slot_index = flat * CAP + position
    owners = jnp.arange(rows_count * TOP, dtype=jnp.int32) // TOP
    source = jnp.full((EXPERTS * CAP,), rows_count, jnp.int32).at[slot_index].set(owners)
    return (slot_index, source)


def inverse_rms(values):
    return lax.rsqrt(jnp.mean(values * values, axis=-1, keepdims=True) + EPSILON)


def norm_back(normed, inverse, gain, grad):
    scaled = gain * grad
    return inverse * (scaled - normed * jnp.mean(normed * scaled, axis=-1, keepdims=True))


def masked_scores(query_nope, query_rope, key_nope, key_rope, row_start, valid_length, score_scale):
    raw = jnp.einsum("ihd,jhd->hij", query_nope, key_nope, preferred_element_type=jnp.float32)
    raw = (
        raw + jnp.einsum("ihd,jd->hij", query_rope, key_rope, preferred_element_type=jnp.float32)
    ) * score_scale
    query_rows = row_start + jnp.arange(query_nope.shape[0], dtype=jnp.int32)
    key_rows = jnp.arange(key_nope.shape[0], dtype=jnp.int32)
    allowed = (key_rows[None, :] <= query_rows[:, None]) & (key_rows[None, :] < valid_length)
    return jnp.where(allowed[None], raw, NEGATIVE)


def body(
    hidden,
    lengths,
    routes,
    attn_gain,
    w_query,
    w_kv_down,
    kv_gain,
    w_kv_up,
    w_out,
    ffn_gain,
    w_router,
    w_expert_in,
    w_expert_out,
    w_shared_in,
    w_shared_out,
    cotangent,
):
    gathered = (
        lax.all_gather(attn_gain, "dp", axis=0, tiled=True),
        lax.all_gather(w_query, "dp", axis=0, tiled=True),
        lax.all_gather(w_kv_down, "dp", axis=0, tiled=True),
        lax.all_gather(kv_gain, "dp", axis=0, tiled=True),
        lax.all_gather(w_kv_up, "dp", axis=0, tiled=True),
        lax.all_gather(w_out, "dp", axis=1, tiled=True),
        lax.all_gather(ffn_gain, "dp", axis=0, tiled=True),
        lax.all_gather(w_router, "dp", axis=0, tiled=True),
        lax.all_gather(w_expert_in, "dp", axis=2, tiled=True),
        lax.all_gather(w_expert_out, "dp", axis=2, tiled=True),
        lax.all_gather(w_shared_in, "dp", axis=1, tiled=True),
        lax.all_gather(w_shared_out, "dp", axis=1, tiled=True),
    )
    (
        gain_attn,
        query_w,
        down_w,
        gain_kv,
        up_w,
        out_w,
        gain_ffn,
        router_w,
        expert_in,
        expert_out,
        shared_in,
        shared_out,
    ) = gathered
    seq_rows, width = hidden.shape
    heads_here = query_w.shape[1] // (NOPE + ROPE)
    score_scale = (NOPE + ROPE) ** (-0.5)
    valid_length = lengths[0]
    cosine, sine = angle_tables(seq_rows)
    inputs = hidden.astype(jnp.float32)
    attn_inverse = inverse_rms(inputs)
    attn_hat = inputs * attn_inverse
    attn_scale = gain_attn.astype(jnp.float32)
    normed_low = (attn_hat * attn_scale).astype(jnp.bfloat16)
    query = jnp.dot(normed_low, query_w, preferred_element_type=jnp.float32).reshape(
        seq_rows, heads_here, NOPE + ROPE
    )
    query_nope = query[..., :NOPE].astype(jnp.bfloat16)
    query_rope = rotate(query[..., NOPE:], cosine[:, None, :], sine[:, None, :]).astype(
        jnp.bfloat16
    )
    latent_all = jnp.dot(normed_low, down_w, preferred_element_type=jnp.float32)
    latent = latent_all[:, :LATENT]
    kv_inverse = inverse_rms(latent)
    latent_hat = latent * kv_inverse
    kv_scale = gain_kv.astype(jnp.float32)
    latent_low = (latent_hat * kv_scale).astype(jnp.bfloat16)
    key_rope = rotate(latent_all[:, LATENT:], cosine, sine).astype(jnp.bfloat16)
    keys_values = jnp.dot(latent_low, up_w, preferred_element_type=jnp.float32).astype(jnp.bfloat16)
    keys_values = keys_values.reshape(seq_rows, heads_here, NOPE + VDIM)
    key_nope = keys_values[..., :NOPE]
    values = keys_values[..., NOPE:]
    block_rows = min(512, seq_rows)
    blocks = seq_rows // block_rows
    block_starts = jnp.arange(blocks, dtype=jnp.int32) * block_rows
    nope_blocks = query_nope.reshape(blocks, block_rows, heads_here, NOPE)
    rope_blocks = query_rope.reshape(blocks, block_rows, heads_here, ROPE)

    def attend(items):
        nope_blk, rope_blk, row_start = items
        scores = masked_scores(
            nope_blk, rope_blk, key_nope, key_rope, row_start, valid_length, score_scale
        )
        highest = jnp.max(scores, axis=-1, keepdims=True)
        expo = jnp.exp(scores - highest)
        totals = jnp.sum(expo, axis=-1, keepdims=True)
        weights_low = (expo / totals).astype(jnp.bfloat16)
        out_blk = jnp.einsum(
            "hij,jhd->ihd", weights_low, values, preferred_element_type=jnp.float32
        )
        return (out_blk, (highest + jnp.log(totals))[..., 0])

    attended, log_totals = lax.map(attend, (nope_blocks, rope_blocks, block_starts))
    attended_low = attended.reshape(seq_rows, heads_here * VDIM).astype(jnp.bfloat16)
    attn_part = jnp.dot(attended_low, out_w, preferred_element_type=jnp.float32)
    residual = inputs + lax.psum(attn_part.astype(jnp.bfloat16), "tensor").astype(jnp.float32)
    ffn_inverse = inverse_rms(residual)
    ffn_hat = residual * ffn_inverse
    ffn_scale = gain_ffn.astype(jnp.float32)
    ffn_low = (ffn_hat * ffn_scale).astype(jnp.bfloat16)
    router_probs = jax.nn.softmax(
        jnp.dot(ffn_low, router_w, preferred_element_type=jnp.float32), axis=-1
    )
    route_onehot = (
        routes[:, :, None] == jnp.arange(EXPERTS, dtype=jnp.int32)[None, None, :]
    ).astype(jnp.float32)
    gate_values = jnp.sum(route_onehot * router_probs[:, None, :], axis=-1)
    slot_index, source = slot_table(routes, seq_rows)
    slot_gates = (
        jnp.zeros((EXPERTS * CAP,), jnp.float32).at[slot_index].set(gate_values.reshape(-1))
    )
    source_blocks = source.reshape(EXPERTS, CAP)
    gate_blocks = slot_gates.reshape(EXPERTS, CAP)
    ffn_pad = jnp.concatenate([ffn_low, jnp.zeros((1, width), jnp.bfloat16)], 0)

    def expert_forward(routed_pad, items):
        weight_in, weight_out, source_rows, gate_row = items
        rows_in = ffn_pad[source_rows]
        gate_up = jnp.einsum("rd,gdf->grf", rows_in, weight_in, preferred_element_type=jnp.float32)
        active = (jax.nn.silu(gate_up[0]) * gate_up[1]).astype(jnp.bfloat16)
        out_rows = jnp.dot(active, weight_out, preferred_element_type=jnp.float32)
        routed_pad = routed_pad.at[source_rows].add(gate_row[:, None] * out_rows)
        return (routed_pad, gate_up)

    routed_pad, gate_ups = lax.scan(
        expert_forward,
        jnp.zeros((seq_rows + 1, width), jnp.float32),
        (expert_in, expert_out, source_blocks, gate_blocks),
    )
    shared_pre = jnp.einsum("sd,gdf->gsf", ffn_low, shared_in, preferred_element_type=jnp.float32)
    shared_silu = jax.nn.silu(shared_pre[0])
    shared_act = (shared_silu * shared_pre[1]).astype(jnp.bfloat16)
    shared_part = jnp.dot(shared_act, shared_out, preferred_element_type=jnp.float32)
    ffn_total = lax.psum(
        (routed_pad[:seq_rows] + shared_part).astype(jnp.bfloat16), "tensor"
    ).astype(jnp.float32)
    output = (residual + ffn_total).astype(jnp.bfloat16)
    back_set = (
        lax.all_gather(attn_gain, "dp", axis=0, tiled=True),
        lax.all_gather(w_query, "dp", axis=0, tiled=True),
        lax.all_gather(w_kv_down, "dp", axis=0, tiled=True),
        lax.all_gather(kv_gain, "dp", axis=0, tiled=True),
        lax.all_gather(w_kv_up, "dp", axis=0, tiled=True),
        lax.all_gather(w_out, "dp", axis=1, tiled=True),
        lax.all_gather(ffn_gain, "dp", axis=0, tiled=True),
        lax.all_gather(w_router, "dp", axis=0, tiled=True),
        lax.all_gather(w_expert_in, "dp", axis=2, tiled=True),
        lax.all_gather(w_expert_out, "dp", axis=2, tiled=True),
        lax.all_gather(w_shared_in, "dp", axis=1, tiled=True),
        lax.all_gather(w_shared_out, "dp", axis=1, tiled=True),
    )
    (
        gain_attn,
        query_w,
        down_w,
        gain_kv,
        up_w,
        out_w,
        gain_ffn,
        router_w,
        expert_in,
        expert_out,
        shared_in,
        shared_out,
    ) = back_set
    valid_rows = (jnp.arange(seq_rows, dtype=jnp.int32) < valid_length).astype(jnp.float32)
    cot = cotangent.astype(jnp.float32) * valid_rows[:, None]
    cot_low = cot.astype(jnp.bfloat16)
    cot_pad = jnp.concatenate([cot, jnp.zeros((1, width), jnp.float32)], 0)
    shared_act_grad = jnp.dot(cot_low, shared_out.T, preferred_element_type=jnp.float32)
    shared_sig = jax.nn.sigmoid(shared_pre[0])
    shared_pre_grad = jnp.stack(
        [
            shared_act_grad
            * shared_pre[1]
            * shared_sig
            * (1.0 + shared_pre[0] * (1.0 - shared_sig)),
            shared_act_grad * shared_silu,
        ]
    ).astype(jnp.bfloat16)
    grad_shared_in = jnp.einsum(
        "sd,gsf->gdf", ffn_low, shared_pre_grad, preferred_element_type=jnp.float32
    )
    grad_shared_out = jnp.dot(shared_act.T, cot_low, preferred_element_type=jnp.float32)
    ffn_grad = jnp.einsum(
        "gsf,gdf->sd", shared_pre_grad, shared_in, preferred_element_type=jnp.float32
    )

    def expert_backward(grad_pad, items):
        weight_in, weight_out, source_rows, gate_row, gate_up = items
        rows_in = ffn_pad[source_rows]
        cot_rows = cot_pad[source_rows]
        gate_silu = jax.nn.silu(gate_up[0])
        active = (gate_silu * gate_up[1]).astype(jnp.bfloat16)
        out_rows = jnp.dot(active, weight_out, preferred_element_type=jnp.float32)
        gate_grad = jnp.sum(cot_rows * out_rows, axis=1)
        out_grad = (gate_row[:, None] * cot_rows).astype(jnp.bfloat16)
        act_grad = jnp.dot(out_grad, weight_out.T, preferred_element_type=jnp.float32)
        sigmoid_gate = jax.nn.sigmoid(gate_up[0])
        pre_low = jnp.stack(
            [
                act_grad * gate_up[1] * sigmoid_gate * (1.0 + gate_up[0] * (1.0 - sigmoid_gate)),
                act_grad * gate_silu,
            ]
        ).astype(jnp.bfloat16)
        in_weight_grad = jnp.einsum(
            "rd,grf->gdf", rows_in, pre_low, preferred_element_type=jnp.float32
        )
        out_weight_grad = jnp.dot(active.T, out_grad, preferred_element_type=jnp.float32)
        rows_grad = jnp.einsum(
            "grf,gdf->rd", pre_low, weight_in, preferred_element_type=jnp.float32
        )
        grad_pad = grad_pad.at[source_rows].add(rows_grad)
        return (grad_pad, (in_weight_grad, out_weight_grad, gate_grad))

    grad_pad, (grad_expert_in, grad_expert_out, slot_gate_grad) = lax.scan(
        expert_backward,
        jnp.zeros((seq_rows + 1, width), jnp.float32),
        (expert_in, expert_out, source_blocks, gate_blocks, gate_ups),
    )
    pair_gate_grad = slot_gate_grad.reshape(-1)[slot_index].reshape(seq_rows, TOP)
    probs_grad = jnp.sum(route_onehot * pair_gate_grad[:, :, None], axis=1)
    logits_grad = router_probs * (
        probs_grad - jnp.sum(router_probs * probs_grad, axis=-1, keepdims=True)
    )
    router_part = jnp.dot(
        ffn_low.T, logits_grad, precision=lax.Precision.HIGHEST, preferred_element_type=jnp.float32
    )
    ffn_grad = (
        ffn_grad
        + grad_pad[:seq_rows]
        + jnp.dot(
            logits_grad,
            router_w.T,
            precision=lax.Precision.HIGHEST,
            preferred_element_type=jnp.float32,
        )
    )
    residual_part = norm_back(ffn_hat, ffn_inverse, ffn_scale, ffn_grad)
    ffn_gain_part = jnp.sum(ffn_grad * ffn_hat, axis=0)
    residual_sum, grad_ffn_gain, grad_router = (
        lax.psum(residual_part.astype(jnp.bfloat16), "tensor").astype(jnp.float32),
        lax.psum(ffn_gain_part.astype(jnp.bfloat16), "tensor").astype(jnp.float32),
        lax.psum(router_part.astype(jnp.bfloat16), "tensor").astype(jnp.float32),
    )
    residual_grad = cot + residual_sum
    residual_low = residual_grad.astype(jnp.bfloat16)
    grad_out_w = jnp.dot(attended_low.T, residual_low, preferred_element_type=jnp.float32)
    attended_grad = jnp.dot(residual_low, out_w.T, preferred_element_type=jnp.float32).astype(
        jnp.bfloat16
    )
    grad_blocks = attended_grad.reshape(blocks, block_rows, heads_here, VDIM)

    def attend_back(carry, items):
        key_grad, value_grad, rope_grad = carry
        nope_blk, rope_blk, dout_blk, total_blk, row_start = items
        scores = masked_scores(
            nope_blk, rope_blk, key_nope, key_rope, row_start, valid_length, score_scale
        )
        probs = jnp.exp(scores - total_blk[..., None])
        prob_grad = jnp.einsum("ihd,jhd->hij", dout_blk, values, preferred_element_type=jnp.float32)
        centre = jnp.sum(probs * prob_grad, axis=-1, keepdims=True)
        score_grad = (probs * (prob_grad - centre)).astype(jnp.bfloat16)
        nope_grad = (
            jnp.einsum("hij,jhd->ihd", score_grad, key_nope, preferred_element_type=jnp.float32)
            * score_scale
        )
        rope_part = (
            jnp.einsum("hij,jd->ihd", score_grad, key_rope, preferred_element_type=jnp.float32)
            * score_scale
        )
        key_grad = (
            key_grad
            + jnp.einsum("hij,ihd->jhd", score_grad, nope_blk, preferred_element_type=jnp.float32)
            * score_scale
        )
        rope_grad = (
            rope_grad
            + jnp.einsum("hij,ihd->jd", score_grad, rope_blk, preferred_element_type=jnp.float32)
            * score_scale
        )
        value_grad = value_grad + jnp.einsum(
            "hij,ihd->jhd", probs.astype(jnp.bfloat16), dout_blk, preferred_element_type=jnp.float32
        )
        return ((key_grad, value_grad, rope_grad), (nope_grad, rope_part))

    start_carry = (
        jnp.zeros((seq_rows, heads_here, NOPE), jnp.float32),
        jnp.zeros((seq_rows, heads_here, VDIM), jnp.float32),
        jnp.zeros((seq_rows, ROPE), jnp.float32),
    )
    (key_grad, value_grad, rope_grad), (query_nope_grad, query_rope_grad) = lax.scan(
        attend_back, start_carry, (nope_blocks, rope_blocks, grad_blocks, log_totals, block_starts)
    )
    query_nope_grad = query_nope_grad.reshape(seq_rows, heads_here, NOPE)
    query_rope_grad = rotate_back(
        query_rope_grad.reshape(seq_rows, heads_here, ROPE), cosine[:, None, :], sine[:, None, :]
    )
    query_grad = (
        jnp.concatenate([query_nope_grad, query_rope_grad], -1)
        .astype(jnp.bfloat16)
        .reshape(seq_rows, heads_here * (NOPE + ROPE))
    )
    grad_query_w = jnp.dot(normed_low.T, query_grad, preferred_element_type=jnp.float32)
    normed_grad_q = jnp.dot(query_grad, query_w.T, preferred_element_type=jnp.float32)
    kv_grad = (
        jnp.concatenate([key_grad, value_grad], -1)
        .astype(jnp.bfloat16)
        .reshape(seq_rows, heads_here * (NOPE + VDIM))
    )
    grad_up_w = jnp.dot(latent_low.T, kv_grad, preferred_element_type=jnp.float32)
    latent_part = jnp.dot(kv_grad, up_w.T, preferred_element_type=jnp.float32)
    key_rope_part = rotate_back(rope_grad, cosine, sine)
    latent_grad, key_rope_grad = (
        lax.psum(latent_part.astype(jnp.bfloat16), "tensor").astype(jnp.float32),
        lax.psum(key_rope_part.astype(jnp.bfloat16), "tensor").astype(jnp.float32),
    )
    grad_kv_gain = jnp.sum(latent_grad * latent_hat, axis=0)
    down_grad = jnp.concatenate(
        [norm_back(latent_hat, kv_inverse, kv_scale, latent_grad), key_rope_grad], -1
    ).astype(jnp.bfloat16)
    grad_down_w = jnp.dot(normed_low.T, down_grad, preferred_element_type=jnp.float32)
    normed_grad_kv = jnp.dot(down_grad, down_w.T, preferred_element_type=jnp.float32)
    input_part = norm_back(attn_hat, attn_inverse, attn_scale, normed_grad_q)
    attn_gain_part = jnp.sum(normed_grad_q * attn_hat, axis=0)
    input_sum, attn_gain_sum = (
        lax.psum(input_part.astype(jnp.bfloat16), "tensor").astype(jnp.float32),
        lax.psum(attn_gain_part.astype(jnp.bfloat16), "tensor").astype(jnp.float32),
    )
    input_grad = (
        residual_grad + input_sum + norm_back(attn_hat, attn_inverse, attn_scale, normed_grad_kv)
    )
    grad_attn_gain = attn_gain_sum + jnp.sum(normed_grad_kv * attn_hat, axis=0)
    summed = (
        lax.psum_scatter(
            grad_attn_gain.astype(jnp.bfloat16), "dp", scatter_dimension=0, tiled=True
        ).astype(jnp.float32),
        lax.psum_scatter(
            grad_query_w.astype(jnp.bfloat16), "dp", scatter_dimension=0, tiled=True
        ).astype(jnp.float32),
        lax.psum_scatter(
            grad_down_w.astype(jnp.bfloat16), "dp", scatter_dimension=0, tiled=True
        ).astype(jnp.float32),
        lax.psum_scatter(
            grad_kv_gain.astype(jnp.bfloat16), "dp", scatter_dimension=0, tiled=True
        ).astype(jnp.float32),
        lax.psum_scatter(
            grad_up_w.astype(jnp.bfloat16), "dp", scatter_dimension=0, tiled=True
        ).astype(jnp.float32),
        lax.psum_scatter(
            grad_out_w.astype(jnp.bfloat16), "dp", scatter_dimension=1, tiled=True
        ).astype(jnp.float32),
        lax.psum_scatter(
            grad_ffn_gain.astype(jnp.bfloat16), "dp", scatter_dimension=0, tiled=True
        ).astype(jnp.float32),
        lax.psum_scatter(
            grad_router.astype(jnp.bfloat16), "dp", scatter_dimension=0, tiled=True
        ).astype(jnp.float32),
        lax.psum_scatter(
            grad_expert_in.astype(jnp.bfloat16), "dp", scatter_dimension=2, tiled=True
        ).astype(jnp.float32),
        lax.psum_scatter(
            grad_expert_out.astype(jnp.bfloat16), "dp", scatter_dimension=2, tiled=True
        ).astype(jnp.float32),
        lax.psum_scatter(
            grad_shared_in.astype(jnp.bfloat16), "dp", scatter_dimension=1, tiled=True
        ).astype(jnp.float32),
        lax.psum_scatter(
            grad_shared_out.astype(jnp.bfloat16), "dp", scatter_dimension=1, tiled=True
        ).astype(jnp.float32),
    )
    return (
        output,
        input_grad.astype(jnp.bfloat16),
        summed[0],
        summed[1],
        summed[2],
        summed[3],
        summed[4],
        summed[5],
        summed[6],
        summed[7],
        summed[8],
        summed[9],
        summed[10],
        summed[11],
    )


def solution(mesh):
    return jax.shard_map(
        body,
        mesh=mesh,
        in_specs=(
            P("dp", None),
            P("dp"),
            P("dp", None),
            P("dp"),
            P("dp", "tensor"),
            P("dp", None),
            P("dp"),
            P("dp", "tensor"),
            P("tensor", "dp"),
            P("dp"),
            P("dp", None),
            P(None, None, "dp", "tensor"),
            P(None, "tensor", "dp"),
            P(None, "dp", "tensor"),
            P("tensor", "dp"),
            P("dp", None),
        ),
        out_specs=(
            P("dp", None),
            P("dp", None),
            P("dp"),
            P("dp", "tensor"),
            P("dp", None),
            P("dp"),
            P("dp", "tensor"),
            P("tensor", "dp"),
            P("dp"),
            P("dp", None),
            P(None, None, "dp", "tensor"),
            P(None, "tensor", "dp"),
            P(None, "dp", "tensor"),
            P("tensor", "dp"),
        ),
        check_vma=False,
    )
```

profile of v0, /device:TPU:10, one launch (start us, length us, event | category | flops | bytes accessed | tf_op | source)
XLA Modules:
  0.0 3799.5 jit_solution(7034175215972010855)
XLA Ops:
  25.0 14.7 all-reduce.2
  49.0 17.3 all-gather.15.cloned.1.call-done
  71.2 33.5 all-gather.11.cloned.1.call-done
  115.4 21.9 while.59
  168.4 23.5 scatter_custom_fusion.2
  198.8 12.2 all_gather.52
  211.6 39.8 %all-reduce.15.cloned.1.call-done = bf16[1024,2048]{1,0:T(8,128)(2,1)} async-done(((bf16[1024,2048]{1,0:T(8,128)(2,1)}), bf16[1024,2048]{1,0:T(8,128)(2,1)}) %all-reduce.15.cloned.1.call-update) | async-done | bytes 4194320 | tf_op jit(solution)/shard_map/psum | solution.py:170
  266.5 23.2 scatter_custom_fusion.3
  289.7 21.3 all-gather.23.cloned.1.call-done
  311.0 11.0 fusion.121
  322.0 26.9 all-gather.25.cloned.1.call-done
  369.5 182.2 %all-gather.21.cloned.1.call-done = bf16[16,352,2048]{2,1,0:T(8,128)(2,1)} async-done(((bf16[16,352,256]{2,1,0:T(8,128)(2,1)}), bf16[16,352,2048]{2,1,0:T(8,128)(2,1)}) %all-gather.21.cloned.1.call-update) | async-done | bytes 23068688 | tf_op jit(solution)/shard_map/all_gather | solution.py:101
  551.7 396.0 %all-gather.19.cloned.1.call-done = bf16[16,2,2048,352]{2,3,1,0:T(8,128)(2,1)} async-done(((bf16[16,2,256,352]{2,3,1,0:T(8,128)(2,1)}), bf16[16,2,2048,352]{2,3,1,0:T(8,128)(2,1)}) %all-gather.19.cloned.1.call-update) | async-done | bytes 46137360 | tf_op jit(solution)/shard_map/all_gather | solution.py:100
  952.2 513.7 %while.60 = (s32[]{:T(128)}, f32[1025,2048]{1,0:T(8,128)}, f32[16,2,512,352]{2,3,1,0:T(8,128)}, s32[16,512]{1,0:T(8,128)S(1)}, f32[16,512]{1,0:T(8,128)S(1)}, /*...) while((s32[]{:T(128)}, f32[1025,2048]{1,0:T(8,128)}, ...), condition=%wide.region_18.19_spmd, body=%wide.region_16.18_spmd.sunk | while | flops 2217773568 | bytes 31747684 | solution.py:199
  969.1 15.5 scatter_custom_fusion.13
  1001.2 15.5 scatter_custom_fusion.13
  1033.3 15.5 scatter_custom_fusion.13
  1065.4 15.5 scatter_custom_fusion.13
  1097.4 15.5 scatter_custom_fusion.13
  1129.6 15.5 scatter_custom_fusion.13
  1161.6 15.5 scatter_custom_fusion.13
  1193.7 15.5 scatter_custom_fusion.13
  1225.8 15.5 scatter_custom_fusion.13
  1257.8 15.5 scatter_custom_fusion.13
  1289.9 15.5 scatter_custom_fusion.13
  1322.0 15.5 scatter_custom_fusion.13
  1354.1 15.5 scatter_custom_fusion.13
  1386.1 15.5 scatter_custom_fusion.13
  1418.3 15.5 scatter_custom_fusion.13
  1450.4 15.5 scatter_custom_fusion.13
  1470.3 846.4 %while.61 = (s32[]{:T(128)}, f32[1025,2048]{1,0:T(8,128)}, bf16[16,2,2048,352]{2,3,1,0:T(8,128)(2,1)}, bf16[16,352,2048]{2,1,0:T(8,128)(2,1)}, f32[16,512]{1,0:T...) while((s32[]{:T(128)}, f32[1025,2048]{1,0:T(8,128)}, ...), condition=%wide.region_23.24_spmd, body=%wide.region_20.23_spmd.sunk | while | flops 5179951104 | bytes 81764560 | solution.py:290
  1499.6 15.4 scatter_custom_fusion.15
  1552.4 15.4 scatter_custom_fusion.15
  1605.2 15.4 scatter_custom_fusion.15
  1658.1 15.4 scatter_custom_fusion.15
  1711.0 15.4 scatter_custom_fusion.15
  1763.9 15.4 scatter_custom_fusion.15
  1816.7 15.4 scatter_custom_fusion.15
  1869.6 15.4 scatter_custom_fusion.15
  1922.5 15.4 scatter_custom_fusion.15
  1975.4 15.4 scatter_custom_fusion.15
  2028.2 15.4 scatter_custom_fusion.15
  2081.2 15.4 scatter_custom_fusion.15
  2134.0 15.4 scatter_custom_fusion.15
  2186.8 15.4 scatter_custom_fusion.15
  2239.8 15.4 scatter_custom_fusion.15
  2292.6 15.4 scatter_custom_fusion.15
  2316.8 34.3 gather_fusion.3
  2352.0 12.4 multiply_reduce_fusion.2
  2368.5 107.0 %all-reduce.17.cloned.1.call-done = bf16[1024,2048]{1,0:T(8,128)(2,1)} async-done(((bf16[1024,2048]{1,0:T(8,128)(2,1)}), bf16[1024,2048]{1,0:T(8,128)(2,1)}) %all-reduce.17.cloned.1.call-update) | async-done | bytes 4194320 | tf_op jit(solution)/shard_map/psum | solution.py:316
  2485.1 101.9 %while.62 = (s32[]{:T(128)}, f32[1024,4,128]{0,2,1:T(8,128)S(1)}, f32[1024,4,128]{0,2,1:T(8,128)}, f32[1024,64]{0,1:T(8,128)S(1)}, bf16[2,512,4,128]{3,1,0,2:T(8...) while((s32[]{:T(128)}, f32[1024,4,128]{0,2,1:T(8,128)S(1)}, ...), condition=%wide.region_30.31_spmd.clone, body=%wide.region_28.30_spmd.clone.sunk | while | flops 3514891776 | bytes 188530160 | solution.py:366
  2514.4 10.4 dynamic_update_slice.54
  2564.9 10.4 dynamic_update_slice.54
  2628.9 19.4 all-reduce.21.cloned.1.call-done
  2701.8 52.1 %reduce-scatter.22.cloned.1.call-done = bf16[2,256,704]{1,2,0:T(8,128)(2,1)} async-done(((bf16[2,2048,704]{1,2,0:T(8,128)(2,1)}), bf16[2,256,704]{1,2,0:T(8,128)(2,1)}) %reduce-scatter.22.cloned.1.call-update) | async-done | bytes 720912 | tf_op jit(solution)/shard_map/reduce_scatter | solution.py:439
  2764.2 13.4 all-reduce.6
  2795.3 21.6 reduce-scatter.14.cloned.1.call-done
  2818.6 34.6 reduce-scatter.16.cloned.1.call-done
  2855.0 35.4 reduce-scatter.12.cloned.1.call-done
  2892.2 39.1 %reduce-scatter.10.cloned.1.call-done = bf16[256,768]{1,0:T(8,128)(2,1)} async-done(((bf16[2048,768]{1,0:T(8,128)(2,1)}), bf16[256,768]{1,0:T(8,128)(2,1)}) %reduce-scatter.10.cloned.1.call-update) | async-done | bytes 393232 | tf_op jit(solution)/shard_map/reduce_scatter | solution.py:412
  2933.2 178.4 %all-reduce.19.cloned.1.call-done = (bf16[1024,2048]{1,0:T(8,128)(2,1)}, bf16[1024,2048]{1,0:T(8,128)(2,1)}) async-done(((bf16[1024,2048]{1,0:T(8,128)(2,1)}, bf16[1024,2048]{1,0:T(8,128)(2,1)}), (bf16[1024,2048]{1,0:T(8,128)(2,1)}, bf16[1024,2048]{1,0:T(8,128)(2,1)})) %all-reduce.19.cloned.1.call-update) | async-done | bytes 8388624 | tf_op jit(solution)/shard_map/psum | solution.py:208
  3111.6 18.7 fusion.109
  3130.3 209.0 %reduce-scatter.20.cloned.1.call-done = bf16[16,352,256]{2,1,0:T(8,128)(2,1)} async-done(((bf16[16,352,2048]{2,1,0:T(8,128)(2,1)}), bf16[16,352,256]{2,1,0:T(8,128)(2,1)}) %reduce-scatter.20.cloned.1.call-update) | async-done | bytes 2883600 | tf_op jit(solution)/shard_map/reduce_scatter | solution.py:436
  3344.2 439.7 %reduce-scatter.18.cloned.1.call-done = bf16[16,2,256,352]{2,3,1,0:T(8,128)(2,1)} async-done(((bf16[16,2,2048,352]{2,3,1,0:T(8,128)(2,1)}), bf16[16,2,256,352]{2,3,1,0:T(8,128)(2,1)}) %reduce-scatter.18.cloned.1.call-update) | async-done | bytes 5767184 | tf_op jit(solution)/shard_map/reduce_scatter | solution.py:433
  (726 shorter events, 1245.2 us)
Async XLA Ops:
  7.2 16.3 copy-start.71
  7.2 17.5 copy-start.80
  7.2 35.4 all-gather.13.cloned.1.call-start
  7.9 58.4 %all-gather.15.cloned.1.call-start = ((), (), s32[]{:S(2)}) async-start(), calls=%async_computation.11 | async-start | bytes 1179648 | tf_op jit(solution)/shard_map/all_gather | solution.py:96
  8.7 96.0 %all-gather.11.cloned.1.call-start = ((), (), s32[]{:S(2)}) async-start(), calls=%async_computation.9 | async-start | bytes 3538944 | tf_op jit(solution)/shard_map/all_gather | solution.py:93
  9.4 131.7 %all-gather.17.cloned.1.call-start = ((), (), s32[]{:S(2)}) async-start(), calls=%async_computation.12 | async-start | bytes 2359296 | tf_op jit(solution)/shard_map/all_gather | solution.py:97
  10.0 241.4 %all-reduce.15.cloned.1.call-start = ((), (), s32[]{:S(2)}) async-start(), calls=%async_computation.13 | async-start | bytes 8388608 | tf_op jit(solution)/shard_map/psum | solution.py:170
  10.1 38.3 %copy-start.72 = (f32[32]{0:T(128)}, f32[32]{0:T(128)S(1)}, u32[]{:S(2)}) copy-start(f32[32]{0:T(128)S(1)} %multiply_exponential_fusion) | copy-start | bytes 388
  20.3 27.9 copy-start.51
  23.4 24.8 copy-start.59
  39.6 26.7 copy-start.67
  48.2 20.8 copy-start.23
  49.0 62.5 %copy-start.29 = (f32[1024,32]{0,1:T(8,128)}, f32[1024,32]{0,1:T(8,128)S(1)}, u32[]{:S(2)}) copy-start(f32[1024,32]{0,1:T(8,128)S(1)} %get-tuple-element.566) | copy-start | bytes 393220
  49.0 62.5 %copy-start.31 = (f32[1024,32]{0,1:T(8,128)}, f32[1024,32]{0,1:T(8,128)S(1)}, u32[]{:S(2)}) copy-start(f32[1024,32]{0,1:T(8,128)S(1)} %get-tuple-element.567) | copy-start | bytes 393220
  49.0 20.0 copy-start.65
  137.3 10.1 copy-start.8
  137.3 10.1 copy-start.15
  137.3 10.1 copy-start.17
  137.3 10.1 copy-start.21
  137.3 10.1 copy-start.48
  147.5 163.5 %all-gather.23.cloned.1.call-start = ((), (), s32[]{:S(2)}) async-start(), calls=%async_computation.16 | async-start | bytes 6488064 | tf_op jit(solution)/shard_map/all_gather | solution.py:102
  148.1 200.8 %all-gather.25.cloned.1.call-start = ((), (), s32[]{:S(2)}) async-start(), calls=%async_computation.17 | async-start | bytes 3244032 | tf_op jit(solution)/shard_map/all_gather | solution.py:103
  148.8 402.8 %all-gather.21.cloned.1.call-start = ((), (), s32[]{:S(2)}) async-start(), calls=%async_computation.15 | async-start | bytes 25952256 | tf_op jit(solution)/shard_map/all_gather | solution.py:101
  149.6 798.1 %all-gather.19.cloned.1.call-start = ((), (), s32[]{:S(2)}) async-start(), calls=%async_computation.14 | async-start | bytes 51904512 | tf_op jit(solution)/shard_map/all_gather | solution.py:100
  150.3 2325.2 %all-reduce.17.cloned.1.call-start = ((), (), s32[]{:S(2)}) async-start(), calls=%async_computation.18 | async-start | bytes 8388608 | tf_op jit(solution)/shard_map/psum | solution.py:316
  161.9 94.5 %copy-start.46 = (f32[8,1,256]{2,1,0:T(1,128)}, f32[8,1,256]{2,1,0:T(1,128)S(1)}, u32[]{:S(2)}) copy-start(f32[8,1,256]{2,1,0:T(1,128)S(1)} %convert_element_type.286) | copy-start | bytes 24580
  192.0 156.9 %copy-start.61 = (f32[1024]{0:T(1024)}, f32[1024]{0:T(1024)S(1)}, u32[]{:S(2)}) copy-start(f32[1024]{0:T(1024)S(1)} %fusion.156) | copy-start | bytes 12292
  211.0 52.0 %copy-start.42 = (bf16[2048,16]{0,1:T(8,128)(2,1)}, bf16[2048,16]{0,1:T(8,128)(2,1)S(1)}, u32[]{:S(2)}) copy-start(bf16[2048,16]{0,1:T(8,128)(2,1)S(1)} %all_gather.52) | copy-start | bytes 196612
  264.6 57.4 %copy-start.55 = (f32[1024]{0:T(1024)}, f32[1024]{0:T(1024)S(1)}, u32[]{:S(2)}) copy-start(f32[1024]{0:T(1024)S(1)} %get-tuple-element.568) | copy-start | bytes 12292
  264.6 57.4 %copy-start.63 = (f32[1024]{0:T(1024)}, f32[1024]{0:T(1024)S(1)}, u32[]{:S(2)}) copy-start(f32[1024]{0:T(1024)S(1)} %fusion.148) | copy-start | bytes 12292
  348.9 11.4 copy-start.74
  359.1 10.4 copy-start.84
  1470.3 846.4 %copy-start.50 = (s32[6144]{0:T(1024)S(1)}, s32[6144]{0:T(1024)}, u32[]{:S(2)}) copy-start(s32[6144]{0:T(1024)} %broadcast_clamp_fusion) | copy-start | bytes 73732
  2316.7 35.0 copy-start.45
  2316.8 35.1 copy-start.28
  2316.8 35.1 copy-start.56
  2316.8 35.1 copy-start.64
  2316.8 35.2 copy-start.34
  2316.8 35.2 copy-start.43
  2316.8 35.2 copy-start.47
  2316.8 35.2 copy-start.54
  2351.9 12.5 copy-start.36
  2351.9 12.4 copy-start.57
  2352.0 12.4 copy-start.5
  2352.0 12.4 copy-start.13
  2368.4 279.9 %all-reduce.21.cloned.1.call-start = ((), (), s32[]{:S(2)}) async-start(), calls=%async_computation.29 | async-start | bytes 2359296 | tf_op jit(solution)/shard_map/psum | solution.py:390
  2368.5 116.6 %copy-start.9 = (bf16[1024,4,128]{2,0,1:T(8,128)(2,1)S(1)}, bf16[1024,4,128]{2,0,1:T(8,128)(2,1)}, u32[]{:S(2)}) copy-start(bf16[1024,4,128]{2,0,1:T(8,128)(2,1)} %copy-done.8) | copy-start | bytes 3145732
  2368.5 116.6 %copy-start.22 = (bf16[1024,64]{0,1:T(8,128)(2,1)S(1)}, bf16[1024,64]{0,1:T(8,128)(2,1)}, u32[]{:S(2)}) copy-start(bf16[1024,64]{0,1:T(8,128)(2,1)} %copy-done.21) | copy-start | bytes 393220
  2368.5 116.6 %copy-start.49 = (f32[2,4,512]{2,1,0:T(4,128)S(1)}, f32[2,4,512]{2,1,0:T(4,128)}, u32[]{:S(2)}) copy-start(f32[2,4,512]{2,1,0:T(4,128)} %copy-done.48) | copy-start | bytes 49156
  2593.5 106.4 %reduce-scatter.24.cloned.1.call-start = ((), (), s32[]{:S(2)}) async-start(), calls=%async_computation.26 | async-start | bytes 3244032 | tf_op jit(solution)/shard_map/reduce_scatter | solution.py:442
  2601.2 152.7 %reduce-scatter.22.cloned.1.call-start = ((), (), s32[]{:S(2)}) async-start(), calls=%async_computation.25 | async-start | bytes 6488064 | tf_op jit(solution)/shard_map/reduce_scatter | solution.py:439
  2611.4 172.9 %reduce-scatter.26.cloned.1.call-start = ((), (), s32[]{:S(2)}) async-start(), calls=%async_computation.27 | async-start | bytes 73728 | tf_op jit(solution)/shard_map/reduce_scatter | solution.py:430
  2616.8 200.1 %reduce-scatter.14.cloned.1.call-start = ((), (), s32[]{:S(2)}) async-start(), calls=%async_computation.21 | async-start | bytes 1179648 | tf_op jit(solution)/shard_map/reduce_scatter | solution.py:421
  2620.9 232.3 %reduce-scatter.16.cloned.1.call-start = ((), (), s32[]{:S(2)}) async-start(), calls=%async_computation.22 | async-start | bytes 2359296 | tf_op jit(solution)/shard_map/reduce_scatter | solution.py:424
  2628.6 24.4 copy-start.52
  2628.6 24.4 copy-start.60
  2628.6 261.7 %reduce-scatter.12.cloned.1.call-start = ((), (), s32[]{:S(2)}) async-start(), calls=%async_computation.20 | async-start | bytes 2654208 | tf_op jit(solution)/shard_map/reduce_scatter | solution.py:415
  2657.3 273.9 %reduce-scatter.10.cloned.1.call-start = ((), (), s32[]{:S(2)}) async-start(), calls=%async_computation.19 | async-start | bytes 3538944 | tf_op jit(solution)/shard_map/reduce_scatter | solution.py:412
  2664.8 8.8 copy-start.76
  2673.1 438.5 %all-reduce.19.cloned.1.call-start = ((), (), s32[]{:S(2)}) async-start(), calls=%async_computation.28 | async-start | bytes 16777216 | tf_op jit(solution)/shard_map/psum | solution.py:208
  2673.6 7.9 copy-start.26
  2697.2 642.1 %reduce-scatter.20.cloned.1.call-start = ((), (), s32[]{:S(2)}) async-start(), calls=%async_computation.24 | async-start | bytes 25952256 | tf_op jit(solution)/shard_map/reduce_scatter | solution.py:436
  2697.8 1086.1 %reduce-scatter.18.cloned.1.call-start = ((), (), s32[]{:S(2)}) async-start(), calls=%async_computation.23 | async-start | bytes 51904512 | tf_op jit(solution)/shard_map/reduce_scatter | solution.py:433
  2697.9 66.3 %copy-start.69 = (bf16[2048]{0:T(1024)(128)(2,1)S(1)}, bf16[2048]{0:T(1024)(128)(2,1)}, u32[]{:S(2)}) copy-start(bf16[2048]{0:T(1024)(128)(2,1)} %get-tuple-element.432) | copy-start | bytes 12292
  (70 other events, 267.6 us)
Sparse Core Ops, SparseCore 0:
  9.6 32.8 all-gather.12
  44.2 22.1 all-gather.14
  68.0 36.6 all-gather.10
  106.1 29.6 all-gather.16
  147.6 103.6 all-reduce.14
  252.9 58.0 all-gather.22
  312.7 36.1 all-gather.24
  350.6 201.0 all-gather.20
  553.4 394.2 all-gather.18
  2368.5 106.9 all-reduce.16
  2593.6 54.6 all-reduce.20
  2650.6 34.8 reduce-scatter.23
  2688.5 65.3 reduce-scatter.21
  2756.6 27.6 reduce-scatter.25
  2786.4 30.4 reduce-scatter.13
  2819.1 34.0 reduce-scatter.15
  2855.4 34.9 reduce-scatter.11
  2892.5 38.6 reduce-scatter.9
  2935.6 175.9 all-reduce.18
  3113.9 225.3 reduce-scatter.19
  3341.8 442.0 reduce-scatter.17
where the time goes:
time: 3820 us; the launch traced here: 3800 us
  waiting for transfers between devices  1870 us (49%)
  matrix products  705 us (18%)
  other arithmetic  597 us (16%)
  local copies, waits for them, and re-layouts  530 us (14%)
  blocking collectives  75.8 us (2%)
    reduce_scatter x1, waiting for transfers between devices, body(): lax.psum_scatter(grad_expert_in.astype(jnp.bfloat16), 'dp', scatter_dimen...  440 us
    all_gather x1, waiting for transfers between devices, body(): lax.all_gather(w_expert_in, 'dp', axis=2, tiled=True)  396 us
    scatter-add x16, other arithmetic, expert_forward(): routed_pad = routed_pad.at[source_rows].add(gate_row[:, None] * out_rows)  249 us
    scatter-add x16, other arithmetic, expert_backward(): grad_pad = grad_pad.at[source_rows].add(rows_grad)  247 us
    reduce_scatter x1, waiting for transfers between devices, body(): lax.psum_scatter(grad_expert_out.astype(jnp.bfloat16), 'dp', scatter_dime...  209 us
    all_gather x1, waiting for transfers between devices, body(): lax.all_gather(w_expert_out, 'dp', axis=2, tiled=True)  182 us
    psum x1, waiting for transfers between devices, body(): lax.psum((routed_pad[:seq_rows] + shared_part).astype(jnp.bfloat16), 'ten...  178 us
    gather x16, local copies, waits for them, and re-layouts, expert_backward(): cot_rows = cot_pad[source_rows]  141 us
  transfers between devices with their start and end apart: 21, of which 19 were waited for; matrix products, arithmetic and copies ran while one was open for 7% of the time, Pallas kernels for 0%

commit v1 on v0

v1 whole, which is shorter than its diff:
```python
import functools
import math

import jax
import jax.numpy as jnp
from jax import lax
from jax.experimental import pallas as pl
from jax.experimental.pallas import tpu as pltpu
from jax.sharding import PartitionSpec as P

NOPE = 128
ROPE = 64
VDIM = 128
LATENT = 512
TOP = 6
EXPERTS = 16
CAP = 512

EPSILON = 1e-06
NEGATIVE = -1e30
F32 = jnp.float32
BF16 = jnp.bfloat16


def dot(a, b):
    return jnp.dot(a, b, preferred_element_type=F32)


def dot_nt(a, b):
    return lax.dot_general(a, b, (((1,), (1,)), ((), ())), preferred_element_type=F32)


def dot_tn(a, b):
    return lax.dot_general(a, b, (((0,), (0,)), ((), ())), preferred_element_type=F32)


def rotate(first, second, cosine, sine):
    return first * cosine - second * sine, second * cosine + first * sine


def rotate_back(first, second, cosine, sine):
    return first * cosine + second * sine, second * cosine - first * sine


def angle_tables(rows_count):
    positions = jnp.arange(rows_count, dtype=F32)
    freqs = jnp.exp(jnp.arange(ROPE // 2, dtype=F32) * (-2.0 * math.log(10000.0) / ROPE))
    angles = positions[:, None] * freqs[None, :]
    return (jnp.cos(angles), jnp.sin(angles))


def inverse_rms(values):
    return lax.rsqrt(jnp.mean(values * values, axis=-1, keepdims=True) + EPSILON)


class Layout:
    def __init__(self, n_dp, n_tensor):
        self.dp, self.t = n_dp, n_tensor
        self.q = n_dp * n_tensor // EXPERTS
        self.z = n_dp // self.q
        if self.z * self.t != EXPERTS or self.z * self.q != n_dp:
            raise ValueError("mesh")
        self.z_groups = [[c + self.q * z for z in range(self.z)] for c in range(self.q)]

    def over_t(self, values, k):
        if k == 0:
            return values
        return lax.ppermute(values, "tensor", [(i, i ^ k) for i in range(self.t)])

    def over_z(self, values, k):
        if k == 0:
            return values
        return lax.ppermute(values, "dp", [(d, d ^ (k * self.q)) for d in range(self.dp)])

    def over_c(self, values, k):
        if k == 0:
            return values
        return lax.ppermute(values, "dp", [(d, d ^ k) for d in range(self.dp)])


def piece_columns(lay, part, d_loc):
    ratio = lay.q * d_loc // part

    def block(ids, kz):
        return ids[0] ^ kz ^ (ids[2] // ratio)

    def first(ids, kc):
        offset = (ids[1] ^ kc) * d_loc
        return pl.multiple_of(((offset // part) ^ (ids[2] % ratio)) * part + offset % part, 128)

    return block, first


def lay_out_weights(lay, ids, stacks, f_loc, d_loc, width):
    ffe = f_loc * lay.t
    block, first = piece_columns(lay, width // lay.t, d_loc)

    def kernel(ids_ref, *refs):
        sources, (in_ref, out_ref) = refs[: lay.q], refs[lay.q :]
        for kc in range(lay.q):
            columns = pl.ds(first(ids_ref, kc), d_loc)
            for g in range(2):
                in_ref[g, :, columns] = sources[kc][0, g]
            out_ref[:, columns] = sources[kc][0, 2]

    own_in, own_out = pl.pallas_call(
        kernel,
        out_shape=(
            jax.ShapeDtypeStruct((2, ffe, width), BF16),
            jax.ShapeDtypeStruct((ffe, width), BF16),
        ),
        grid_spec=pltpu.PrefetchScalarGridSpec(
            num_scalar_prefetch=1,
            grid=(lay.t, lay.z),
            in_specs=[
                pl.BlockSpec((1, 3, f_loc, d_loc), lambda kt, kz, ids: (kt * lay.z + kz, 0, 0, 0))
            ]
            * lay.q,
            out_specs=(
                pl.BlockSpec(
                    (2, f_loc, lay.q * d_loc), lambda kt, kz, ids: (0, kt, block(ids, kz))
                ),
                pl.BlockSpec((f_loc, lay.q * d_loc), lambda kt, kz, ids: (kt, block(ids, kz))),
            ),
        ),
        cost_estimate=pl.CostEstimate(
            flops=0, bytes_accessed=12 * ffe * width, transcendentals=0
        ),
        compiler_params=pltpu.CompilerParams(vmem_limit_bytes=32 << 20),
        name="lay_out_weights",
    )(ids, *stacks)
    return own_in.reshape(2 * ffe, width), own_out


def take_apart(lay, ids, grad_in, grad_out, f_loc, d_loc, width):
    ffe = f_loc * lay.t
    block, first = piece_columns(lay, width // lay.t, d_loc)

    def kernel(ids_ref, in_ref, out_ref, *targets):
        for kc in range(lay.q):
            columns = pl.ds(first(ids_ref, kc), d_loc)
            for g in range(2):
                targets[kc][0, g] = in_ref[g, :, columns]
            targets[kc][0, 2] = out_ref[:, columns]

    shape = jax.ShapeDtypeStruct((lay.t * lay.z, 3, f_loc, d_loc), BF16)
    spec = pl.BlockSpec((1, 3, f_loc, d_loc), lambda kt, kz, ids: (kt * lay.z + kz, 0, 0, 0))
    return pl.pallas_call(
        kernel,
        out_shape=(shape,) * lay.q,
        grid_spec=pltpu.PrefetchScalarGridSpec(
            num_scalar_prefetch=1,
            grid=(lay.t, lay.z),
            in_specs=[
                pl.BlockSpec(
                    (2, f_loc, lay.q * d_loc), lambda kt, kz, ids: (0, kt, block(ids, kz))
                ),
                pl.BlockSpec((f_loc, lay.q * d_loc), lambda kt, kz, ids: (kt, block(ids, kz))),
            ],
            out_specs=(spec,) * lay.q,
        ),
        cost_estimate=pl.CostEstimate(
            flops=0, bytes_accessed=12 * ffe * width, transcendentals=0
        ),
        compiler_params=pltpu.CompilerParams(vmem_limit_bytes=32 << 20),
        name="take_apart",
    )(ids, grad_in.reshape(2, ffe, width), grad_out)


def home_gradients(lay, ids, pieces, f_loc, d_loc):
    def kernel(ids_ref, piece_ref, in_ref, out_ref):
        in_ref[0] = piece_ref[0, :2].astype(F32)
        out_ref[0] = piece_ref[0, 2].astype(F32)

    def pick(e, ids):
        return ((ids[2] ^ (e % lay.t)) * lay.z + (ids[0] ^ (e // lay.t)), 0, 0, 0)

    grad_in, grad_out = pl.pallas_call(
        kernel,
        out_shape=(
            jax.ShapeDtypeStruct((EXPERTS, 2, f_loc, d_loc), F32),
            jax.ShapeDtypeStruct((EXPERTS, f_loc, d_loc), F32),
        ),
        grid_spec=pltpu.PrefetchScalarGridSpec(
            num_scalar_prefetch=1,
            grid=(EXPERTS,),
            in_specs=[pl.BlockSpec((1, 3, f_loc, d_loc), pick)],
            out_specs=(
                pl.BlockSpec((1, 2, f_loc, d_loc), lambda e, ids: (e, 0, 0, 0)),
                pl.BlockSpec((1, f_loc, d_loc), lambda e, ids: (e, 0, 0)),
            ),
        ),
        cost_estimate=pl.CostEstimate(
            flops=0, bytes_accessed=18 * EXPERTS * f_loc * d_loc, transcendentals=0
        ),
        name="home_gradients",
    )(ids, pieces)
    return jnp.swapaxes(grad_in, 2, 3), grad_out


def score_block(q_ref, r_ref, k_ref, kr_ref, head, step, keys, block, length, scale):
    half = r_ref.shape[1] // 2
    lanes = lax.broadcasted_iota(jnp.int32, r_ref.shape, 1) % half // (ROPE // 2)
    turned = jnp.where(lanes == head, r_ref[...], jnp.zeros_like(r_ref))
    raw = lax.dot_general(
        q_ref[...], k_ref[:keys], (((1,), (1,)), ((), ())), preferred_element_type=F32
    ) + lax.dot_general(
        turned, kr_ref[:keys], (((1,), (1,)), ((), ())), preferred_element_type=F32
    )
    rows = lax.broadcasted_iota(jnp.int32, raw.shape, 0) + step * block
    cols = lax.broadcasted_iota(jnp.int32, raw.shape, 1)
    allowed = (cols <= rows) & (cols < length)
    return jnp.where(allowed, raw * scale, NEGATIVE), turned


def attend(length, query, query_rope, kv, key_rope, heads, scale):
    rows = query.shape[0]
    block = min(256, rows)
    steps = rows // block

    def kernel(len_ref, q_ref, r_ref, k_ref, v_ref, kr_ref, o_ref, total_ref):
        head, step = pl.program_id(0), pl.program_id(1)
        for n in range(steps):

            @pl.when(step == n)
            def _(n=n):
                keys = (n + 1) * block
                scores, _ = score_block(
                    q_ref, r_ref, k_ref, kr_ref, head, n, keys, block, len_ref[0], scale
                )
                highest = jnp.max(scores, axis=-1, keepdims=True)
                expo = jnp.exp(scores - highest)
                totals = jnp.sum(expo, axis=-1, keepdims=True)
                weights = (expo * (1.0 / totals)).astype(BF16)
                o_ref[...] = dot(weights, v_ref[:keys]).astype(BF16)
                total_ref[0] = jnp.broadcast_to(highest + jnp.log(totals), (block, 128))

    return pl.pallas_call(
        kernel,
        out_shape=(
            jax.ShapeDtypeStruct((rows, heads * VDIM), BF16),
            jax.ShapeDtypeStruct((heads, rows, 128), F32),
        ),
        grid_spec=pltpu.PrefetchScalarGridSpec(
            num_scalar_prefetch=1,
            grid=(heads, steps),
            in_specs=[
                pl.BlockSpec((block, NOPE), lambda h, i, n: (i, h)),
                pl.BlockSpec((block, query_rope.shape[1]), lambda h, i, n: (i, 0)),
                pl.BlockSpec((rows, NOPE), lambda h, i, n: (0, 2 * h)),
                pl.BlockSpec((rows, VDIM), lambda h, i, n: (0, 2 * h + 1)),
                pl.BlockSpec((rows, key_rope.shape[1]), lambda h, i, n: (0, 0)),
            ],
            out_specs=(
                pl.BlockSpec((block, VDIM), lambda h, i, n: (i, h)),
                pl.BlockSpec((1, block, 128), lambda h, i, n: (h, i, 0)),
            ),
        ),
        cost_estimate=pl.CostEstimate(
            flops=heads * rows * rows * 512,
            bytes_accessed=8 * rows * heads * 512,
            transcendentals=heads * rows * rows,
        ),
        compiler_params=pltpu.CompilerParams(vmem_limit_bytes=32 << 20),
        name="attend",
    )(length, query, query_rope, kv, kv, key_rope)


def attend_back(length, query, query_rope, kv, key_rope, out_grad, log_totals, heads, scale):
    rows = query.shape[0]
    block = min(256, rows)
    steps = rows // block
    turned_cols = query_rope.shape[1]

    def kernel(
        len_ref, q_ref, r_ref, k_ref, v_ref, kr_ref, do_ref, total_ref,
        dq_ref, dr_ref, dkv_ref, dkr_ref, dk_acc, dv_acc,
    ):
        head, step = pl.program_id(0), pl.program_id(1)

        @pl.when(step == 0)
        def _():
            dk_acc[...] = jnp.zeros_like(dk_acc)
            dv_acc[...] = jnp.zeros_like(dv_acc)

        @pl.when((step == 0) & (head == 0))
        def _():
            dr_ref[...] = jnp.zeros_like(dr_ref)
            dkr_ref[...] = jnp.zeros_like(dkr_ref)

        for n in range(steps):

            @pl.when(step == n)
            def _(n=n):
                keys = (n + 1) * block
                scores, turned = score_block(
                    q_ref, r_ref, k_ref, kr_ref, head, n, keys, block, len_ref[0], scale
                )
                probs = jnp.exp(scores - total_ref[0][:, :1])
                prob_grad = lax.dot_general(
                    do_ref[...], v_ref[:keys], (((1,), (1,)), ((), ())), preferred_element_type=F32
                )
                centre = jnp.sum(probs * prob_grad, axis=-1, keepdims=True)
                score_grad = (probs * (prob_grad - centre)).astype(BF16)
                probs_low = probs.astype(BF16)
                dq_ref[...] = (dot(score_grad, k_ref[:keys]) * scale).astype(BF16)
                half = turned_cols // 2
                lanes = lax.broadcasted_iota(jnp.int32, (block, turned_cols), 1)
                lanes = lanes % half // (ROPE // 2)
                turned_grad = dot(score_grad, kr_ref[:keys]) * scale
                dr_ref[n * block : keys] += jnp.where(lanes == head, turned_grad, 0.0)
                dk_acc[:keys] += dot_tn(score_grad, q_ref[...]) * scale
                dkr_ref[:keys] += dot_tn(score_grad, turned) * scale
                dv_acc[:keys] += dot_tn(probs_low, do_ref[...])

        @pl.when(step == steps - 1)
        def _():
            dkv_ref[:, :NOPE] = dk_acc[...].astype(BF16)
            dkv_ref[:, NOPE:] = dv_acc[...].astype(BF16)

    return pl.pallas_call(
        kernel,
        out_shape=(
            jax.ShapeDtypeStruct((rows, heads * NOPE), BF16),
            jax.ShapeDtypeStruct((rows, turned_cols), F32),
            jax.ShapeDtypeStruct((rows, heads * (NOPE + VDIM)), BF16),
            jax.ShapeDtypeStruct((rows, turned_cols), F32),
        ),
        grid_spec=pltpu.PrefetchScalarGridSpec(
            num_scalar_prefetch=1,
            grid=(heads, steps),
            in_specs=[
                pl.BlockSpec((block, NOPE), lambda h, i, n: (i, h)),
                pl.BlockSpec((block, turned_cols), lambda h, i, n: (i, 0)),
                pl.BlockSpec((rows, NOPE), lambda h, i, n: (0, 2 * h)),
                pl.BlockSpec((rows, VDIM), lambda h, i, n: (0, 2 * h + 1)),
                pl.BlockSpec((rows, turned_cols), lambda h, i, n: (0, 0)),
                pl.BlockSpec((block, VDIM), lambda h, i, n: (i, h)),
                pl.BlockSpec((1, block, 128), lambda h, i, n: (h, i, 0)),
            ],
            out_specs=(
                pl.BlockSpec((block, NOPE), lambda h, i, n: (i, h)),
                pl.BlockSpec((rows, turned_cols), lambda h, i, n: (0, 0)),
                pl.BlockSpec((rows, NOPE + VDIM), lambda h, i, n: (0, h)),
                pl.BlockSpec((rows, turned_cols), lambda h, i, n: (0, 0)),
            ),
            scratch_shapes=[pltpu.VMEM((rows, NOPE), F32), pltpu.VMEM((rows, VDIM), F32)],
        ),
        cost_estimate=pl.CostEstimate(
            flops=heads * rows * rows * 1600,
            bytes_accessed=16 * rows * heads * 512,
            transcendentals=heads * rows * rows,
        ),
        compiler_params=pltpu.CompilerParams(vmem_limit_bytes=40 << 20),
        name="attend_back",
    )(length, query, query_rope, kv, kv, key_rope, out_grad, log_totals)


def in_order(values, me, count):
    zero = jnp.zeros_like(values[0])
    ordered = []
    for j in range(count):
        total = zero
        for k in range(count):
            total = jnp.where((me ^ k) == j, values[k], total)
        ordered.append(total)
    return jnp.stack(ordered)


def body(
    lay,
    hidden,
    lengths,
    routes,
    attn_gain,
    w_query,
    w_kv_down,
    kv_gain,
    w_kv_up,
    w_out,
    ffn_gain,
    w_router,
    w_expert_in,
    w_expert_out,
    w_shared_in,
    w_shared_out,
    cotangent,
):
    rows, width = hidden.shape
    nz, nt, nq, ndp = lay.z, lay.t, lay.q, lay.dp
    me_dp = lax.axis_index("dp")
    me_t = lax.axis_index("tensor")
    me_z = me_dp // nq
    me_c = me_dp % nq
    part = width // nt
    d_loc = w_query.shape[0]
    f_loc = w_expert_out.shape[1]
    ffe = f_loc * nt
    heads = w_query.shape[1] // (NOPE + ROPE)
    score_scale = (NOPE + ROPE) ** (-0.5)

    def own_part(values):
        return lax.dynamic_slice_in_dim(values, me_t * part, part, 1)

    def gather_z(values):
        return lax.all_gather(values, "dp", axis=0, tiled=False, axis_index_groups=lay.z_groups)

    def scatter_z(values):
        return lax.psum_scatter(
            values, "dp", scatter_dimension=0, tiled=False, axis_index_groups=lay.z_groups
        )

    def gather_t(values):
        return lax.all_gather(values, "tensor", axis=1, tiled=True)

    def scatter_t(values):
        return lax.psum_scatter(values, "tensor", scatter_dimension=1, tiled=True)

    ids = jnp.stack([me_z, me_c, me_t]).astype(jnp.int32)

    packed = jnp.concatenate(
        [jnp.swapaxes(w_expert_in, 2, 3), w_expert_out[:, None]], 1
    ).reshape(nz, nt, 3, f_loc, d_loc)
    plane = [
        lay.over_t(lax.dynamic_index_in_dim(packed, me_t ^ k, 1, keepdims=False), k)
        for k in range(nt)
    ]
    pieces = jnp.stack(
        [
            lay.over_z(lax.dynamic_index_in_dim(plane[kt], me_z ^ kz, 0, keepdims=False), kz)
            for kt in range(nt)
            for kz in range(nz)
        ]
    )
    own_in, own_out = lay_out_weights(
        lay, ids, [lay.over_c(pieces, k) for k in range(nq)], f_loc, d_loc, width
    )

    lat_loc = kv_gain.shape[0]
    q_rows, down_rows, out_rows = w_query.shape[1], w_kv_down.shape[1], w_out.shape[0]
    half = ROPE // 2

    def by_kind(turned):
        split = turned.reshape(heads, NOPE + ROPE, -1)
        return jnp.concatenate(
            [
                split[:, :NOPE].reshape(heads * NOPE, -1),
                split[:, NOPE : NOPE + half].reshape(heads * half, -1),
                split[:, NOPE + half :].reshape(heads * half, -1),
            ],
            0,
        )

    def by_head(rows_in):
        nope = rows_in[: heads * NOPE].reshape(heads, NOPE, -1)
        first = rows_in[heads * NOPE : heads * (NOPE + half)].reshape(heads, half, -1)
        second = rows_in[heads * (NOPE + half) :].reshape(heads, half, -1)
        return jnp.concatenate([nope, first, second], 1).reshape(heads * (NOPE + ROPE), -1)

    gains = jnp.stack([attn_gain, ffn_gain, jnp.pad(kv_gain, (0, d_loc - lat_loc))])
    front_pack = jnp.concatenate(
        [
            by_kind(jnp.transpose(w_query)),
            jnp.transpose(w_kv_down),
            jnp.transpose(w_router),
            jnp.pad(gains, ((0, 13), (0, 0))),
            w_out,
            w_kv_up.reshape(-1, d_loc),
        ],
        0,
    )
    front = lax.all_gather(front_pack, "dp", axis=0, tiled=False)

    def rows_of(first, count):
        return jnp.swapaxes(front[:, first : first + count], 0, 1).reshape(count, width)

    query_t = rows_of(0, q_rows)
    down_t = rows_of(q_rows, down_rows)
    at = q_rows + down_rows
    router_t = rows_of(at, EXPERTS)
    gain_attn = front[:, at + EXPERTS].reshape(-1)
    gain_ffn = front[:, at + EXPERTS + 1].reshape(-1)
    gain_kv = front[:, at + EXPERTS + 2, :lat_loc].reshape(-1)
    at = at + 2 * EXPERTS
    out_w = rows_of(at, out_rows)
    up_w = front[:, at + out_rows :].reshape(LATENT, heads * (NOPE + VDIM))

    route_own = jnp.pad(jnp.transpose(routes), ((0, -TOP % 8), (0, 0)), constant_values=-1)
    route_all = in_order([lay.over_z(route_own, k) for k in range(nz)], me_z, nz)
    plane_ids = me_z * nt + (me_t ^ jnp.arange(nt, dtype=jnp.int32))
    member = jnp.any(route_all[:, :, :, None] == plane_ids[None, None, None, :], axis=1)
    row_ids = lax.broadcasted_iota(jnp.int32, (rows, rows), 0)
    col_ids = lax.broadcasted_iota(jnp.int32, (rows, rows), 1)
    before = (col_ids < row_ids).astype(BF16)
    position = jnp.einsum("ij,sje->sie", before, member.astype(BF16), preferred_element_type=F32)
    key = jnp.where(member, position.astype(jnp.int32), -1)
    key = jnp.transpose(key, (0, 2, 1))
    slots_iota = lax.broadcasted_iota(jnp.int32, (1, 1, CAP, 1), 2)
    place = (key[:, :, None, :] == slots_iota).astype(BF16)
    own_place = key[:, 0, None, :] == slots_iota[0]

    def dispatch(values):
        picked = jnp.einsum("sepk,skd->espd", place, values, preferred_element_type=F32)
        picked = picked.astype(BF16).reshape(nt, nz * CAP, part)
        return jnp.concatenate([lay.over_t(picked[k], k) for k in range(nt)], 1)

    def send_back(values):
        return [lay.over_t(values[:, k * part : (k + 1) * part], k) for k in range(nt)]

    def combine(parts):
        parts = jnp.stack(parts).reshape(nt, nz, CAP, part)
        summed = jnp.einsum("sepk,espd->skd", place, parts, preferred_element_type=F32)
        return scatter_z(summed.astype(BF16)).astype(F32)

    valid_length = lengths[0]
    valid_rows = lax.broadcasted_iota(jnp.int32, (rows, 1), 0) < valid_length
    cot_low = jnp.where(valid_rows, cotangent, jnp.zeros_like(cotangent))
    cot_part = own_part(cot_low)
    cot_rows = dispatch(gather_z(cot_part))

    cosine, sine = angle_tables(rows)
    wide_cos, wide_sin = jnp.tile(cosine, (1, heads)), jnp.tile(sine, (1, heads))
    inputs = hidden.astype(F32)
    attn_inverse = inverse_rms(inputs)
    attn_scale = gain_attn.astype(F32)
    normed_low = (inputs * attn_inverse * attn_scale).astype(BF16)
    query = dot_nt(normed_low, query_t)
    nope_cols = heads * NOPE
    query_nope = query[:, :nope_cols].astype(BF16)
    query_rope = jnp.concatenate(
        rotate(
            query[:, nope_cols : nope_cols + heads * half],
            query[:, nope_cols + heads * half :],
            wide_cos,
            wide_sin,
        ),
        1,
    ).astype(BF16)
    latent_all = dot_nt(normed_low, down_t)
    latent = latent_all[:, :LATENT]
    kv_inverse = inverse_rms(latent)
    latent_hat = latent * kv_inverse
    kv_scale = gain_kv.astype(F32)
    latent_low = (latent_hat * kv_scale).astype(BF16)
    key_first, key_second = rotate(
        latent_all[:, LATENT : LATENT + half], latent_all[:, LATENT + half :], cosine, sine
    )
    key_rope = jnp.concatenate(
        [jnp.tile(key_first, (1, heads)), jnp.tile(key_second, (1, heads))], 1
    ).astype(BF16)
    keys_values = dot(latent_low, up_w).astype(BF16)
    attended_low, log_totals = attend(
        lengths, query_nope, query_rope, keys_values, key_rope, heads, score_scale
    )
    attn_sum = scatter_t(dot(attended_low, out_w).astype(BF16)).astype(F32)
    residual = own_part(hidden).astype(F32) + attn_sum

    def row_mean(values):
        partial = jnp.sum(values, axis=-1).reshape(-1, 128)
        return lax.psum(partial, "tensor").reshape(-1, 1) * (1.0 / width)

    ffn_inverse = lax.rsqrt(row_mean(residual * residual) + EPSILON)
    ffn_hat = residual * ffn_inverse
    ffn_scale = lax.dynamic_slice_in_dim(gain_ffn, me_t * part, part, 0).astype(F32)
    ffn_part = (ffn_hat * ffn_scale).astype(BF16)

    expert_rows = dispatch(gather_z(ffn_part))
    ffn_low = gather_t(ffn_part)
    router_probs = jax.nn.softmax(dot_nt(ffn_low, router_t), axis=-1)
    probs_turned = jnp.transpose(router_probs).reshape(EXPERTS, -1, 128)
    own_probs = in_order(
        [
            lay.over_z(
                lax.dynamic_index_in_dim(
                    probs_turned, (me_z ^ k) * nt + me_t, 0, keepdims=False
                ),
                k,
            )
            for k in range(nz)
        ],
        me_z,
        nz,
    ).reshape(nz, rows)
    gate_rows = jnp.sum(jnp.where(own_place, own_probs[:, None, :], 0.0), axis=-1).reshape(
        nz * CAP, 1
    )
    gate_up = dot_nt(expert_rows, own_in)
    gate_pre, up_pre = gate_up[:, :ffe], gate_up[:, ffe:]
    gate_sig = jax.nn.sigmoid(gate_pre)
    gate_silu = gate_pre * gate_sig
    active = (gate_silu * up_pre).astype(BF16)
    rows_out = (dot(active, own_out) * gate_rows).astype(BF16)
    out_parts = send_back(rows_out)
    active_grad_raw = dot_nt(cot_rows, own_out)
    gate_grad = jnp.sum(active.astype(F32) * active_grad_raw, axis=-1).reshape(nz, CAP)
    active_grad = active_grad_raw * gate_rows
    pre_low = jnp.concatenate(
        [
            active_grad * up_pre * gate_sig * (1.0 + gate_pre * (1.0 - gate_sig)),
            active_grad * gate_silu,
        ],
        1,
    ).astype(BF16)
    gated_active = (active.astype(F32) * gate_rows).astype(BF16)
    rows_grad = dot(pre_low, own_in).astype(BF16)
    grad_parts = send_back(rows_grad)
    routed = combine(out_parts)
    grad_in_own = dot_tn(pre_low, expert_rows).astype(BF16)
    grad_out_own = dot_tn(gated_active, cot_rows).astype(BF16)
    grad_pieces = take_apart(lay, ids, grad_in_own, grad_out_own, f_loc, d_loc, width)
    grad_parts, grad_pieces = lax.optimization_barrier((grad_parts, grad_pieces))
    routed_grad = combine(grad_parts)

    token_grad = jnp.sum(jnp.where(own_place, gate_grad[:, :, None], 0.0), axis=1)
    token_grad = token_grad.reshape(nz, -1, 128)
    token_plane = jnp.stack(
        [
            lay.over_z(lax.dynamic_index_in_dim(token_grad, me_z ^ k, 0, keepdims=False), k)
            for k in range(nz)
        ]
    )
    token_home = jnp.stack([lay.over_t(token_plane, k) for k in range(nt)])
    experts = jnp.arange(EXPERTS, dtype=jnp.int32)
    came_from = (me_t ^ (experts % nt)) * nz + (me_z ^ (experts // nt))
    probs_grad = lax.dot_general(
        token_home.reshape(EXPERTS, rows),
        (experts[:, None] == came_from[None, :]).astype(F32),
        (((0,), (0,)), ((), ())),
        precision=lax.Precision.HIGHEST,
        preferred_element_type=F32,
    )

    ffs = w_shared_out.shape[0]
    shared_all = lax.all_gather(
        jnp.concatenate([jnp.swapaxes(w_shared_in, 1, 2).reshape(2 * ffs, d_loc), w_shared_out], 0),
        "dp",
        axis=0,
        tiled=False,
    )
    shared_in = jnp.swapaxes(shared_all[:, : 2 * ffs], 0, 1).reshape(2 * ffs, width)
    shared_out = jnp.swapaxes(shared_all[:, 2 * ffs :], 0, 1).reshape(ffs, width)
    shared_pre = dot_nt(ffn_low, shared_in)
    shared_gate, shared_up = shared_pre[:, :ffs], shared_pre[:, ffs:]
    shared_sig = jax.nn.sigmoid(shared_gate)
    shared_silu = shared_gate * shared_sig
    shared_act = (shared_silu * shared_up).astype(BF16)
    shared_part = scatter_t(dot(shared_act, shared_out).astype(BF16)).astype(F32)
    shared_act_grad = dot_nt(cot_low, shared_out)
    shared_pre_grad = jnp.concatenate(
        [
            shared_act_grad * shared_up * shared_sig * (1.0 + shared_gate * (1.0 - shared_sig)),
            shared_act_grad * shared_silu,
        ],
        1,
    ).astype(BF16)
    grad_shared_in = dot_tn(shared_pre_grad, ffn_low)
    grad_shared_out = dot_tn(shared_act, cot_low)
    shared_grad = scatter_t(dot(shared_pre_grad, shared_in).astype(BF16)).astype(F32)

    logits_grad = router_probs * (
        probs_grad - jnp.sum(router_probs * probs_grad, axis=-1, keepdims=True)
    )
    router_part = lax.dot_general(
        logits_grad,
        ffn_low.astype(F32),
        (((0,), (0,)), ((), ())),
        precision=lax.Precision.HIGHEST,
        preferred_element_type=F32,
    )
    router_slice = lax.dynamic_slice_in_dim(router_t, me_t * part, part, 1)
    ffn_grad = (
        shared_grad
        + routed_grad
        + lax.dot_general(
            logits_grad,
            router_slice.astype(F32),
            (((1,), (0,)), ((), ())),
            precision=lax.Precision.HIGHEST,
            preferred_element_type=F32,
        )
    )
    scaled = ffn_scale * ffn_grad
    ffn_gain_part = jnp.sum(ffn_grad * ffn_hat, axis=0)
    residual_grad = cot_part.astype(F32) + ffn_inverse * (
        scaled - ffn_hat * row_mean(ffn_hat * scaled)
    )
    residual_low = gather_t(residual_grad.astype(BF16))

    output = gather_t((residual + routed + shared_part).astype(BF16))

    grad_class = sum(lay.over_c(grad_pieces[k], k).astype(F32) for k in range(nq)).astype(BF16)
    grad_class = grad_class.reshape(nt, nz, 3, f_loc, d_loc)
    grad_plane = [lay.over_z(grad_class[:, k], k) for k in range(nz)]
    grad_home = jnp.stack(
        [lay.over_t(grad_plane[kz][kt], kt) for kt in range(nt) for kz in range(nz)]
    )
    grad_expert_in, grad_expert_out = home_gradients(lay, ids, grad_home, f_loc, d_loc)

    grad_out_w = dot_tn(attended_low, residual_low)
    attended_grad = dot_nt(residual_low, out_w).astype(BF16)
    query_nope_grad, query_turned_grad, kv_grad, rope_grad = attend_back(
        lengths,
        query_nope,
        query_rope,
        keys_values,
        key_rope,
        attended_grad,
        log_totals,
        heads,
        score_scale,
    )
    turned_first, turned_second = rotate_back(
        query_turned_grad[:, : heads * half], query_turned_grad[:, heads * half :], wide_cos, wide_sin
    )
    query_grad = jnp.concatenate(
        [query_nope_grad, turned_first.astype(BF16), turned_second.astype(BF16)], 1
    )
    rope_sum = rope_grad.reshape(rows, 2, heads, half).sum(2)
    key_rope_part = jnp.concatenate(
        rotate_back(rope_sum[:, 0], rope_sum[:, 1], cosine, sine), 1
    )
    latent_part = dot_nt(kv_grad, up_w)
    latent_sum = lax.psum(
        jnp.concatenate([latent_part, key_rope_part], -1).astype(BF16), "tensor"
    ).astype(F32)
    normed_grad_q = scatter_t(dot(query_grad, query_t).astype(BF16)).astype(F32)
    latent_grad, key_rope_grad = latent_sum[:, :LATENT], latent_sum[:, LATENT:]
    grad_kv_gain = jnp.sum(latent_grad * latent_hat, axis=0)
    scaled_kv = kv_scale * latent_grad
    latent_back = kv_inverse * (
        scaled_kv - latent_hat * jnp.mean(latent_hat * scaled_kv, axis=-1, keepdims=True)
    )
    down_grad = jnp.concatenate([latent_back, key_rope_grad], -1).astype(BF16)
    down_slice = lax.dynamic_slice_in_dim(down_t, me_t * part, part, 1)
    normed_grad = normed_grad_q + dot(down_grad, down_slice)
    attn_hat = own_part(hidden).astype(F32) * attn_inverse
    scaled_in = lax.dynamic_slice_in_dim(attn_scale, me_t * part, part, 0) * normed_grad
    attn_gain_part = jnp.sum(normed_grad * attn_hat, axis=0)
    input_grad = residual_grad + attn_inverse * (
        scaled_in - attn_hat * row_mean(attn_hat * scaled_in)
    )
    grad_hidden = gather_t(input_grad.astype(BF16))

    def sum_dp(values):
        return lax.psum_scatter(values, "dp", scatter_dimension=0, tiled=False).astype(F32)

    def by_owner(values):
        return jnp.swapaxes(values.astype(BF16).reshape(-1, ndp, d_loc), 0, 1)

    gain_parts = lax.all_gather(
        jnp.concatenate([attn_gain_part[None], ffn_gain_part[None]], 0), "tensor", axis=1, tiled=True
    )
    kv_gain_row = jnp.pad(
        grad_kv_gain.reshape(ndp, lat_loc), ((0, 0), (0, d_loc - lat_loc))
    ).reshape(1, width)
    front_sum = sum_dp(
        jnp.concatenate(
            [
                by_owner(dot_tn(query_grad, normed_low)),
                by_owner(dot_tn(down_grad, normed_low)),
                by_owner(router_part),
                by_owner(jnp.pad(jnp.concatenate([gain_parts, kv_gain_row], 0), ((0, 13), (0, 0)))),
                by_owner(grad_out_w),
                dot_tn(latent_low, kv_grad).astype(BF16).reshape(ndp, -1, d_loc),
            ],
            1,
        )
    )
    shared_sum = sum_dp(
        jnp.concatenate([by_owner(grad_shared_in), by_owner(grad_shared_out)], 1)
    )
    at = q_rows + down_rows
    gain_rows = front_sum[at + EXPERTS : at + EXPERTS + 3]
    return (
        output,
        grad_hidden,
        gain_rows[0],
        jnp.transpose(by_head(front_sum[:q_rows])),
        jnp.transpose(front_sum[q_rows:at]),
        gain_rows[2, :lat_loc],
        front_sum[at + 2 * EXPERTS + out_rows :].reshape(w_kv_up.shape),
        front_sum[at + 2 * EXPERTS : at + 2 * EXPERTS + out_rows],
        gain_rows[1],
        jnp.transpose(front_sum[at : at + EXPERTS]),
        grad_expert_in,
        grad_expert_out,
        jnp.swapaxes(shared_sum[: 2 * ffs].reshape(2, ffs, d_loc), 1, 2),
        shared_sum[2 * ffs :],
    )


def solution(mesh):
    return jax.shard_map(
        functools.partial(body, Layout(mesh.shape["dp"], mesh.shape["tensor"])),
        mesh=mesh,
        in_specs=(
            P("dp", None),
            P("dp"),
            P("dp", None),
            P("dp"),
            P("dp", "tensor"),
            P("dp", None),
            P("dp"),
            P("dp", "tensor"),
            P("tensor", "dp"),
            P("dp"),
            P("dp", None),
            P(None, None, "dp", "tensor"),
            P(None, "tensor", "dp"),
            P(None, "dp", "tensor"),
            P("tensor", "dp"),
            P("dp", None),
        ),
        out_specs=(
            P("dp", None),
            P("dp", None),
            P("dp"),
            P("dp", "tensor"),
            P("dp", None),
            P("dp"),
            P("dp", "tensor"),
            P("tensor", "dp"),
            P("dp"),
            P("dp", None),
            P(None, None, "dp", "tensor"),
            P(None, "tensor", "dp"),
            P(None, "dp", "tensor"),
            P("tensor", "dp"),
        ),
        check_vma=False,
    )
```

time: 3820 us -> 1960 us (0.51)
  waiting for transfers between devices: 1870 us -> 1180 us
  other arithmetic: 597 us -> 73 us
  matrix products: 705 us -> 320 us
  local copies, waits for them, and re-layouts: 530 us -> 178 us
  Pallas kernels: 0 us -> 80.9 us
  starting transfers between devices: 1.46 us -> 66 us
  blocking collectives: 75.8 us -> 33.4 us
    ppermute x0 -> x56, waiting for transfers between devices: none -> 892 us  [the longest x24 533 us: over_z(): lax.ppermute(values, 'dp', [(d, d ^ k * self.q) for d in range(self.dp)])]
    reduce_scatter x9 -> x8, waiting for transfers between devices: 838 us -> 122 us  [the longest x2 61.6 us: scatter_z(): lax.psum_scatter(values, 'dp', scatter_dimension=0, tiled=False, axis_ind...]
    all_gather x8, waiting for transfers between devices: 680 us -> 139 us  [the longest x1 79.8 us: body(): front = lax.all_gather(front_pack, 'dp', axis=0, tiled=False)]
    scatter-add x32 -> x0, other arithmetic: 496 us -> none  [the longest x16 249 us: expert_forward(): routed_pad = routed_pad.at[source_rows].add(gate_row[:, None] * out_rows)]
    gather x49 -> x0, local copies, waits for them, and re-layouts: 404 us -> none  [the longest x16 141 us: expert_backward(): cot_rows = cot_pad[source_rows]]
    dot_general x155 -> x33, matrix products: 705 us -> 320 us  [the longest x9 92.5 us: dot_nt(): lax.dot_general(a, b, (((1,), (1,)), ((), ())), preferred_element_type=F32)]
    psum x4 -> x1, waiting for transfers between devices: 345 us -> 29.6 us  [body(): lax.psum(jnp.concatenate([latent_part, key_rope_part], -1).astype(BF16),...]
    pallas_call x0 -> x5, Pallas kernels: none -> 80.9 us  [the longest x1 21.7 us: attend_back(): pl.pallas_call(kernel, out_shape=(jax.ShapeDtypeStruct((rows, heads * NOP...]
  transfers between devices with their start and end apart: 21 -> 73, of which waited for: 19 -> 43; matrix products, arithmetic and copies ran while one was open for 7% -> 23% of each run, Pallas kernels for 0% -> 2%
where the time goes in v1:
time: 1960 us; the launch traced here: 1950 us
  waiting for transfers between devices  1180 us (60%)
  matrix products  320 us (16%)
  local copies, waits for them, and re-layouts  178 us (9%)
  Pallas kernels  80.9 us (4%)
  other arithmetic  73 us (4%)
  starting transfers between devices  66 us (3%)
  blocking collectives  33.4 us (2%)
    ppermute x24, waiting for transfers between devices, over_z(): lax.ppermute(values, 'dp', [(d, d ^ k * self.q) for d in range(self.dp)])  533 us
    ppermute x30, waiting for transfers between devices, over_t(): return lax.ppermute(values, 'tensor', [(i, i ^ k) for i in range(self.t)])  345 us
    dot_general x9, matrix products, dot_nt(): lax.dot_general(a, b, (((1,), (1,)), ((), ())), preferred_element_type=F32)  92.5 us
    dot_general x8, matrix products, dot_tn(): lax.dot_general(a, b, (((0,), (0,)), ((), ())), preferred_element_type=F32)  82.5 us
    dot_general x8, matrix products, dot(): return jnp.dot(a, b, preferred_element_type=F32)  82.5 us
    unnamed x239, local copies, waits for them, and re-layouts  82.2 us
    all_gather x1, waiting for transfers between devices, body(): front = lax.all_gather(front_pack, 'dp', axis=0, tiled=False)  79.8 us
    reduce_scatter x2, waiting for transfers between devices, scatter_z(): lax.psum_scatter(values, 'dp', scatter_dimension=0, tiled=False, axis_ind...  61.6 us
  transfers between devices with their start and end apart: 73, of which 43 were waited for; matrix products, arithmetic and copies ran while one was open for 23% of the time, Pallas kernels for 2%

profile of v1, /device:TPU:10, one launch (start us, length us, event | category | flops | bytes accessed | tf_op | source)
XLA Modules:
  0.0 1953.1 jit_solution(9576835934293964071)
XLA Ops:
  20.3 79.8 %all-gather.21.cloned.1.call-done = bf16[17152,256]{1,0:T(8,128)(2,1)} async-done(((bf16[2144,256]{1,0:T(8,128)(2,1)}), bf16[17152,256]{1,0:T(8,128)(2,1)}) %all-gather.21.cloned.1.call-update) | async-done | bytes 8781840 | tf_op jit(solution)/shard_map/all_gather | solution.py:472
  127.4 8.3 fusion.129
  152.5 14.6 attend.1
  202.2 42.2 %collective-permute-done.6 = bf16[3,352,256]{2,1,0:T(8,128)(2,1)} collective-permute-done((bf16[3,352,256]{2,1,0:T(8,128)(2,1)}, bf16[3,352,256]{2,1,0:T(8,128)(2,1)}, u32[]{:S(2)}, u32[]{:S(2)}) %collective-permute-start.6) | collective-permute-done | bytes 540704 | tf_op jit(solution)/shard_map/ppermute | solution.py:73
  249.2 50.7 %collective-permute-done.8 = bf16[3,352,256]{2,1,0:T(8,128)(2,1)} collective-permute-done((bf16[3,352,256]{2,1,0:T(8,128)(2,1)}, bf16[3,352,256]{2,1,0:T(8,128)(2,1)}, u32[]{:S(2)}, u32[]{:S(2)}) %collective-permute-start.8) | collective-permute-done | bytes 540704 | tf_op jit(solution)/shard_map/ppermute | solution.py:73
  309.3 35.5 %collective-permute-done.10 = bf16[3,352,256]{2,1,0:T(8,128)(2,1)S(1)} collective-permute-done((bf16[3,352,256]{2,1,0:T(8,128)(2,1)S(1)}, bf16[3,352,256]{2,1,0:T(8,128)(2,1)S(1)}, u32[]{:S(2)}, u32[]{:S(2)}) %collective-permute-start.10) | collective-permute-done | bytes 540704 | tf_op jit(solution)/shard_map/ppermute | solution.py:73
  346.5 45.5 %collective-permute-done.12 = bf16[3,352,256]{2,1,0:T(8,128)(2,1)S(1)} collective-permute-done((bf16[3,352,256]{2,1,0:T(8,128)(2,1)S(1)}, bf16[3,352,256]{2,1,0:T(8,128)(2,1)S(1)}, u32[]{:S(2)}, u32[]{:S(2)}) %collective-permute-start.12) | collective-permute-done | bytes 540704 | tf_op jit(solution)/shard_map/ppermute | solution.py:73
  399.1 25.6 %collective-permute-done.14 = bf16[3,352,256]{2,1,0:T(8,128)(2,1)S(1)} collective-permute-done((bf16[3,352,256]{2,1,0:T(8,128)(2,1)S(1)}, bf16[3,352,256]{2,1,0:T(8,128)(2,1)S(1)}, u32[]{:S(2)}, u32[]{:S(2)}) %collective-permute-start.14) | collective-permute-done | bytes 540704 | tf_op jit(solution)/shard_map/ppermute | solution.py:73
  425.5 27.2 %collective-permute-done.15 = bf16[3,352,256]{2,1,0:T(8,128)(2,1)S(1)} collective-permute-done((bf16[3,352,256]{2,1,0:T(8,128)(2,1)S(1)}, bf16[3,352,256]{2,1,0:T(8,128)(2,1)S(1)}, u32[]{:S(2)}, u32[]{:S(2)}) %collective-permute-start.15) | collective-permute-done | bytes 540704 | tf_op jit(solution)/shard_map/ppermute | solution.py:73
  455.5 8.5 psum.28
  478.0 17.1 collective-permute-done.18
  496.0 16.4 collective-permute-done.19
  513.2 11.1 collective-permute-done.20
  532.5 15.0 convert_bitcast_fusion
  550.2 16.5 lay_out_weights.1
  569.3 5.6 slice_bitcast_fusion
  574.9 8.3 copy.181
  596.8 6.0 all-gather.23.cloned.1.call-done
  602.9 14.9 convert_bitcast_fusion.1
  624.0 9.6 fusion.140
  633.6 5.4 multiply_convert_fusion.5
  640.7 8.4 convolution_convert_fusion.4
  651.3 32.3 %collective-permute-done.3 = bf16[2048,512]{1,0:T(8,128)(2,1)} collective-permute-done((bf16[2048,512]{1,0:T(8,128)(2,1)}, bf16[2048,512]{1,0:T(8,128)(2,1)}, u32[]{:S(2)}, u32[]{:S(2)}) %collective-permute-start.3) | collective-permute-done | bytes 2097184 | tf_op jit(solution)/shard_map/ppermute | solution.py:68
  686.4 52.8 %collective-permute-done.5 = bf16[2048,512]{1,0:T(8,128)(2,1)} collective-permute-done((bf16[2048,512]{1,0:T(8,128)(2,1)}, bf16[2048,512]{1,0:T(8,128)(2,1)}, u32[]{:S(2)}, u32[]{:S(2)}) %collective-permute-start.5) | collective-permute-done | bytes 2097184 | tf_op jit(solution)/shard_map/ppermute | solution.py:68
  739.1 32.5 %fusion.61 = f32[2048,2816]{1,0:T(8,128)} fusion(bf16[2816,2048]{1,0:T(8,128)(2,1)} %bitcast.583, bf16[2048,512]{1,0:T(8,128)(2,1)} %collective-permute-done.5, bf16[2048,512]{1,0:T(8,128)(2,1)} %collective-permute-done.4, bf16[2048,512]{1,0:T(8,128)(2,1)} %collective-permute-done.3, bf16[2048,512]{1,0:T(8,128)(2,1)} %bitcast.523), kind=kOutput, calls=%fused_computation.136 | convolution fusion | flops 23655874560 | bytes 42991616 | tf_op jit(solution)/shard_map/dot_general | solution.py:30
  771.6 22.8 %collective-permute-done.28 = bf16[2048,512]{1,0:T(8,128)(2,1)} collective-permute-done((bf16[2048,512]{1,0:T(8,128)(2,1)}, bf16[2048,512]{1,0:T(8,128)(2,1)}, u32[]{:S(2)}, u32[]{:S(2)}) %collective-permute-start.28) | collective-permute-done | bytes 2097184 | tf_op jit(solution)/shard_map/ppermute | solution.py:68
  794.4 43.0 %collective-permute-done.29 = bf16[2048,512]{1,0:T(8,128)(2,1)} collective-permute-done((bf16[2048,512]{1,0:T(8,128)(2,1)}, bf16[2048,512]{1,0:T(8,128)(2,1)}, u32[]{:S(2)}, u32[]{:S(2)}) %collective-permute-start.29) | collective-permute-done | bytes 2097184 | tf_op jit(solution)/shard_map/ppermute | solution.py:68
  839.0 23.1 %fusion.9 = (f32[2048]{0:T(1024)S(1)}, bf16[2048,1408]{1,0:T(8,128)(2,1)}, f32[2048,1408]{1,0:T(8,128)}) fusion(f32[2048,2816]{1,0:T(8,128)} %fusion.61, bf16[1408,2048]{1,0:T(8,128)(2,1)} %copy-done.7, bf16[2048,512]{1,0:T(8,128)(2,1)} %collective-permute-done.30, bf16[2048,512]{1,0:T(8,128)(2,1)} %collective-permute-done.29, ...), kind=kOutput, calls=%fused_computation.14 | convolution fusion | flops 11870664704 | bytes 54534144 | tf_op jit(solution)/shard_map/dot_general | solution.py:30
  864.9 15.9 multiply_convert_fusion.2
  880.8 30.6 %convolution_convert_fusion.3 = bf16[2048,2048]{1,0:T(8,128)(2,1)S(1)} fusion(bf16[2816,2048]{1,0:T(8,128)(2,1)} %bitcast.584, bf16[2048,1408]{1,0:T(8,128)(2,1)} %get-tuple-element.105, bf16[2048,1408]{1,0:T(8,128)(2,1)S(1)} %get-tuple-element.104), kind=kOutput, calls=%fused_computation.53 | convolution fusion | flops 23649583104 | bytes 31457280 | tf_op jit(solution)/shard_map/dot_general | solution.py:26
  917.8 32.1 %convolution_convert_fusion = bf16[2816,2048]{1,0:T(8,128)(2,1)} fusion(bf16[2048,1408]{1,0:T(8,128)(2,1)} %get-tuple-element.105, bf16[2048,1408]{1,0:T(8,128)(2,1)} %copy-done.30, bf16[2048,512]{1,0:T(8,128)(2,1)} %collective-permute-done.5, bf16[2048,512]{1,0:T(8,128)(2,1)} %collective-permute-done.4, bf16[2048,512]{1,0:T(8,128)(2,1)} %collective-permute-done.3, ...), kind=kOutput, calls=%fused_computation.21 | convolution fusion | flops 23684710400 | bytes 31457280 | tf_op jit(solution)/shard_map/dot_general | solution.py:34
  949.9 20.1 %convolution_convert_fusion.2.out_ref = bf16[1408,2048]{1,0:T(8,128)(2,1)} fusion(bf16[2048,1408]{1,0:T(8,128)(2,1)} %get-tuple-element.103, f32[2048]{0:T(1024)S(1)} %bitcast.555, bf16[2048,512]{1,0:T(8,128)(2,1)} %collective-permute-done.30, bf16[2048,512]{1,0:T(8,128)(2,1)} %collective-permute-done.29, bf16[2048,512]{1,0:T(8,128)(2,1)} %collective-permute-done.28, ...), kind=kOutput, calls=%fused_computation.52 | convolution fusion | flops 11856248832 | bytes 19931136 | tf_op jit(solution)/shard_map/dot_general | solution.py:34
  972.6 13.6 take_apart.1
  986.3 20.1 %collective-permute-done.32 = bf16[2048,512]{1,0:T(8,128)(2,1)} collective-permute-done((bf16[2048,512]{1,0:T(8,128)(2,1)}, bf16[2048,512]{1,0:T(8,128)(2,1)}, u32[]{:S(2)}, u32[]{:S(2)}) %collective-permute-start.32) | collective-permute-done | bytes 2097184 | tf_op jit(solution)/shard_map/ppermute | solution.py:68
  1010.2 11.3 bitcast_convert_fusion
  1022.9 6.8 convolution_convert_fusion.5
  1029.8 17.3 multiply_convert_fusion
  1051.7 45.1 %collective-permute-done.25 = bf16[2048,512]{1,0:T(8,128)(2,1)S(1)} collective-permute-done((bf16[2048,512]{1,0:T(8,128)(2,1)S(1)}, bf16[2048,512]{1,0:T(8,128)(2,1)S(1)}, u32[]{:S(2)}, u32[]{:S(2)}) %collective-permute-start.25) | collective-permute-done | bytes 2097184 | tf_op jit(solution)/shard_map/ppermute | solution.py:68
  1096.8 14.2 collective-permute-done.26
  1111.0 51.3 %collective-permute-done.27 = bf16[2048,512]{1,0:T(8,128)(2,1)S(1)} collective-permute-done((bf16[2048,512]{1,0:T(8,128)(2,1)S(1)}, bf16[2048,512]{1,0:T(8,128)(2,1)S(1)}, u32[]{:S(2)}, u32[]{:S(2)}) %collective-permute-start.27) | collective-permute-done | bytes 2097184 | tf_op jit(solution)/shard_map/ppermute | solution.py:68
  1163.4 11.3 bitcast_convert_fusion.1
  1189.2 5.5 multiply_reduce_fusion
  1194.8 8.8 psum.29
  1203.6 61.6 %reduce-scatter.11.cloned.1.call-done = bf16[1,1024,512]{2,1,0:T(8,128)(2,1)} async-done(((bf16[4,1024,512]{2,1,0:T(8,128)(2,1)}), bf16[1,1024,512]{2,1,0:T(8,128)(2,1)}) %reduce-scatter.11.cloned.1.call-update) | async-done | bytes 1048592 | tf_op jit(solution)/shard_map/reduce_scatter | solution.py:409
  1270.0 52.9 %all-gather.17.cloned.1.call-done = bf16[1024,2048]{1,0:T(8,128)(2,1)} async-done(((bf16[1024,512]{1,0:T(8,128)(2,1)}), bf16[1024,2048]{1,0:T(8,128)(2,1)}) %all-gather.17.cloned.1.call-update) | async-done | bytes 4194320 | tf_op jit(solution)/shard_map/all_gather | solution.py:414
  1322.9 5.2 convolution_convert_fusion.16.do_ref
  1333.4 21.7 %attend_back.1 = (bf16[1024,512]{1,0:T(8,128)(2,1)S(1)}, f32[1024,256]{1,0:T(8,128)S(1)}, bf16[1024,1024]{1,0:T(8,128)(2,1)S(1)}, f32[1024,256]{1,0:T(8,128)S(1)}) custom-call(s32[1]{0:T(128)} %copy.304.len_ref, bf16[1024,512]{1,0:T(8,128)(2,1)S(1)} %slice.545.q_ref, bf16[1024,256]{1,0:T(8,128)(2,1)S(1)} %copy-done.3, bf16[1024,1024]{1,0:T(8,128)(2,1)S(1)} %copy-done.9, ...), custom_call_target="tpu_custom_call" | custom-call | flops 6710886400 | bytes 33554432 | tf_op jit(solution)/shard_map/attend_back/pallas_call | solution.py:321
  1364.4 7.0 convolution_convert_fusion.7
  1372.9 9.4 convolution_convert_fusion.1
  1394.7 29.6 %all-reduce.7.cloned.1.call-done = bf16[1024,576]{0,1:T(8,128)(2,1)} async-done(((bf16[1024,576]{0,1:T(8,128)(2,1)}), bf16[1024,576]{0,1:T(8,128)(2,1)}) %all-reduce.7.cloned.1.call-update) | async-done | bytes 1179664 | tf_op jit(solution)/shard_map/psum | solution.py:723
  1431.2 60.7 %reduce-scatter.19.cloned.1.call-done = bf16[1024,512]{1,0:T(8,128)(2,1)} async-done(((bf16[1024,2048]{1,0:T(8,128)(2,1)}), bf16[1024,512]{1,0:T(8,128)(2,1)}) %reduce-scatter.19.cloned.1.call-update) | async-done | bytes 1048592 | tf_op jit(solution)/shard_map/reduce_scatter | solution.py:417
  1491.9 5.3 fusion.53
  1497.2 8.2 psum.31
  1517.4 6.4 convolution_convert_fusion.8
  1538.8 8.0 all_gather.51
  1550.1 13.7 collective-permute-done.40
  1563.8 5.6 add_convert_fusion
  1576.6 123.7 %collective-permute-done.41 = bf16[4,3,352,256]{3,2,1,0:T(8,128)(2,1)S(1)} collective-permute-done((bf16[4,3,352,256]{3,2,1,0:T(8,128)(2,1)S(1)}, bf16[4,3,352,256]{3,2,1,0:T(8,128)(2,1)S(1)}, u32[]{:S(2)}, u32[]{:S(2)}) %collective-permute-start.41) | collective-permute-done | bytes 2162720 | tf_op jit(solution)/shard_map/ppermute | solution.py:73
  1705.3 128.1 %collective-permute-done.43 = bf16[4,3,352,256]{3,2,1,0:T(8,128)(2,1)S(1)} collective-permute-done((bf16[4,3,352,256]{3,2,1,0:T(8,128)(2,1)S(1)}, bf16[4,3,352,256]{3,2,1,0:T(8,128)(2,1)S(1)}, u32[]{:S(2)}, u32[]{:S(2)}) %collective-permute-start.43) | collective-permute-done | bytes 2162720 | tf_op jit(solution)/shard_map/ppermute | solution.py:73
  1839.5 9.0 collective-permute-done.46
  1850.9 8.0 collective-permute-done.47
  1865.8 27.1 %collective-permute-done.50 = bf16[3,352,256]{2,1,0:T(8,128)(2,1)S(1)} collective-permute-done((bf16[3,352,256]{2,1,0:T(8,128)(2,1)S(1)}, bf16[3,352,256]{2,1,0:T(8,128)(2,1)S(1)}, u32[]{:S(2)}, u32[]{:S(2)}) %collective-permute-start.50) | collective-permute-done | bytes 540704 | tf_op jit(solution)/shard_map/ppermute | solution.py:68
  1895.2 13.3 collective-permute-done.51
  1912.8 14.5 home_gradients.1
  (506 shorter events, 333.1 us)
Async XLA Ops:
  8.0 92.1 %all-gather.21.cloned.1.call-start = ((), (), s32[]{:S(2)}) async-start(), calls=%async_computation.21 | async-start | bytes 9879552 | tf_op jit(solution)/shard_map/all_gather | solution.py:472
  16.0 437.6 %reduce-scatter.9.cloned.1.call-start = ((), (), s32[]{:S(2)}) async-start(), calls=%async_computation.8 | async-start | bytes 5242880 | tf_op jit(solution)/shard_map/reduce_scatter | solution.py:417
  174.7 357.8 %all-gather.27.cloned.1.call-start = ((), (), s32[]{:S(2)}) async-start(), calls=%async_computation.24 | async-start | bytes 5242880 | tf_op jit(solution)/shard_map/all_gather | solution.py:406
  180.6 388.7 %all-gather.25.cloned.1.call-start = ((), (), s32[]{:S(2)}) async-start(), calls=%async_computation.23 | async-start | bytes 9732096 | tf_op jit(solution)/shard_map/all_gather | solution.py:634
  181.7 406.3 %all-gather.13.cloned.1.call-start = ((), (), s32[]{:S(2)}) async-start(), calls=%async_computation.9 | async-start | bytes 5242880 | tf_op jit(solution)/shard_map/all_gather | solution.py:414
  192.0 109.8 %collective-permute-start.9 = (bf16[4,3,352,256]{3,2,1,0:T(8,128)(2,1)}, bf16[4,3,352,256]{3,2,1,0:T(8,128)(2,1)}, u32[]{:S(2)}, u32[]{:S(2)}) collective-permute-start(bf16[4,3,352,256]{3,2,1,0:T(8,128)(2,1)} %get-tuple-element.118), channel_id=1, source_target_pairs={{0,1},{1,0},{2,3},{3,2},{4,5},{5,4},{6,7},{7,6},{8,9},{9,8},{10,11... | collective-permute-start | bytes 6488072 | tf_op jit(solution)/shard_map/ppermute | solution.py:68
  194.9 49.6 %collective-permute-start.6 = (bf16[3,352,256]{2,1,0:T(8,128)(2,1)}, bf16[3,352,256]{2,1,0:T(8,128)(2,1)}, u32[]{:S(2)}, u32[]{:S(2)}) collective-permute-start(bf16[3,352,256]{2,1,0:T(8,128)(2,1)} %get-tuple-element.121), channel_id=1, source_target_pairs={{0,8},{4,12},{8,0},{12,4},{16,24},{20,28},{24,16},{28,20},{1,9},{5... | collective-permute-start | bytes 1622024 | tf_op jit(solution)/shard_map/ppermute | solution.py:73
  197.4 49.9 %collective-permute-start.7 = (bf16[3,352,256]{2,1,0:T(8,128)(2,1)}, bf16[3,352,256]{2,1,0:T(8,128)(2,1)}, u32[]{:S(2)}, u32[]{:S(2)}) collective-permute-start(bf16[3,352,256]{2,1,0:T(8,128)(2,1)} %get-tuple-element.120), channel_id=1, source_target_pairs={{0,16},{4,20},{8,24},{12,28},{16,0},{20,4},{24,8},{28,12},{1,17},{... | collective-permute-start | bytes 1622024 | tf_op jit(solution)/shard_map/ppermute | solution.py:73
  198.6 101.4 %collective-permute-start.8 = (bf16[3,352,256]{2,1,0:T(8,128)(2,1)}, bf16[3,352,256]{2,1,0:T(8,128)(2,1)}, u32[]{:S(2)}, u32[]{:S(2)}) collective-permute-start(bf16[3,352,256]{2,1,0:T(8,128)(2,1)} %get-tuple-element.119), channel_id=1, source_target_pairs={{0,24},{4,28},{8,16},{12,20},{16,8},{20,12},{24,0},{28,4},{1,25},{... | collective-permute-start | bytes 1622024 | tf_op jit(solution)/shard_map/ppermute | solution.py:73
  198.8 194.0 %collective-permute-start.13 = (bf16[4,3,352,256]{3,2,1,0:T(8,128)(2,1)}, bf16[4,3,352,256]{3,2,1,0:T(8,128)(2,1)}, u32[]{:S(2)}, u32[]{:S(2)}) collective-permute-start(bf16[4,3,352,256]{3,2,1,0:T(8,128)(2,1)} %get-tuple-element.117), channel_id=1, source_target_pairs={{0,2},{1,3},{2,0},{3,1},{4,6},{5,7},{6,4},{7,5},{8,10},{9,11},{10,... | collective-permute-start | bytes 6488072 | tf_op jit(solution)/shard_map/ppermute | solution.py:68
  304.3 40.5 %collective-permute-start.10 = (bf16[3,352,256]{2,1,0:T(8,128)(2,1)S(1)}, bf16[3,352,256]{2,1,0:T(8,128)(2,1)S(1)}, u32[]{:S(2)}, u32[]{:S(2)}) collective-permute-start(bf16[3,352,256]{2,1,0:T(8,128)(2,1)S(1)} %get-tuple-element.166), channel_id=1, source_target_pairs={{0,8},{4,12},{8,0},{12,4},{16,24},{20,28},{24,16},{28,20},{1,9},{5... | collective-permute-start | bytes 1622024 | tf_op jit(solution)/shard_map/ppermute | solution.py:73
  304.3 41.4 %collective-permute-start.11 = (bf16[3,352,256]{2,1,0:T(8,128)(2,1)S(1)}, bf16[3,352,256]{2,1,0:T(8,128)(2,1)S(1)}, u32[]{:S(2)}, u32[]{:S(2)}) collective-permute-start(bf16[3,352,256]{2,1,0:T(8,128)(2,1)S(1)} %get-tuple-element.165), channel_id=1, source_target_pairs={{0,16},{4,20},{8,24},{12,28},{16,0},{20,4},{24,8},{28,12},{1,17},{... | collective-permute-start | bytes 1622024 | tf_op jit(solution)/shard_map/ppermute | solution.py:73
  306.0 86.1 %collective-permute-start.12 = (bf16[3,352,256]{2,1,0:T(8,128)(2,1)S(1)}, bf16[3,352,256]{2,1,0:T(8,128)(2,1)S(1)}, u32[]{:S(2)}, u32[]{:S(2)}) collective-permute-start(bf16[3,352,256]{2,1,0:T(8,128)(2,1)S(1)} %get-tuple-element.164), channel_id=1, source_target_pairs={{0,24},{4,28},{8,16},{12,20},{16,8},{20,12},{24,0},{28,4},{1,25},{... | collective-permute-start | bytes 1622024 | tf_op jit(solution)/shard_map/ppermute | solution.py:73
  307.8 164.3 %collective-permute-start.17 = (bf16[4,3,352,256]{3,2,1,0:T(8,128)(2,1)S(1)}, bf16[4,3,352,256]{3,2,1,0:T(8,128)(2,1)}, u32[]{:S(2)}, u32[]{:S(2)}) collective-permute-start(bf16[4,3,352,256]{3,2,1,0:T(8,128)(2,1)S(1)} %get-tuple-element.116), channel_id=1, source_target_pairs={{0,3},{1,2},{2,1},{3,0},{4,7},{5,6},{6,5},{7,4},{8,11},{9,10},{10,... | collective-permute-start | bytes 6488072 | tf_op jit(solution)/shard_map/ppermute | solution.py:68
  395.6 29.1 %collective-permute-start.14 = (bf16[3,352,256]{2,1,0:T(8,128)(2,1)S(1)}, bf16[3,352,256]{2,1,0:T(8,128)(2,1)S(1)}, u32[]{:S(2)}, u32[]{:S(2)}) collective-permute-start(bf16[3,352,256]{2,1,0:T(8,128)(2,1)S(1)} %get-tuple-element.162), channel_id=1, source_target_pairs={{0,8},{4,12},{8,0},{12,4},{16,24},{20,28},{24,16},{28,20},{1,9},{5... | collective-permute-start | bytes 1622024 | tf_op jit(solution)/shard_map/ppermute | solution.py:73
  395.6 57.1 %collective-permute-start.15 = (bf16[3,352,256]{2,1,0:T(8,128)(2,1)S(1)}, bf16[3,352,256]{2,1,0:T(8,128)(2,1)S(1)}, u32[]{:S(2)}, u32[]{:S(2)}) collective-permute-start(bf16[3,352,256]{2,1,0:T(8,128)(2,1)S(1)} %get-tuple-element.161), channel_id=1, source_target_pairs={{0,16},{4,20},{8,24},{12,28},{16,0},{20,4},{24,8},{28,12},{1,17},{... | collective-permute-start | bytes 1622024 | tf_op jit(solution)/shard_map/ppermute | solution.py:73
  396.6 73.6 %collective-permute-start.16 = (bf16[3,352,256]{2,1,0:T(8,128)(2,1)}, bf16[3,352,256]{2,1,0:T(8,128)(2,1)}, u32[]{:S(2)}, u32[]{:S(2)}) collective-permute-start(bf16[3,352,256]{2,1,0:T(8,128)(2,1)} %get-tuple-element.160), channel_id=1, source_target_pairs={{0,24},{4,28},{8,16},{12,20},{16,8},{20,12},{24,0},{28,4},{1,25},{... | collective-permute-start | bytes 1622024 | tf_op jit(solution)/shard_map/ppermute | solution.py:73
  467.6 135.3 %all-gather.23.cloned.1.call-start = ((), (), s32[]{:S(2)}) async-start(), calls=%async_computation.22 | async-start | bytes 5242880 | tf_op jit(solution)/shard_map/all_gather | solution.py:406
  474.6 20.6 %collective-permute-start.18 = (bf16[3,352,256]{2,1,0:T(8,128)(2,1)S(1)}, bf16[3,352,256]{2,1,0:T(8,128)(2,1)S(1)}, u32[]{:S(2)}, u32[]{:S(2)}) collective-permute-start(bf16[3,352,256]{2,1,0:T(8,128)(2,1)S(1)} %get-tuple-element.158), channel_id=1, source_target_pairs={{0,8},{4,12},{8,0},{12,4},{16,24},{20,28},{24,16},{28,20},{1,9},{5... | collective-permute-start | bytes 1622024 | tf_op jit(solution)/shard_map/ppermute | solution.py:73
  476.5 35.9 %collective-permute-start.19 = (bf16[3,352,256]{2,1,0:T(8,128)(2,1)S(1)}, bf16[3,352,256]{2,1,0:T(8,128)(2,1)S(1)}, u32[]{:S(2)}, u32[]{:S(2)}) collective-permute-start(bf16[3,352,256]{2,1,0:T(8,128)(2,1)S(1)} %get-tuple-element.157), channel_id=1, source_target_pairs={{0,16},{4,20},{8,24},{12,28},{16,0},{20,4},{24,8},{28,12},{1,17},{... | collective-permute-start | bytes 1622024 | tf_op jit(solution)/shard_map/ppermute | solution.py:73
  476.5 47.8 %collective-permute-start.20 = (bf16[3,352,256]{2,1,0:T(8,128)(2,1)S(1)}, bf16[3,352,256]{2,1,0:T(8,128)(2,1)S(1)}, u32[]{:S(2)}, u32[]{:S(2)}) collective-permute-start(bf16[3,352,256]{2,1,0:T(8,128)(2,1)S(1)} %get-tuple-element.156), channel_id=1, source_target_pairs={{0,24},{4,28},{8,16},{12,20},{16,8},{20,12},{24,0},{28,4},{1,25},{... | collective-permute-start | bytes 1622024 | tf_op jit(solution)/shard_map/ppermute | solution.py:73
  525.2 25.1 %collective-permute-start.21 = (bf16[16,3,352,256]{3,2,1,0:T(8,128)(2,1)}, bf16[16,3,352,256]{3,2,1,0:T(8,128)(2,1)}, u32[]{:S(2)}, u32[]{:S(2)}) collective-permute-start(bf16[16,3,352,256]{3,2,1,0:T(8,128)(2,1)} %bitcast_dynamic-update-slice_fusion.12.refs_0_), channel_id=1, source_target_pairs={{0,4},{4,0},{8,12},{12,8},{16,20},{20,16},{24,28},{28,24},{1,5},{5... | collective-permute-start | bytes 25952264 | tf_op jit(solution)/shard_map/ppermute | solution.py:78
  525.2 664.0 %reduce-scatter.15.cloned.1.call-start = ((), (), s32[]{:S(2)}) async-start(), calls=%async_computation.13 | async-start | bytes 5242880 | tf_op jit(solution)/shard_map/reduce_scatter | solution.py:417
  592.7 46.3 %collective-permute-start.22 = (f32[8,128]{1,0:T(8,128)S(1)}, f32[8,128]{1,0:T(8,128)S(1)}, u32[]{:S(2)}, u32[]{:S(2)}) collective-permute-start(f32[8,128]{1,0:T(8,128)S(1)} %get-tuple-element.189), channel_id=1, source_target_pairs={{0,24},{4,28},{8,16},{12,20},{16,8},{20,12},{24,0},{28,4},{1,25},{... | collective-permute-start | bytes 12296 | tf_op jit(solution)/shard_map/ppermute | solution.py:73
  593.9 55.2 %collective-permute-start.23 = (f32[8,128]{1,0:T(8,128)S(1)}, f32[8,128]{1,0:T(8,128)S(1)}, u32[]{:S(2)}, u32[]{:S(2)}) collective-permute-start(f32[8,128]{1,0:T(8,128)S(1)} %get-tuple-element.188), channel_id=1, source_target_pairs={{0,16},{4,20},{8,24},{12,28},{16,0},{20,4},{24,8},{28,12},{1,17},{... | collective-permute-start | bytes 12296 | tf_op jit(solution)/shard_map/ppermute | solution.py:73
  596.8 53.9 %collective-permute-start.24 = (f32[8,128]{1,0:T(8,128)S(1)}, f32[8,128]{1,0:T(8,128)S(1)}, u32[]{:S(2)}, u32[]{:S(2)}) collective-permute-start(f32[8,128]{1,0:T(8,128)S(1)} %get-tuple-element.187), channel_id=1, source_target_pairs={{0,8},{4,12},{8,0},{12,4},{16,24},{20,28},{24,16},{28,20},{1,9},{5... | collective-permute-start | bytes 12296 | tf_op jit(solution)/shard_map/ppermute | solution.py:73
  621.9 61.6 %collective-permute-start.3 = (bf16[2048,512]{1,0:T(8,128)(2,1)}, bf16[2048,512]{1,0:T(8,128)(2,1)}, u32[]{:S(2)}, u32[]{:S(2)}) collective-permute-start(bf16[2048,512]{1,0:T(8,128)(2,1)} %bitcast.33), channel_id=1, source_target_pairs={{0,1},{1,0},{2,3},{3,2},{4,5},{5,4},{6,7},{7,6},{8,9},{9,8},{10,11... | collective-permute-start | bytes 6291464 | tf_op jit(solution)/shard_map/ppermute | solution.py:68
  622.3 64.0 %collective-permute-start.4 = (bf16[2048,512]{1,0:T(8,128)(2,1)}, bf16[2048,512]{1,0:T(8,128)(2,1)}, u32[]{:S(2)}, u32[]{:S(2)}) collective-permute-start(bf16[2048,512]{1,0:T(8,128)(2,1)} %bitcast.34), channel_id=1, source_target_pairs={{0,2},{1,3},{2,0},{3,1},{4,6},{5,7},{6,4},{7,5},{8,10},{9,11},{10,... | collective-permute-start | bytes 6291464 | tf_op jit(solution)/shard_map/ppermute | solution.py:68
  639.1 100.1 %collective-permute-start.5 = (bf16[2048,512]{1,0:T(8,128)(2,1)}, bf16[2048,512]{1,0:T(8,128)(2,1)}, u32[]{:S(2)}, u32[]{:S(2)}) collective-permute-start(bf16[2048,512]{1,0:T(8,128)(2,1)} %bitcast.35), channel_id=1, source_target_pairs={{0,3},{1,2},{2,1},{3,0},{4,7},{5,6},{6,5},{7,4},{8,11},{9,10},{10,... | collective-permute-start | bytes 6291464 | tf_op jit(solution)/shard_map/ppermute | solution.py:68
  649.1 540.1 %reduce-scatter.17.cloned.1.call-start = ((), (), s32[]{:S(2)}) async-start(), calls=%async_computation.14 | async-start | bytes 5242880 | tf_op jit(solution)/shard_map/reduce_scatter | solution.py:409
  649.2 145.2 %collective-permute-start.28 = (bf16[2048,512]{1,0:T(8,128)(2,1)}, bf16[2048,512]{1,0:T(8,128)(2,1)}, u32[]{:S(2)}, u32[]{:S(2)}) collective-permute-start(bf16[2048,512]{1,0:T(8,128)(2,1)} %bitcast.522), channel_id=1, source_target_pairs={{0,1},{1,0},{2,3},{3,2},{4,5},{5,4},{6,7},{7,6},{8,9},{9,8},{10,11... | collective-permute-start | bytes 6291464 | tf_op jit(solution)/shard_map/ppermute | solution.py:68
  650.7 186.7 %collective-permute-start.29 = (bf16[2048,512]{1,0:T(8,128)(2,1)}, bf16[2048,512]{1,0:T(8,128)(2,1)}, u32[]{:S(2)}, u32[]{:S(2)}) collective-permute-start(bf16[2048,512]{1,0:T(8,128)(2,1)} %bitcast.521), channel_id=1, source_target_pairs={{0,2},{1,3},{2,0},{3,1},{4,6},{5,7},{6,4},{7,5},{8,10},{9,11},{10,... | collective-permute-start | bytes 6291464 | tf_op jit(solution)/shard_map/ppermute | solution.py:68
  683.6 155.4 %collective-permute-start.30 = (bf16[2048,512]{1,0:T(8,128)(2,1)}, bf16[2048,512]{1,0:T(8,128)(2,1)}, u32[]{:S(2)}, u32[]{:S(2)}) collective-permute-start(bf16[2048,512]{1,0:T(8,128)(2,1)} %bitcast.520), channel_id=1, source_target_pairs={{0,3},{1,2},{2,1},{3,0},{4,7},{5,6},{6,5},{7,4},{8,11},{9,10},{10,... | collective-permute-start | bytes 6291464 | tf_op jit(solution)/shard_map/ppermute | solution.py:68
  914.4 71.9 %collective-permute-start.31 = (bf16[2048,512]{1,0:T(8,128)(2,1)}, bf16[2048,512]{1,0:T(8,128)(2,1)}, u32[]{:S(2)}, u32[]{:S(2)}) collective-permute-start(bf16[2048,512]{1,0:T(8,128)(2,1)} %get-tuple-element.124), channel_id=1, source_target_pairs={{0,1},{1,0},{2,3},{3,2},{4,5},{5,4},{6,7},{7,6},{8,9},{9,8},{10,11... | collective-permute-start | bytes 6291464 | tf_op jit(solution)/shard_map/ppermute | solution.py:68
  915.2 91.1 %collective-permute-start.32 = (bf16[2048,512]{1,0:T(8,128)(2,1)}, bf16[2048,512]{1,0:T(8,128)(2,1)}, u32[]{:S(2)}, u32[]{:S(2)}) collective-permute-start(bf16[2048,512]{1,0:T(8,128)(2,1)} %get-tuple-element.123), channel_id=1, source_target_pairs={{0,2},{1,3},{2,0},{3,1},{4,6},{5,7},{6,4},{7,5},{8,10},{9,11},{10,... | collective-permute-start | bytes 6291464 | tf_op jit(solution)/shard_map/ppermute | solution.py:68
  916.7 89.7 %collective-permute-start.33 = (bf16[2048,512]{1,0:T(8,128)(2,1)}, bf16[2048,512]{1,0:T(8,128)(2,1)}, u32[]{:S(2)}, u32[]{:S(2)}) collective-permute-start(bf16[2048,512]{1,0:T(8,128)(2,1)} %get-tuple-element.122), channel_id=1, source_target_pairs={{0,3},{1,2},{2,1},{3,0},{4,7},{5,6},{6,5},{7,4},{8,11},{9,10},{10,... | collective-permute-start | bytes 6291464 | tf_op jit(solution)/shard_map/ppermute | solution.py:68
  1021.5 182.0 %reduce-scatter.13.cloned.1.call-start = ((), (), s32[]{:S(2)}) async-start(), calls=%async_computation.11 | async-start | bytes 5242880 | tf_op jit(solution)/shard_map/reduce_scatter | solution.py:417
  1029.7 235.4 %reduce-scatter.11.cloned.1.call-start = ((), (), s32[]{:S(2)}) async-start(), calls=%async_computation.10 | async-start | bytes 5242880 | tf_op jit(solution)/shard_map/reduce_scatter | solution.py:409
  1048.2 48.6 %collective-permute-start.25 = (bf16[2048,512]{1,0:T(8,128)(2,1)S(1)}, bf16[2048,512]{1,0:T(8,128)(2,1)S(1)}, u32[]{:S(2)}, u32[]{:S(2)}) collective-permute-start(bf16[2048,512]{1,0:T(8,128)(2,1)S(1)} %get-tuple-element.129), channel_id=1, source_target_pairs={{0,1},{1,0},{2,3},{3,2},{4,5},{5,4},{6,7},{7,6},{8,9},{9,8},{10,11... | collective-permute-start | bytes 6291464 | tf_op jit(solution)/shard_map/ppermute | solution.py:68
  1049.6 61.4 %collective-permute-start.26 = (bf16[2048,512]{1,0:T(8,128)(2,1)S(1)}, bf16[2048,512]{1,0:T(8,128)(2,1)S(1)}, u32[]{:S(2)}, u32[]{:S(2)}) collective-permute-start(bf16[2048,512]{1,0:T(8,128)(2,1)S(1)} %get-tuple-element.128), channel_id=1, source_target_pairs={{0,2},{1,3},{2,0},{3,1},{4,6},{5,7},{6,4},{7,5},{8,10},{9,11},{10,... | collective-permute-start | bytes 6291464 | tf_op jit(solution)/shard_map/ppermute | solution.py:68
  1050.2 112.1 %collective-permute-start.27 = (bf16[2048,512]{1,0:T(8,128)(2,1)S(1)}, bf16[2048,512]{1,0:T(8,128)(2,1)S(1)}, u32[]{:S(2)}, u32[]{:S(2)}) collective-permute-start(bf16[2048,512]{1,0:T(8,128)(2,1)S(1)} %get-tuple-element.127), channel_id=1, source_target_pairs={{0,3},{1,2},{2,1},{3,0},{4,7},{5,6},{6,5},{7,4},{8,11},{9,10},{10,... | collective-permute-start | bytes 6291464 | tf_op jit(solution)/shard_map/ppermute | solution.py:68
  1174.8 148.1 %all-gather.17.cloned.1.call-start = ((), (), s32[]{:S(2)}) async-start(), calls=%async_computation.15 | async-start | bytes 5242880 | tf_op jit(solution)/shard_map/all_gather | solution.py:414
  1269.9 154.4 %all-reduce.7.cloned.1.call-start = ((), (), s32[]{:S(2)}) async-start(), calls=%async_computation.17 | async-start | bytes 2359296 | tf_op jit(solution)/shard_map/psum | solution.py:723
  1363.0 128.9 %reduce-scatter.19.cloned.1.call-start = ((), (), s32[]{:S(2)}) async-start(), calls=%async_computation.16 | async-start | bytes 5242880 | tf_op jit(solution)/shard_map/reduce_scatter | solution.py:417
  1371.5 555.7 %reduce-scatter.23.cloned.1.call-start = ((), (), s32[]{:S(2)}) async-start(), calls=%async_computation.20 | async-start | bytes 9732096 | tf_op jit(solution)/shard_map/reduce_scatter | solution.py:745
  1392.6 538.3 %all-gather.15.cloned.1.call-start = ((), (), s32[]{:S(2)}) async-start(), calls=%async_computation.12 | async-start | bytes 5242880 | tf_op jit(solution)/shard_map/all_gather | solution.py:414
  1393.3 537.6 %all-gather.19.cloned.1.call-start = ((), (), s32[]{:S(2)}) async-start(), calls=%async_computation.18 | async-start | bytes 5242880 | tf_op jit(solution)/shard_map/all_gather | solution.py:414
  1508.8 422.1 %reduce-scatter.21.cloned.1.call-start = ((), (), s32[]{:S(2)}) async-start(), calls=%async_computation.19 | async-start | bytes 9879552 | tf_op jit(solution)/shard_map/reduce_scatter | solution.py:745
  1550.0 13.8 collective-permute-start.40
  1570.0 130.3 %collective-permute-start.41 = (bf16[4,3,352,256]{3,2,1,0:T(8,128)(2,1)S(1)}, bf16[4,3,352,256]{3,2,1,0:T(8,128)(2,1)S(1)}, u32[]{:S(2)}, u32[]{:S(2)}) collective-permute-start(bf16[4,3,352,256]{3,2,1,0:T(8,128)(2,1)S(1)} %get-tuple-element.115), channel_id=1, source_target_pairs={{0,8},{4,12},{8,0},{12,4},{16,24},{20,28},{24,16},{28,20},{1,9},{5... | collective-permute-start | bytes 6488072 | tf_op jit(solution)/shard_map/ppermute | solution.py:73
  1571.4 132.3 %collective-permute-start.42 = (bf16[4,3,352,256]{3,2,1,0:T(8,128)(2,1)S(1)}, bf16[4,3,352,256]{3,2,1,0:T(8,128)(2,1)S(1)}, u32[]{:S(2)}, u32[]{:S(2)}) collective-permute-start(bf16[4,3,352,256]{3,2,1,0:T(8,128)(2,1)S(1)} %get-tuple-element.114), channel_id=1, source_target_pairs={{0,16},{4,20},{8,24},{12,28},{16,0},{20,4},{24,8},{28,12},{1,17},{... | collective-permute-start | bytes 6488072 | tf_op jit(solution)/shard_map/ppermute | solution.py:73
  1573.6 259.8 %collective-permute-start.43 = (bf16[4,3,352,256]{3,2,1,0:T(8,128)(2,1)S(1)}, bf16[4,3,352,256]{3,2,1,0:T(8,128)(2,1)S(1)}, u32[]{:S(2)}, u32[]{:S(2)}) collective-permute-start(bf16[4,3,352,256]{3,2,1,0:T(8,128)(2,1)S(1)} %get-tuple-element.113), channel_id=1, source_target_pairs={{0,24},{4,28},{8,16},{12,20},{16,8},{20,12},{24,0},{28,4},{1,25},{... | collective-permute-start | bytes 6488072 | tf_op jit(solution)/shard_map/ppermute | solution.py:73
  1573.7 261.3 %collective-permute-start.44 = (bf16[3,352,256]{2,1,0:T(8,128)(2,1)S(1)}, bf16[3,352,256]{2,1,0:T(8,128)(2,1)S(1)}, u32[]{:S(2)}, u32[]{:S(2)}) collective-permute-start(bf16[3,352,256]{2,1,0:T(8,128)(2,1)S(1)} %get-tuple-element.111), channel_id=1, source_target_pairs={{0,1},{1,0},{2,3},{3,2},{4,5},{5,4},{6,7},{7,6},{8,9},{9,8},{10,11... | collective-permute-start | bytes 1622024 | tf_op jit(solution)/shard_map/ppermute | solution.py:68
  1575.3 285.8 %collective-permute-start.48 = (bf16[3,352,256]{2,1,0:T(8,128)(2,1)S(1)}, bf16[3,352,256]{2,1,0:T(8,128)(2,1)S(1)}, u32[]{:S(2)}, u32[]{:S(2)}) collective-permute-start(bf16[3,352,256]{2,1,0:T(8,128)(2,1)S(1)} %get-tuple-element.112), channel_id=1, source_target_pairs={{0,2},{1,3},{2,0},{3,1},{4,6},{5,7},{6,4},{7,5},{8,10},{9,11},{10,... | collective-permute-start | bytes 1622024 | tf_op jit(solution)/shard_map/ppermute | solution.py:68
  1700.3 209.1 %collective-permute-start.52 = (bf16[3,352,256]{2,1,0:T(8,128)(2,1)S(1)}, bf16[3,352,256]{2,1,0:T(8,128)(2,1)S(1)}, u32[]{:S(2)}, u32[]{:S(2)}) collective-permute-start(bf16[3,352,256]{2,1,0:T(8,128)(2,1)S(1)} %get-tuple-element.110), channel_id=1, source_target_pairs={{0,3},{1,2},{2,1},{3,0},{4,7},{5,6},{6,5},{7,4},{8,11},{9,10},{10,... | collective-permute-start | bytes 1622024 | tf_op jit(solution)/shard_map/ppermute | solution.py:68
  1703.6 133.6 %collective-permute-start.45 = (bf16[3,352,256]{2,1,0:T(8,128)(2,1)S(1)}, bf16[3,352,256]{2,1,0:T(8,128)(2,1)S(1)}, u32[]{:S(2)}, u32[]{:S(2)}) collective-permute-start(bf16[3,352,256]{2,1,0:T(8,128)(2,1)S(1)} %get-tuple-element.154), channel_id=1, source_target_pairs={{0,1},{1,0},{2,3},{3,2},{4,5},{5,4},{6,7},{7,6},{8,9},{9,8},{10,11... | collective-permute-start | bytes 1622024 | tf_op jit(solution)/shard_map/ppermute | solution.py:68
  1833.4 15.2 collective-permute-start.46
  1834.9 23.9 %collective-permute-start.47 = (bf16[3,352,256]{2,1,0:T(8,128)(2,1)S(1)}, bf16[3,352,256]{2,1,0:T(8,128)(2,1)S(1)}, u32[]{:S(2)}, u32[]{:S(2)}) collective-permute-start(bf16[3,352,256]{2,1,0:T(8,128)(2,1)S(1)} %get-tuple-element.146), channel_id=1, source_target_pairs={{0,1},{1,0},{2,3},{3,2},{4,5},{5,4},{6,7},{7,6},{8,9},{9,8},{10,11... | collective-permute-start | bytes 1622024 | tf_op jit(solution)/shard_map/ppermute | solution.py:68
  1837.2 25.3 %collective-permute-start.49 = (bf16[3,352,256]{2,1,0:T(8,128)(2,1)S(1)}, bf16[3,352,256]{2,1,0:T(8,128)(2,1)S(1)}, u32[]{:S(2)}, u32[]{:S(2)}) collective-permute-start(bf16[3,352,256]{2,1,0:T(8,128)(2,1)S(1)} %get-tuple-element.153), channel_id=1, source_target_pairs={{0,2},{1,3},{2,0},{3,1},{4,6},{5,7},{6,4},{7,5},{8,10},{9,11},{10,... | collective-permute-start | bytes 1622024 | tf_op jit(solution)/shard_map/ppermute | solution.py:68
  1848.6 44.4 %collective-permute-start.50 = (bf16[3,352,256]{2,1,0:T(8,128)(2,1)S(1)}, bf16[3,352,256]{2,1,0:T(8,128)(2,1)S(1)}, u32[]{:S(2)}, u32[]{:S(2)}) collective-permute-start(bf16[3,352,256]{2,1,0:T(8,128)(2,1)S(1)} %get-tuple-element.149), channel_id=1, source_target_pairs={{0,2},{1,3},{2,0},{3,1},{4,6},{5,7},{6,4},{7,5},{8,10},{9,11},{10,... | collective-permute-start | bytes 1622024 | tf_op jit(solution)/shard_map/ppermute | solution.py:68
  1858.9 49.6 %collective-permute-start.51 = (bf16[3,352,256]{2,1,0:T(8,128)(2,1)S(1)}, bf16[3,352,256]{2,1,0:T(8,128)(2,1)S(1)}, u32[]{:S(2)}, u32[]{:S(2)}) collective-permute-start(bf16[3,352,256]{2,1,0:T(8,128)(2,1)S(1)} %get-tuple-element.145), channel_id=1, source_target_pairs={{0,2},{1,3},{2,0},{3,1},{4,6},{5,7},{6,4},{7,5},{8,10},{9,11},{10,... | collective-permute-start | bytes 1622024 | tf_op jit(solution)/shard_map/ppermute | solution.py:68
  1861.2 49.1 %collective-permute-start.53 = (bf16[3,352,256]{2,1,0:T(8,128)(2,1)S(1)}, bf16[3,352,256]{2,1,0:T(8,128)(2,1)S(1)}, u32[]{:S(2)}, u32[]{:S(2)}) collective-permute-start(bf16[3,352,256]{2,1,0:T(8,128)(2,1)S(1)} %get-tuple-element.152), channel_id=1, source_target_pairs={{0,3},{1,2},{2,1},{3,0},{4,7},{5,6},{6,5},{7,4},{8,11},{9,10},{10,... | collective-permute-start | bytes 1622024 | tf_op jit(solution)/shard_map/ppermute | solution.py:68
  1862.5 48.6 %collective-permute-start.54 = (bf16[3,352,256]{2,1,0:T(8,128)(2,1)S(1)}, bf16[3,352,256]{2,1,0:T(8,128)(2,1)S(1)}, u32[]{:S(2)}, u32[]{:S(2)}) collective-permute-start(bf16[3,352,256]{2,1,0:T(8,128)(2,1)S(1)} %get-tuple-element.148), channel_id=1, source_target_pairs={{0,3},{1,2},{2,1},{3,0},{4,7},{5,6},{6,5},{7,4},{8,11},{9,10},{10,... | collective-permute-start | bytes 1622024 | tf_op jit(solution)/shard_map/ppermute | solution.py:68
  1892.9 19.0 collective-permute-start.55
  (103 other events, 1998.8 us)
Sparse Core Ops, SparseCore 0:
  16.1 83.9 all-gather.20
  174.8 76.6 reduce-scatter.8
  649.2 132.2 reduce-scatter.14
  1021.6 78.3 reduce-scatter.16
  1103.1 82.4 reduce-scatter.12
  1188.4 76.7 reduce-scatter.10
  1395.4 53.0 all-gather.14
  1509.0 53.4 all-gather.18
Sparse Core Ops, SparseCore 1:
  180.7 123.7 all-gather.26
  306.6 154.7 all-gather.24
  467.6 54.2 all-gather.12
  525.3 77.5 all-gather.22
  1270.0 52.8 all-gather.16
  1363.1 61.2 all-reduce.6
  1427.7 64.1 reduce-scatter.18
  1494.2 144.4 reduce-scatter.22
  1641.0 207.3 reduce-scatter.20

commit v2 on v1

--- a/solution.py
+++ b/solution.py
@@ -78,27 +78,13 @@
         return lax.ppermute(values, "dp", [(d, d ^ k) for d in range(self.dp)])
 
 
-def piece_columns(lay, part, d_loc):
-    ratio = lay.q * d_loc // part
-
-    def block(ids, kz):
-        return ids[0] ^ kz ^ (ids[2] // ratio)
-
-    def first(ids, kc):
-        offset = (ids[1] ^ kc) * d_loc
-        return pl.multiple_of(((offset // part) ^ (ids[2] % ratio)) * part + offset % part, 128)
-
-    return block, first
-
-
 def lay_out_weights(lay, ids, stacks, f_loc, d_loc, width):
     ffe = f_loc * lay.t
-    block, first = piece_columns(lay, width // lay.t, d_loc)
 
     def kernel(ids_ref, *refs):
         sources, (in_ref, out_ref) = refs[: lay.q], refs[lay.q :]
         for kc in range(lay.q):
-            columns = pl.ds(first(ids_ref, kc), d_loc)
+            columns = pl.ds(pl.multiple_of((ids_ref[1] ^ kc) * d_loc, 128), d_loc)
             for g in range(2):
                 in_ref[g, :, columns] = sources[kc][0, g]
             out_ref[:, columns] = sources[kc][0, 2]
@@ -113,14 +99,14 @@
             num_scalar_prefetch=1,
             grid=(lay.t, lay.z),
             in_specs=[
-                pl.BlockSpec((1, 3, f_loc, d_loc), lambda kt, kz, ids: (kt * lay.z + kz, 0, 0, 0))
+                pl.BlockSpec((1, 3, f_loc, d_loc), lambda kt, kz, ids: (kz * lay.t + kt, 0, 0, 0))
             ]
             * lay.q,
             out_specs=(
                 pl.BlockSpec(
-                    (2, f_loc, lay.q * d_loc), lambda kt, kz, ids: (0, kt, block(ids, kz))
+                    (2, f_loc, lay.q * d_loc), lambda kt, kz, ids: (0, kt, kz)
                 ),
-                pl.BlockSpec((f_loc, lay.q * d_loc), lambda kt, kz, ids: (kt, block(ids, kz))),
+                pl.BlockSpec((f_loc, lay.q * d_loc), lambda kt, kz, ids: (kt, kz)),
             ),
         ),
         cost_estimate=pl.CostEstimate(
@@ -134,17 +120,16 @@
 
 def take_apart(lay, ids, grad_in, grad_out, f_loc, d_loc, width):
     ffe = f_loc * lay.t
-    block, first = piece_columns(lay, width // lay.t, d_loc)
 
     def kernel(ids_ref, in_ref, out_ref, *targets):
         for kc in range(lay.q):
-            columns = pl.ds(first(ids_ref, kc), d_loc)
+            columns = pl.ds(pl.multiple_of((ids_ref[1] ^ kc) * d_loc, 128), d_loc)
             for g in range(2):
                 targets[kc][0, g] = in_ref[g, :, columns]
             targets[kc][0, 2] = out_ref[:, columns]
 
     shape = jax.ShapeDtypeStruct((lay.t * lay.z, 3, f_loc, d_loc), BF16)
-    spec = pl.BlockSpec((1, 3, f_loc, d_loc), lambda kt, kz, ids: (kt * lay.z + kz, 0, 0, 0))
+    spec = pl.BlockSpec((1, 3, f_loc, d_loc), lambda kt, kz, ids: (kz * lay.t + kt, 0, 0, 0))
     return pl.pallas_call(
         kernel,
         out_shape=(shape,) * lay.q,
@@ -153,9 +138,9 @@
             grid=(lay.t, lay.z),
             in_specs=[
                 pl.BlockSpec(
-                    (2, f_loc, lay.q * d_loc), lambda kt, kz, ids: (0, kt, block(ids, kz))
+                    (2, f_loc, lay.q * d_loc), lambda kt, kz, ids: (0, kt, kz)
                 ),
-                pl.BlockSpec((f_loc, lay.q * d_loc), lambda kt, kz, ids: (kt, block(ids, kz))),
+                pl.BlockSpec((f_loc, lay.q * d_loc), lambda kt, kz, ids: (kt, kz)),
             ],
             out_specs=(spec,) * lay.q,
         ),
@@ -173,7 +158,7 @@
         out_ref[0] = piece_ref[0, 2].astype(F32)
 
     def pick(e, ids):
-        return ((ids[2] ^ (e % lay.t)) * lay.z + (ids[0] ^ (e // lay.t)), 0, 0, 0)
+        return (e % lay.t * lay.z + e // lay.t, 0, 0, 0)
 
     grad_in, grad_out = pl.pallas_call(
         kernel,
@@ -196,6 +181,33 @@
         name="home_gradients",
     )(ids, pieces)
     return jnp.swapaxes(grad_in, 2, 3), grad_out
+
+
+def join_columns(parts, me, count):
+    rows, part = parts[0].shape
+    block = min(256, rows)
+
+    def kernel(me_ref, *refs):
+        for k in range(count):
+
+            @pl.when(pl.program_id(1) == k)
+            def _(k=k):
+                refs[count][...] = refs[k][...]
+
+    return pl.pallas_call(
+        kernel,
+        out_shape=jax.ShapeDtypeStruct((rows, count * part), parts[0].dtype),
+        grid_spec=pltpu.PrefetchScalarGridSpec(
+            num_scalar_prefetch=1,
+            grid=(rows // block, count),
+            in_specs=[pl.BlockSpec((block, part), lambda i, k, me: (i, 0))] * count,
+            out_specs=pl.BlockSpec((block, part), lambda i, k, me: (i, me[0] ^ k)),
+        ),
+        cost_estimate=pl.CostEstimate(
+            flops=0, bytes_accessed=4 * rows * part * count, transcendentals=0
+        ),
+        name="join_columns",
+    )(me.reshape(1).astype(jnp.int32), *parts)
 
 
 def score_block(q_ref, r_ref, k_ref, kr_ref, head, step, keys, block, length, scale):
@@ -414,27 +426,41 @@
         return lax.all_gather(values, "tensor", axis=1, tiled=True)
 
     def scatter_t(values):
-        return lax.psum_scatter(values, "tensor", scatter_dimension=1, tiled=True)
+        return lax.psum_scatter(
+            values.astype(BF16), "tensor", scatter_dimension=1, tiled=True
+        ).astype(F32)
+
+    def swap_t(values):
+        return lax.all_to_all(values, "tensor", split_axis=0, concat_axis=0, tiled=True)
+
+    def swap_z(values):
+        return lax.all_to_all(
+            values,
+            "dp",
+            split_axis=0,
+            concat_axis=0,
+            axis_index_groups=lay.z_groups,
+            tiled=True,
+        )
+
+    def gather_t_direct(values):
+        return join_columns([lay.over_t(values, k) for k in range(nt)], me_t, nt)
+
+    def part_for(values, k):
+        return lax.dynamic_slice_in_dim(values, (me_t ^ k) * part, part, 1)
+
+    def scatter_t_direct(values):
+        total = part_for(values, 0)
+        for k in range(1, nt):
+            total = total + lay.over_t(part_for(values, k).astype(BF16), k).astype(F32)
+        return total
 
     ids = jnp.stack([me_z, me_c, me_t]).astype(jnp.int32)
 
     packed = jnp.concatenate(
         [jnp.swapaxes(w_expert_in, 2, 3), w_expert_out[:, None]], 1
     ).reshape(nz, nt, 3, f_loc, d_loc)
-    plane = [
-        lay.over_t(lax.dynamic_index_in_dim(packed, me_t ^ k, 1, keepdims=False), k)
-        for k in range(nt)
-    ]
-    pieces = jnp.stack(
-        [
-            lay.over_z(lax.dynamic_index_in_dim(plane[kt], me_z ^ kz, 0, keepdims=False), kz)
-            for kt in range(nt)
-            for kz in range(nz)
-        ]
-    )
-    own_in, own_out = lay_out_weights(
-        lay, ids, [lay.over_c(pieces, k) for k in range(nq)], f_loc, d_loc, width
-    )
+    by_column = swap_t(jnp.swapaxes(packed, 0, 1))
 
     lat_loc = kv_gain.shape[0]
     q_rows, down_rows, out_rows = w_query.shape[1], w_kv_down.shape[1], w_out.shape[0]
@@ -471,6 +497,52 @@
     )
     front = lax.all_gather(front_pack, "dp", axis=0, tiled=False)
 
+    valid_length = lengths[0]
+    valid_rows = lax.broadcasted_iota(jnp.int32, (rows, 1), 0) < valid_length
+    cot_low = jnp.where(valid_rows, cotangent, jnp.zeros_like(cotangent))
+    cot_part = own_part(cot_low)
+    route_rows = jnp.transpose(routes).astype(BF16).reshape(-1)
+    route_rows = jnp.pad(route_rows, (0, -route_rows.shape[0] % (16 * part))).reshape(-1, part)
+    front, by_column, cot_ready = lax.optimization_barrier(
+        (front, by_column, jnp.concatenate([cot_part, route_rows], 0))
+    )
+    by_plane = swap_z(jnp.swapaxes(by_column, 0, 1))
+    cot_all = gather_z(cot_ready)
+
+    route_all = cot_all[:, rows:].reshape(nz, -1)[:, : TOP * rows].reshape(nz, TOP, rows)
+    plane_ids = (me_z * nt + jnp.arange(nt, dtype=jnp.int32)).astype(F32)
+    member = jnp.any(route_all.astype(F32)[:, :, :, None] == plane_ids[None, None, None, :], axis=1)
+    row_ids = lax.broadcasted_iota(jnp.int32, (rows, rows), 0)
+    col_ids = lax.broadcasted_iota(jnp.int32, (rows, rows), 1)
+    before = (col_ids < row_ids).astype(BF16)
+    position = jnp.einsum("ij,sje->sei", before, member.astype(BF16), preferred_element_type=F32)
+    key = jnp.where(jnp.swapaxes(member, 1, 2), position.astype(jnp.int32), -1)
+    slots_iota = lax.broadcasted_iota(jnp.int32, (1, 1, CAP, 1), 2)
+
+    def place_of(keys):
+        return (keys[:, :, None, :] == slots_iota).astype(BF16)
+
+    place = place_of(key)
+    keys_near = [lax.dynamic_index_in_dim(key, me_t ^ k, 1, keepdims=False) for k in range(nt)]
+    place_near = place_of(jnp.stack(keys_near, 1))
+    own_place = keys_near[0][:, None, :] == slots_iota[0]
+
+    def pick_rows(values):
+        picked = jnp.einsum("sepk,skd->espd", place, values, preferred_element_type=F32)
+        return picked.astype(BF16).reshape(nt, nz * CAP, part)
+
+    def send_out(picked):
+        return jnp.swapaxes(swap_t(picked), 0, 1).reshape(nz * CAP, width)
+
+    def send_back(values):
+        return [lay.over_t(part_for(values, k), k) for k in range(nt)]
+
+    def combine(parts):
+        parts = jnp.stack(parts).reshape(nt, nz, CAP, part)
+        summed = jnp.einsum("sepk,espd->skd", place_near, parts, preferred_element_type=F32)
+        return summed.astype(BF16)
+
+
     def rows_of(first, count):
         return jnp.swapaxes(front[:, first : first + count], 0, 1).reshape(count, width)
 
@@ -484,39 +556,6 @@
     at = at + 2 * EXPERTS
     out_w = rows_of(at, out_rows)
     up_w = front[:, at + out_rows :].reshape(LATENT, heads * (NOPE + VDIM))
-
-    route_own = jnp.pad(jnp.transpose(routes), ((0, -TOP % 8), (0, 0)), constant_values=-1)
-    route_all = in_order([lay.over_z(route_own, k) for k in range(nz)], me_z, nz)
-    plane_ids = me_z * nt + (me_t ^ jnp.arange(nt, dtype=jnp.int32))
-    member = jnp.any(route_all[:, :, :, None] == plane_ids[None, None, None, :], axis=1)
-    row_ids = lax.broadcasted_iota(jnp.int32, (rows, rows), 0)
-    col_ids = lax.broadcasted_iota(jnp.int32, (rows, rows), 1)
-    before = (col_ids < row_ids).astype(BF16)
-    position = jnp.einsum("ij,sje->sie", before, member.astype(BF16), preferred_element_type=F32)
-    key = jnp.where(member, position.astype(jnp.int32), -1)
-    key = jnp.transpose(key, (0, 2, 1))
-    slots_iota = lax.broadcasted_iota(jnp.int32, (1, 1, CAP, 1), 2)
-    place = (key[:, :, None, :] == slots_iota).astype(BF16)
-    own_place = key[:, 0, None, :] == slots_iota[0]
-
-    def dispatch(values):
-        picked = jnp.einsum("sepk,skd->espd", place, values, preferred_element_type=F32)
-        picked = picked.astype(BF16).reshape(nt, nz * CAP, part)
-        return jnp.concatenate([lay.over_t(picked[k], k) for k in range(nt)], 1)
-
-    def send_back(values):
-        return [lay.over_t(values[:, k * part : (k + 1) * part], k) for k in range(nt)]
-
-    def combine(parts):
-        parts = jnp.stack(parts).reshape(nt, nz, CAP, part)
-        summed = jnp.einsum("sepk,espd->skd", place, parts, preferred_element_type=F32)
-        return scatter_z(summed.astype(BF16)).astype(F32)
-
-    valid_length = lengths[0]
-    valid_rows = lax.broadcasted_iota(jnp.int32, (rows, 1), 0) < valid_length
-    cot_low = jnp.where(valid_rows, cotangent, jnp.zeros_like(cotangent))
-    cot_part = own_part(cot_low)
-    cot_rows = dispatch(gather_z(cot_part))
 
     cosine, sine = angle_tables(rows)
     wide_cos, wide_sin = jnp.tile(cosine, (1, heads)), jnp.tile(sine, (1, heads))
@@ -552,7 +591,8 @@
     attended_low, log_totals = attend(
         lengths, query_nope, query_rope, keys_values, key_rope, heads, score_scale
     )
-    attn_sum = scatter_t(dot(attended_low, out_w).astype(BF16)).astype(F32)
+    attn_part, cot_all = lax.optimization_barrier((dot(attended_low, out_w), cot_all))
+    attn_sum = scatter_t(attn_part)
     residual = own_part(hidden).astype(F32) + attn_sum
 
     def row_mean(values):
@@ -564,8 +604,21 @@
     ffn_scale = lax.dynamic_slice_in_dim(gain_ffn, me_t * part, part, 0).astype(F32)
     ffn_part = (ffn_hat * ffn_scale).astype(BF16)
 
-    expert_rows = dispatch(gather_z(ffn_part))
+    ffn_part, cot_picked = lax.optimization_barrier((ffn_part, pick_rows(cot_all[:, :rows])))
+    ffn_all = gather_z(ffn_part)
+    cot_rows = send_out(cot_picked)
+    picked = pick_rows(ffn_all)
     ffn_low = gather_t(ffn_part)
+    shared_pack = jnp.concatenate(
+        [jnp.swapaxes(w_shared_in, 1, 2).reshape(-1, d_loc), w_shared_out], 0
+    )
+    picked, shared_pack = lax.optimization_barrier((picked, shared_pack))
+    expert_rows = send_out(picked)
+    shared_all = lax.all_gather(shared_pack, "dp", axis=0, tiled=False)
+    pieces = by_plane.reshape(nz * nt, 3, f_loc, d_loc)
+    own_in, own_out = lay_out_weights(
+        lay, ids, [lay.over_c(pieces, k) for k in range(nq)], f_loc, d_loc, width
+    )
     router_probs = jax.nn.softmax(dot_nt(ffn_low, router_t), axis=-1)
     probs_turned = jnp.transpose(router_probs).reshape(EXPERTS, -1, 128)
     own_probs = in_order(
@@ -608,8 +661,12 @@
     grad_in_own = dot_tn(pre_low, expert_rows).astype(BF16)
     grad_out_own = dot_tn(gated_active, cot_rows).astype(BF16)
     grad_pieces = take_apart(lay, ids, grad_in_own, grad_out_own, f_loc, d_loc, width)
-    grad_parts, grad_pieces = lax.optimization_barrier((grad_parts, grad_pieces))
-    routed_grad = combine(grad_parts)
+    grad_parts, grad_pieces, routed = lax.optimization_barrier((grad_parts, grad_pieces, routed))
+    routed = scatter_z(routed).astype(F32)
+    routed_grad = scatter_z(combine(grad_parts)).astype(F32)
+    grad_class = sum(lay.over_c(grad_pieces[k], k).astype(F32) for k in range(nq)).astype(BF16)
+    routed_grad, grad_class = lax.optimization_barrier((routed_grad, grad_class))
+    grad_plane = swap_z(grad_class.reshape(nz, nt, 3, f_loc, d_loc))
 
     token_grad = jnp.sum(jnp.where(own_place, gate_grad[:, :, None], 0.0), axis=1)
     token_grad = token_grad.reshape(nz, -1, 128)
@@ -631,12 +688,6 @@
     )
 
     ffs = w_shared_out.shape[0]
-    shared_all = lax.all_gather(
-        jnp.concatenate([jnp.swapaxes(w_shared_in, 1, 2).reshape(2 * ffs, d_loc), w_shared_out], 0),
-        "dp",
-        axis=0,
-        tiled=False,
-    )
     shared_in = jnp.swapaxes(shared_all[:, : 2 * ffs], 0, 1).reshape(2 * ffs, width)
     shared_out = jnp.swapaxes(shared_all[:, 2 * ffs :], 0, 1).reshape(ffs, width)
     shared_pre = dot_nt(ffn_low, shared_in)
@@ -644,7 +695,7 @@
     shared_sig = jax.nn.sigmoid(shared_gate)
     shared_silu = shared_gate * shared_sig
     shared_act = (shared_silu * shared_up).astype(BF16)
-    shared_part = scatter_t(dot(shared_act, shared_out).astype(BF16)).astype(F32)
+    shared_part = scatter_t_direct(dot(shared_act, shared_out))
     shared_act_grad = dot_nt(cot_low, shared_out)
     shared_pre_grad = jnp.concatenate(
         [
@@ -655,7 +706,7 @@
     ).astype(BF16)
     grad_shared_in = dot_tn(shared_pre_grad, ffn_low)
     grad_shared_out = dot_tn(shared_act, cot_low)
-    shared_grad = scatter_t(dot(shared_pre_grad, shared_in).astype(BF16)).astype(F32)
+    shared_grad = scatter_t_direct(dot(shared_pre_grad, shared_in))
 
     logits_grad = router_probs * (
         probs_grad - jnp.sum(router_probs * probs_grad, axis=-1, keepdims=True)
@@ -686,15 +737,7 @@
     )
     residual_low = gather_t(residual_grad.astype(BF16))
 
-    output = gather_t((residual + routed + shared_part).astype(BF16))
-
-    grad_class = sum(lay.over_c(grad_pieces[k], k).astype(F32) for k in range(nq)).astype(BF16)
-    grad_class = grad_class.reshape(nt, nz, 3, f_loc, d_loc)
-    grad_plane = [lay.over_z(grad_class[:, k], k) for k in range(nz)]
-    grad_home = jnp.stack(
-        [lay.over_t(grad_plane[kz][kt], kt) for kt in range(nt) for kz in range(nz)]
-    )
-    grad_expert_in, grad_expert_out = home_gradients(lay, ids, grad_home, f_loc, d_loc)
+    output = gather_t_direct((residual + routed + shared_part).astype(BF16))
 
     grad_out_w = dot_tn(attended_low, residual_low)
     attended_grad = dot_nt(residual_low, out_w).astype(BF16)
@@ -720,25 +763,22 @@
         rotate_back(rope_sum[:, 0], rope_sum[:, 1], cosine, sine), 1
     )
     latent_part = dot_nt(kv_grad, up_w)
-    latent_sum = lax.psum(
-        jnp.concatenate([latent_part, key_rope_part], -1).astype(BF16), "tensor"
-    ).astype(F32)
-    normed_grad_q = scatter_t(dot(query_grad, query_t).astype(BF16)).astype(F32)
-    latent_grad, key_rope_grad = latent_sum[:, :LATENT], latent_sum[:, LATENT:]
-    grad_kv_gain = jnp.sum(latent_grad * latent_hat, axis=0)
-    scaled_kv = kv_scale * latent_grad
+    grad_kv_gain = jnp.sum(latent_part * latent_hat, axis=0)
+    scaled_kv = kv_scale * latent_part
     latent_back = kv_inverse * (
         scaled_kv - latent_hat * jnp.mean(latent_hat * scaled_kv, axis=-1, keepdims=True)
     )
-    down_grad = jnp.concatenate([latent_back, key_rope_grad], -1).astype(BF16)
-    down_slice = lax.dynamic_slice_in_dim(down_t, me_t * part, part, 1)
-    normed_grad = normed_grad_q + dot(down_grad, down_slice)
+    down_grad = jnp.concatenate([latent_back, key_rope_part], -1).astype(BF16)
+    normed_grad = scatter_t(dot(query_grad, query_t) + dot(down_grad, down_t))
+    normed_grad, grad_plane = lax.optimization_barrier((normed_grad, grad_plane))
     attn_hat = own_part(hidden).astype(F32) * attn_inverse
     scaled_in = lax.dynamic_slice_in_dim(attn_scale, me_t * part, part, 0) * normed_grad
     attn_gain_part = jnp.sum(normed_grad * attn_hat, axis=0)
     input_grad = residual_grad + attn_inverse * (
         scaled_in - attn_hat * row_mean(attn_hat * scaled_in)
     )
+    grad_home = swap_t(jnp.swapaxes(grad_plane, 0, 1)).reshape(EXPERTS, 3, f_loc, d_loc)
+    grad_expert_in, grad_expert_out = home_gradients(lay, ids, grad_home, f_loc, d_loc)
     grad_hidden = gather_t(input_grad.astype(BF16))
 
     def sum_dp(values):
@@ -747,41 +787,44 @@
     def by_owner(values):
         return jnp.swapaxes(values.astype(BF16).reshape(-1, ndp, d_loc), 0, 1)
 
-    gain_parts = lax.all_gather(
-        jnp.concatenate([attn_gain_part[None], ffn_gain_part[None]], 0), "tensor", axis=1, tiled=True
-    )
+    def spread(values):
+        return lax.dynamic_update_slice(
+            jnp.zeros((1, width), F32), values[None], (jnp.int32(0), me_t * part)
+        )
+
     kv_gain_row = jnp.pad(
         grad_kv_gain.reshape(ndp, lat_loc), ((0, 0), (0, d_loc - lat_loc))
     ).reshape(1, width)
+    gain_grads = jnp.concatenate([spread(attn_gain_part), spread(ffn_gain_part), kv_gain_row], 0)
     front_sum = sum_dp(
         jnp.concatenate(
             [
+                by_owner(dot_tn(down_grad, normed_low)),
+                by_owner(jnp.pad(gain_grads, ((0, 13), (0, 0)))),
+                by_owner(router_part),
                 by_owner(dot_tn(query_grad, normed_low)),
-                by_owner(dot_tn(down_grad, normed_low)),
-                by_owner(router_part),
-                by_owner(jnp.pad(jnp.concatenate([gain_parts, kv_gain_row], 0), ((0, 13), (0, 0)))),
                 by_owner(grad_out_w),
                 dot_tn(latent_low, kv_grad).astype(BF16).reshape(ndp, -1, d_loc),
             ],
             1,
         )
     )
-    shared_sum = sum_dp(
-        jnp.concatenate([by_owner(grad_shared_in), by_owner(grad_shared_out)], 1)
-    )
-    at = q_rows + down_rows
-    gain_rows = front_sum[at + EXPERTS : at + EXPERTS + 3]
+    shared_grads = jnp.concatenate([by_owner(grad_shared_in), by_owner(grad_shared_out)], 1)
+    front_sum, shared_grads = lax.optimization_barrier((front_sum, shared_grads))
+    shared_sum = sum_dp(shared_grads)
+    own_sum = lax.psum(front_sum[: down_rows + EXPERTS], "tensor")
+    at = down_rows + 2 * EXPERTS
     return (
         output,
         grad_hidden,
-        gain_rows[0],
-        jnp.transpose(by_head(front_sum[:q_rows])),
-        jnp.transpose(front_sum[q_rows:at]),
-        gain_rows[2, :lat_loc],
-        front_sum[at + 2 * EXPERTS + out_rows :].reshape(w_kv_up.shape),
-        front_sum[at + 2 * EXPERTS : at + 2 * EXPERTS + out_rows],
-        gain_rows[1],
-        jnp.transpose(front_sum[at : at + EXPERTS]),
+        own_sum[down_rows],
+        jnp.transpose(by_head(front_sum[at : at + q_rows])),
+        jnp.transpose(own_sum[:down_rows]),
+        own_sum[down_rows + 2, :lat_loc],
+        front_sum[at + q_rows + out_rows :].reshape(w_kv_up.shape),
+        front_sum[at + q_rows : at + q_rows + out_rows],
+        own_sum[down_rows + 1],
+        jnp.transpose(front_sum[down_rows + EXPERTS : at]),
         grad_expert_in,
         grad_expert_out,
         jnp.swapaxes(shared_sum[: 2 * ffs].reshape(2, ffs, d_loc), 1, 2),

time: 1960 us -> 1850 us (0.944)
  waiting for transfers between devices: 1180 us -> 1010 us
  blocking collectives: 33.4 us -> 58.4 us
  matrix products: 320 us -> 296 us
  other arithmetic: 73 us -> 94.6 us
    ppermute x24 -> x6, waiting for transfers between devices: 533 us -> 3.67 us  [over_z(): lax.ppermute(values, 'dp', [(d, d ^ k * self.q) for d in range(self.dp)])]
    all_to_all x0 -> x6, waiting for transfers between devices: none -> 396 us  [the longest x4 240 us: swap_t(): lax.all_to_all(values, 'tensor', split_axis=0, concat_axis=0, tiled=True)]
    reduce_scatter x2, waiting for transfers between devices: 0.01 us -> 148 us  [sum_dp(): lax.psum_scatter(values, 'dp', scatter_dimension=0, tiled=False).astype(F32)]
    all_gather x1, waiting for transfers between devices: 79.8 us -> 0.01 us  [body(): front = lax.all_gather(front_pack, 'dp', axis=0, tiled=False)]
    ppermute x30 -> x18, waiting for transfers between devices: 345 us -> 280 us  [over_t(): return lax.ppermute(values, 'tensor', [(i, i ^ k) for i in range(self.t)])]
    reduce_scatter x2, waiting for transfers between devices: 61.6 us -> 5.31 us  [scatter_z(): lax.psum_scatter(values, 'dp', scatter_dimension=0, tiled=False, axis_ind...]
    transpose x2 -> x7, local copies, waits for them, and re-layouts: 1.46 us -> 49.2 us  [the longest x2 23 us: send_out(): return jnp.swapaxes(swap_t(picked), 0, 1).reshape(nz * CAP, width)]
    all_to_all x0 -> x6, starting transfers between devices: none -> 37.3 us  [the longest x4 25.1 us: swap_t(): lax.all_to_all(values, 'tensor', split_axis=0, concat_axis=0, tiled=True)]
  transfers between devices with their start and end apart: 73 -> 46, of which waited for: 43 -> 24; matrix products, arithmetic and copies ran while one was open for 23% -> 28% of each run, Pallas kernels for 2% -> 5%
where the time goes in v2:
time: 1850 us; the launch traced here: 1830 us
  waiting for transfers between devices  1010 us (55%)
  matrix products  296 us (16%)
  local copies, waits for them, and re-layouts  189 us (10%)
  other arithmetic  94.6 us (5%)
  Pallas kernels  90.1 us (5%)
  starting transfers between devices  72.7 us (4%)
  blocking collectives  58.4 us (3%)
    ppermute x18, waiting for transfers between devices, over_t(): return lax.ppermute(values, 'tensor', [(i, i ^ k) for i in range(self.t)])  280 us
    all_to_all x4, waiting for transfers between devices, swap_t(): lax.all_to_all(values, 'tensor', split_axis=0, concat_axis=0, tiled=True)  240 us
    all_to_all x2, waiting for transfers between devices, swap_z(): lax.all_to_all(values, 'dp', split_axis=0, concat_axis=0, axis_index_grou...  156 us
    reduce_scatter x2, waiting for transfers between devices, sum_dp(): lax.psum_scatter(values, 'dp', scatter_dimension=0, tiled=False).astype(F32)  148 us
    dot_general x9, matrix products, dot_nt(): lax.dot_general(a, b, (((1,), (1,)), ((), ())), preferred_element_type=F32)  90.4 us
    dot_general x8, matrix products, dot_tn(): lax.dot_general(a, b, (((0,), (0,)), ((), ())), preferred_element_type=F32)  78.7 us
    reduce_scatter x2, waiting for transfers between devices, scatter_t(): lax.psum_scatter(values.astype(BF16), 'tensor', scatter_dimension=1, tile...  70.6 us
    dot_general x8, matrix products, dot(): return jnp.dot(a, b, preferred_element_type=F32)  70.6 us
  transfers between devices with their start and end apart: 46, of which 24 were waited for; matrix products, arithmetic and copies ran while one was open for 28% of the time, Pallas kernels for 5%

profile of v2, /device:TPU:10, one launch (start us, length us, event | category | flops | bytes accessed | tf_op | source)
XLA Modules:
  0.0 1829.8 jit_solution(4058081057593166868)
XLA Ops:
  19.5 6.9 maximum_bitcast_fusion
  26.4 8.4 copy.293
  34.8 6.4 all-to-all-start
  47.8 88.2 %all-to-all-done = bf16[4,4,3,352,256]{4,3,2,1,0:T(8,128)(2,1)} async-done(((bf16[4,4,3,352,256]{4,3,2,1,0:T(8,128)(2,1)}), bf16[4,4,3,352,256]{4,3,2,1,0:T(8,128)(2,1)}, u32[]{:S(2)}, u32[]{:S(2)}) %all-to-all-start) | async-done | bytes 8650784 | tf_op jit(solution)/shard_map/all_to_all | solution.py:434
  147.3 6.4 fusion.121
  177.5 7.7 copy.308
  185.2 5.9 all-to-all-start.2
  204.0 14.6 attend.1
  225.5 39.2 %all-gather.20.cloned.1.call-done = bf16[4160,512]{1,0:T(8,128)(2,1)} async-done(((bf16[1040,512]{1,0:T(8,128)(2,1)}), bf16[4160,512]{1,0:T(8,128)(2,1)}) %all-gather.20.cloned.1.call-update) | async-done | bytes 4259856 | tf_op jit(solution)/shard_map/all_gather | solution.py:418
  266.6 13.3 convert_bitcast_fusion.1
  279.9 7.6 copy.306
  287.5 44.4 %reduce-scatter.7.cloned.1.call-done = bf16[1024,512]{1,0:T(8,128)(2,1)} async-done(((bf16[1024,2048]{1,0:T(8,128)(2,1)}), bf16[1024,512]{1,0:T(8,128)(2,1)}) %reduce-scatter.7.cloned.1.call-update) | async-done | bytes 1048592 | tf_op jit(solution)/shard_map/reduce_scatter | solution.py:429
  333.9 8.1 psum.28
  345.5 122.1 %all-to-all-done.2 = bf16[4,4,3,352,256]{4,3,2,1,0:T(8,128)(2,1)} async-done(((bf16[4,4,3,352,256]{4,3,2,1,0:T(8,128)(2,1)}), bf16[4,4,3,352,256]{4,3,2,1,0:T(8,128)(2,1)}, u32[]{:S(2)}, u32[]{:S(2)}) %all-to-all-start.2) | async-done | bytes 8650784 | tf_op jit(solution)/shard_map/all_to_all | solution.py:437
  467.6 6.2 all-to-all-start.1
  474.9 13.2 convert_bitcast_fusion
  488.0 7.6 copy.314
  495.7 103.8 %all-to-all-done.1 = bf16[4,2048,512]{2,1,0:T(8,128)(2,1)} async-done(((bf16[4,2048,512]{2,1,0:T(8,128)(2,1)}), bf16[4,2048,512]{2,1,0:T(8,128)(2,1)}, u32[]{:S(2)}, u32[]{:S(2)}) %all-to-all-start.1) | async-done | bytes 8388640 | tf_op jit(solution)/shard_map/all_to_all | solution.py:434
  599.4 6.2 all-to-all-start.3
  618.2 11.5 copy.307
  629.9 16.4 lay_out_weights.1
  648.8 48.1 %all-to-all-done.3 = bf16[4,2048,512]{2,1,0:T(8,128)(2,1)} async-done(((bf16[4,2048,512]{2,1,0:T(8,128)(2,1)}), bf16[4,2048,512]{2,1,0:T(8,128)(2,1)}, u32[]{:S(2)}, u32[]{:S(2)}) %all-to-all-start.3) | async-done | bytes 8388640 | tf_op jit(solution)/shard_map/all_to_all | solution.py:434
  696.9 11.5 copy.315
  708.4 31.3 %fusion.132 = f32[2048,2816]{0,1:T(8,128)} fusion(bf16[2816,2048]{1,0:T(8,128)(2,1)} %bitcast.458, bf16[2048,2048]{0,1:T(8,128)(2,1)} %bitcast.376), kind=kOutput, calls=%fused_computation.288 | convolution fusion | flops 23622320128 | bytes 42991616 | tf_op jit(solution)/shard_map/dot_general | solution.py:30
  739.7 26.9 %fusion.9 = (f32[2048]{0:T(1024)S(1)}, bf16[2048,1408]{0,1:T(8,128)(2,1)}, f32[2048,1408]{0,1:T(8,128)}) fusion(f32[2048,2816]{0,1:T(8,128)} %fusion.132, bf16[1408,2048]{1,0:T(8,128)(2,1)} %copy-done.6, bf16[2048,2048]{0,1:T(8,128)(2,1)} %bitcast.374), kind=kOutput, calls=%fused_computation.15 | convolution fusion | flops 11837110272 | bytes 54534144 | tf_op jit(solution)/shard_map/dot_general | solution.py:30
  769.5 18.9 %multiply_convert_fusion.3 = (bf16[2048,1408]{0,1:T(8,128)(2,1)}, bf16[2048,1408]{0,1:T(8,128)(2,1)}) fusion(f32[2048,2816]{0,1:T(8,128)} %fusion.132, f32[2048,1408]{0,1:T(8,128)} %get-tuple-element.235, f32[2048]{0:T(1024)S(1)} %bitcast.426), kind=kLoop, calls=%fused_computation.19 | loop fusion | flops 40370176 | bytes 46145536 | tf_op jit(solution)/shard_map/convert.20
  788.3 30.2 %convolution_convert_fusion.3 = bf16[2048,2048]{1,0:T(8,128)(2,1)S(1)} fusion(bf16[2816,2048]{1,0:T(8,128)(2,1)} %bitcast.459, bf16[2048,1408]{0,1:T(8,128)(2,1)} %get-tuple-element.180, bf16[2048,1408]{0,1:T(8,128)(2,1)} %get-tuple-element.179), kind=kOutput, calls=%fused_computation.54 | convolution fusion | flops 23649583104 | bytes 31457280 | tf_op jit(solution)/shard_map/dot_general | solution.py:26
  823.7 15.8 multiply_convert_fusion
  846.6 30.6 %convolution_convert_fusion = bf16[2816,2048]{1,0:T(8,128)(2,1)} fusion(bf16[2048,2048]{0,1:T(8,128)(2,1)} %bitcast.377, bf16[2048,1408]{0,1:T(8,128)(2,1)} %get-tuple-element.180, bf16[2048,1408]{0,1:T(8,128)(2,1)} %get-tuple-element.179), kind=kOutput, calls=%fused_computation.22 | convolution fusion | flops 23651155968 | bytes 31457280 | tf_op jit(solution)/shard_map/dot_general | solution.py:34
  877.3 16.5 convolution_convert_fusion.2.out_ref
  893.8 13.6 take_apart.1
  907.4 8.0 collective-permute-done.9
  916.9 86.6 %collective-permute-done.8 = bf16[2048,512]{1,0:T(8,128)(2,1)} collective-permute-done((bf16[2048,512]{1,0:T(8,128)(2,1)}, bf16[2048,512]{1,0:T(8,128)(2,1)}, u32[]{:S(2)}, u32[]{:S(2)}) %collective-permute-start.8) | collective-permute-done | bytes 2097184 | tf_op jit(solution)/shard_map/ppermute | solution.py:68
  1007.4 11.3 bitcast_convert_fusion.1
  1022.6 11.3 bitcast_convert_fusion
  1054.1 5.6 slice_bitcast_fusion
  1059.7 8.7 copy.321
  1073.4 6.7 fusion.130
  1084.4 6.7 fusion.55
  1113.3 7.3 collective-permute-done.18
  1123.2 10.0 add_convert_fusion
  1133.2 10.1 collective-permute-done.17
  1148.4 42.3 %psum.29 = f32[8,128]{1,0:T(8,128)S(1)} all-reduce(f32[8,128]{1,0:T(8,128)S(1)} %bitcast.432), channel_id=1, replica_groups=mesh['dp'=8,'tensor'=4] {'tensor'}, use_global_device_ids=true, to_apply=%region_15.16 | all-reduce | flops 1024 | bytes 8192 | tf_op jit(solution)/shard_map/psum | solution.py:600
  1191.4 5.8 fusion.123
  1197.2 6.3 all-to-all-start.4
  1203.6 46.9 %all-gather.14.cloned.1.call-done = bf16[1024,2048]{1,0:T(8,128)(2,1)} async-done(((bf16[1024,512]{1,0:T(8,128)(2,1)}), bf16[1024,2048]{1,0:T(8,128)(2,1)}) %all-gather.14.cloned.1.call-update) | async-done | bytes 4194320 | tf_op jit(solution)/shard_map/all_gather | solution.py:426
  1260.2 21.7 %attend_back.1 = (bf16[1024,512]{1,0:T(8,128)(2,1)S(1)}, f32[1024,256]{1,0:T(8,128)S(1)}, bf16[1024,1024]{1,0:T(8,128)(2,1)S(1)}, f32[1024,256]{1,0:T(8,128)S(1)}) custom-call(s32[1]{0:T(128)} %copy.404.len_ref, bf16[1024,512]{1,0:T(8,128)(2,1)S(1)} %slice.277.q_ref, bf16[1024,256]{1,0:T(8,128)(2,1)S(1)} %copy-done.2, bf16[1024,1024]{1,0:T(8,128)(2,1)S(1)} %copy-done.8, ...), custom_call_target="tpu_custom_call" | custom-call | flops 6710886400 | bytes 33554432 | tf_op jit(solution)/shard_map/attend_back/pallas_call | solution.py:333
  1295.3 5.3 add_convert_fusion.1
  1311.0 5.4 convolution_convert_fusion.6
  1321.9 5.3 convolution_convert_fusion.4
  1327.2 26.2 %reduce-scatter.13.cloned.1.call-done = bf16[1024,512]{1,0:T(8,128)(2,1)} async-done(((bf16[1024,2048]{1,0:T(8,128)(2,1)}), bf16[1024,512]{1,0:T(8,128)(2,1)}) %reduce-scatter.13.cloned.1.call-update) | async-done | bytes 1048592 | tf_op jit(solution)/shard_map/reduce_scatter | solution.py:429
  1354.9 34.4 %all-to-all-done.4 = bf16[4,4,3,352,256]{4,3,2,1,0:T(8,128)(2,1)} async-done(((bf16[4,4,3,352,256]{4,3,2,1,0:T(8,128)(2,1)}), bf16[4,4,3,352,256]{4,3,2,1,0:T(8,128)(2,1)}, u32[]{:S(2)}, u32[]{:S(2)}) %all-to-all-start.4) | async-done | bytes 8650784 | tf_op jit(solution)/shard_map/all_to_all | solution.py:437
  1397.1 8.0 psum.30
  1409.2 6.1 convolution_convert_fusion.5
  1418.0 7.2 convolution_convert_fusion.1
  1429.4 60.3 %reduce-scatter.15.cloned.1.call-done = bf16[1,2144,256]{2,1,0:T(8,128)(2,1)} async-done(((bf16[8,2144,256]{2,1,0:T(8,128)(2,1)}), bf16[1,2144,256]{2,1,0:T(8,128)(2,1)}) %reduce-scatter.15.cloned.1.call-update) | async-done | bytes 1097744 | tf_op jit(solution)/shard_map/reduce_scatter | solution.py:785
  1492.5 7.7 copy.341
  1500.2 6.3 all-to-all-start.5
  1510.0 141.5 %collective-permute-done.13.refs_1_ = bf16[1024,512]{1,0:T(8,128)(2,1)S(1)} collective-permute-done((bf16[1024,512]{1,0:T(8,128)(2,1)S(1)}, bf16[1024,512]{1,0:T(8,128)(2,1)S(1)}, u32[]{:S(2)}, u32[]{:S(2)}) %collective-permute-start.13) | collective-permute-done | bytes 1048608 | tf_op jit(solution)/shard_map/ppermute | solution.py:68
  1651.5 24.0 %collective-permute-done.14.refs_2_ = bf16[1024,512]{1,0:T(8,128)(2,1)S(1)} collective-permute-done((bf16[1024,512]{1,0:T(8,128)(2,1)S(1)}, bf16[1024,512]{1,0:T(8,128)(2,1)S(1)}, u32[]{:S(2)}, u32[]{:S(2)}) %collective-permute-start.14) | collective-permute-done | bytes 1048608 | tf_op jit(solution)/shard_map/ppermute | solution.py:68
  1676.5 9.2 join_columns.1
  1685.7 14.5 home_gradients.1
  1703.7 22.0 %all-reduce.7.cloned.1.call-done = f32[592,256]{1,0:T(8,128)} async-done(((f32[592,256]{1,0:T(8,128)}), f32[592,256]{1,0:T(8,128)}) %all-reduce.7.cloned.1.call-update) | async-done | bytes 606224 | tf_op jit(solution)/shard_map/psum | solution.py:815
  1730.1 87.3 %reduce-scatter.17.cloned.1.call-done = bf16[1,2112,256]{2,1,0:T(8,128)(2,1)} async-done(((bf16[8,2112,256]{2,1,0:T(8,128)(2,1)}), bf16[1,2112,256]{2,1,0:T(8,128)(2,1)}) %reduce-scatter.17.cloned.1.call-update) | async-done | bytes 1081360 | tf_op jit(solution)/shard_map/reduce_scatter | solution.py:785
  (418 shorter events, 260.5 us)
Async XLA Ops:
  7.2 128.7 %all-gather.18.cloned.1.call-start = ((), (), s32[]{:S(2)}) async-start(), calls=%async_computation.22 | async-start | bytes 9879552 | tf_op jit(solution)/shard_map/all_gather | solution.py:498
  34.8 101.2 %all-to-all-start = ((bf16[4,4,3,352,256]{4,3,2,1,0:T(8,128)(2,1)}), bf16[4,4,3,352,256]{4,3,2,1,0:T(8,128)(2,1)}, u32[]{:S(2)}, u32[]{:S(2)}) async-start(bf16[4,4,3,352,256]{4,3,2,1,0:T(8,128)(2,1)} %copy.293), calls=%async_computation | async-start | bytes 17301504 | tf_op jit(solution)/shard_map/all_to_all | solution.py:434
  41.1 223.6 %all-gather.20.cloned.1.call-start = ((), (), s32[]{:S(2)}) async-start(), calls=%async_computation.23 | async-start | bytes 5324800 | tf_op jit(solution)/shard_map/all_gather | solution.py:418
  136.0 25.2 %copy-start.79 = (f32[32]{0:T(128)}, f32[32]{0:T(128)S(1)}, u32[]{:S(2)}) copy-start(f32[32]{0:T(128)S(1)} %multiply_exponential_fusion) | copy-start | bytes 388
  161.2 41.4 %copy-start.24 = (f32[1024,576]{0,1:T(8,128)}, f32[1024,576]{0,1:T(8,128)S(1)}, u32[]{:S(2)}) copy-start(f32[1024,576]{0,1:T(8,128)S(1)} %fusion.119) | copy-start | bytes 7077892
  185.2 282.4 %all-to-all-start.2 = ((bf16[4,4,3,352,256]{4,3,2,1,0:T(8,128)(2,1)}), bf16[4,4,3,352,256]{4,3,2,1,0:T(8,128)(2,1)}, u32[]{:S(2)}, u32[]{:S(2)}) async-start(bf16[4,4,3,352,256]{4,3,2,1,0:T(8,128)(2,1)} %copy.308), calls=%async_computation.3 | async-start | bytes 17301504 | tf_op jit(solution)/shard_map/all_to_all | solution.py:437
  191.1 140.8 %reduce-scatter.7.cloned.1.call-start = ((), (), s32[]{:S(2)}) async-start(), calls=%async_computation.12 | async-start | bytes 5242880 | tf_op jit(solution)/shard_map/reduce_scatter | solution.py:429
  264.7 210.2 %all-gather.22.cloned.1.call-start = ((), (), s32[]{:S(2)}) async-start(), calls=%async_computation.24 | async-start | bytes 5242880 | tf_op jit(solution)/shard_map/all_gather | solution.py:418
  264.9 77.1 %copy-start.71 = (f32[512]{0:T(512)}, f32[512]{0:T(512)S(1)}, u32[]{:S(2)}) copy-start(f32[512]{0:T(512)S(1)} %dynamic-slice_convert_fusion.6) | copy-start | bytes 6148
  345.5 128.3 %copy-start.53 = (bf16[2,256,704]{1,2,0:T(8,128)(2,1)S(1)}, bf16[2,256,704]{1,2,0:T(8,128)(2,1)}, u32[]{:S(2)}) copy-start(bf16[2,256,704]{1,2,0:T(8,128)(2,1)} %param.29) | copy-start | bytes 2162692
  345.5 128.3 %copy-start.54 = (bf16[704,256]{1,0:T(8,128)(2,1)S(1)}, bf16[704,256]{1,0:T(8,128)(2,1)}, u32[]{:S(2)}) copy-start(bf16[704,256]{1,0:T(8,128)(2,1)} %param.30) | copy-start | bytes 1081348
  467.6 131.8 %all-to-all-start.1 = ((bf16[4,2048,512]{2,1,0:T(8,128)(2,1)}), bf16[4,2048,512]{2,1,0:T(8,128)(2,1)}, u32[]{:S(2)}, u32[]{:S(2)}) async-start(bf16[4,2048,512]{2,1,0:T(8,128)(2,1)} %bitcast.361), calls=%async_computation.2 | async-start | bytes 16777216 | tf_op jit(solution)/shard_map/all_to_all | solution.py:434
  473.8 132.9 %all-gather.12.cloned.1.call-start = ((), (), s32[]{:S(2)}) async-start(), calls=%async_computation.13 | async-start | bytes 5242880 | tf_op jit(solution)/shard_map/all_gather | solution.py:426
  473.8 156.1 %collective-permute-start = (bf16[16,3,352,256]{3,2,1,0:T(8,128)(2,1)}, bf16[16,3,352,256]{3,2,1,0:T(8,128)(2,1)}, u32[]{:S(2)}, u32[]{:S(2)}) collective-permute-start(bf16[16,3,352,256]{3,2,1,0:T(8,128)(2,1)} %bitcast.41.refs_0_), channel_id=1, source_target_pairs={{0,4},{4,0},{8,12},{12,8},{16,20},{20,16},{24,28},{28,24},{1,5},{5... | collective-permute-start | bytes 25952264 | tf_op jit(solution)/shard_map/ppermute | solution.py:78
  599.4 97.5 %all-to-all-start.3 = ((bf16[4,2048,512]{2,1,0:T(8,128)(2,1)}), bf16[4,2048,512]{2,1,0:T(8,128)(2,1)}, u32[]{:S(2)}, u32[]{:S(2)}) async-start(bf16[4,2048,512]{2,1,0:T(8,128)(2,1)} %bitcast.360), calls=%async_computation.4 | async-start | bytes 16777216 | tf_op jit(solution)/shard_map/all_to_all | solution.py:434
  605.6 448.4 %all-gather.24.cloned.1.call-start = ((), (), s32[]{:S(2)}) async-start(), calls=%async_computation.25 | async-start | bytes 9732096 | tf_op jit(solution)/shard_map/all_gather | solution.py:617
  605.7 288.1 %copy-start.5 = (s32[3]{0:T(128)}, s32[3]{0:T(128)S(1)}, u32[]{:S(2)}) copy-start(s32[3]{0:T(128)S(1)} %pad_add_fusion.1.ids_ref) | copy-start | bytes 40
  606.6 23.1 %copy-start.55 = (bf16[8,2,8,256]{3,2,0,1:T(8,128)(2,1)}, bf16[8,2,8,256]{3,2,0,1:T(8,128)(2,1)S(1)}, u32[]{:S(2)}) copy-start(bf16[8,2,8,256]{3,2,0,1:T(8,128)(2,1)S(1)} %copy.358) | copy-start | bytes 196612
  610.8 18.9 %collective-permute-start.1 = (f32[8,128]{1,0:T(8,128)S(1)}, f32[8,128]{1,0:T(8,128)S(1)}, u32[]{:S(2)}, u32[]{:S(2)}) collective-permute-start(f32[8,128]{1,0:T(8,128)S(1)} %get-tuple-element.226), channel_id=1, source_target_pairs={{0,24},{4,28},{8,16},{12,20},{16,8},{20,12},{24,0},{28,4},{1,25},{... | collective-permute-start | bytes 12296 | tf_op jit(solution)/shard_map/ppermute | solution.py:73
  613.2 16.5 collective-permute-start.2
  617.5 12.3 collective-permute-start.3
  629.7 482.1 %reduce-scatter.11.cloned.1.call-start = ((), (), s32[]{:S(2)}) async-start(), calls=%async_computation.15 | async-start | bytes 5242880 | tf_op jit(solution)/shard_map/reduce_scatter | solution.py:421
  769.5 54.2 %slice-start = ((s8[5767168]{0:T(1024)(128)(4,1)}), s8[4194304]{0:T(1024)(128)(4,1)S(1)}, s32[]{:S(2)}) async-start(s8[5767168]{0:T(1024)(128)(4,1)} %bitcast.357), calls=%async_computation.26 | async-start | bytes 8388608
  788.3 35.4 %slice-start.1 = ((s8[5767168]{0:T(1024)(128)(4,1)}), s8[1572864]{0:T(1024)(128)(4,1)S(1)}, s32[]{:S(2)}) async-start(s8[5767168]{0:T(1024)(128)(4,1)} %bitcast.357), calls=%async_computation.27 | async-start | bytes 3145728
  821.6 197.1 %collective-permute-start.4 = (bf16[2048,512]{1,0:T(8,128)(2,1)}, bf16[2048,512]{1,0:T(8,128)(2,1)}, u32[]{:S(2)}, u32[]{:S(2)}) collective-permute-start(bf16[2048,512]{1,0:T(8,128)(2,1)} %get-tuple-element.194), channel_id=1, source_target_pairs={{0,1},{1,0},{2,3},{3,2},{4,5},{5,4},{6,7},{7,6},{8,9},{9,8},{10,11... | collective-permute-start | bytes 6291464 | tf_op jit(solution)/shard_map/ppermute | solution.py:68
  822.1 196.6 %collective-permute-start.5 = (bf16[2048,512]{1,0:T(8,128)(2,1)}, bf16[2048,512]{1,0:T(8,128)(2,1)}, u32[]{:S(2)}, u32[]{:S(2)}) collective-permute-start(bf16[2048,512]{1,0:T(8,128)(2,1)} %get-tuple-element.193), channel_id=1, source_target_pairs={{0,2},{1,3},{2,0},{3,1},{4,6},{5,7},{6,4},{7,5},{8,10},{9,11},{10,... | collective-permute-start | bytes 6291464 | tf_op jit(solution)/shard_map/ppermute | solution.py:68
  843.2 72.3 %collective-permute-start.9 = (bf16[2048,512]{1,0:T(8,128)(2,1)}, bf16[2048,512]{1,0:T(8,128)(2,1)}, u32[]{:S(2)}, u32[]{:S(2)}) collective-permute-start(bf16[2048,512]{1,0:T(8,128)(2,1)} %get-tuple-element.189), channel_id=1, source_target_pairs={{0,3},{1,2},{2,1},{3,0},{4,7},{5,6},{6,5},{7,4},{8,11},{9,10},{10,... | collective-permute-start | bytes 6291464 | tf_op jit(solution)/shard_map/ppermute | solution.py:68
  844.6 159.0 %collective-permute-start.8 = (bf16[2048,512]{1,0:T(8,128)(2,1)}, bf16[2048,512]{1,0:T(8,128)(2,1)}, u32[]{:S(2)}, u32[]{:S(2)}) collective-permute-start(bf16[2048,512]{1,0:T(8,128)(2,1)} %get-tuple-element.190), channel_id=1, source_target_pairs={{0,2},{1,3},{2,0},{3,1},{4,6},{5,7},{6,4},{7,5},{8,10},{9,11},{10,... | collective-permute-start | bytes 6291464 | tf_op jit(solution)/shard_map/ppermute | solution.py:68
  845.1 158.4 %collective-permute-start.7 = (bf16[2048,512]{1,0:T(8,128)(2,1)}, bf16[2048,512]{1,0:T(8,128)(2,1)}, u32[]{:S(2)}, u32[]{:S(2)}) collective-permute-start(bf16[2048,512]{1,0:T(8,128)(2,1)} %get-tuple-element.191), channel_id=1, source_target_pairs={{0,1},{1,0},{2,3},{3,2},{4,5},{5,4},{6,7},{7,6},{8,9},{9,8},{10,11... | collective-permute-start | bytes 6291464 | tf_op jit(solution)/shard_map/ppermute | solution.py:68
  893.8 109.7 %copy-start.27 = (bf16[2048,512]{1,0:T(8,128)(2,1)S(1)}, bf16[2048,512]{1,0:T(8,128)(2,1)}, u32[]{:S(2)}) copy-start(bf16[2048,512]{1,0:T(8,128)(2,1)} %get-tuple-element.188) | copy-start | bytes 6291460
  907.4 100.0 %copy-start = (bf16[16,3,352,256]{3,2,1,0:T(8,128)(2,1)}, bf16[16,3,352,256]{3,2,1,0:T(8,128)(2,1)S(1)}, u32[]{:S(2)}) copy-start(bf16[16,3,352,256]{3,2,1,0:T(8,128)(2,1)S(1)} %get-tuple-element.67) | copy-start | bytes 25952260
  915.4 103.3 %collective-permute-start.6 = (bf16[2048,512]{1,0:T(8,128)(2,1)}, bf16[2048,512]{1,0:T(8,128)(2,1)}, u32[]{:S(2)}, u32[]{:S(2)}) collective-permute-start(bf16[2048,512]{1,0:T(8,128)(2,1)} %get-tuple-element.192), channel_id=1, source_target_pairs={{0,3},{1,2},{2,1},{3,0},{4,7},{5,6},{6,5},{7,4},{8,11},{9,10},{10,... | collective-permute-start | bytes 6291464 | tf_op jit(solution)/shard_map/ppermute | solution.py:68
  1033.9 157.5 %reduce-scatter.9.cloned.1.call-start = ((), (), s32[]{:S(2)}) async-start(), calls=%async_computation.14 | async-start | bytes 5242880 | tf_op jit(solution)/shard_map/reduce_scatter | solution.py:421
  1034.6 6.6 collective-permute-start.22
  1036.9 5.9 collective-permute-start.21
  1041.2 3.7 collective-permute-start.20
  1044.8 4.6 collective-permute-start.25
  1044.8 4.6 collective-permute-start.24
  1046.9 3.7 collective-permute-start.23
  1050.6 70.1 %collective-permute-start.19 = (bf16[16,3,352,256]{3,2,1,0:T(8,128)(2,1)}, bf16[16,3,352,256]{3,2,1,0:T(8,128)(2,1)}, u32[]{:S(2)}, u32[]{:S(2)}) collective-permute-start(bf16[16,3,352,256]{3,2,1,0:T(8,128)(2,1)} %get-tuple-element.68), channel_id=1, source_target_pairs={{0,4},{4,0},{8,12},{12,8},{16,20},{20,16},{24,28},{28,24},{1,5},{5... | collective-permute-start | bytes 25952264 | tf_op jit(solution)/shard_map/ppermute | solution.py:78
  1054.0 196.5 %all-gather.14.cloned.1.call-start = ((), (), s32[]{:S(2)}) async-start(), calls=%async_computation.16 | async-start | bytes 5242880 | tf_op jit(solution)/shard_map/all_gather | solution.py:426
  1093.5 27.1 %collective-permute-start.18 = (bf16[1024,512]{1,0:T(8,128)(2,1)}, bf16[1024,512]{1,0:T(8,128)(2,1)S(1)}, u32[]{:S(2)}, u32[]{:S(2)}) collective-permute-start(bf16[1024,512]{1,0:T(8,128)(2,1)} %get-tuple-element.186), channel_id=1, source_target_pairs={{0,3},{1,2},{2,1},{3,0},{4,7},{5,6},{6,5},{7,4},{8,11},{9,10},{10,... | collective-permute-start | bytes 3145736 | tf_op jit(solution)/shard_map/ppermute | solution.py:68
  1095.1 48.1 %collective-permute-start.17 = (bf16[1024,512]{1,0:T(8,128)(2,1)}, bf16[1024,512]{1,0:T(8,128)(2,1)}, u32[]{:S(2)}, u32[]{:S(2)}) collective-permute-start(bf16[1024,512]{1,0:T(8,128)(2,1)} %get-tuple-element.187), channel_id=1, source_target_pairs={{0,2},{1,3},{2,0},{3,1},{4,6},{5,7},{6,4},{7,5},{8,10},{9,11},{10,... | collective-permute-start | bytes 3145736 | tf_op jit(solution)/shard_map/ppermute | solution.py:68
  1096.5 46.8 %collective-permute-start.16 = (bf16[1024,512]{1,0:T(8,128)(2,1)}, bf16[1024,512]{1,0:T(8,128)(2,1)}, u32[]{:S(2)}, u32[]{:S(2)}) collective-permute-start(bf16[1024,512]{1,0:T(8,128)(2,1)} %get-tuple-element.185), channel_id=1, source_target_pairs={{0,1},{1,0},{2,3},{3,2},{4,5},{5,4},{6,7},{7,6},{8,9},{9,8},{10,11... | collective-permute-start | bytes 3145736 | tf_op jit(solution)/shard_map/ppermute | solution.py:68
  1105.6 85.2 %collective-permute-start.12 = (bf16[1024,512]{1,0:T(8,128)(2,1)}, bf16[1024,512]{1,0:T(8,128)(2,1)S(1)}, u32[]{:S(2)}, u32[]{:S(2)}) collective-permute-start(bf16[1024,512]{1,0:T(8,128)(2,1)} %get-tuple-element.197), channel_id=1, source_target_pairs={{0,3},{1,2},{2,1},{3,0},{4,7},{5,6},{6,5},{7,4},{8,11},{9,10},{10,... | collective-permute-start | bytes 3145736 | tf_op jit(solution)/shard_map/ppermute | solution.py:68
  1120.6 70.1 %collective-permute-start.11 = (bf16[1024,512]{1,0:T(8,128)(2,1)}, bf16[1024,512]{1,0:T(8,128)(2,1)}, u32[]{:S(2)}, u32[]{:S(2)}) collective-permute-start(bf16[1024,512]{1,0:T(8,128)(2,1)} %get-tuple-element.198), channel_id=1, source_target_pairs={{0,2},{1,3},{2,0},{3,1},{4,6},{5,7},{6,4},{7,5},{8,10},{9,11},{10,... | collective-permute-start | bytes 3145736 | tf_op jit(solution)/shard_map/ppermute | solution.py:68
  1121.6 21.7 %copy-start.48 = (bf16[1024,512]{1,0:T(8,128)(2,1)S(1)}, bf16[1024,512]{1,0:T(8,128)(2,1)}, u32[]{:S(2)}) copy-start(bf16[1024,512]{1,0:T(8,128)(2,1)} %copy-done.47) | copy-start | bytes 3145732
  1121.6 21.7 %copy-start.63 = (f32[1024]{0:T(1024)S(1)}, f32[1024]{0:T(1024)}, u32[]{:S(2)}) copy-start(f32[1024]{0:T(1024)} %copy-done.62) | copy-start | bytes 12292
  1121.6 21.7 %copy-start.72 = (f32[512]{0:T(512)S(1)}, f32[512]{0:T(512)}, u32[]{:S(2)}) copy-start(f32[512]{0:T(512)} %copy-done.71) | copy-start | bytes 6148
  1121.6 69.2 %collective-permute-start.10 = (bf16[1024,512]{1,0:T(8,128)(2,1)}, bf16[1024,512]{1,0:T(8,128)(2,1)}, u32[]{:S(2)}, u32[]{:S(2)}) collective-permute-start(bf16[1024,512]{1,0:T(8,128)(2,1)} %get-tuple-element.196), channel_id=1, source_target_pairs={{0,1},{1,0},{2,3},{3,2},{4,5},{5,4},{6,7},{7,6},{8,9},{9,8},{10,11... | collective-permute-start | bytes 3145736 | tf_op jit(solution)/shard_map/ppermute | solution.py:68
  1197.2 53.2 %copy-start.42 = (bf16[512,8,256]{0,2,1:T(8,128)(2,1)S(1)}, bf16[512,8,256]{0,2,1:T(8,128)(2,1)}, u32[]{:S(2)}) copy-start(bf16[512,8,256]{0,2,1:T(8,128)(2,1)} %copy.305) | copy-start | bytes 6291460
  1197.2 192.0 %all-to-all-start.4 = ((bf16[4,4,3,352,256]{4,3,2,1,0:T(8,128)(2,1)}), bf16[4,4,3,352,256]{4,3,2,1,0:T(8,128)(2,1)}, u32[]{:S(2)}, u32[]{:S(2)}) async-start(bf16[4,4,3,352,256]{4,3,2,1,0:T(8,128)(2,1)} %bitcast.359), calls=%async_computation.8 | async-start | bytes 17301504 | tf_op jit(solution)/shard_map/all_to_all | solution.py:437
  1203.6 149.8 %reduce-scatter.13.cloned.1.call-start = ((), (), s32[]{:S(2)}) async-start(), calls=%async_computation.17 | async-start | bytes 5242880 | tf_op jit(solution)/shard_map/reduce_scatter | solution.py:429
  1260.2 24.5 %copy-start.74 = (f32[1024]{0:T(1024)S(1)}, f32[1024]{0:T(1024)}, u32[]{:S(2)}) copy-start(f32[1024]{0:T(1024)} %copy-done.73) | copy-start | bytes 12292
  1260.2 24.5 %copy-start.78 = (f32[512]{0:T(512)S(1)}, f32[512]{0:T(512)}, u32[]{:S(2)}) copy-start(f32[512]{0:T(512)} %copy-done.77) | copy-start | bytes 6148
  1300.6 189.0 %reduce-scatter.15.cloned.1.call-start = ((), (), s32[]{:S(2)}) async-start(), calls=%async_computation.19 | async-start | bytes 9879552 | tf_op jit(solution)/shard_map/reduce_scatter | solution.py:785
  1397.1 288.6 %all-gather.16.cloned.1.call-start = ((), (), s32[]{:S(2)}) async-start(), calls=%async_computation.18 | async-start | bytes 5242880 | tf_op jit(solution)/shard_map/all_gather | solution.py:426
  1408.9 316.7 %all-reduce.7.cloned.1.call-start = ((), (), s32[]{:S(2)}) async-start(), calls=%async_computation.20 | async-start | bytes 1212416 | tf_op jit(solution)/shard_map/psum | solution.py:815
  1492.0 325.5 %reduce-scatter.17.cloned.1.call-start = ((), (), s32[]{:S(2)}) async-start(), calls=%async_computation.21 | async-start | bytes 9732096 | tf_op jit(solution)/shard_map/reduce_scatter | solution.py:785
  1500.2 185.5 %all-to-all-start.5 = ((bf16[4,4,3,352,256]{4,3,2,1,0:T(8,128)(2,1)}), bf16[4,4,3,352,256]{4,3,2,1,0:T(8,128)(2,1)}, u32[]{:S(2)}, u32[]{:S(2)}) async-start(bf16[4,4,3,352,256]{4,3,2,1,0:T(8,128)(2,1)} %copy.341), calls=%async_computation.10 | async-start | bytes 17301504 | tf_op jit(solution)/shard_map/all_to_all | solution.py:434
  1506.5 145.0 %collective-permute-start.13 = (bf16[1024,512]{1,0:T(8,128)(2,1)S(1)}, bf16[1024,512]{1,0:T(8,128)(2,1)S(1)}, u32[]{:S(2)}, u32[]{:S(2)}) collective-permute-start(bf16[1024,512]{1,0:T(8,128)(2,1)S(1)} %copy-done.32), channel_id=1, source_target_pairs={{0,1},{1,0},{2,3},{3,2},{4,5},{5,4},{6,7},{7,6},{8,9},{9,8},{10,11... | collective-permute-start | bytes 3145736 | tf_op jit(solution)/shard_map/ppermute | solution.py:68
  1506.7 168.8 %collective-permute-start.14 = (bf16[1024,512]{1,0:T(8,128)(2,1)S(1)}, bf16[1024,512]{1,0:T(8,128)(2,1)S(1)}, u32[]{:S(2)}, u32[]{:S(2)}) collective-permute-start(bf16[1024,512]{1,0:T(8,128)(2,1)S(1)} %copy-done.32), channel_id=1, source_target_pairs={{0,2},{1,3},{2,0},{3,1},{4,6},{5,7},{6,4},{7,5},{8,10},{9,11},{10,... | collective-permute-start | bytes 3145736 | tf_op jit(solution)/shard_map/ppermute | solution.py:68
  1508.6 167.9 %collective-permute-start.15 = (bf16[1024,512]{1,0:T(8,128)(2,1)S(1)}, bf16[1024,512]{1,0:T(8,128)(2,1)}, u32[]{:S(2)}, u32[]{:S(2)}) collective-permute-start(bf16[1024,512]{1,0:T(8,128)(2,1)S(1)} %copy-done.32), channel_id=1, source_target_pairs={{0,3},{1,2},{2,1},{3,0},{4,7},{5,6},{6,5},{7,4},{8,11},{9,10},{10,... | collective-permute-start | bytes 3145736 | tf_op jit(solution)/shard_map/ppermute | solution.py:68
  1651.5 24.0 %copy-start.50 = (bf16[1024,512]{1,0:T(8,128)(2,1)}, bf16[1024,512]{1,0:T(8,128)(2,1)S(1)}, u32[]{:S(2)}) copy-start(bf16[1024,512]{1,0:T(8,128)(2,1)S(1)} %collective-permute-done.13.refs_1_) | copy-start | bytes 3145732
  (71 other events, 396.0 us)
Sparse Core Ops, SparseCore 0:
  19.6 83.9 all-gather.17
  136.1 128.5 all-gather.19
  268.2 63.6 reduce-scatter.6
  345.6 111.7 all-gather.21
  476.8 120.2 all-gather.11
  629.8 81.3 all-gather.23
  1034.0 77.7 reduce-scatter.10
  1114.1 77.2 reduce-scatter.8
  1197.4 53.0 all-gather.13
  1300.7 52.6 reduce-scatter.12
  1397.2 92.3 reduce-scatter.14
  1492.1 183.3 all-gather.15
  1679.4 46.2 all-reduce.6
  1727.9 89.4 reduce-scatter.16

commit v3 on v2

--- a/solution.py
+++ b/solution.py
@@ -503,10 +503,19 @@
     cot_part = own_part(cot_low)
     route_rows = jnp.transpose(routes).astype(BF16).reshape(-1)
     route_rows = jnp.pad(route_rows, (0, -route_rows.shape[0] % (16 * part))).reshape(-1, part)
-    front, by_column, cot_ready = lax.optimization_barrier(
-        (front, by_column, jnp.concatenate([cot_part, route_rows], 0))
-    )
-    by_plane = swap_z(jnp.swapaxes(by_column, 0, 1))
+    inputs = hidden.astype(F32)
+    attn_inverse = inverse_rms(inputs)
+    cosine, sine = angle_tables(rows)
+    wide_cos, wide_sin = jnp.tile(cosine, (1, heads)), jnp.tile(sine, (1, heads))
+    front, cot_ready, attn_inverse, wide_cos, wide_sin = lax.optimization_barrier(
+        (
+            front,
+            jnp.concatenate([cot_part, route_rows], 0),
+            attn_inverse,
+            wide_cos,
+            wide_sin,
+        )
+    )
     cot_all = gather_z(cot_ready)
 
     route_all = cot_all[:, rows:].reshape(nz, -1)[:, : TOP * rows].reshape(nz, TOP, rows)
@@ -527,19 +536,19 @@
     place_near = place_of(jnp.stack(keys_near, 1))
     own_place = keys_near[0][:, None, :] == slots_iota[0]
 
-    def pick_rows(values):
-        picked = jnp.einsum("sepk,skd->espd", place, values, preferred_element_type=F32)
+    def pick_rows(places, values):
+        picked = jnp.einsum("sepk,skd->espd", places, values, preferred_element_type=F32)
         return picked.astype(BF16).reshape(nt, nz * CAP, part)
 
     def send_out(picked):
         return jnp.swapaxes(swap_t(picked), 0, 1).reshape(nz * CAP, width)
 
     def send_back(values):
-        return [lay.over_t(part_for(values, k), k) for k in range(nt)]
+        return swap_t(jnp.swapaxes(values.reshape(nz * CAP, nt, part), 0, 1))
 
     def combine(parts):
-        parts = jnp.stack(parts).reshape(nt, nz, CAP, part)
-        summed = jnp.einsum("sepk,espd->skd", place_near, parts, preferred_element_type=F32)
+        parts = parts.reshape(nt, nz, CAP, part)
+        summed = jnp.einsum("sepk,espd->skd", place, parts, preferred_element_type=F32)
         return summed.astype(BF16)
 
 
@@ -557,10 +566,6 @@
     out_w = rows_of(at, out_rows)
     up_w = front[:, at + out_rows :].reshape(LATENT, heads * (NOPE + VDIM))
 
-    cosine, sine = angle_tables(rows)
-    wide_cos, wide_sin = jnp.tile(cosine, (1, heads)), jnp.tile(sine, (1, heads))
-    inputs = hidden.astype(F32)
-    attn_inverse = inverse_rms(inputs)
     attn_scale = gain_attn.astype(F32)
     normed_low = (inputs * attn_inverse * attn_scale).astype(BF16)
     query = dot_nt(normed_low, query_t)
@@ -575,17 +580,28 @@
         ),
         1,
     ).astype(BF16)
-    latent_all = dot_nt(normed_low, down_t)
+    turned_t = jnp.concatenate(
+        [down_t[:LATENT]]
+        + [down_t[LATENT : LATENT + half]] * heads
+        + [down_t[LATENT + half :]] * heads,
+        0,
+    )
+    latent_all = dot_nt(normed_low, turned_t)
+    latent_all, by_column = lax.optimization_barrier((latent_all, by_column))
+    by_plane = swap_z(jnp.swapaxes(by_column, 0, 1))
     latent = latent_all[:, :LATENT]
     kv_inverse = inverse_rms(latent)
     latent_hat = latent * kv_inverse
     kv_scale = gain_kv.astype(F32)
     latent_low = (latent_hat * kv_scale).astype(BF16)
-    key_first, key_second = rotate(
-        latent_all[:, LATENT : LATENT + half], latent_all[:, LATENT + half :], cosine, sine
-    )
     key_rope = jnp.concatenate(
-        [jnp.tile(key_first, (1, heads)), jnp.tile(key_second, (1, heads))], 1
+        rotate(
+            latent_all[:, LATENT : LATENT + heads * half],
+            latent_all[:, LATENT + heads * half :],
+            wide_cos,
+            wide_sin,
+        ),
+        1,
     ).astype(BF16)
     keys_values = dot(latent_low, up_w).astype(BF16)
     attended_low, log_totals = attend(
@@ -604,11 +620,12 @@
     ffn_scale = lax.dynamic_slice_in_dim(gain_ffn, me_t * part, part, 0).astype(F32)
     ffn_part = (ffn_hat * ffn_scale).astype(BF16)
 
-    ffn_part, cot_picked = lax.optimization_barrier((ffn_part, pick_rows(cot_all[:, :rows])))
+    ffn_part, cot_picked = lax.optimization_barrier((ffn_part, pick_rows(place_near, cot_all[:, :rows])))
     ffn_all = gather_z(ffn_part)
-    cot_rows = send_out(cot_picked)
-    picked = pick_rows(ffn_all)
-    ffn_low = gather_t(ffn_part)
+    cot_rows = join_columns([lay.over_t(cot_picked[k], k) for k in range(nt)], me_t, nt)
+    ffn_low = gather_t_direct(ffn_part)
+    ffn_all, cot_rows, ffn_low = lax.optimization_barrier((ffn_all, cot_rows, ffn_low))
+    picked = pick_rows(place, ffn_all)
     shared_pack = jnp.concatenate(
         [jnp.swapaxes(w_shared_in, 1, 2).reshape(-1, d_loc), w_shared_out], 0
     )
@@ -643,6 +660,7 @@
     gate_silu = gate_pre * gate_sig
     active = (gate_silu * up_pre).astype(BF16)
     rows_out = (dot(active, own_out) * gate_rows).astype(BF16)
+    rows_out, cot_rows = lax.optimization_barrier((rows_out, cot_rows))
     out_parts = send_back(rows_out)
     active_grad_raw = dot_nt(cot_rows, own_out)
     gate_grad = jnp.sum(active.astype(F32) * active_grad_raw, axis=-1).reshape(nz, CAP)
@@ -656,16 +674,18 @@
     ).astype(BF16)
     gated_active = (active.astype(F32) * gate_rows).astype(BF16)
     rows_grad = dot(pre_low, own_in).astype(BF16)
+    rows_grad, out_parts = lax.optimization_barrier((rows_grad, out_parts))
     grad_parts = send_back(rows_grad)
-    routed = combine(out_parts)
+    routed, pre_low = lax.optimization_barrier((combine(out_parts), pre_low))
+    routed = scatter_z(routed).astype(F32)
     grad_in_own = dot_tn(pre_low, expert_rows).astype(BF16)
     grad_out_own = dot_tn(gated_active, cot_rows).astype(BF16)
+    grad_parts, grad_in_own, grad_out_own = lax.optimization_barrier(
+        (grad_parts, grad_in_own, grad_out_own)
+    )
     grad_pieces = take_apart(lay, ids, grad_in_own, grad_out_own, f_loc, d_loc, width)
-    grad_parts, grad_pieces, routed = lax.optimization_barrier((grad_parts, grad_pieces, routed))
-    routed = scatter_z(routed).astype(F32)
+    grad_class = sum(lay.over_c(grad_pieces[k], k).astype(F32) for k in range(nq)).astype(BF16)
     routed_grad = scatter_z(combine(grad_parts)).astype(F32)
-    grad_class = sum(lay.over_c(grad_pieces[k], k).astype(F32) for k in range(nq)).astype(BF16)
-    routed_grad, grad_class = lax.optimization_barrier((routed_grad, grad_class))
     grad_plane = swap_z(grad_class.reshape(nz, nt, 3, f_loc, d_loc))
 
     token_grad = jnp.sum(jnp.where(own_place, gate_grad[:, :, None], 0.0), axis=1)
@@ -739,6 +759,17 @@
 
     output = gather_t_direct((residual + routed + shared_part).astype(BF16))
 
+    def sum_dp(values):
+        return lax.psum_scatter(values, "dp", scatter_dimension=0, tiled=False).astype(F32)
+
+    def by_owner(values):
+        return jnp.swapaxes(values.astype(BF16).reshape(-1, ndp, d_loc), 0, 1)
+
+    shared_grads = jnp.concatenate([by_owner(grad_shared_in), by_owner(grad_shared_out)], 1)
+    residual_low, shared_grads, grad_plane = lax.optimization_barrier(
+        (residual_low, shared_grads, grad_plane)
+    )
+    shared_sum = sum_dp(shared_grads)
     grad_out_w = dot_tn(attended_low, residual_low)
     attended_grad = dot_nt(residual_low, out_w).astype(BF16)
     query_nope_grad, query_turned_grad, kv_grad, rope_grad = attend_back(
@@ -760,7 +791,10 @@
     )
     rope_sum = rope_grad.reshape(rows, 2, heads, half).sum(2)
     key_rope_part = jnp.concatenate(
-        rotate_back(rope_sum[:, 0], rope_sum[:, 1], cosine, sine), 1
+        rotate_back(
+            rope_sum[:, 0], rope_sum[:, 1], wide_cos[:, :half], wide_sin[:, :half]
+        ),
+        1,
     )
     latent_part = dot_nt(kv_grad, up_w)
     grad_kv_gain = jnp.sum(latent_part * latent_hat, axis=0)
@@ -769,23 +803,17 @@
         scaled_kv - latent_hat * jnp.mean(latent_hat * scaled_kv, axis=-1, keepdims=True)
     )
     down_grad = jnp.concatenate([latent_back, key_rope_part], -1).astype(BF16)
-    normed_grad = scatter_t(dot(query_grad, query_t) + dot(down_grad, down_t))
-    normed_grad, grad_plane = lax.optimization_barrier((normed_grad, grad_plane))
+    normed_grad = scatter_t_direct(dot(query_grad, query_t) + dot(down_grad, down_t))
+    grad_home = swap_t(jnp.swapaxes(grad_plane, 0, 1)).reshape(EXPERTS, 3, f_loc, d_loc)
+    normed_grad, grad_home = lax.optimization_barrier((normed_grad, grad_home))
     attn_hat = own_part(hidden).astype(F32) * attn_inverse
     scaled_in = lax.dynamic_slice_in_dim(attn_scale, me_t * part, part, 0) * normed_grad
     attn_gain_part = jnp.sum(normed_grad * attn_hat, axis=0)
     input_grad = residual_grad + attn_inverse * (
         scaled_in - attn_hat * row_mean(attn_hat * scaled_in)
     )
-    grad_home = swap_t(jnp.swapaxes(grad_plane, 0, 1)).reshape(EXPERTS, 3, f_loc, d_loc)
     grad_expert_in, grad_expert_out = home_gradients(lay, ids, grad_home, f_loc, d_loc)
-    grad_hidden = gather_t(input_grad.astype(BF16))
-
-    def sum_dp(values):
-        return lax.psum_scatter(values, "dp", scatter_dimension=0, tiled=False).astype(F32)
-
-    def by_owner(values):
-        return jnp.swapaxes(values.astype(BF16).reshape(-1, ndp, d_loc), 0, 1)
+    grad_hidden = gather_t_direct(input_grad.astype(BF16))
 
     def spread(values):
         return lax.dynamic_update_slice(
@@ -809,9 +837,6 @@
             1,
         )
     )
-    shared_grads = jnp.concatenate([by_owner(grad_shared_in), by_owner(grad_shared_out)], 1)
-    front_sum, shared_grads = lax.optimization_barrier((front_sum, shared_grads))
-    shared_sum = sum_dp(shared_grads)
     own_sum = lax.psum(front_sum[: down_rows + EXPERTS], "tensor")
     at = down_rows + 2 * EXPERTS
     return (

time: 1850 us -> 1690 us (0.914)
  waiting for transfers between devices: 1010 us -> 767 us
  Pallas kernels: 90.1 us -> 127 us
  blocking collectives: 58.4 us -> 90.6 us
  matrix products: 296 us -> 315 us
    reduce_scatter x2, waiting for transfers between devices: 148 us -> 0.01 us  [sum_dp(): lax.psum_scatter(values, 'dp', scatter_dimension=0, tiled=False).astype(F32)]
    reduce_scatter x2, waiting for transfers between devices: 5.31 us -> 133 us  [scatter_z(): lax.psum_scatter(values, 'dp', scatter_dimension=0, tiled=False, axis_ind...]
    ppermute x18 -> x24, waiting for transfers between devices: 280 us -> 168 us  [over_t(): return lax.ppermute(values, 'tensor', [(i, i ^ k) for i in range(self.t)])]
    all_to_all x4 -> x5, waiting for transfers between devices: 240 us -> 145 us  [swap_t(): lax.all_to_all(values, 'tensor', split_axis=0, concat_axis=0, tiled=True)]
    all_gather x1, waiting for transfers between devices: 0.01 us -> 54.4 us  [body(): front = lax.all_gather(front_pack, 'dp', axis=0, tiled=False)]
    reduce_scatter x2 -> x1, waiting for transfers between devices: 70.6 us -> 17.3 us  [scatter_t(): lax.psum_scatter(values.astype(BF16), 'tensor', scatter_dimension=1, tile...]
    all_gather x2, waiting for transfers between devices: 39.2 us -> 0.01 us  [gather_z(): lax.all_gather(values, 'dp', axis=0, tiled=False, axis_index_groups=lay.z...]
    pallas_call x1 -> x4, Pallas kernels: 9.18 us -> 45.8 us  [join_columns(): pl.pallas_call(kernel, out_shape=jax.ShapeDtypeStruct((rows, count * part...]
  transfers between devices with their start and end apart: 46 -> 50, of which waited for: 24 -> 20; matrix products, arithmetic and copies ran while one was open for 28% -> 32% of each run, Pallas kernels for 5% -> 8%
where the time goes in v3:
time: 1690 us; the launch traced here: 1680 us
  waiting for transfers between devices  767 us (45%)
  matrix products  315 us (19%)
  local copies, waits for them, and re-layouts  196 us (12%)
  Pallas kernels  127 us (8%)
  blocking collectives  90.6 us (5%)
  starting transfers between devices  87.4 us (5%)
  other arithmetic  80.2 us (5%)
    all_to_all x2, waiting for transfers between devices, swap_z(): lax.all_to_all(values, 'dp', split_axis=0, concat_axis=0, axis_index_grou...  170 us
    ppermute x24, waiting for transfers between devices, over_t(): return lax.ppermute(values, 'tensor', [(i, i ^ k) for i in range(self.t)])  168 us
    all_to_all x5, waiting for transfers between devices, swap_t(): lax.all_to_all(values, 'tensor', split_axis=0, concat_axis=0, tiled=True)  145 us
    reduce_scatter x2, waiting for transfers between devices, scatter_z(): lax.psum_scatter(values, 'dp', scatter_dimension=0, tiled=False, axis_ind...  133 us
    dot_general x9, matrix products, dot_nt(): lax.dot_general(a, b, (((1,), (1,)), ((), ())), preferred_element_type=F32)  106 us
    psum x3, blocking collectives, row_mean(): return lax.psum(partial, 'tensor').reshape(-1, 1) * (1.0 / width)  90.6 us
    dot_general x8, matrix products, dot_tn(): lax.dot_general(a, b, (((0,), (0,)), ((), ())), preferred_element_type=F32)  79.1 us
    dot_general x8, matrix products, dot(): return jnp.dot(a, b, preferred_element_type=F32)  66.5 us
  transfers between devices with their start and end apart: 50, of which 20 were waited for; matrix products, arithmetic and copies ran while one was open for 32% of the time, Pallas kernels for 8%

profile of v3, /device:TPU:10, one launch (start us, length us, event | category | flops | bytes accessed | tf_op | source)
XLA Modules:
  0.0 1680.3 jit_solution(7648237160613109454)
XLA Ops:
  15.2 7.7 maximum_bitcast_fusion
  22.9 8.6 copy.380
  31.5 6.3 all-to-all-start
  44.9 54.4 %all-gather.12.cloned.1.call-done = bf16[17152,256]{1,0:T(8,128)(2,1)} async-done(((bf16[2144,256]{1,0:T(8,128)(2,1)}), bf16[17152,256]{1,0:T(8,128)(2,1)}) %all-gather.12.cloned.1.call-update) | async-done | bytes 8781840 | tf_op jit(solution)/shard_map/all_gather | solution.py:498
  110.3 7.8 concatenate.60
  119.0 8.4 fusion.109
  145.3 6.5 fusion.111
  162.3 14.9 attend.1
  184.0 7.7 copy.390
  191.6 6.6 all-to-all-start.2
  200.8 13.5 convert_bitcast_fusion.1
  214.2 7.4 copy.386
  221.7 17.3 %reduce-scatter.6.cloned.1.call-done = bf16[1024,512]{1,0:T(8,128)(2,1)} async-done(((bf16[1024,2048]{1,0:T(8,128)(2,1)}), bf16[1024,512]{1,0:T(8,128)(2,1)}) %reduce-scatter.6.cloned.1.call-update) | async-done | bytes 1048592 | tf_op jit(solution)/shard_map/reduce_scatter | solution.py:429
  240.9 8.1 psum.28
  254.2 6.4 slice_bitcast_fusion.3
  265.5 13.5 collective-permute-done.3.refs_1_
  281.3 169.9 %all-to-all-done.2 = bf16[4,4,3,352,256]{4,3,2,1,0:T(8,128)(2,1)} async-done(((bf16[4,4,3,352,256]{4,3,2,1,0:T(8,128)(2,1)}), bf16[4,4,3,352,256]{4,3,2,1,0:T(8,128)(2,1)}, u32[]{:S(2)}, u32[]{:S(2)}) %all-to-all-start.2) | async-done | bytes 8650784 | tf_op jit(solution)/shard_map/all_to_all | solution.py:437
  453.4 9.2 join_columns.5
  462.7 18.1 %join_columns.4 = bf16[2048,2048]{1,0:T(8,128)(2,1)} custom-call(s32[1]{0:T(128)} %bitcast.me_ref, bf16[2048,512]{1,0:T(8,128)(2,1)} %get-tuple-element.211.refs_0_, bf16[2048,512]{1,0:T(8,128)(2,1)} %collective-permute-done.refs_1_, bf16[2048,512]{1,0:T(8,128)(2,1)} %collective-permute-done.1.refs_2_, bf16[2048,512]{1,0:T(8,128)(2,1)} %collective-permute-done.2.refs_3_), custom_call_target="tpu_custom_call" | custom-call | bytes 16777216 | tf_op jit(solution)/shard_map/join_columns/pallas_call | solution.py:197
  480.8 16.2 convert_bitcast_fusion
  497.0 7.5 copy.388
  525.5 16.7 lay_out_weights.1
  544.7 58.6 %all-to-all-done.1 = bf16[4,2048,512]{2,1,0:T(8,128)(2,1)} async-done(((bf16[4,2048,512]{2,1,0:T(8,128)(2,1)}), bf16[4,2048,512]{2,1,0:T(8,128)(2,1)}, u32[]{:S(2)}, u32[]{:S(2)}) %all-to-all-start.1) | async-done | bytes 8388640 | tf_op jit(solution)/shard_map/all_to_all | solution.py:434
  603.3 11.4 copy.389
  614.7 32.3 %fusion.121 = f32[2048,2816]{1,0:T(8,128)} fusion(bf16[2048,2048]{0,1:T(8,128)(2,1)} %bitcast.392, bf16[2816,2048]{1,0:T(8,128)(2,1)} %bitcast.479), kind=kOutput, calls=%fused_computation.280 | convolution fusion | flops 23622320128 | bytes 42991616 | tf_op jit(solution)/shard_map/dot_general | solution.py:30
  647.0 9.1 multiply_convert_fusion.3
  658.7 15.2 multiply_convert_fusion
  673.9 29.7 %multiply_convert_fusion.2 = (bf16[2048,1408]{1,0:T(8,128)(2,1)}, bf16[2048,1408]{1,0:T(8,128)(2,1)}, f32[2048]{0:T(1024)}) fusion(f32[2048,2816]{1,0:T(8,128)} %fusion.121, f32[2048]{0:T(1024)S(1)} %bitcast.467, bf16[2048,1408]{1,0:T(8,128)(2,1)} %copy-done.33, bf16[2048,2048]{1,0:T(8,128)(2,1)} %join_columns.4, bf16[1408,2048]{1,0:T(8,128)(2,1)S(1)} %copy-done.8), kind=kOutput, calls=%fused_computation.18 | convolution fusion | flops 11860178944 | bytes 54542336 | tf_op jit(solution)/shard_map/dot_general | solution.py:30
  703.6 7.6 copy.488
  711.1 6.6 all-to-all-start.3
  717.7 11.3 pad_maximum_fusion
  729.1 18.4 %convolution_convert_fusion.2.out_ref = bf16[1408,2048]{1,0:T(8,128)(2,1)} fusion(bf16[2048,2048]{1,0:T(8,128)(2,1)} %join_columns.4, bf16[2048,1408]{1,0:T(8,128)(2,1)} %copy-done.33, f32[2048]{0:T(1024)S(1)} %bitcast.468), kind=kOutput, calls=%fused_computation.42 | convolution fusion | flops 11822694400 | bytes 19931136 | tf_op jit(solution)/shard_map/dot_general | solution.py:34
  747.5 28.6 %convolution_convert_fusion.3 = bf16[2048,2048]{1,0:T(8,128)(2,1)} fusion(bf16[2816,2048]{1,0:T(8,128)(2,1)} %bitcast.480, bf16[2048,1408]{1,0:T(8,128)(2,1)S(1)} %bitcast.406, bf16[2048,1408]{1,0:T(8,128)(2,1)S(1)} %bitcast.404), kind=kOutput, calls=%fused_computation.43 | convolution fusion | flops 23649583104 | bytes 31457280 | tf_op jit(solution)/shard_map/dot_general | solution.py:26
  776.1 33.6 %all-to-all-done.3 = bf16[4,2048,512]{2,1,0:T(8,128)(2,1)} async-done(((bf16[4,2048,512]{2,1,0:T(8,128)(2,1)}), bf16[4,2048,512]{2,1,0:T(8,128)(2,1)}, u32[]{:S(2)}, u32[]{:S(2)}) %all-to-all-start.3) | async-done | bytes 8388640 | tf_op jit(solution)/shard_map/all_to_all | solution.py:434
  809.7 7.5 copy.487
  817.1 6.3 all-to-all-start.4
  823.5 12.3 bitcast_convert_fusion.1
  835.8 31.5 %convolution_convert_fusion = bf16[2816,2048]{1,0:T(8,128)(2,1)} fusion(bf16[2048,2816]{1,0:T(8,128)(2,1)} %pad_maximum_fusion, bf16[2048,2048]{0,1:T(8,128)(2,1)} %bitcast.393), kind=kOutput, calls=%fused_computation.22 | convolution fusion | flops 23628087296 | bytes 31457280 | tf_op jit(solution)/shard_map/dot_general | solution.py:34
  867.3 47.5 %all-to-all-done.4 = bf16[4,2048,512]{2,1,0:T(8,128)(2,1)} async-done(((bf16[4,2048,512]{2,1,0:T(8,128)(2,1)}), bf16[4,2048,512]{2,1,0:T(8,128)(2,1)}, u32[]{:S(2)}, u32[]{:S(2)}) %all-to-all-start.4) | async-done | bytes 8388640 | tf_op jit(solution)/shard_map/all_to_all | solution.py:434
  914.8 12.1 bitcast_convert_fusion
  929.6 14.1 take_apart.1
  959.4 8.3 copy.399
  967.7 10.0 add_convert_fusion
  977.7 8.2 all-to-all-start.5
  986.0 10.5 fusion.122
  1007.8 6.7 fusion.45
  1024.1 17.4 %collective-permute-done.22 = f32[4,8,128]{2,1,0:T(8,128)S(1)} collective-permute-done((f32[4,8,128]{2,1,0:T(8,128)S(1)}, f32[4,8,128]{2,1,0:T(8,128)S(1)}, u32[]{:S(2)}, u32[]{:S(2)}) %collective-permute-start.22) | collective-permute-done | bytes 16416 | tf_op jit(solution)/shard_map/ppermute | solution.py:68
  1045.1 19.0 %collective-permute-done.24 = f32[4,8,128]{2,1,0:T(8,128)S(1)} collective-permute-done((f32[4,8,128]{2,1,0:T(8,128)S(1)}, f32[4,8,128]{2,1,0:T(8,128)S(1)}, u32[]{:S(2)}, u32[]{:S(2)}) %collective-permute-start.24) | collective-permute-done | bytes 16416 | tf_op jit(solution)/shard_map/ppermute | solution.py:68
  1067.5 7.2 multiply_reduce_fusion.1
  1074.7 36.1 %psum.29 = f32[8,128]{1,0:T(8,128)S(1)} all-reduce(f32[8,128]{1,0:T(8,128)S(1)} %bitcast.450), channel_id=1, replica_groups=mesh['dp'=8,'tensor'=4] {'tensor'}, use_global_device_ids=true, to_apply=%region_15.16 | all-reduce | flops 1024 | bytes 8192 | tf_op jit(solution)/shard_map/psum | solution.py:616
  1110.9 133.1 %reduce-scatter.8.cloned.1.call-done = bf16[1,1024,512]{2,1,0:T(8,128)(2,1)} async-done(((bf16[4,1024,512]{2,1,0:T(8,128)(2,1)}), bf16[1,1024,512]{2,1,0:T(8,128)(2,1)}) %reduce-scatter.8.cloned.1.call-update) | async-done | bytes 1048592 | tf_op jit(solution)/shard_map/reduce_scatter | solution.py:421
  1250.1 9.8 convolution_convert_fusion.1
  1270.3 33.4 %all-gather.10.cloned.1.call-done = bf16[1024,2048]{1,0:T(8,128)(2,1)} async-done(((bf16[1024,512]{1,0:T(8,128)(2,1)}), bf16[1024,2048]{1,0:T(8,128)(2,1)}) %all-gather.10.cloned.1.call-update) | async-done | bytes 4194320 | tf_op jit(solution)/shard_map/all_gather | solution.py:426
  1313.0 21.6 %attend_back.1 = (bf16[1024,512]{1,0:T(8,128)(2,1)S(1)}, f32[1024,256]{1,0:T(8,128)S(1)}, bf16[1024,1024]{1,0:T(8,128)(2,1)S(1)}, f32[1024,256]{1,0:T(8,128)S(1)}) custom-call(s32[1]{0:T(128)} %copy.509.len_ref, bf16[1024,512]{1,0:T(8,128)(2,1)S(1)} %slice.351.q_ref, bf16[1024,256]{1,0:T(8,128)(2,1)S(1)} %copy-done.3, bf16[1024,1024]{1,0:T(8,128)(2,1)S(1)} %copy-done.10, ...), custom_call_target="tpu_custom_call" | custom-call | flops 6710886400 | bytes 33554432 | tf_op jit(solution)/shard_map/attend_back/pallas_call | solution.py:333
  1340.0 7.7 copy.419
  1347.7 6.2 all-to-all-start.6
  1394.6 76.5 %collective-permute-done.26 = bf16[1024,512]{1,0:T(8,128)(2,1)} collective-permute-done((bf16[1024,512]{1,0:T(8,128)(2,1)}, bf16[1024,512]{1,0:T(8,128)(2,1)}, u32[]{:S(2)}, u32[]{:S(2)}) %collective-permute-start.26) | collective-permute-done | bytes 1048608 | tf_op jit(solution)/shard_map/ppermute | solution.py:68
  1472.4 21.4 %collective-permute-done.28 = bf16[1024,512]{1,0:T(8,128)(2,1)} collective-permute-done((bf16[1024,512]{1,0:T(8,128)(2,1)}, bf16[1024,512]{1,0:T(8,128)(2,1)}, u32[]{:S(2)}, u32[]{:S(2)}) %collective-permute-start.28) | collective-permute-done | bytes 1048608 | tf_op jit(solution)/shard_map/ppermute | solution.py:68
  1509.6 46.4 %psum.30 = f32[8,128]{1,0:T(8,128)S(1)} all-reduce(f32[8,128]{1,0:T(8,128)S(1)} %bitcast.449), channel_id=1, replica_groups=mesh['dp'=8,'tensor'=4] {'tensor'}, use_global_device_ids=true, to_apply=%region_19.20 | all-reduce | flops 1024 | bytes 8192 | tf_op jit(solution)/shard_map/psum | solution.py:616
  1562.9 9.2 join_columns.6
  1572.1 14.5 home_gradients.1
  1586.6 17.8 %collective-permute-done.30.refs_2_ = bf16[1024,512]{1,0:T(8,128)(2,1)S(1)} collective-permute-done((bf16[1024,512]{1,0:T(8,128)(2,1)}, bf16[1024,512]{1,0:T(8,128)(2,1)S(1)}, u32[]{:S(2)}, u32[]{:S(2)}) %collective-permute-start.30) | collective-permute-done | bytes 1048608 | tf_op jit(solution)/shard_map/ppermute | solution.py:68
  1605.6 9.2 join_columns.7
  1627.0 41.9 %all-reduce.7.cloned.1.call-done = f32[592,256]{1,0:T(8,128)} async-done(((f32[592,256]{1,0:T(8,128)}), f32[592,256]{1,0:T(8,128)}) %all-reduce.7.cloned.1.call-update) | async-done | bytes 606224 | tf_op jit(solution)/shard_map/psum | solution.py:840
  (450 shorter events, 265.4 us)
Async XLA Ops:
  7.2 92.1 %all-gather.12.cloned.1.call-start = ((), (), s32[]{:S(2)}) async-start(), calls=%async_computation.19 | async-start | bytes 9879552 | tf_op jit(solution)/shard_map/all_gather | solution.py:498
  31.5 101.0 %all-to-all-start = ((bf16[4,4,3,352,256]{4,3,2,1,0:T(8,128)(2,1)}), bf16[4,4,3,352,256]{4,3,2,1,0:T(8,128)(2,1)}, u32[]{:S(2)}, u32[]{:S(2)}) async-start(bf16[4,4,3,352,256]{4,3,2,1,0:T(8,128)(2,1)} %copy.380), calls=%async_computation | async-start | bytes 17301504 | tf_op jit(solution)/shard_map/all_to_all | solution.py:434
  37.8 146.2 %all-gather.14.cloned.1.call-start = ((), (), s32[]{:S(2)}) async-start(), calls=%async_computation.20 | async-start | bytes 5324800 | tf_op jit(solution)/shard_map/all_gather | solution.py:418
  43.3 102.0 %copy-start.75 = (f32[1024]{0:T(1024)}, f32[1024]{0:T(1024)S(1)}, u32[]{:S(2)}) copy-start(f32[1024]{0:T(1024)S(1)} %add_rsqrt_fusion.1) | copy-start | bytes 12292
  101.0 137.9 %reduce-scatter.6.cloned.1.call-start = ((), (), s32[]{:S(2)}) async-start(), calls=%async_computation.12 | async-start | bytes 5242880 | tf_op jit(solution)/shard_map/reduce_scatter | solution.py:429
  191.6 259.6 %all-to-all-start.2 = ((bf16[4,4,3,352,256]{4,3,2,1,0:T(8,128)(2,1)}), bf16[4,4,3,352,256]{4,3,2,1,0:T(8,128)(2,1)}, u32[]{:S(2)}, u32[]{:S(2)}) async-start(bf16[4,4,3,352,256]{4,3,2,1,0:T(8,128)(2,1)} %copy.390), calls=%async_computation.3 | async-start | bytes 17301504 | tf_op jit(solution)/shard_map/all_to_all | solution.py:437
  198.2 282.6 %all-gather.16.cloned.1.call-start = ((), (), s32[]{:S(2)}) async-start(), calls=%async_computation.21 | async-start | bytes 5242880 | tf_op jit(solution)/shard_map/all_gather | solution.py:418
  198.3 50.7 %copy-start.77 = (f32[512]{0:T(512)}, f32[512]{0:T(512)S(1)}, u32[]{:S(2)}) copy-start(f32[512]{0:T(512)S(1)} %dynamic-slice_convert_fusion.9) | copy-start | bytes 6148
  252.6 198.7 %copy-start.56 = (bf16[704,256]{1,0:T(8,128)(2,1)S(1)}, bf16[704,256]{1,0:T(8,128)(2,1)}, u32[]{:S(2)}) copy-start(bf16[704,256]{1,0:T(8,128)(2,1)} %param.30) | copy-start | bytes 1081348
  252.6 26.4 %collective-permute-start.3 = (bf16[1024,512]{1,0:T(8,128)(2,1)}, bf16[1024,512]{1,0:T(8,128)(2,1)S(1)}, u32[]{:S(2)}, u32[]{:S(2)}) collective-permute-start(bf16[1024,512]{1,0:T(8,128)(2,1)} %multiply_convert_fusion.8.refs_0_), channel_id=1, source_target_pairs={{0,1},{1,0},{2,3},{3,2},{4,5},{5,4},{6,7},{7,6},{8,9},{9,8},{10,11... | collective-permute-start | bytes 3145736 | tf_op jit(solution)/shard_map/ppermute | solution.py:68
  260.6 202.1 %collective-permute-start = (bf16[2048,512]{1,0:T(8,128)(2,1)}, bf16[2048,512]{1,0:T(8,128)(2,1)}, u32[]{:S(2)}, u32[]{:S(2)}) collective-permute-start(bf16[2048,512]{1,0:T(8,128)(2,1)} %get-tuple-element.210), channel_id=1, source_target_pairs={{0,1},{1,0},{2,3},{3,2},{4,5},{5,4},{6,7},{7,6},{8,9},{9,8},{10,11... | collective-permute-start | bytes 6291464 | tf_op jit(solution)/shard_map/ppermute | solution.py:68
  261.1 201.5 %collective-permute-start.1 = (bf16[2048,512]{1,0:T(8,128)(2,1)}, bf16[2048,512]{1,0:T(8,128)(2,1)}, u32[]{:S(2)}, u32[]{:S(2)}) collective-permute-start(bf16[2048,512]{1,0:T(8,128)(2,1)} %get-tuple-element.209), channel_id=1, source_target_pairs={{0,2},{1,3},{2,0},{3,1},{4,6},{5,7},{6,4},{7,5},{8,10},{9,11},{10,... | collective-permute-start | bytes 6291464 | tf_op jit(solution)/shard_map/ppermute | solution.py:68
  262.5 200.2 %collective-permute-start.2 = (bf16[2048,512]{1,0:T(8,128)(2,1)}, bf16[2048,512]{1,0:T(8,128)(2,1)}, u32[]{:S(2)}, u32[]{:S(2)}) collective-permute-start(bf16[2048,512]{1,0:T(8,128)(2,1)} %get-tuple-element.208), channel_id=1, source_target_pairs={{0,3},{1,2},{2,1},{3,0},{4,7},{5,6},{6,5},{7,4},{8,11},{9,10},{10,... | collective-permute-start | bytes 6291464 | tf_op jit(solution)/shard_map/ppermute | solution.py:68
  264.1 187.2 %collective-permute-start.4 = (bf16[1024,512]{1,0:T(8,128)(2,1)S(1)}, bf16[1024,512]{1,0:T(8,128)(2,1)}, u32[]{:S(2)}, u32[]{:S(2)}) collective-permute-start(bf16[1024,512]{1,0:T(8,128)(2,1)S(1)} %copy-done.26), channel_id=1, source_target_pairs={{0,2},{1,3},{2,0},{3,1},{4,6},{5,7},{6,4},{7,5},{8,10},{9,11},{10,... | collective-permute-start | bytes 3145736 | tf_op jit(solution)/shard_map/ppermute | solution.py:68
  279.0 174.4 %copy-start.52 = (bf16[1024,512]{1,0:T(8,128)(2,1)}, bf16[1024,512]{1,0:T(8,128)(2,1)S(1)}, u32[]{:S(2)}) copy-start(bf16[1024,512]{1,0:T(8,128)(2,1)S(1)} %collective-permute-done.3.refs_1_) | copy-start | bytes 3145732
  279.0 174.4 %collective-permute-start.5 = (bf16[1024,512]{1,0:T(8,128)(2,1)S(1)}, bf16[1024,512]{1,0:T(8,128)(2,1)}, u32[]{:S(2)}, u32[]{:S(2)}) collective-permute-start(bf16[1024,512]{1,0:T(8,128)(2,1)S(1)} %copy-done.26), channel_id=1, source_target_pairs={{0,3},{1,2},{2,1},{3,0},{4,7},{5,6},{6,5},{7,4},{8,11},{9,10},{10,... | collective-permute-start | bytes 3145736 | tf_op jit(solution)/shard_map/ppermute | solution.py:68
  451.3 74.3 %collective-permute-start.6 = (bf16[16,3,352,256]{3,2,1,0:T(8,128)(2,1)}, bf16[16,3,352,256]{3,2,1,0:T(8,128)(2,1)}, u32[]{:S(2)}, u32[]{:S(2)}) collective-permute-start(bf16[16,3,352,256]{3,2,1,0:T(8,128)(2,1)} %bitcast.53.refs_0_), channel_id=1, source_target_pairs={{0,4},{4,0},{8,12},{12,8},{16,20},{20,16},{24,28},{28,24},{1,5},{5... | collective-permute-start | bytes 25952264 | tf_op jit(solution)/shard_map/ppermute | solution.py:78
  504.5 98.8 %all-to-all-start.1 = ((bf16[4,2048,512]{2,1,0:T(8,128)(2,1)}), bf16[4,2048,512]{2,1,0:T(8,128)(2,1)}, u32[]{:S(2)}, u32[]{:S(2)}) async-start(bf16[4,2048,512]{2,1,0:T(8,128)(2,1)} %bitcast.368), calls=%async_computation.2 | async-start | bytes 16777216 | tf_op jit(solution)/shard_map/all_to_all | solution.py:434
  510.6 443.2 %all-gather.18.cloned.1.call-start = ((), (), s32[]{:S(2)}) async-start(), calls=%async_computation.22 | async-start | bytes 9732096 | tf_op jit(solution)/shard_map/all_gather | solution.py:634
  515.0 6.0 collective-permute-start.7
  516.5 5.9 collective-permute-start.8
  520.8 3.6 collective-permute-start.9
  520.9 406.1 %copy-start.6 = (s32[3]{0:T(128)}, s32[3]{0:T(128)S(1)}, u32[]{:S(2)}) copy-start(s32[3]{0:T(128)S(1)} %pad_add_fusion.1.ids_ref) | copy-start | bytes 40
  711.1 98.5 %all-to-all-start.3 = ((bf16[4,2048,512]{2,1,0:T(8,128)(2,1)}), bf16[4,2048,512]{2,1,0:T(8,128)(2,1)}, u32[]{:S(2)}, u32[]{:S(2)}) async-start(bf16[4,2048,512]{2,1,0:T(8,128)(2,1)} %bitcast.370), calls=%async_computation.4 | async-start | bytes 16777216 | tf_op jit(solution)/shard_map/all_to_all | solution.py:434
  717.7 29.7 %slice-start.2 = ((s8[5767168]{0:T(1024)(128)(4,1)}), s8[4194304]{0:T(1024)(128)(4,1)S(1)}, s32[]{:S(2)}) async-start(s8[5767168]{0:T(1024)(128)(4,1)} %bitcast.403), calls=%async_computation.25 | async-start | bytes 8388608
  717.7 29.7 %slice-start.4 = ((s8[5767168]{0:T(1024)(128)(4,1)}), s8[4194304]{0:T(1024)(128)(4,1)S(1)}, s32[]{:S(2)}) async-start(s8[5767168]{0:T(1024)(128)(4,1)} %bitcast.405), calls=%async_computation.27 | async-start | bytes 8388608
  817.1 97.7 %all-to-all-start.4 = ((bf16[4,2048,512]{2,1,0:T(8,128)(2,1)}), bf16[4,2048,512]{2,1,0:T(8,128)(2,1)}, u32[]{:S(2)}, u32[]{:S(2)}) async-start(bf16[4,2048,512]{2,1,0:T(8,128)(2,1)} %bitcast.371), calls=%async_computation.6 | async-start | bytes 16777216 | tf_op jit(solution)/shard_map/all_to_all | solution.py:434
  823.5 244.0 %reduce-scatter.10.cloned.1.call-start = ((), (), s32[]{:S(2)}) async-start(), calls=%async_computation.14 | async-start | bytes 5242880 | tf_op jit(solution)/shard_map/reduce_scatter | solution.py:421
  926.9 317.0 %reduce-scatter.8.cloned.1.call-start = ((), (), s32[]{:S(2)}) async-start(), calls=%async_computation.13 | async-start | bytes 5242880 | tf_op jit(solution)/shard_map/reduce_scatter | solution.py:421
  947.2 20.5 %collective-permute-start.25 = (bf16[16,3,352,256]{3,2,1,0:T(8,128)(2,1)}, bf16[16,3,352,256]{3,2,1,0:T(8,128)(2,1)}, u32[]{:S(2)}, u32[]{:S(2)}) collective-permute-start(bf16[16,3,352,256]{3,2,1,0:T(8,128)(2,1)} %get-tuple-element.85), channel_id=1, source_target_pairs={{0,4},{4,0},{8,12},{12,8},{16,20},{20,16},{24,28},{28,24},{1,5},{5... | collective-permute-start | bytes 25952264 | tf_op jit(solution)/shard_map/ppermute | solution.py:78
  948.7 66.6 %collective-permute-start.19 = (f32[8,128]{1,0:T(8,128)S(1)}, f32[8,128]{1,0:T(8,128)S(1)}, u32[]{:S(2)}, u32[]{:S(2)}) collective-permute-start(f32[8,128]{1,0:T(8,128)S(1)} %get-tuple-element.249), channel_id=1, source_target_pairs={{0,8},{4,12},{8,0},{12,4},{16,24},{20,28},{24,16},{28,20},{1,9},{5... | collective-permute-start | bytes 12296 | tf_op jit(solution)/shard_map/ppermute | solution.py:73
  952.2 63.2 %collective-permute-start.20 = (f32[8,128]{1,0:T(8,128)S(1)}, f32[8,128]{1,0:T(8,128)S(1)}, u32[]{:S(2)}, u32[]{:S(2)}) collective-permute-start(f32[8,128]{1,0:T(8,128)S(1)} %get-tuple-element.248), channel_id=1, source_target_pairs={{0,16},{4,20},{8,24},{12,28},{16,0},{20,4},{24,8},{28,12},{1,17},{... | collective-permute-start | bytes 12296 | tf_op jit(solution)/shard_map/ppermute | solution.py:73
  952.2 63.2 %collective-permute-start.21 = (f32[8,128]{1,0:T(8,128)S(1)}, f32[8,128]{1,0:T(8,128)S(1)}, u32[]{:S(2)}, u32[]{:S(2)}) collective-permute-start(f32[8,128]{1,0:T(8,128)S(1)} %get-tuple-element.247), channel_id=1, source_target_pairs={{0,24},{4,28},{8,16},{12,20},{16,8},{20,12},{24,0},{28,4},{1,25},{... | collective-permute-start | bytes 12296 | tf_op jit(solution)/shard_map/ppermute | solution.py:73
  977.7 326.0 %all-to-all-start.5 = ((bf16[4,4,3,352,256]{4,3,2,1,0:T(8,128)(2,1)}), bf16[4,4,3,352,256]{4,3,2,1,0:T(8,128)(2,1)}, u32[]{:S(2)}, u32[]{:S(2)}) async-start(bf16[4,4,3,352,256]{4,3,2,1,0:T(8,128)(2,1)} %bitcast.367), calls=%async_computation.8 | async-start | bytes 17301504 | tf_op jit(solution)/shard_map/all_to_all | solution.py:437
  986.0 317.7 %all-gather.10.cloned.1.call-start = ((), (), s32[]{:S(2)}) async-start(), calls=%async_computation.15 | async-start | bytes 5242880 | tf_op jit(solution)/shard_map/all_gather | solution.py:426
  1015.0 50.8 %collective-permute-start.16 = (bf16[1024,512]{1,0:T(8,128)(2,1)S(1)}, bf16[1024,512]{1,0:T(8,128)(2,1)S(1)}, u32[]{:S(2)}, u32[]{:S(2)}) collective-permute-start(bf16[1024,512]{1,0:T(8,128)(2,1)S(1)} %get-tuple-element.202), channel_id=1, source_target_pairs={{0,1},{1,0},{2,3},{3,2},{4,5},{5,4},{6,7},{7,6},{8,9},{9,8},{10,11... | collective-permute-start | bytes 3145736 | tf_op jit(solution)/shard_map/ppermute | solution.py:68
  1015.4 26.1 %collective-permute-start.22 = (f32[4,8,128]{2,1,0:T(8,128)S(1)}, f32[4,8,128]{2,1,0:T(8,128)S(1)}, u32[]{:S(2)}, u32[]{:S(2)}) collective-permute-start(f32[4,8,128]{2,1,0:T(8,128)S(1)} %get-tuple-element.245), channel_id=1, source_target_pairs={{0,1},{1,0},{2,3},{3,2},{4,5},{5,4},{6,7},{7,6},{8,9},{9,8},{10,11... | collective-permute-start | bytes 49160 | tf_op jit(solution)/shard_map/ppermute | solution.py:68
  1017.2 27.5 %collective-permute-start.23 = (f32[4,8,128]{2,1,0:T(8,128)S(1)}, f32[4,8,128]{2,1,0:T(8,128)S(1)}, u32[]{:S(2)}, u32[]{:S(2)}) collective-permute-start(f32[4,8,128]{2,1,0:T(8,128)S(1)} %get-tuple-element.245), channel_id=1, source_target_pairs={{0,2},{1,3},{2,0},{3,1},{4,6},{5,7},{6,4},{7,5},{8,10},{9,11},{10,... | collective-permute-start | bytes 49160 | tf_op jit(solution)/shard_map/ppermute | solution.py:68
  1017.5 50.0 %collective-permute-start.17 = (bf16[1024,512]{1,0:T(8,128)(2,1)S(1)}, bf16[1024,512]{1,0:T(8,128)(2,1)}, u32[]{:S(2)}, u32[]{:S(2)}) collective-permute-start(bf16[1024,512]{1,0:T(8,128)(2,1)S(1)} %get-tuple-element.204), channel_id=1, source_target_pairs={{0,2},{1,3},{2,0},{3,1},{4,6},{5,7},{6,4},{7,5},{8,10},{9,11},{10,... | collective-permute-start | bytes 3145736 | tf_op jit(solution)/shard_map/ppermute | solution.py:68
  1019.2 48.3 %collective-permute-start.18 = (bf16[1024,512]{1,0:T(8,128)(2,1)S(1)}, bf16[1024,512]{1,0:T(8,128)(2,1)}, u32[]{:S(2)}, u32[]{:S(2)}) collective-permute-start(bf16[1024,512]{1,0:T(8,128)(2,1)S(1)} %get-tuple-element.203), channel_id=1, source_target_pairs={{0,3},{1,2},{2,1},{3,0},{4,7},{5,6},{6,5},{7,4},{8,11},{9,10},{10,... | collective-permute-start | bytes 3145736 | tf_op jit(solution)/shard_map/ppermute | solution.py:68
  1024.0 43.2 %copy-start.49 = (f32[1024,16]{0,1:T(8,128)S(1)}, f32[1024,16]{0,1:T(8,128)}, u32[]{:S(2)}) copy-start(f32[1024,16]{0,1:T(8,128)} %copy-done.48) | copy-start | bytes 196612
  1024.0 43.2 %copy-start.67 = (f32[1024]{0:T(1024)S(1)}, f32[1024]{0:T(1024)}, u32[]{:S(2)}) copy-start(f32[1024]{0:T(1024)} %copy-done.66) | copy-start | bytes 12292
  1024.0 43.2 %copy-start.71 = (f32[1024]{0:T(1024)S(1)}, f32[1024]{0:T(1024)}, u32[]{:S(2)}) copy-start(f32[1024]{0:T(1024)} %copy-done.70) | copy-start | bytes 12292
  1024.0 43.5 %copy-start.21 = (bf16[1024,512]{1,0:T(8,128)(2,1)S(1)}, bf16[1024,512]{1,0:T(8,128)(2,1)}, u32[]{:S(2)}) copy-start(bf16[1024,512]{1,0:T(8,128)(2,1)} %reduce-scatter.6.cloned.1.call-done) | copy-start | bytes 3145732
  1024.1 43.5 %copy-start.69 = (f32[1024]{0:T(1024)S(1)}, f32[1024]{0:T(1024)}, u32[]{:S(2)}) copy-start(f32[1024]{0:T(1024)} %copy-done.68) | copy-start | bytes 12292
  1024.1 43.5 %copy-start.78 = (f32[512]{0:T(512)S(1)}, f32[512]{0:T(512)}, u32[]{:S(2)}) copy-start(f32[512]{0:T(512)} %copy-done.77) | copy-start | bytes 6148
  1041.5 22.6 %collective-permute-start.24 = (f32[4,8,128]{2,1,0:T(8,128)S(1)}, f32[4,8,128]{2,1,0:T(8,128)S(1)}, u32[]{:S(2)}, u32[]{:S(2)}) collective-permute-start(f32[4,8,128]{2,1,0:T(8,128)S(1)} %get-tuple-element.245), channel_id=1, source_target_pairs={{0,3},{1,2},{2,1},{3,0},{4,7},{5,6},{6,5},{7,4},{8,11},{9,10},{10,... | collective-permute-start | bytes 49160 | tf_op jit(solution)/shard_map/ppermute | solution.py:68
  1044.7 66.2 %collective-permute-start.10 = (bf16[1024,512]{1,0:T(8,128)(2,1)}, bf16[1024,512]{1,0:T(8,128)(2,1)}, u32[]{:S(2)}, u32[]{:S(2)}) collective-permute-start(bf16[1024,512]{1,0:T(8,128)(2,1)} %get-tuple-element.205), channel_id=1, source_target_pairs={{0,1},{1,0},{2,3},{3,2},{4,5},{5,4},{6,7},{7,6},{8,9},{9,8},{10,11... | collective-permute-start | bytes 3145736 | tf_op jit(solution)/shard_map/ppermute | solution.py:68
  1064.1 46.7 %collective-permute-start.11 = (bf16[1024,512]{1,0:T(8,128)(2,1)}, bf16[1024,512]{1,0:T(8,128)(2,1)}, u32[]{:S(2)}, u32[]{:S(2)}) collective-permute-start(bf16[1024,512]{1,0:T(8,128)(2,1)} %get-tuple-element.207), channel_id=1, source_target_pairs={{0,2},{1,3},{2,0},{3,1},{4,6},{5,7},{6,4},{7,5},{8,10},{9,11},{10,... | collective-permute-start | bytes 3145736 | tf_op jit(solution)/shard_map/ppermute | solution.py:68
  1065.8 45.0 %collective-permute-start.12 = (bf16[1024,512]{1,0:T(8,128)(2,1)}, bf16[1024,512]{1,0:T(8,128)(2,1)}, u32[]{:S(2)}, u32[]{:S(2)}) collective-permute-start(bf16[1024,512]{1,0:T(8,128)(2,1)} %get-tuple-element.206), channel_id=1, source_target_pairs={{0,3},{1,2},{2,1},{3,0},{4,7},{5,6},{6,5},{7,4},{8,11},{9,10},{10,... | collective-permute-start | bytes 3145736 | tf_op jit(solution)/shard_map/ppermute | solution.py:68
  1250.1 364.7 %reduce-scatter.14.cloned.1.call-start = ((), (), s32[]{:S(2)}) async-start(), calls=%async_computation.18 | async-start | bytes 9732096 | tf_op jit(solution)/shard_map/reduce_scatter | solution.py:763
  1270.3 34.4 %copy-start.22 = (bf16[8,72,8,256]{3,2,1,0:T(8,128)(2,1)S(1)}, bf16[8,72,8,256]{3,2,1,0:T(8,128)(2,1)}, u32[]{:S(2)}) copy-start(bf16[8,72,8,256]{3,2,1,0:T(8,128)(2,1)} %get-tuple-element.195) | copy-start | bytes 7077892
  1347.7 149.1 %all-to-all-start.6 = ((bf16[4,4,3,352,256]{4,3,2,1,0:T(8,128)(2,1)}), bf16[4,4,3,352,256]{4,3,2,1,0:T(8,128)(2,1)}, u32[]{:S(2)}, u32[]{:S(2)}) async-start(bf16[4,4,3,352,256]{4,3,2,1,0:T(8,128)(2,1)} %copy.419), calls=%async_computation.9 | async-start | bytes 17301504 | tf_op jit(solution)/shard_map/all_to_all | solution.py:434
  1353.9 264.5 %reduce-scatter.12.cloned.1.call-start = ((), (), s32[]{:S(2)}) async-start(), calls=%async_computation.16 | async-start | bytes 9879552 | tf_op jit(solution)/shard_map/reduce_scatter | solution.py:763
  1374.5 96.5 %collective-permute-start.26 = (bf16[1024,512]{1,0:T(8,128)(2,1)}, bf16[1024,512]{1,0:T(8,128)(2,1)}, u32[]{:S(2)}, u32[]{:S(2)}) collective-permute-start(bf16[1024,512]{1,0:T(8,128)(2,1)} %get-tuple-element.199), channel_id=1, source_target_pairs={{0,1},{1,0},{2,3},{3,2},{4,5},{5,4},{6,7},{7,6},{8,9},{9,8},{10,11... | collective-permute-start | bytes 3145736 | tf_op jit(solution)/shard_map/ppermute | solution.py:68
  1374.6 97.8 %collective-permute-start.27 = (bf16[1024,512]{1,0:T(8,128)(2,1)}, bf16[1024,512]{1,0:T(8,128)(2,1)}, u32[]{:S(2)}, u32[]{:S(2)}) collective-permute-start(bf16[1024,512]{1,0:T(8,128)(2,1)} %get-tuple-element.201), channel_id=1, source_target_pairs={{0,2},{1,3},{2,0},{3,1},{4,6},{5,7},{6,4},{7,5},{8,10},{9,11},{10,... | collective-permute-start | bytes 3145736 | tf_op jit(solution)/shard_map/ppermute | solution.py:68
  1376.6 117.2 %collective-permute-start.28 = (bf16[1024,512]{1,0:T(8,128)(2,1)}, bf16[1024,512]{1,0:T(8,128)(2,1)}, u32[]{:S(2)}, u32[]{:S(2)}) collective-permute-start(bf16[1024,512]{1,0:T(8,128)(2,1)} %get-tuple-element.200), channel_id=1, source_target_pairs={{0,3},{1,2},{2,1},{3,0},{4,7},{5,6},{6,5},{7,4},{8,11},{9,10},{10,... | collective-permute-start | bytes 3145736 | tf_op jit(solution)/shard_map/ppermute | solution.py:68
  1504.9 164.0 %all-reduce.7.cloned.1.call-start = ((), (), s32[]{:S(2)}) async-start(), calls=%async_computation.17 | async-start | bytes 1212416 | tf_op jit(solution)/shard_map/psum | solution.py:840
  1506.1 55.4 %collective-permute-start.13 = (bf16[1024,512]{1,0:T(8,128)(2,1)S(1)}, bf16[1024,512]{1,0:T(8,128)(2,1)}, u32[]{:S(2)}, u32[]{:S(2)}) collective-permute-start(bf16[1024,512]{1,0:T(8,128)(2,1)S(1)} %copy-done.34), channel_id=1, source_target_pairs={{0,1},{1,0},{2,3},{3,2},{4,5},{5,4},{6,7},{7,6},{8,9},{9,8},{10,11... | collective-permute-start | bytes 3145736 | tf_op jit(solution)/shard_map/ppermute | solution.py:68
  1507.6 55.3 %collective-permute-start.14 = (bf16[1024,512]{1,0:T(8,128)(2,1)S(1)}, bf16[1024,512]{1,0:T(8,128)(2,1)}, u32[]{:S(2)}, u32[]{:S(2)}) collective-permute-start(bf16[1024,512]{1,0:T(8,128)(2,1)S(1)} %copy-done.34), channel_id=1, source_target_pairs={{0,2},{1,3},{2,0},{3,1},{4,6},{5,7},{6,4},{7,5},{8,10},{9,11},{10,... | collective-permute-start | bytes 3145736 | tf_op jit(solution)/shard_map/ppermute | solution.py:68
  1508.1 54.7 %collective-permute-start.15 = (bf16[1024,512]{1,0:T(8,128)(2,1)S(1)}, bf16[1024,512]{1,0:T(8,128)(2,1)}, u32[]{:S(2)}, u32[]{:S(2)}) collective-permute-start(bf16[1024,512]{1,0:T(8,128)(2,1)S(1)} %copy-done.34), channel_id=1, source_target_pairs={{0,3},{1,2},{2,1},{3,0},{4,7},{5,6},{6,5},{7,4},{8,11},{9,10},{10,... | collective-permute-start | bytes 3145736 | tf_op jit(solution)/shard_map/ppermute | solution.py:68
  1559.4 27.2 %collective-permute-start.29 = (bf16[1024,512]{1,0:T(8,128)(2,1)}, bf16[1024,512]{1,0:T(8,128)(2,1)S(1)}, u32[]{:S(2)}, u32[]{:S(2)}) collective-permute-start(bf16[1024,512]{1,0:T(8,128)(2,1)} %fusion.38.refs_0_), channel_id=1, source_target_pairs={{0,1},{1,0},{2,3},{3,2},{4,5},{5,4},{6,7},{7,6},{8,9},{9,8},{10,11... | collective-permute-start | bytes 3145736 | tf_op jit(solution)/shard_map/ppermute | solution.py:68
  1560.9 43.5 %collective-permute-start.30 = (bf16[1024,512]{1,0:T(8,128)(2,1)}, bf16[1024,512]{1,0:T(8,128)(2,1)S(1)}, u32[]{:S(2)}, u32[]{:S(2)}) collective-permute-start(bf16[1024,512]{1,0:T(8,128)(2,1)} %fusion.38.refs_0_), channel_id=1, source_target_pairs={{0,2},{1,3},{2,0},{3,1},{4,6},{5,7},{6,4},{7,5},{8,10},{9,11},{10,... | collective-permute-start | bytes 3145736 | tf_op jit(solution)/shard_map/ppermute | solution.py:68
  1561.5 44.1 %collective-permute-start.31 = (bf16[1024,512]{1,0:T(8,128)(2,1)}, bf16[1024,512]{1,0:T(8,128)(2,1)}, u32[]{:S(2)}, u32[]{:S(2)}) collective-permute-start(bf16[1024,512]{1,0:T(8,128)(2,1)} %fusion.38.refs_0_), channel_id=1, source_target_pairs={{0,3},{1,2},{2,1},{3,0},{4,7},{5,6},{6,5},{7,4},{8,11},{9,10},{10,... | collective-permute-start | bytes 3145736 | tf_op jit(solution)/shard_map/ppermute | solution.py:68
  (84 other events, 637.0 us)
Sparse Core Ops, SparseCore 0:
  15.3 83.9 all-gather.11
  101.5 80.3 all-gather.13
  185.4 53.5 reduce-scatter.5
  252.7 185.8 all-gather.15
  521.1 82.2 all-gather.17
  927.1 131.9 reduce-scatter.9
  1061.3 182.5 reduce-scatter.7
  1250.2 53.4 all-gather.9
  1306.1 89.3 reduce-scatter.13
  1505.0 90.5 reduce-scatter.11
  1620.9 47.9 all-reduce.6

commit v4 on v3

--- a/solution.py
+++ b/solution.py
@@ -82,12 +82,12 @@
     ffe = f_loc * lay.t
 
     def kernel(ids_ref, *refs):
-        sources, (in_ref, out_ref) = refs[: lay.q], refs[lay.q :]
+        sources, (in_ref, out_ref) = refs[: 3 * lay.q], refs[3 * lay.q :]
         for kc in range(lay.q):
             columns = pl.ds(pl.multiple_of((ids_ref[1] ^ kc) * d_loc, 128), d_loc)
             for g in range(2):
-                in_ref[g, :, columns] = sources[kc][0, g]
-            out_ref[:, columns] = sources[kc][0, 2]
+                in_ref[g, :, columns] = sources[3 * kc + g][0]
+            out_ref[:, columns] = sources[3 * kc + 2][0]
 
     own_in, own_out = pl.pallas_call(
         kernel,
@@ -99,13 +99,11 @@
             num_scalar_prefetch=1,
             grid=(lay.t, lay.z),
             in_specs=[
-                pl.BlockSpec((1, 3, f_loc, d_loc), lambda kt, kz, ids: (kz * lay.t + kt, 0, 0, 0))
+                pl.BlockSpec((1, f_loc, d_loc), lambda kt, kz, ids: (kz * lay.t + kt, 0, 0))
             ]
-            * lay.q,
+            * (3 * lay.q),
             out_specs=(
-                pl.BlockSpec(
-                    (2, f_loc, lay.q * d_loc), lambda kt, kz, ids: (0, kt, kz)
-                ),
+                pl.BlockSpec((2, f_loc, lay.q * d_loc), lambda kt, kz, ids: (0, kt, kz)),
                 pl.BlockSpec((f_loc, lay.q * d_loc), lambda kt, kz, ids: (kt, kz)),
             ),
         ),
@@ -125,24 +123,22 @@
         for kc in range(lay.q):
             columns = pl.ds(pl.multiple_of((ids_ref[1] ^ kc) * d_loc, 128), d_loc)
             for g in range(2):
-                targets[kc][0, g] = in_ref[g, :, columns]
-            targets[kc][0, 2] = out_ref[:, columns]
-
-    shape = jax.ShapeDtypeStruct((lay.t * lay.z, 3, f_loc, d_loc), BF16)
-    spec = pl.BlockSpec((1, 3, f_loc, d_loc), lambda kt, kz, ids: (kz * lay.t + kt, 0, 0, 0))
+                targets[3 * kc + g][0] = in_ref[g, :, columns]
+            targets[3 * kc + 2][0] = out_ref[:, columns]
+
+    shape = jax.ShapeDtypeStruct((lay.t * lay.z, f_loc, d_loc), BF16)
+    spec = pl.BlockSpec((1, f_loc, d_loc), lambda kt, kz, ids: (kz * lay.t + kt, 0, 0))
     return pl.pallas_call(
         kernel,
-        out_shape=(shape,) * lay.q,
+        out_shape=(shape,) * (3 * lay.q),
         grid_spec=pltpu.PrefetchScalarGridSpec(
             num_scalar_prefetch=1,
             grid=(lay.t, lay.z),
             in_specs=[
-                pl.BlockSpec(
-                    (2, f_loc, lay.q * d_loc), lambda kt, kz, ids: (0, kt, kz)
-                ),
+                pl.BlockSpec((2, f_loc, lay.q * d_loc), lambda kt, kz, ids: (0, kt, kz)),
                 pl.BlockSpec((f_loc, lay.q * d_loc), lambda kt, kz, ids: (kt, kz)),
             ],
-            out_specs=(spec,) * lay.q,
+            out_specs=(spec,) * (3 * lay.q),
         ),
         cost_estimate=pl.CostEstimate(
             flops=0, bytes_accessed=12 * ffe * width, transcendentals=0
@@ -152,40 +148,36 @@
     )(ids, grad_in.reshape(2, ffe, width), grad_out)
 
 
-def home_gradients(lay, ids, pieces, f_loc, d_loc):
-    def kernel(ids_ref, piece_ref, in_ref, out_ref):
-        in_ref[0] = piece_ref[0, :2].astype(F32)
-        out_ref[0] = piece_ref[0, 2].astype(F32)
-
-    def pick(e, ids):
-        return (e % lay.t * lay.z + e // lay.t, 0, 0, 0)
-
+def home_gradients(lay, pieces, f_loc, d_loc):
+    def kernel(gate_ref, up_ref, down_ref, in_ref, out_ref):
+        in_ref[0, 0] = gate_ref[0].astype(F32)
+        in_ref[0, 1] = up_ref[0].astype(F32)
+        out_ref[0] = down_ref[0].astype(F32)
+
+    spec = pl.BlockSpec((1, f_loc, d_loc), lambda e: (e % lay.t * lay.z + e // lay.t, 0, 0))
     grad_in, grad_out = pl.pallas_call(
         kernel,
         out_shape=(
             jax.ShapeDtypeStruct((EXPERTS, 2, f_loc, d_loc), F32),
             jax.ShapeDtypeStruct((EXPERTS, f_loc, d_loc), F32),
         ),
-        grid_spec=pltpu.PrefetchScalarGridSpec(
-            num_scalar_prefetch=1,
-            grid=(EXPERTS,),
-            in_specs=[pl.BlockSpec((1, 3, f_loc, d_loc), pick)],
-            out_specs=(
-                pl.BlockSpec((1, 2, f_loc, d_loc), lambda e, ids: (e, 0, 0, 0)),
-                pl.BlockSpec((1, f_loc, d_loc), lambda e, ids: (e, 0, 0)),
-            ),
+        grid=(EXPERTS,),
+        in_specs=[spec] * 3,
+        out_specs=(
+            pl.BlockSpec((1, 2, f_loc, d_loc), lambda e: (e, 0, 0, 0)),
+            pl.BlockSpec((1, f_loc, d_loc), lambda e: (e, 0, 0)),
         ),
         cost_estimate=pl.CostEstimate(
             flops=0, bytes_accessed=18 * EXPERTS * f_loc * d_loc, transcendentals=0
         ),
         name="home_gradients",
-    )(ids, pieces)
+    )(*pieces)
     return jnp.swapaxes(grad_in, 2, 3), grad_out
 
 
 def join_columns(parts, me, count):
     rows, part = parts[0].shape
-    block = min(256, rows)
+    block = min(512, rows)
 
     def kernel(me_ref, *refs):
         for k in range(count):
@@ -501,26 +493,18 @@
     valid_rows = lax.broadcasted_iota(jnp.int32, (rows, 1), 0) < valid_length
     cot_low = jnp.where(valid_rows, cotangent, jnp.zeros_like(cotangent))
     cot_part = own_part(cot_low)
-    route_rows = jnp.transpose(routes).astype(BF16).reshape(-1)
-    route_rows = jnp.pad(route_rows, (0, -route_rows.shape[0] % (16 * part))).reshape(-1, part)
+    route_own = jnp.pad(jnp.transpose(routes), ((0, -TOP % 8), (0, 0)), constant_values=-1)
+    route_all = in_order([lay.over_z(route_own, k) for k in range(nz)], me_z, nz)
     inputs = hidden.astype(F32)
     attn_inverse = inverse_rms(inputs)
     cosine, sine = angle_tables(rows)
     wide_cos, wide_sin = jnp.tile(cosine, (1, heads)), jnp.tile(sine, (1, heads))
-    front, cot_ready, attn_inverse, wide_cos, wide_sin = lax.optimization_barrier(
-        (
-            front,
-            jnp.concatenate([cot_part, route_rows], 0),
-            attn_inverse,
-            wide_cos,
-            wide_sin,
-        )
-    )
-    cot_all = gather_z(cot_ready)
-
-    route_all = cot_all[:, rows:].reshape(nz, -1)[:, : TOP * rows].reshape(nz, TOP, rows)
-    plane_ids = (me_z * nt + jnp.arange(nt, dtype=jnp.int32)).astype(F32)
-    member = jnp.any(route_all.astype(F32)[:, :, :, None] == plane_ids[None, None, None, :], axis=1)
+    front, attn_inverse, wide_cos, wide_sin = lax.optimization_barrier(
+        (front, attn_inverse, wide_cos, wide_sin)
+    )
+
+    plane_ids = me_z * nt + jnp.arange(nt, dtype=jnp.int32)
+    member = jnp.any(route_all[:, :, :, None] == plane_ids[None, None, None, :], axis=1)
     row_ids = lax.broadcasted_iota(jnp.int32, (rows, rows), 0)
     col_ids = lax.broadcasted_iota(jnp.int32, (rows, rows), 1)
     before = (col_ids < row_ids).astype(BF16)
@@ -532,12 +516,11 @@
         return (keys[:, :, None, :] == slots_iota).astype(BF16)
 
     place = place_of(key)
-    keys_near = [lax.dynamic_index_in_dim(key, me_t ^ k, 1, keepdims=False) for k in range(nt)]
-    place_near = place_of(jnp.stack(keys_near, 1))
-    own_place = keys_near[0][:, None, :] == slots_iota[0]
-
-    def pick_rows(places, values):
-        picked = jnp.einsum("sepk,skd->espd", places, values, preferred_element_type=F32)
+    own_key = lax.dynamic_index_in_dim(key, me_t, 1, keepdims=False)
+    own_place = own_key[:, None, :] == slots_iota[0]
+
+    def pick_rows(values):
+        picked = jnp.einsum("sepk,skd->espd", place, values, preferred_element_type=F32)
         return picked.astype(BF16).reshape(nt, nz * CAP, part)
 
     def send_out(picked):
@@ -588,7 +571,8 @@
     )
     latent_all = dot_nt(normed_low, turned_t)
     latent_all, by_column = lax.optimization_barrier((latent_all, by_column))
-    by_plane = swap_z(jnp.swapaxes(by_column, 0, 1))
+    by_column = jnp.transpose(by_column, (2, 1, 0, 3, 4))
+    by_plane = [swap_z(by_column[g]) for g in range(3)]
     latent = latent_all[:, :LATENT]
     kv_inverse = inverse_rms(latent)
     latent_hat = latent * kv_inverse
@@ -607,7 +591,7 @@
     attended_low, log_totals = attend(
         lengths, query_nope, query_rope, keys_values, key_rope, heads, score_scale
     )
-    attn_part, cot_all = lax.optimization_barrier((dot(attended_low, out_w), cot_all))
+    attn_part, by_plane[0] = lax.optimization_barrier((dot(attended_low, out_w), by_plane[0]))
     attn_sum = scatter_t(attn_part)
     residual = own_part(hidden).astype(F32) + attn_sum
 
@@ -620,21 +604,27 @@
     ffn_scale = lax.dynamic_slice_in_dim(gain_ffn, me_t * part, part, 0).astype(F32)
     ffn_part = (ffn_hat * ffn_scale).astype(BF16)
 
-    ffn_part, cot_picked = lax.optimization_barrier((ffn_part, pick_rows(place_near, cot_all[:, :rows])))
     ffn_all = gather_z(ffn_part)
-    cot_rows = join_columns([lay.over_t(cot_picked[k], k) for k in range(nt)], me_t, nt)
     ffn_low = gather_t_direct(ffn_part)
-    ffn_all, cot_rows, ffn_low = lax.optimization_barrier((ffn_all, cot_rows, ffn_low))
-    picked = pick_rows(place, ffn_all)
+    ffn_all, ffn_low = lax.optimization_barrier((ffn_all, ffn_low))
+    picked = pick_rows(ffn_all)
+    picked, cot_ready = lax.optimization_barrier((picked, cot_part))
+    expert_rows = send_out(picked)
+    cot_picked = pick_rows(gather_z(cot_ready))
     shared_pack = jnp.concatenate(
         [jnp.swapaxes(w_shared_in, 1, 2).reshape(-1, d_loc), w_shared_out], 0
     )
-    picked, shared_pack = lax.optimization_barrier((picked, shared_pack))
-    expert_rows = send_out(picked)
+    cot_picked, shared_pack = lax.optimization_barrier((cot_picked, shared_pack))
+    cot_rows = send_out(cot_picked)
     shared_all = lax.all_gather(shared_pack, "dp", axis=0, tiled=False)
-    pieces = by_plane.reshape(nz * nt, 3, f_loc, d_loc)
+    pieces = [plane.reshape(nz * nt, f_loc, d_loc) for plane in by_plane]
     own_in, own_out = lay_out_weights(
-        lay, ids, [lay.over_c(pieces, k) for k in range(nq)], f_loc, d_loc, width
+        lay,
+        ids,
+        [lay.over_c(pieces[g], k) for k in range(nq) for g in range(3)],
+        f_loc,
+        d_loc,
+        width,
     )
     router_probs = jax.nn.softmax(dot_nt(ffn_low, router_t), axis=-1)
     probs_turned = jnp.transpose(router_probs).reshape(EXPERTS, -1, 128)
@@ -680,13 +670,20 @@
     routed = scatter_z(routed).astype(F32)
     grad_in_own = dot_tn(pre_low, expert_rows).astype(BF16)
     grad_out_own = dot_tn(gated_active, cot_rows).astype(BF16)
-    grad_parts, grad_in_own, grad_out_own = lax.optimization_barrier(
-        (grad_parts, grad_in_own, grad_out_own)
+    grad_parts, grad_in_own, grad_out_own, routed = lax.optimization_barrier(
+        (grad_parts, grad_in_own, grad_out_own, routed)
     )
     grad_pieces = take_apart(lay, ids, grad_in_own, grad_out_own, f_loc, d_loc, width)
-    grad_class = sum(lay.over_c(grad_pieces[k], k).astype(F32) for k in range(nq)).astype(BF16)
     routed_grad = scatter_z(combine(grad_parts)).astype(F32)
-    grad_plane = swap_z(grad_class.reshape(nz, nt, 3, f_loc, d_loc))
+    grad_class = [
+        sum(lay.over_c(grad_pieces[3 * k + g], k).astype(F32) for k in range(nq)).astype(BF16)
+        for g in range(3)
+    ]
+    routed_grad, grad_class = lax.optimization_barrier((routed_grad, grad_class))
+    grad_plane = [swap_z(grad_class[g].reshape(nz, nt, f_loc, d_loc)) for g in range(3)]
+
+    def to_columns(values):
+        return swap_t(jnp.swapaxes(values, 0, 1)).reshape(EXPERTS, f_loc, d_loc)
 
     token_grad = jnp.sum(jnp.where(own_place, gate_grad[:, :, None], 0.0), axis=1)
     token_grad = token_grad.reshape(nz, -1, 128)
@@ -755,9 +752,10 @@
     residual_grad = cot_part.astype(F32) + ffn_inverse * (
         scaled - ffn_hat * row_mean(ffn_hat * scaled)
     )
-    residual_low = gather_t(residual_grad.astype(BF16))
-
-    output = gather_t_direct((residual + routed + shared_part).astype(BF16))
+    residual_ready, grad_plane[0] = lax.optimization_barrier(
+        (residual_grad.astype(BF16), grad_plane[0])
+    )
+    residual_low = gather_t(residual_ready)
 
     def sum_dp(values):
         return lax.psum_scatter(values, "dp", scatter_dimension=0, tiled=False).astype(F32)
@@ -766,8 +764,8 @@
         return jnp.swapaxes(values.astype(BF16).reshape(-1, ndp, d_loc), 0, 1)
 
     shared_grads = jnp.concatenate([by_owner(grad_shared_in), by_owner(grad_shared_out)], 1)
-    residual_low, shared_grads, grad_plane = lax.optimization_barrier(
-        (residual_low, shared_grads, grad_plane)
+    residual_low, shared_grads, grad_plane[1] = lax.optimization_barrier(
+        (residual_low, shared_grads, grad_plane[1])
     )
     shared_sum = sum_dp(shared_grads)
     grad_out_w = dot_tn(attended_low, residual_low)
@@ -783,6 +781,13 @@
         heads,
         score_scale,
     )
+    grad_home = [to_columns(grad_plane[0]), None, None]
+    query_turned_grad, routed, shared_part, grad_plane[2] = lax.optimization_barrier(
+        (query_turned_grad, routed, shared_part, grad_plane[2])
+    )
+    grad_home[1] = to_columns(grad_plane[1])
+    grad_home[2] = to_columns(grad_plane[2])
+    output = gather_t_direct((residual + routed + shared_part).astype(BF16))
     turned_first, turned_second = rotate_back(
         query_turned_grad[:, : heads * half], query_turned_grad[:, heads * half :], wide_cos, wide_sin
     )
@@ -804,7 +809,6 @@
     )
     down_grad = jnp.concatenate([latent_back, key_rope_part], -1).astype(BF16)
     normed_grad = scatter_t_direct(dot(query_grad, query_t) + dot(down_grad, down_t))
-    grad_home = swap_t(jnp.swapaxes(grad_plane, 0, 1)).reshape(EXPERTS, 3, f_loc, d_loc)
     normed_grad, grad_home = lax.optimization_barrier((normed_grad, grad_home))
     attn_hat = own_part(hidden).astype(F32) * attn_inverse
     scaled_in = lax.dynamic_slice_in_dim(attn_scale, me_t * part, part, 0) * normed_grad
@@ -812,7 +816,7 @@
     input_grad = residual_grad + attn_inverse * (
         scaled_in - attn_hat * row_mean(attn_hat * scaled_in)
     )
-    grad_expert_in, grad_expert_out = home_gradients(lay, ids, grad_home, f_loc, d_loc)
+    grad_expert_in, grad_expert_out = home_gradients(lay, grad_home, f_loc, d_loc)
     grad_hidden = gather_t_direct(input_grad.astype(BF16))
 
     def spread(values):

time: 1690 us -> 1690 us (level)
  blocking collectives: 90.6 us -> 24.3 us
  starting transfers between devices: 87.4 us -> 124 us
  Pallas kernels: 127 us -> 98.2 us
  local copies, waits for them, and re-layouts: 196 us -> 217 us
    ppermute x6 -> x9, waiting for transfers between devices: 3.44 us -> 173 us  [over_z(): lax.ppermute(values, 'dp', [(d, d ^ k * self.q) for d in range(self.dp)])]
    all_to_all x2 -> x6, waiting for transfers between devices: 170 us -> 62.3 us  [swap_z(): lax.all_to_all(values, 'dp', split_axis=0, concat_axis=0, axis_index_grou...]
    reduce_scatter x2, waiting for transfers between devices: 133 us -> 29.8 us  [scatter_z(): lax.psum_scatter(values, 'dp', scatter_dimension=0, tiled=False, axis_ind...]
    psum x3, blocking collectives: 90.6 us -> 24.3 us  [row_mean(): return lax.psum(partial, 'tensor').reshape(-1, 1) * (1.0 / width)]
    all_to_all x5 -> x8, waiting for transfers between devices: 145 us -> 205 us  [swap_t(): lax.all_to_all(values, 'tensor', split_axis=0, concat_axis=0, tiled=True)]
    ppermute x24 -> x21, waiting for transfers between devices: 168 us -> 110 us  [over_t(): return lax.ppermute(values, 'tensor', [(i, i ^ k) for i in range(self.t)])]
    all_gather x1, waiting for transfers between devices: 0.02 us -> 41.7 us  [body(): shared_all = lax.all_gather(shared_pack, 'dp', axis=0, tiled=False)]
    all_gather x1, waiting for transfers between devices: 33.4 us -> 0.01 us  [gather_t(): return lax.all_gather(values, 'tensor', axis=1, tiled=True)]
  transfers between devices with their start and end apart: 50 -> 61, of which waited for: 20 -> 32; matrix products, arithmetic and copies ran while one was open for 32% -> 31% of each run, Pallas kernels for 8% -> 6%
where the time goes in v4:
time: 1690 us; the launch traced here: 1670 us
  waiting for transfers between devices  775 us (46%)
  matrix products  326 us (19%)
  local copies, waits for them, and re-layouts  217 us (13%)
  starting transfers between devices  124 us (7%)
  Pallas kernels  98.2 us (6%)
  other arithmetic  91.6 us (5%)
  blocking collectives  24.3 us (1%)
    all_to_all x8, waiting for transfers between devices, swap_t(): lax.all_to_all(values, 'tensor', split_axis=0, concat_axis=0, tiled=True)  205 us
    ppermute x9, waiting for transfers between devices, over_z(): lax.ppermute(values, 'dp', [(d, d ^ k * self.q) for d in range(self.dp)])  173 us
    ppermute x21, waiting for transfers between devices, over_t(): return lax.ppermute(values, 'tensor', [(i, i ^ k) for i in range(self.t)])  110 us
    dot_general x9, matrix products, dot_nt(): lax.dot_general(a, b, (((1,), (1,)), ((), ())), preferred_element_type=F32)  101 us
    dot_general x8, matrix products, dot_tn(): lax.dot_general(a, b, (((0,), (0,)), ((), ())), preferred_element_type=F32)  83.1 us
    dot_general x8, matrix products, dot(): return jnp.dot(a, b, preferred_element_type=F32)  80.6 us
    all_to_all x6, waiting for transfers between devices, swap_z(): lax.all_to_all(values, 'dp', split_axis=0, concat_axis=0, axis_index_grou...  62.3 us
    all_gather x1, waiting for transfers between devices, body(): front = lax.all_gather(front_pack, 'dp', axis=0, tiled=False)  58.9 us
  transfers between devices with their start and end apart: 61, of which 32 were waited for; matrix products, arithmetic and copies ran while one was open for 31% of the time, Pallas kernels for 6%

profile of v4, /device:TPU:10, one launch (start us, length us, event | category | flops | bytes accessed | tf_op | source)
XLA Modules:
  0.0 1673.7 jit_solution(12977253790252692240)
XLA Ops:
  20.2 6.9 maximum_bitcast_fusion
  27.1 8.4 copy.408
  45.5 58.9 %all-gather.12.cloned.1.call-done = bf16[17152,256]{1,0:T(8,128)(2,1)} async-done(((bf16[2144,256]{1,0:T(8,128)(2,1)}), bf16[17152,256]{1,0:T(8,128)(2,1)}) %all-gather.12.cloned.1.call-update) | async-done | bytes 8781840 | tf_op jit(solution)/shard_map/all_gather | solution.py:490
  115.7 7.7 concatenate.56
  124.3 8.4 fusion.104
  188.6 14.6 attend.1
  213.5 7.8 all-to-all-start.3
  221.5 42.2 %reduce-scatter.6.cloned.1.call-done = bf16[1024,512]{1,0:T(8,128)(2,1)} async-done(((bf16[1024,2048]{1,0:T(8,128)(2,1)}), bf16[1024,512]{1,0:T(8,128)(2,1)}) %reduce-scatter.6.cloned.1.call-update) | async-done | bytes 1048592 | tf_op jit(solution)/shard_map/reduce_scatter | solution.py:421
  265.6 8.1 psum.28
  282.8 8.2 all-to-all-start.4
  300.8 119.4 %collective-permute-done.3 = s32[8,1024]{1,0:T(8,128)S(1)} collective-permute-done((s32[8,1024]{1,0:T(8,128)S(1)}, s32[8,1024]{1,0:T(8,128)S(1)}, u32[]{:S(2)}, u32[]{:S(2)}) %collective-permute-start.3) | collective-permute-done | bytes 32800 | tf_op jit(solution)/shard_map/ppermute | solution.py:73
  431.2 16.2 convert_bitcast_fusion.1
  447.4 7.5 copy.416
  454.9 6.5 all-to-all-start.2
  476.0 17.2 %lay_out_weights.1 = (bf16[2,1408,2048]{2,1,0:T(8,128)(2,1)}, bf16[1408,2048]{1,0:T(8,128)(2,1)}) custom-call(s32[3]{0:T(128)S(1)} %pad_add_fusion.1.ids_ref, bf16[16,352,256]{2,1,0:T(8,128)(2,1)S(1)} %bitcast.380, bf16[16,352,256]{2,1,0:T(8,128)(2,1)} %bitcast.60.refs_1_, bf16[16,352,256]{2,1,0:T(8,128)(2,1)} %bitcast.62.refs_2_, ...), custom_call_target="tpu_custom_call" | custom-call | bytes 34603008 | tf_op jit(solution)/shard_map/lay_out_weights/pallas_call | solution.py:92
  494.3 56.9 %all-to-all-done.2 = bf16[4,2048,512]{2,1,0:T(8,128)(2,1)} async-done(((bf16[4,2048,512]{2,1,0:T(8,128)(2,1)}), bf16[4,2048,512]{2,1,0:T(8,128)(2,1)}, u32[]{:S(2)}, u32[]{:S(2)}) %all-to-all-start.2) | async-done | bytes 8388640 | tf_op jit(solution)/shard_map/all_to_all | solution.py:426
  551.2 11.4 copy.423
  562.6 16.3 convert_bitcast_fusion
  578.9 7.3 copy.418
  592.6 32.1 %fusion.117 = f32[2048,2816]{1,0:T(8,128)} fusion(bf16[2048,2048]{0,1:T(8,128)(2,1)} %bitcast.407, bf16[2816,2048]{1,0:T(8,128)(2,1)} %bitcast.489), kind=kOutput, calls=%fused_computation.276 | convolution fusion | flops 23622320128 | bytes 42991616 | tf_op jit(solution)/shard_map/dot_general | solution.py:30
  624.7 9.0 multiply_convert_fusion.3
  636.2 17.7 %multiply_convert_fusion = bf16[2048,2048]{1,0:T(8,128)(2,1)} fusion(bf16[2048,1408]{1,0:T(8,128)(2,1)S(1)} %multiply_convert_fusion.3, bf16[1408,2048]{1,0:T(8,128)(2,1)} %get-tuple-element.86, f32[2048]{0:T(1024)S(1)} %bitcast.478), kind=kOutput, calls=%fused_computation.5 | convolution fusion | flops 11819548672 | bytes 19931136 | tf_op jit(solution)/shard_map/dot_general | solution.py:26
  653.8 29.5 %all-to-all-done.5 = bf16[4,2048,512]{2,1,0:T(8,128)(2,1)} async-done(((bf16[4,2048,512]{2,1,0:T(8,128)(2,1)}), bf16[4,2048,512]{2,1,0:T(8,128)(2,1)}, u32[]{:S(2)}, u32[]{:S(2)}) %all-to-all-start.5) | async-done | bytes 8388640 | tf_op jit(solution)/shard_map/all_to_all | solution.py:426
  683.3 11.4 copy.431
  694.7 7.4 copy.522
  708.3 28.6 %multiply_convert_fusion.2 = (bf16[2048,1408]{1,0:T(8,128)(2,1)S(1)}, bf16[2048,1408]{1,0:T(8,128)(2,1)}, f32[2048]{0:T(1024)}) fusion(f32[2048,2816]{1,0:T(8,128)} %fusion.117, f32[2048]{0:T(1024)S(1)} %bitcast.479, bf16[2048,1408]{1,0:T(8,128)(2,1)} %copy-done.32, bf16[2048,2048]{0,1:T(8,128)(2,1)} %bitcast.409, bf16[1408,2048]{1,0:T(8,128)(2,1)} %get-tuple-element.86), kind=kOutput, calls=%fused_computation.16 | convolution fusion | flops 11860178944 | bytes 54542336 | tf_op jit(solution)/shard_map/dot_general | solution.py:30
  736.9 8.8 pad_maximum_fusion
  745.7 28.6 %convolution_convert_fusion.3 = bf16[2048,2048]{1,0:T(8,128)(2,1)} fusion(bf16[2816,2048]{1,0:T(8,128)(2,1)} %bitcast.490, bf16[2048,1408]{1,0:T(8,128)(2,1)S(1)} %copy-done.33, bf16[2048,1408]{1,0:T(8,128)(2,1)S(1)} %get-tuple-element.221), kind=kOutput, calls=%fused_computation.41 | convolution fusion | flops 23649583104 | bytes 31457280 | tf_op jit(solution)/shard_map/dot_general | solution.py:26
  774.3 25.3 %all-to-all-done.6 = bf16[4,2048,512]{2,1,0:T(8,128)(2,1)} async-done(((bf16[4,2048,512]{2,1,0:T(8,128)(2,1)}), bf16[4,2048,512]{2,1,0:T(8,128)(2,1)}, u32[]{:S(2)}, u32[]{:S(2)}) %all-to-all-start.6) | async-done | bytes 8388640 | tf_op jit(solution)/shard_map/all_to_all | solution.py:426
  799.6 12.5 bitcast_convert_fusion.1
  812.7 7.7 copy.521
  826.6 19.1 %convolution_convert_fusion.2.out_ref = bf16[1408,2048]{1,0:T(8,128)(2,1)} fusion(bf16[2048,2048]{0,1:T(8,128)(2,1)} %bitcast.410, bf16[2048,1408]{1,0:T(8,128)(2,1)} %copy-done.32, f32[2048]{0:T(1024)S(1)} %bitcast.480), kind=kOutput, calls=%fused_computation.40 | convolution fusion | flops 11822694400 | bytes 19931136 | tf_op jit(solution)/shard_map/dot_general | solution.py:34
  845.7 31.7 %convolution_convert_fusion = bf16[2816,2048]{1,0:T(8,128)(2,1)} fusion(bf16[2048,2816]{1,0:T(8,128)(2,1)} %pad_maximum_fusion, bf16[2048,2048]{0,1:T(8,128)(2,1)} %bitcast.408), kind=kOutput, calls=%fused_computation.20 | convolution fusion | flops 23628087296 | bytes 31457280 | tf_op jit(solution)/shard_map/dot_general | solution.py:34
  877.4 10.8 reduce-scatter.8.cloned.1.call-done
  891.0 26.9 %all-to-all-done.7 = bf16[4,2048,512]{2,1,0:T(8,128)(2,1)} async-done(((bf16[4,2048,512]{2,1,0:T(8,128)(2,1)}), bf16[4,2048,512]{2,1,0:T(8,128)(2,1)}, u32[]{:S(2)}, u32[]{:S(2)}) %all-to-all-start.7) | async-done | bytes 8388640 | tf_op jit(solution)/shard_map/all_to_all | solution.py:426
  917.9 12.2 bitcast_convert_fusion
  930.8 41.7 %all-gather.18.cloned.1.call-done = bf16[16896,256]{1,0:T(8,128)(2,1)} async-done(((bf16[2112,256]{1,0:T(8,128)(2,1)}), bf16[16896,256]{1,0:T(8,128)(2,1)}) %all-gather.18.cloned.1.call-update) | async-done | bytes 8650768 | tf_op jit(solution)/shard_map/all_gather | solution.py:619
  978.1 8.3 copy.420
  986.4 12.1 take_apart.1
  999.3 10.8 fusion.116
  1015.4 7.6 multiply_convert_fusion.6
  1034.2 19.0 %reduce-scatter.10.cloned.1.call-done = bf16[1,1024,512]{2,1,0:T(8,128)(2,1)} async-done(((bf16[4,1024,512]{2,1,0:T(8,128)(2,1)}), bf16[1,1024,512]{2,1,0:T(8,128)(2,1)}) %reduce-scatter.10.cloned.1.call-update) | async-done | bytes 1048592 | tf_op jit(solution)/shard_map/reduce_scatter | solution.py:413
  1059.8 10.0 fusion.39
  1077.9 46.4 %collective-permute-done.20 = f32[8,128]{1,0:T(8,128)S(1)} collective-permute-done((f32[8,128]{1,0:T(8,128)S(1)}, f32[8,128]{1,0:T(8,128)S(1)}, u32[]{:S(2)}, u32[]{:S(2)}) %collective-permute-start.20) | collective-permute-done | bytes 4128 | tf_op jit(solution)/shard_map/ppermute | solution.py:73
  1142.3 8.0 psum.29
  1167.4 7.8 convolution_convert_fusion.1
  1179.3 35.7 %all-to-all-done.9 = bf16[4,4,352,256]{3,2,1,0:T(8,128)(2,1)S(1)} async-done(((bf16[4,4,352,256]{3,2,1,0:T(8,128)(2,1)}), bf16[4,4,352,256]{3,2,1,0:T(8,128)(2,1)S(1)}, u32[]{:S(2)}, u32[]{:S(2)}) %all-to-all-start.9) | async-done | bytes 2883616 | tf_op jit(solution)/shard_map/all_to_all | solution.py:429
  1216.6 8.2 all-to-all-start.10
  1237.7 19.5 %collective-permute-done.26 = bf16[1024,512]{1,0:T(8,128)(2,1)S(1)} collective-permute-done((bf16[1024,512]{1,0:T(8,128)(2,1)S(1)}, bf16[1024,512]{1,0:T(8,128)(2,1)S(1)}, u32[]{:S(2)}, u32[]{:S(2)}) %collective-permute-start.26) | collective-permute-done | bytes 1048608 | tf_op jit(solution)/shard_map/ppermute | solution.py:68
  1257.2 20.3 %collective-permute-done.25 = bf16[1024,512]{1,0:T(8,128)(2,1)S(1)} collective-permute-done((bf16[1024,512]{1,0:T(8,128)(2,1)S(1)}, bf16[1024,512]{1,0:T(8,128)(2,1)S(1)}, u32[]{:S(2)}, u32[]{:S(2)}) %collective-permute-start.25) | collective-permute-done | bytes 1048608 | tf_op jit(solution)/shard_map/ppermute | solution.py:68
  1286.2 21.9 %attend_back.1 = (bf16[1024,512]{1,0:T(8,128)(2,1)S(1)}, f32[1024,256]{1,0:T(8,128)S(1)}, bf16[1024,1024]{1,0:T(8,128)(2,1)S(1)}, f32[1024,256]{1,0:T(8,128)S(1)}) custom-call(s32[1]{0:T(128)} %copy.543.len_ref, bf16[1024,512]{1,0:T(8,128)(2,1)S(1)} %copy-done.1, bf16[1024,256]{1,0:T(8,128)(2,1)S(1)} %copy-done.3, bf16[1024,1024]{1,0:T(8,128)(2,1)S(1)} %copy-done.7, ...), custom_call_target="tpu_custom_call" | custom-call | flops 6710886400 | bytes 33554432 | tf_op jit(solution)/shard_map/attend_back/pallas_call | solution.py:325
  1310.4 24.6 %all-to-all-done.10 = bf16[4,4,352,256]{3,2,1,0:T(8,128)(2,1)} async-done(((bf16[4,4,352,256]{3,2,1,0:T(8,128)(2,1)}), bf16[4,4,352,256]{3,2,1,0:T(8,128)(2,1)}, u32[]{:S(2)}, u32[]{:S(2)}) %all-to-all-start.10) | async-done | bytes 2883616 | tf_op jit(solution)/shard_map/all_to_all | solution.py:429
  1335.0 7.3 all-to-all-start.11
  1358.9 12.0 all-to-all-done.11
  1377.8 8.0 convolution_add_fusion
  1406.1 23.6 %all-to-all-done.12 = bf16[4,4,352,256]{3,2,1,0:T(8,128)(2,1)} async-done(((bf16[4,4,352,256]{3,2,1,0:T(8,128)(2,1)}), bf16[4,4,352,256]{3,2,1,0:T(8,128)(2,1)}, u32[]{:S(2)}, u32[]{:S(2)}) %all-to-all-start.12) | async-done | bytes 2883616 | tf_op jit(solution)/shard_map/all_to_all | solution.py:426
  1457.0 27.2 %all-to-all-done.13 = bf16[4,4,352,256]{3,2,1,0:T(8,128)(2,1)} async-done(((bf16[4,4,352,256]{3,2,1,0:T(8,128)(2,1)}), bf16[4,4,352,256]{3,2,1,0:T(8,128)(2,1)}, u32[]{:S(2)}, u32[]{:S(2)}) %all-to-all-start.13) | async-done | bytes 2883616 | tf_op jit(solution)/shard_map/all_to_all | solution.py:426
  1493.0 8.3 psum.30
  1513.0 19.9 %collective-permute-done.27.refs_1_ = bf16[1024,512]{1,0:T(8,128)(2,1)S(1)} collective-permute-done((bf16[1024,512]{1,0:T(8,128)(2,1)}, bf16[1024,512]{1,0:T(8,128)(2,1)S(1)}, u32[]{:S(2)}, u32[]{:S(2)}) %collective-permute-start.27) | collective-permute-done | bytes 1048608 | tf_op jit(solution)/shard_map/ppermute | solution.py:68
  1535.3 13.7 home_gradients.1
  1549.0 8.0 collective-permute-done.28.refs_2_
  1563.3 14.7 collective-permute-done.33.refs_1_
  1577.9 18.6 %collective-permute-done.34.refs_2_ = bf16[1024,512]{1,0:T(8,128)(2,1)S(1)} collective-permute-done((bf16[1024,512]{1,0:T(8,128)(2,1)}, bf16[1024,512]{1,0:T(8,128)(2,1)S(1)}, u32[]{:S(2)}, u32[]{:S(2)}) %collective-permute-start.34) | collective-permute-done | bytes 1048608 | tf_op jit(solution)/shard_map/ppermute | solution.py:68
  1615.1 47.4 %all-reduce.7.cloned.1.call-done = f32[592,256]{1,0:T(8,128)} async-done(((f32[592,256]{1,0:T(8,128)}), f32[592,256]{1,0:T(8,128)}) %all-reduce.7.cloned.1.call-update) | async-done | bytes 606224 | tf_op jit(solution)/shard_map/psum | solution.py:844
  (459 shorter events, 397.6 us)
Async XLA Ops:
  7.2 97.1 %all-gather.12.cloned.1.call-start = ((), (), s32[]{:S(2)}) async-start(), calls=%async_computation.26 | async-start | bytes 9879552 | tf_op jit(solution)/shard_map/all_gather | solution.py:490
  35.5 101.0 %all-to-all-start = ((bf16[4,4,3,352,256]{4,3,1,2,0:T(8,128)(2,1)}), bf16[4,4,3,352,256]{4,3,1,2,0:T(8,128)(2,1)}, u32[]{:S(2)}, u32[]{:S(2)}) async-start(bf16[4,4,3,352,256]{4,3,1,2,0:T(8,128)(2,1)} %copy.408), calls=%async_computation | async-start | bytes 17301504 | tf_op jit(solution)/shard_map/all_to_all | solution.py:426
  44.9 115.8 %copy-start.73 = (f32[1024]{0:T(1024)}, f32[1024]{0:T(1024)S(1)}, u32[]{:S(2)}) copy-start(f32[1024]{0:T(1024)S(1)} %add_rsqrt_fusion.1) | copy-start | bytes 12292
  143.8 66.1 %all-to-all-start.1 = ((bf16[4,4,352,256]{3,2,1,0:T(8,128)(2,1)}), bf16[4,4,352,256]{3,2,1,0:T(8,128)(2,1)S(1)}, u32[]{:S(2)}, u32[]{:S(2)}) async-start(bf16[4,4,352,256]{3,2,1,0:T(8,128)(2,1)} %copy.414), calls=%async_computation.1 | async-start | bytes 5767168 | tf_op jit(solution)/shard_map/all_to_all | solution.py:429
  149.2 114.5 %reduce-scatter.6.cloned.1.call-start = ((), (), s32[]{:S(2)}) async-start(), calls=%async_computation.19 | async-start | bytes 5242880 | tf_op jit(solution)/shard_map/reduce_scatter | solution.py:421
  213.5 69.3 %all-to-all-start.3 = ((bf16[4,4,352,256]{3,2,1,0:T(8,128)(2,1)}), bf16[4,4,352,256]{3,2,1,0:T(8,128)(2,1)}, u32[]{:S(2)}, u32[]{:S(2)}) async-start(bf16[4,4,352,256]{3,2,1,0:T(8,128)(2,1)} %copy.424), calls=%async_computation.4 | async-start | bytes 5767168 | tf_op jit(solution)/shard_map/all_to_all | solution.py:429
  221.4 209.8 %all-gather.14.cloned.1.call-start = ((), (), s32[]{:S(2)}) async-start(), calls=%async_computation.27 | async-start | bytes 5242880 | tf_op jit(solution)/shard_map/all_gather | solution.py:410
  282.8 172.1 %all-to-all-start.4 = ((bf16[4,4,352,256]{3,2,1,0:T(8,128)(2,1)}), bf16[4,4,352,256]{3,2,1,0:T(8,128)(2,1)}, u32[]{:S(2)}, u32[]{:S(2)}) async-start(bf16[4,4,352,256]{3,2,1,0:T(8,128)(2,1)} %copy.425), calls=%async_computation.5 | async-start | bytes 5767168 | tf_op jit(solution)/shard_map/all_to_all | solution.py:429
  291.1 129.2 %collective-permute-start.3 = (s32[8,1024]{1,0:T(8,128)S(1)}, s32[8,1024]{1,0:T(8,128)S(1)}, u32[]{:S(2)}, u32[]{:S(2)}) collective-permute-start(s32[8,1024]{1,0:T(8,128)S(1)} %pad.24), channel_id=1, source_target_pairs={{0,24},{4,28},{8,16},{12,20},{16,8},{20,12},{24,0},{28,4},{1,25},{... | collective-permute-start | bytes 98312 | tf_op jit(solution)/shard_map/ppermute | solution.py:73
  292.6 127.6 %collective-permute-start.4 = (s32[8,1024]{1,0:T(8,128)S(1)}, s32[8,1024]{1,0:T(8,128)S(1)}, u32[]{:S(2)}, u32[]{:S(2)}) collective-permute-start(s32[8,1024]{1,0:T(8,128)S(1)} %pad.24), channel_id=1, source_target_pairs={{0,16},{4,20},{8,24},{12,28},{16,0},{20,4},{24,8},{28,12},{1,17},{... | collective-permute-start | bytes 98312 | tf_op jit(solution)/shard_map/ppermute | solution.py:73
  296.2 128.8 %collective-permute-start = (bf16[1024,512]{1,0:T(8,128)(2,1)}, bf16[1024,512]{1,0:T(8,128)(2,1)}, u32[]{:S(2)}, u32[]{:S(2)}) collective-permute-start(bf16[1024,512]{1,0:T(8,128)(2,1)} %multiply_convert_fusion.8.refs_0_), channel_id=1, source_target_pairs={{0,1},{1,0},{2,3},{3,2},{4,5},{5,4},{6,7},{7,6},{8,9},{9,8},{10,11... | collective-permute-start | bytes 3145736 | tf_op jit(solution)/shard_map/ppermute | solution.py:68
  297.1 127.9 %collective-permute-start.1 = (bf16[1024,512]{1,0:T(8,128)(2,1)}, bf16[1024,512]{1,0:T(8,128)(2,1)}, u32[]{:S(2)}, u32[]{:S(2)}) collective-permute-start(bf16[1024,512]{1,0:T(8,128)(2,1)} %multiply_convert_fusion.8.refs_0_), channel_id=1, source_target_pairs={{0,2},{1,3},{2,0},{3,1},{4,6},{5,7},{6,4},{7,5},{8,10},{9,11},{10,... | collective-permute-start | bytes 3145736 | tf_op jit(solution)/shard_map/ppermute | solution.py:68
  298.4 126.6 %collective-permute-start.2 = (bf16[1024,512]{1,0:T(8,128)(2,1)}, bf16[1024,512]{1,0:T(8,128)(2,1)}, u32[]{:S(2)}, u32[]{:S(2)}) collective-permute-start(bf16[1024,512]{1,0:T(8,128)(2,1)} %multiply_convert_fusion.8.refs_0_), channel_id=1, source_target_pairs={{0,3},{1,2},{2,1},{3,0},{4,7},{5,6},{6,5},{7,4},{8,11},{9,10},{10,... | collective-permute-start | bytes 3145736 | tf_op jit(solution)/shard_map/ppermute | solution.py:68
  420.2 3.9 collective-permute-start.5
  425.0 137.6 %copy-start.85 = (s32[4,4,1024]{2,1,0:T(4,128)}, s32[4,4,1024]{2,1,0:T(4,128)S(1)}, u32[]{:S(2)}) copy-start(s32[4,4,1024]{2,1,0:T(4,128)S(1)} %fusion.44) | copy-start | bytes 196612
  454.9 96.2 %all-to-all-start.2 = ((bf16[4,2048,512]{2,1,0:T(8,128)(2,1)}), bf16[4,2048,512]{2,1,0:T(8,128)(2,1)}, u32[]{:S(2)}, u32[]{:S(2)}) async-start(bf16[4,2048,512]{2,1,0:T(8,128)(2,1)} %bitcast.381), calls=%async_computation.3 | async-start | bytes 16777216 | tf_op jit(solution)/shard_map/all_to_all | solution.py:426
  461.5 101.1 %all-gather.16.cloned.1.call-start = ((), (), s32[]{:S(2)}) async-start(), calls=%async_computation.28 | async-start | bytes 5242880 | tf_op jit(solution)/shard_map/all_gather | solution.py:410
  462.0 9.8 collective-permute-start.9
  462.1 10.9 collective-permute-start.10
  462.6 13.4 collective-permute-start.11
  469.4 23.8 %collective-permute-start.12 = (f32[8,128]{1,0:T(8,128)S(1)}, f32[8,128]{1,0:T(8,128)S(1)}, u32[]{:S(2)}, u32[]{:S(2)}) collective-permute-start(f32[8,128]{1,0:T(8,128)S(1)} %get-tuple-element.274), channel_id=1, source_target_pairs={{0,24},{4,28},{8,16},{12,20},{16,8},{20,12},{24,0},{28,4},{1,25},{... | collective-permute-start | bytes 12296 | tf_op jit(solution)/shard_map/ppermute | solution.py:73
  470.1 23.0 %collective-permute-start.13 = (f32[8,128]{1,0:T(8,128)S(1)}, f32[8,128]{1,0:T(8,128)S(1)}, u32[]{:S(2)}, u32[]{:S(2)}) collective-permute-start(f32[8,128]{1,0:T(8,128)S(1)} %get-tuple-element.273), channel_id=1, source_target_pairs={{0,16},{4,20},{8,24},{12,28},{16,0},{20,4},{24,8},{28,12},{1,17},{... | collective-permute-start | bytes 12296 | tf_op jit(solution)/shard_map/ppermute | solution.py:73
  471.8 21.4 %collective-permute-start.14 = (f32[8,128]{1,0:T(8,128)S(1)}, f32[8,128]{1,0:T(8,128)S(1)}, u32[]{:S(2)}, u32[]{:S(2)}) collective-permute-start(f32[8,128]{1,0:T(8,128)S(1)} %get-tuple-element.272), channel_id=1, source_target_pairs={{0,8},{4,12},{8,0},{12,4},{16,24},{20,28},{24,16},{28,20},{1,9},{5... | collective-permute-start | bytes 12296 | tf_op jit(solution)/shard_map/ppermute | solution.py:73
  586.2 97.1 %all-to-all-start.5 = ((bf16[4,2048,512]{2,1,0:T(8,128)(2,1)}), bf16[4,2048,512]{2,1,0:T(8,128)(2,1)}, u32[]{:S(2)}, u32[]{:S(2)}) async-start(bf16[4,2048,512]{2,1,0:T(8,128)(2,1)} %bitcast.384), calls=%async_computation.6 | async-start | bytes 16777216 | tf_op jit(solution)/shard_map/all_to_all | solution.py:426
  702.1 97.5 %all-to-all-start.6 = ((bf16[4,2048,512]{2,1,0:T(8,128)(2,1)}), bf16[4,2048,512]{2,1,0:T(8,128)(2,1)}, u32[]{:S(2)}, u32[]{:S(2)}) async-start(bf16[4,2048,512]{2,1,0:T(8,128)(2,1)} %bitcast.383), calls=%async_computation.7 | async-start | bytes 16777216 | tf_op jit(solution)/shard_map/all_to_all | solution.py:426
  708.3 179.8 %reduce-scatter.8.cloned.1.call-start = ((), (), s32[]{:S(2)}) async-start(), calls=%async_computation.20 | async-start | bytes 5242880 | tf_op jit(solution)/shard_map/reduce_scatter | solution.py:413
  812.1 160.4 %all-gather.18.cloned.1.call-start = ((), (), s32[]{:S(2)}) async-start(), calls=%async_computation.29 | async-start | bytes 9732096 | tf_op jit(solution)/shard_map/all_gather | solution.py:619
  820.4 97.5 %all-to-all-start.7 = ((bf16[4,2048,512]{2,1,0:T(8,128)(2,1)}), bf16[4,2048,512]{2,1,0:T(8,128)(2,1)}, u32[]{:S(2)}, u32[]{:S(2)}) async-start(bf16[4,2048,512]{2,1,0:T(8,128)(2,1)} %bitcast.382), calls=%async_computation.8 | async-start | bytes 16777216 | tf_op jit(solution)/shard_map/all_to_all | solution.py:426
  826.6 226.6 %reduce-scatter.10.cloned.1.call-start = ((), (), s32[]{:S(2)}) async-start(), calls=%async_computation.21 | async-start | bytes 5242880 | tf_op jit(solution)/shard_map/reduce_scatter | solution.py:413
  998.5 24.5 %collective-permute-start.15 = (bf16[16,352,256]{2,1,0:T(8,128)(2,1)S(1)}, bf16[16,352,256]{2,1,0:T(8,128)(2,1)}, u32[]{:S(2)}, u32[]{:S(2)}) collective-permute-start(bf16[16,352,256]{2,1,0:T(8,128)(2,1)S(1)} %get-tuple-element.98), channel_id=1, source_target_pairs={{0,4},{4,0},{8,12},{12,8},{16,20},{20,16},{24,28},{28,24},{1,5},{5... | collective-permute-start | bytes 8650760 | tf_op jit(solution)/shard_map/ppermute | solution.py:78
  998.8 28.4 %collective-permute-start.16 = (bf16[16,352,256]{2,1,0:T(8,128)(2,1)S(1)}, bf16[16,352,256]{2,1,0:T(8,128)(2,1)}, u32[]{:S(2)}, u32[]{:S(2)}) collective-permute-start(bf16[16,352,256]{2,1,0:T(8,128)(2,1)S(1)} %get-tuple-element.100), channel_id=1, source_target_pairs={{0,4},{4,0},{8,12},{12,8},{16,20},{20,16},{24,28},{28,24},{1,5},{5... | collective-permute-start | bytes 8650760 | tf_op jit(solution)/shard_map/ppermute | solution.py:78
  999.1 32.5 %collective-permute-start.17 = (bf16[16,352,256]{2,1,0:T(8,128)(2,1)S(1)}, bf16[16,352,256]{2,1,0:T(8,128)(2,1)S(1)}, u32[]{:S(2)}, u32[]{:S(2)}) collective-permute-start(bf16[16,352,256]{2,1,0:T(8,128)(2,1)S(1)} %get-tuple-element.102), channel_id=1, source_target_pairs={{0,4},{4,0},{8,12},{12,8},{16,20},{20,16},{24,28},{28,24},{1,5},{5... | collective-permute-start | bytes 8650760 | tf_op jit(solution)/shard_map/ppermute | solution.py:78
  1054.7 100.1 %all-to-all-start.8 = ((bf16[4,4,352,256]{3,2,1,0:T(8,128)(2,1)}), bf16[4,4,352,256]{3,2,1,0:T(8,128)(2,1)}, u32[]{:S(2)}, u32[]{:S(2)}) async-start(bf16[4,4,352,256]{3,2,1,0:T(8,128)(2,1)} %bitcast.107), calls=%async_computation.11 | async-start | bytes 5767168 | tf_op jit(solution)/shard_map/all_to_all | solution.py:429
  1059.8 155.2 %all-gather.10.cloned.1.call-start = ((), (), s32[]{:S(2)}) async-start(), calls=%async_computation.22 | async-start | bytes 5242880 | tf_op jit(solution)/shard_map/all_gather | solution.py:418
  1069.9 68.5 %copy-start.20 = (bf16[1024,512]{1,0:T(8,128)(2,1)S(1)}, bf16[1024,512]{1,0:T(8,128)(2,1)}, u32[]{:S(2)}) copy-start(bf16[1024,512]{1,0:T(8,128)(2,1)} %reduce-scatter.6.cloned.1.call-done) | copy-start | bytes 3145732
  1070.3 68.0 %collective-permute-start.8 = (bf16[1024,512]{1,0:T(8,128)(2,1)S(1)}, bf16[1024,512]{1,0:T(8,128)(2,1)S(1)}, u32[]{:S(2)}, u32[]{:S(2)}) collective-permute-start(bf16[1024,512]{1,0:T(8,128)(2,1)S(1)} %get-tuple-element.240), channel_id=1, source_target_pairs={{0,3},{1,2},{2,1},{3,0},{4,7},{5,6},{6,5},{7,4},{8,11},{9,10},{10,... | collective-permute-start | bytes 3145736 | tf_op jit(solution)/shard_map/ppermute | solution.py:68
  1071.9 66.5 %collective-permute-start.7 = (bf16[1024,512]{1,0:T(8,128)(2,1)S(1)}, bf16[1024,512]{1,0:T(8,128)(2,1)S(1)}, u32[]{:S(2)}, u32[]{:S(2)}) collective-permute-start(bf16[1024,512]{1,0:T(8,128)(2,1)S(1)} %get-tuple-element.241), channel_id=1, source_target_pairs={{0,2},{1,3},{2,0},{3,1},{4,6},{5,7},{6,4},{7,5},{8,10},{9,11},{10,... | collective-permute-start | bytes 3145736 | tf_op jit(solution)/shard_map/ppermute | solution.py:68
  1072.4 66.0 %collective-permute-start.6 = (bf16[1024,512]{1,0:T(8,128)(2,1)S(1)}, bf16[1024,512]{1,0:T(8,128)(2,1)S(1)}, u32[]{:S(2)}, u32[]{:S(2)}) collective-permute-start(bf16[1024,512]{1,0:T(8,128)(2,1)S(1)} %get-tuple-element.239), channel_id=1, source_target_pairs={{0,1},{1,0},{2,3},{3,2},{4,5},{5,4},{6,7},{7,6},{8,9},{9,8},{10,11... | collective-permute-start | bytes 3145736 | tf_op jit(solution)/shard_map/ppermute | solution.py:68
  1075.4 49.0 %collective-permute-start.20 = (f32[8,128]{1,0:T(8,128)S(1)}, f32[8,128]{1,0:T(8,128)S(1)}, u32[]{:S(2)}, u32[]{:S(2)}) collective-permute-start(f32[8,128]{1,0:T(8,128)S(1)} %get-tuple-element.278), channel_id=1, source_target_pairs={{0,24},{4,28},{8,16},{12,20},{16,8},{20,12},{24,0},{28,4},{1,25},{... | collective-permute-start | bytes 12296 | tf_op jit(solution)/shard_map/ppermute | solution.py:73
  1077.0 47.3 %collective-permute-start.19 = (f32[8,128]{1,0:T(8,128)S(1)}, f32[8,128]{1,0:T(8,128)S(1)}, u32[]{:S(2)}, u32[]{:S(2)}) collective-permute-start(f32[8,128]{1,0:T(8,128)S(1)} %get-tuple-element.279), channel_id=1, source_target_pairs={{0,16},{4,20},{8,24},{12,28},{16,0},{20,4},{24,8},{28,12},{1,17},{... | collective-permute-start | bytes 12296 | tf_op jit(solution)/shard_map/ppermute | solution.py:73
  1124.3 3.6 collective-permute-start.18
  1127.9 4.6 collective-permute-start.23
  1129.4 3.7 collective-permute-start.22
  1132.6 3.7 collective-permute-start.21
  1154.9 60.1 %all-to-all-start.9 = ((bf16[4,4,352,256]{3,2,1,0:T(8,128)(2,1)}), bf16[4,4,352,256]{3,2,1,0:T(8,128)(2,1)S(1)}, u32[]{:S(2)}, u32[]{:S(2)}) async-start(bf16[4,4,352,256]{3,2,1,0:T(8,128)(2,1)} %bitcast.395), calls=%async_computation.12 | async-start | bytes 5767168 | tf_op jit(solution)/shard_map/all_to_all | solution.py:429
  1158.6 445.1 %reduce-scatter.14.cloned.1.call-start = ((), (), s32[]{:S(2)}) async-start(), calls=%async_computation.25 | async-start | bytes 9732096 | tf_op jit(solution)/shard_map/reduce_scatter | solution.py:761
  1216.6 118.4 %all-to-all-start.10 = ((bf16[4,4,352,256]{3,2,1,0:T(8,128)(2,1)}), bf16[4,4,352,256]{3,2,1,0:T(8,128)(2,1)}, u32[]{:S(2)}, u32[]{:S(2)}) async-start(bf16[4,4,352,256]{3,2,1,0:T(8,128)(2,1)} %bitcast.111), calls=%async_computation.13 | async-start | bytes 5767168 | tf_op jit(solution)/shard_map/all_to_all | solution.py:429
  1230.1 27.1 %collective-permute-start.26 = (bf16[1024,512]{1,0:T(8,128)(2,1)S(1)}, bf16[1024,512]{1,0:T(8,128)(2,1)S(1)}, u32[]{:S(2)}, u32[]{:S(2)}) collective-permute-start(bf16[1024,512]{1,0:T(8,128)(2,1)S(1)} %get-tuple-element.237), channel_id=1, source_target_pairs={{0,3},{1,2},{2,1},{3,0},{4,7},{5,6},{6,5},{7,4},{8,11},{9,10},{10,... | collective-permute-start | bytes 3145736 | tf_op jit(solution)/shard_map/ppermute | solution.py:68
  1232.8 44.8 %collective-permute-start.25 = (bf16[1024,512]{1,0:T(8,128)(2,1)S(1)}, bf16[1024,512]{1,0:T(8,128)(2,1)S(1)}, u32[]{:S(2)}, u32[]{:S(2)}) collective-permute-start(bf16[1024,512]{1,0:T(8,128)(2,1)S(1)} %get-tuple-element.238), channel_id=1, source_target_pairs={{0,2},{1,3},{2,0},{3,1},{4,6},{5,7},{6,4},{7,5},{8,10},{9,11},{10,... | collective-permute-start | bytes 3145736 | tf_op jit(solution)/shard_map/ppermute | solution.py:68
  1234.0 43.5 %collective-permute-start.24 = (bf16[1024,512]{1,0:T(8,128)(2,1)S(1)}, bf16[1024,512]{1,0:T(8,128)(2,1)S(1)}, u32[]{:S(2)}, u32[]{:S(2)}) collective-permute-start(bf16[1024,512]{1,0:T(8,128)(2,1)S(1)} %get-tuple-element.236), channel_id=1, source_target_pairs={{0,1},{1,0},{2,3},{3,2},{4,5},{5,4},{6,7},{7,6},{8,9},{9,8},{10,11... | collective-permute-start | bytes 3145736 | tf_op jit(solution)/shard_map/ppermute | solution.py:68
  1335.0 35.9 %all-to-all-start.11 = ((bf16[4,4,352,256]{3,2,1,0:T(8,128)(2,1)}), bf16[4,4,352,256]{3,2,1,0:T(8,128)(2,1)}, u32[]{:S(2)}, u32[]{:S(2)}) async-start(bf16[4,4,352,256]{3,2,1,0:T(8,128)(2,1)} %copy.451), calls=%async_computation.14 | async-start | bytes 5767168 | tf_op jit(solution)/shard_map/all_to_all | solution.py:426
  1371.0 58.7 %all-to-all-start.12 = ((bf16[4,4,352,256]{3,2,1,0:T(8,128)(2,1)}), bf16[4,4,352,256]{3,2,1,0:T(8,128)(2,1)}, u32[]{:S(2)}, u32[]{:S(2)}) async-start(bf16[4,4,352,256]{3,2,1,0:T(8,128)(2,1)} %copy.452), calls=%async_computation.15 | async-start | bytes 5767168 | tf_op jit(solution)/shard_map/all_to_all | solution.py:426
  1391.1 59.5 %collective-permute-start.32 = (bf16[1024,512]{1,0:T(8,128)(2,1)}, bf16[1024,512]{1,0:T(8,128)(2,1)}, u32[]{:S(2)}, u32[]{:S(2)}) collective-permute-start(bf16[1024,512]{1,0:T(8,128)(2,1)} %get-tuple-element.234), channel_id=1, source_target_pairs={{0,3},{1,2},{2,1},{3,0},{4,7},{5,6},{6,5},{7,4},{8,11},{9,10},{10,... | collective-permute-start | bytes 3145736 | tf_op jit(solution)/shard_map/ppermute | solution.py:68
  1392.5 61.2 %collective-permute-start.31 = (bf16[1024,512]{1,0:T(8,128)(2,1)}, bf16[1024,512]{1,0:T(8,128)(2,1)}, u32[]{:S(2)}, u32[]{:S(2)}) collective-permute-start(bf16[1024,512]{1,0:T(8,128)(2,1)} %get-tuple-element.235), channel_id=1, source_target_pairs={{0,2},{1,3},{2,0},{3,1},{4,6},{5,7},{6,4},{7,5},{8,10},{9,11},{10,... | collective-permute-start | bytes 3145736 | tf_op jit(solution)/shard_map/ppermute | solution.py:68
  1392.6 61.4 %collective-permute-start.30 = (bf16[1024,512]{1,0:T(8,128)(2,1)}, bf16[1024,512]{1,0:T(8,128)(2,1)}, u32[]{:S(2)}, u32[]{:S(2)}) collective-permute-start(bf16[1024,512]{1,0:T(8,128)(2,1)} %get-tuple-element.233), channel_id=1, source_target_pairs={{0,1},{1,0},{2,3},{3,2},{4,5},{5,4},{6,7},{7,6},{8,9},{9,8},{10,11... | collective-permute-start | bytes 3145736 | tf_op jit(solution)/shard_map/ppermute | solution.py:68
  1429.7 54.6 %all-to-all-start.13 = ((bf16[4,4,352,256]{3,2,1,0:T(8,128)(2,1)}), bf16[4,4,352,256]{3,2,1,0:T(8,128)(2,1)}, u32[]{:S(2)}, u32[]{:S(2)}) async-start(bf16[4,4,352,256]{3,2,1,0:T(8,128)(2,1)} %copy.453), calls=%async_computation.16 | async-start | bytes 5767168 | tf_op jit(solution)/shard_map/all_to_all | solution.py:426
  1435.2 171.9 %reduce-scatter.12.cloned.1.call-start = ((), (), s32[]{:S(2)}) async-start(), calls=%async_computation.23 | async-start | bytes 9879552 | tf_op jit(solution)/shard_map/reduce_scatter | solution.py:761
  1492.9 169.5 %all-reduce.7.cloned.1.call-start = ((), (), s32[]{:S(2)}) async-start(), calls=%async_computation.24 | async-start | bytes 1212416 | tf_op jit(solution)/shard_map/psum | solution.py:844
  1506.6 26.3 %collective-permute-start.27 = (bf16[1024,512]{1,0:T(8,128)(2,1)}, bf16[1024,512]{1,0:T(8,128)(2,1)S(1)}, u32[]{:S(2)}, u32[]{:S(2)}) collective-permute-start(bf16[1024,512]{1,0:T(8,128)(2,1)} %get-tuple-element.244.refs_0_), channel_id=1, source_target_pairs={{0,1},{1,0},{2,3},{3,2},{4,5},{5,4},{6,7},{7,6},{8,9},{9,8},{10,11... | collective-permute-start | bytes 3145736 | tf_op jit(solution)/shard_map/ppermute | solution.py:68
  1508.1 48.9 %collective-permute-start.28 = (bf16[1024,512]{1,0:T(8,128)(2,1)}, bf16[1024,512]{1,0:T(8,128)(2,1)}, u32[]{:S(2)}, u32[]{:S(2)}) collective-permute-start(bf16[1024,512]{1,0:T(8,128)(2,1)} %get-tuple-element.244.refs_0_), channel_id=1, source_target_pairs={{0,2},{1,3},{2,0},{3,1},{4,6},{5,7},{6,4},{7,5},{8,10},{9,11},{10,... | collective-permute-start | bytes 3145736 | tf_op jit(solution)/shard_map/ppermute | solution.py:68
  1509.5 47.4 %collective-permute-start.29 = (bf16[1024,512]{1,0:T(8,128)(2,1)}, bf16[1024,512]{1,0:T(8,128)(2,1)}, u32[]{:S(2)}, u32[]{:S(2)}) collective-permute-start(bf16[1024,512]{1,0:T(8,128)(2,1)} %get-tuple-element.244.refs_0_), channel_id=1, source_target_pairs={{0,3},{1,2},{2,1},{3,0},{4,7},{5,6},{6,5},{7,4},{8,11},{9,10},{10,... | collective-permute-start | bytes 3145736 | tf_op jit(solution)/shard_map/ppermute | solution.py:68
  1510.1 67.8 %collective-permute-start.33 = (bf16[1024,512]{1,0:T(8,128)(2,1)}, bf16[1024,512]{1,0:T(8,128)(2,1)S(1)}, u32[]{:S(2)}, u32[]{:S(2)}) collective-permute-start(bf16[1024,512]{1,0:T(8,128)(2,1)} %get-tuple-element.243.refs_0_), channel_id=1, source_target_pairs={{0,1},{1,0},{2,3},{3,2},{4,5},{5,4},{6,7},{7,6},{8,9},{9,8},{10,11... | collective-permute-start | bytes 3145736 | tf_op jit(solution)/shard_map/ppermute | solution.py:68
  1511.6 85.0 %collective-permute-start.34 = (bf16[1024,512]{1,0:T(8,128)(2,1)}, bf16[1024,512]{1,0:T(8,128)(2,1)S(1)}, u32[]{:S(2)}, u32[]{:S(2)}) collective-permute-start(bf16[1024,512]{1,0:T(8,128)(2,1)} %get-tuple-element.243.refs_0_), channel_id=1, source_target_pairs={{0,2},{1,3},{2,0},{3,1},{4,6},{5,7},{6,4},{7,5},{8,10},{9,11},{10,... | collective-permute-start | bytes 3145736 | tf_op jit(solution)/shard_map/ppermute | solution.py:68
  1532.9 63.6 %collective-permute-start.35 = (bf16[1024,512]{1,0:T(8,128)(2,1)}, bf16[1024,512]{1,0:T(8,128)(2,1)}, u32[]{:S(2)}, u32[]{:S(2)}) collective-permute-start(bf16[1024,512]{1,0:T(8,128)(2,1)} %get-tuple-element.243.refs_0_), channel_id=1, source_target_pairs={{0,3},{1,2},{2,1},{3,0},{4,7},{5,6},{6,5},{7,4},{8,11},{9,10},{10,... | collective-permute-start | bytes 3145736 | tf_op jit(solution)/shard_map/ppermute | solution.py:68
  (88 other events, 965.7 us)
Sparse Core Ops, SparseCore 0:
  20.3 83.9 all-gather.11
  210.1 53.5 reduce-scatter.5
  277.3 141.9 all-gather.13
  464.2 77.6 all-gather.15
  812.3 75.8 reduce-scatter.7
  890.2 82.2 all-gather.17
  975.4 77.7 reduce-scatter.9
  1155.0 51.5 all-gather.9
  1215.1 150.0 reduce-scatter.13
  1493.1 96.2 reduce-scatter.11
  1609.6 52.7 all-reduce.6

commit v5 on v4

--- a/solution.py
+++ b/solution.py
@@ -149,12 +149,11 @@
 
 
 def home_gradients(lay, pieces, f_loc, d_loc):
-    def kernel(gate_ref, up_ref, down_ref, in_ref, out_ref):
-        in_ref[0, 0] = gate_ref[0].astype(F32)
-        in_ref[0, 1] = up_ref[0].astype(F32)
-        out_ref[0] = down_ref[0].astype(F32)
-
-    spec = pl.BlockSpec((1, f_loc, d_loc), lambda e: (e % lay.t * lay.z + e // lay.t, 0, 0))
+    def kernel(piece_ref, in_ref, out_ref):
+        in_ref[0] = piece_ref[0, :2, 0].astype(F32)
+        out_ref[0] = piece_ref[0, 2, 0].astype(F32)
+
+    spec = pl.BlockSpec((1, 3, 1, f_loc, d_loc), lambda e: (e % lay.t, 0, e // lay.t, 0, 0))
     grad_in, grad_out = pl.pallas_call(
         kernel,
         out_shape=(
@@ -162,7 +161,7 @@
             jax.ShapeDtypeStruct((EXPERTS, f_loc, d_loc), F32),
         ),
         grid=(EXPERTS,),
-        in_specs=[spec] * 3,
+        in_specs=[spec],
         out_specs=(
             pl.BlockSpec((1, 2, f_loc, d_loc), lambda e: (e, 0, 0, 0)),
             pl.BlockSpec((1, f_loc, d_loc), lambda e: (e, 0, 0)),
@@ -171,7 +170,7 @@
             flops=0, bytes_accessed=18 * EXPERTS * f_loc * d_loc, transcendentals=0
         ),
         name="home_gradients",
-    )(*pieces)
+    )(pieces)
     return jnp.swapaxes(grad_in, 2, 3), grad_out
 
 
@@ -499,8 +498,8 @@
     attn_inverse = inverse_rms(inputs)
     cosine, sine = angle_tables(rows)
     wide_cos, wide_sin = jnp.tile(cosine, (1, heads)), jnp.tile(sine, (1, heads))
-    front, attn_inverse, wide_cos, wide_sin = lax.optimization_barrier(
-        (front, attn_inverse, wide_cos, wide_sin)
+    front, attn_inverse, wide_cos, wide_sin, route_all = lax.optimization_barrier(
+        (front, attn_inverse, wide_cos, wide_sin, route_all)
     )
 
     plane_ids = me_z * nt + jnp.arange(nt, dtype=jnp.int32)
@@ -563,13 +562,7 @@
         ),
         1,
     ).astype(BF16)
-    turned_t = jnp.concatenate(
-        [down_t[:LATENT]]
-        + [down_t[LATENT : LATENT + half]] * heads
-        + [down_t[LATENT + half :]] * heads,
-        0,
-    )
-    latent_all = dot_nt(normed_low, turned_t)
+    latent_all = dot_nt(normed_low, down_t)
     latent_all, by_column = lax.optimization_barrier((latent_all, by_column))
     by_column = jnp.transpose(by_column, (2, 1, 0, 3, 4))
     by_plane = [swap_z(by_column[g]) for g in range(3)]
@@ -578,15 +571,20 @@
     latent_hat = latent * kv_inverse
     kv_scale = gain_kv.astype(F32)
     latent_low = (latent_hat * kv_scale).astype(BF16)
-    key_rope = jnp.concatenate(
+    key_turned = jnp.concatenate(
         rotate(
-            latent_all[:, LATENT : LATENT + heads * half],
-            latent_all[:, LATENT + heads * half :],
-            wide_cos,
-            wide_sin,
+            latent_all[:, LATENT : LATENT + half],
+            latent_all[:, LATENT + half :],
+            wide_cos[:, :half],
+            wide_sin[:, :half],
         ),
         1,
     ).astype(BF16)
+    copies = (2 * half, 2 * heads * half)
+    to_col = lax.broadcasted_iota(jnp.int32, copies, 1)
+    from_col = to_col // (heads * half) * half + to_col % half
+    repeat = (lax.broadcasted_iota(jnp.int32, copies, 0) == from_col).astype(BF16)
+    key_rope = dot(key_turned, repeat).astype(BF16)
     keys_values = dot(latent_low, up_w).astype(BF16)
     attended_low, log_totals = attend(
         lengths, query_nope, query_rope, keys_values, key_rope, heads, score_scale
@@ -604,11 +602,11 @@
     ffn_scale = lax.dynamic_slice_in_dim(gain_ffn, me_t * part, part, 0).astype(F32)
     ffn_part = (ffn_hat * ffn_scale).astype(BF16)
 
+    ffn_part, by_plane[1] = lax.optimization_barrier((ffn_part, by_plane[1]))
     ffn_all = gather_z(ffn_part)
     ffn_low = gather_t_direct(ffn_part)
-    ffn_all, ffn_low = lax.optimization_barrier((ffn_all, ffn_low))
+    ffn_all, ffn_low, cot_ready = lax.optimization_barrier((ffn_all, ffn_low, cot_part))
     picked = pick_rows(ffn_all)
-    picked, cot_ready = lax.optimization_barrier((picked, cot_part))
     expert_rows = send_out(picked)
     cot_picked = pick_rows(gather_z(cot_ready))
     shared_pack = jnp.concatenate(
@@ -650,7 +648,7 @@
     gate_silu = gate_pre * gate_sig
     active = (gate_silu * up_pre).astype(BF16)
     rows_out = (dot(active, own_out) * gate_rows).astype(BF16)
-    rows_out, cot_rows = lax.optimization_barrier((rows_out, cot_rows))
+    rows_out, cot_rows, shared_all = lax.optimization_barrier((rows_out, cot_rows, shared_all))
     out_parts = send_back(rows_out)
     active_grad_raw = dot_nt(cot_rows, own_out)
     gate_grad = jnp.sum(active.astype(F32) * active_grad_raw, axis=-1).reshape(nz, CAP)
@@ -666,25 +664,10 @@
     rows_grad = dot(pre_low, own_in).astype(BF16)
     rows_grad, out_parts = lax.optimization_barrier((rows_grad, out_parts))
     grad_parts = send_back(rows_grad)
-    routed, pre_low = lax.optimization_barrier((combine(out_parts), pre_low))
+    routed, pre_low, gated_active = lax.optimization_barrier(
+        (combine(out_parts), pre_low, gated_active)
+    )
     routed = scatter_z(routed).astype(F32)
-    grad_in_own = dot_tn(pre_low, expert_rows).astype(BF16)
-    grad_out_own = dot_tn(gated_active, cot_rows).astype(BF16)
-    grad_parts, grad_in_own, grad_out_own, routed = lax.optimization_barrier(
-        (grad_parts, grad_in_own, grad_out_own, routed)
-    )
-    grad_pieces = take_apart(lay, ids, grad_in_own, grad_out_own, f_loc, d_loc, width)
-    routed_grad = scatter_z(combine(grad_parts)).astype(F32)
-    grad_class = [
-        sum(lay.over_c(grad_pieces[3 * k + g], k).astype(F32) for k in range(nq)).astype(BF16)
-        for g in range(3)
-    ]
-    routed_grad, grad_class = lax.optimization_barrier((routed_grad, grad_class))
-    grad_plane = [swap_z(grad_class[g].reshape(nz, nt, f_loc, d_loc)) for g in range(3)]
-
-    def to_columns(values):
-        return swap_t(jnp.swapaxes(values, 0, 1)).reshape(EXPERTS, f_loc, d_loc)
-
     token_grad = jnp.sum(jnp.where(own_place, gate_grad[:, :, None], 0.0), axis=1)
     token_grad = token_grad.reshape(nz, -1, 128)
     token_plane = jnp.stack(
@@ -704,6 +687,8 @@
         preferred_element_type=F32,
     )
 
+    grad_in_own = dot_tn(pre_low, expert_rows).astype(BF16)
+    grad_out_own = dot_tn(gated_active, cot_rows).astype(BF16)
     ffs = w_shared_out.shape[0]
     shared_in = jnp.swapaxes(shared_all[:, : 2 * ffs], 0, 1).reshape(2 * ffs, width)
     shared_out = jnp.swapaxes(shared_all[:, 2 * ffs :], 0, 1).reshape(ffs, width)
@@ -712,7 +697,7 @@
     shared_sig = jax.nn.sigmoid(shared_gate)
     shared_silu = shared_gate * shared_sig
     shared_act = (shared_silu * shared_up).astype(BF16)
-    shared_part = scatter_t_direct(dot(shared_act, shared_out))
+    shared_full = dot(shared_act, shared_out)
     shared_act_grad = dot_nt(cot_low, shared_out)
     shared_pre_grad = jnp.concatenate(
         [
@@ -723,7 +708,39 @@
     ).astype(BF16)
     grad_shared_in = dot_tn(shared_pre_grad, ffn_low)
     grad_shared_out = dot_tn(shared_act, cot_low)
-    shared_grad = scatter_t_direct(dot(shared_pre_grad, shared_in))
+    shared_grad_full = dot(shared_pre_grad, shared_in)
+
+    (
+        grad_parts,
+        grad_in_own,
+        grad_out_own,
+        routed,
+        probs_grad,
+        shared_full,
+        shared_grad_full,
+    ) = lax.optimization_barrier(
+        (
+            grad_parts,
+            grad_in_own,
+            grad_out_own,
+            routed,
+            probs_grad,
+            shared_full,
+            shared_grad_full,
+        )
+    )
+    shared_both = jnp.concatenate([shared_grad_full, shared_full], 0).astype(BF16)
+    shared_both = swap_t(jnp.swapaxes(shared_both.reshape(2 * rows, nt, part), 0, 1))
+    shared_both = jnp.sum(shared_both.astype(F32), axis=0)
+    shared_grad, shared_part = shared_both[:rows], shared_both[rows:]
+    grad_pieces = take_apart(lay, ids, grad_in_own, grad_out_own, f_loc, d_loc, width)
+    routed_grad = scatter_z(combine(grad_parts)).astype(F32)
+    grad_class = [
+        sum(lay.over_c(grad_pieces[3 * k + g], k).astype(F32) for k in range(nq)).astype(BF16)
+        for g in range(3)
+    ]
+    routed_grad, grad_class = lax.optimization_barrier((routed_grad, grad_class))
+    grad_plane = [swap_z(grad_class[g].reshape(nz, nt, f_loc, d_loc)) for g in range(3)]
 
     logits_grad = router_probs * (
         probs_grad - jnp.sum(router_probs * probs_grad, axis=-1, keepdims=True)
@@ -752,10 +769,7 @@
     residual_grad = cot_part.astype(F32) + ffn_inverse * (
         scaled - ffn_hat * row_mean(ffn_hat * scaled)
     )
-    residual_ready, grad_plane[0] = lax.optimization_barrier(
-        (residual_grad.astype(BF16), grad_plane[0])
-    )
-    residual_low = gather_t(residual_ready)
+    residual_low = gather_t(residual_grad.astype(BF16))
 
     def sum_dp(values):
         return lax.psum_scatter(values, "dp", scatter_dimension=0, tiled=False).astype(F32)
@@ -764,8 +778,8 @@
         return jnp.swapaxes(values.astype(BF16).reshape(-1, ndp, d_loc), 0, 1)
 
     shared_grads = jnp.concatenate([by_owner(grad_shared_in), by_owner(grad_shared_out)], 1)
-    residual_low, shared_grads, grad_plane[1] = lax.optimization_barrier(
-        (residual_low, shared_grads, grad_plane[1])
+    residual_low, shared_grads, grad_plane[0] = lax.optimization_barrier(
+        (residual_low, shared_grads, grad_plane[0])
     )
     shared_sum = sum_dp(shared_grads)
     grad_out_w = dot_tn(attended_low, residual_low)
@@ -781,13 +795,11 @@
         heads,
         score_scale,
     )
-    grad_home = [to_columns(grad_plane[0]), None, None]
-    query_turned_grad, routed, shared_part, grad_plane[2] = lax.optimization_barrier(
-        (query_turned_grad, routed, shared_part, grad_plane[2])
-    )
-    grad_home[1] = to_columns(grad_plane[1])
-    grad_home[2] = to_columns(grad_plane[2])
-    output = gather_t_direct((residual + routed + shared_part).astype(BF16))
+    output_part = lax.optimization_barrier((residual + routed + shared_part).astype(BF16))
+    query_turned_grad, output_parts = lax.optimization_barrier(
+        (query_turned_grad, [lay.over_t(output_part, k) for k in range(nt)])
+    )
+    output = join_columns(output_parts, me_t, nt)
     turned_first, turned_second = rotate_back(
         query_turned_grad[:, : heads * half], query_turned_grad[:, heads * half :], wide_cos, wide_sin
     )
@@ -808,8 +820,12 @@
         scaled_kv - latent_hat * jnp.mean(latent_hat * scaled_kv, axis=-1, keepdims=True)
     )
     down_grad = jnp.concatenate([latent_back, key_rope_part], -1).astype(BF16)
-    normed_grad = scatter_t_direct(dot(query_grad, query_t) + dot(down_grad, down_t))
-    normed_grad, grad_home = lax.optimization_barrier((normed_grad, grad_home))
+    normed_full, grad_plane[1] = lax.optimization_barrier(
+        (dot(query_grad, query_t) + dot(down_grad, down_t), grad_plane[1])
+    )
+    normed_grad = scatter_t_direct(normed_full)
+    normed_grad, grad_plane[2] = lax.optimization_barrier((normed_grad, grad_plane[2]))
+    grad_home = swap_t(jnp.transpose(jnp.stack(grad_plane), (2, 0, 1, 3, 4)))
     attn_hat = own_part(hidden).astype(F32) * attn_inverse
     scaled_in = lax.dynamic_slice_in_dim(attn_scale, me_t * part, part, 0) * normed_grad
     attn_gain_part = jnp.sum(normed_grad * attn_hat, axis=0)
@@ -841,7 +857,10 @@
             1,
         )
     )
-    own_sum = lax.psum(front_sum[: down_rows + EXPERTS], "tensor")
+    own_sum = front_sum[: down_rows + EXPERTS]
+    own_low = own_sum.astype(BF16)
+    for k in range(1, nt):
+        own_sum = own_sum + lay.over_t(own_low, k).astype(F32)
     at = down_rows + 2 * EXPERTS
     return (
         output,

time: 1690 us -> 1650 us (0.976)
  waiting for transfers between devices: 775 us -> 640 us
  blocking collectives: 24.3 us -> 113 us
  other arithmetic: 91.6 us -> 109 us
    ppermute x9, waiting for transfers between devices: 173 us -> 1.48 us  [over_z(): lax.ppermute(values, 'dp', [(d, d ^ k * self.q) for d in range(self.dp)])]
    all_to_all x6, waiting for transfers between devices: 62.3 us -> 204 us  [swap_z(): lax.all_to_all(values, 'dp', split_axis=0, concat_axis=0, axis_index_grou...]
    psum x3, blocking collectives: 24.3 us -> 113 us  [row_mean(): return lax.psum(partial, 'tensor').reshape(-1, 1) * (1.0 / width)]
    psum x1 -> x0, waiting for transfers between devices: 47.4 us -> none  [body(): own_sum = lax.psum(front_sum[:down_rows + EXPERTS], 'tensor')]
    all_gather x1, waiting for transfers between devices: 41.7 us -> 0.01 us  [body(): shared_all = lax.all_gather(shared_pack, 'dp', axis=0, tiled=False)]
    all_gather x2, waiting for transfers between devices: 0.01 us -> 26.9 us  [gather_z(): lax.all_gather(values, 'dp', axis=0, tiled=False, axis_index_groups=lay.z...]
    reduce_scatter x2, waiting for transfers between devices: 29.8 us -> 5.23 us  [scatter_z(): lax.psum_scatter(values, 'dp', scatter_dimension=0, tiled=False, axis_ind...]
    all_to_all x8 -> x7, waiting for transfers between devices: 205 us -> 186 us  [swap_t(): lax.all_to_all(values, 'tensor', split_axis=0, concat_axis=0, tiled=True)]
  transfers between devices with their start and end apart: 61 -> 56, of which waited for: 32 -> 29; matrix products, arithmetic and copies ran while one was open for 31% -> 32% of each run, Pallas kernels for 6% -> 6%
where the time goes in v5:
time: 1650 us; the launch traced here: 1630 us
  waiting for transfers between devices  640 us (39%)
  matrix products  330 us (20%)
  local copies, waits for them, and re-layouts  202 us (12%)
  starting transfers between devices  125 us (8%)
  blocking collectives  113 us (7%)
  other arithmetic  109 us (7%)
  Pallas kernels  97.5 us (6%)
  between operations  16.5 us (1%)
    all_to_all x6, waiting for transfers between devices, swap_z(): lax.all_to_all(values, 'dp', split_axis=0, concat_axis=0, axis_index_grou...  204 us
    all_to_all x7, waiting for transfers between devices, swap_t(): lax.all_to_all(values, 'tensor', split_axis=0, concat_axis=0, tiled=True)  186 us
    psum x3, blocking collectives, row_mean(): return lax.psum(partial, 'tensor').reshape(-1, 1) * (1.0 / width)  113 us
    ppermute x18, waiting for transfers between devices, over_t(): return lax.ppermute(values, 'tensor', [(i, i ^ k) for i in range(self.t)])  111 us
    dot_general x9, matrix products, dot_nt(): lax.dot_general(a, b, (((1,), (1,)), ((), ())), preferred_element_type=F32)  100 us
    dot_general x9, matrix products, dot(): return jnp.dot(a, b, preferred_element_type=F32)  82.2 us
    dot_general x8, matrix products, dot_tn(): lax.dot_general(a, b, (((0,), (0,)), ((), ())), preferred_element_type=F32)  82.1 us
    all_gather x1, waiting for transfers between devices, body(): front = lax.all_gather(front_pack, 'dp', axis=0, tiled=False)  55.1 us
  transfers between devices with their start and end apart: 56, of which 29 were waited for; matrix products, arithmetic and copies ran while one was open for 32% of the time, Pallas kernels for 6%

profile of v5, /device:TPU:10, one launch (start us, length us, event | category | flops | bytes accessed | tf_op | source)
XLA Modules:
  0.0 1632.7 jit_solution(12476039812650574450)
XLA Ops:
  19.5 6.9 maximum_bitcast_fusion
  26.4 8.4 copy.303
  34.8 6.4 all-to-all-start
  50.7 55.1 %all-gather.12.cloned.1.call-done = bf16[17152,256]{1,0:T(8,128)(2,1)} async-done(((bf16[2144,256]{1,0:T(8,128)(2,1)}), bf16[17152,256]{1,0:T(8,128)(2,1)}) %all-gather.12.cloned.1.call-update) | async-done | bytes 8781840 | tf_op jit(solution)/shard_map/all_gather | solution.py:489
  115.4 20.7 %all-to-all-done = bf16[4,4,3,352,256]{4,3,1,2,0:T(8,128)(2,1)} async-done(((bf16[4,4,3,352,256]{4,3,1,2,0:T(8,128)(2,1)}), bf16[4,4,3,352,256]{4,3,1,2,0:T(8,128)(2,1)}, u32[]{:S(2)}, u32[]{:S(2)}) %all-to-all-start) | async-done | bytes 8650784 | tf_op jit(solution)/shard_map/all_to_all | solution.py:425
  162.2 6.4 fusion.116
  190.5 14.6 attend.1
  220.9 43.6 %reduce-scatter.6.cloned.1.call-done = bf16[1024,512]{1,0:T(8,128)(2,1)} async-done(((bf16[1024,2048]{1,0:T(8,128)(2,1)}), bf16[1024,512]{1,0:T(8,128)(2,1)}) %reduce-scatter.6.cloned.1.call-update) | async-done | bytes 1048592 | tf_op jit(solution)/shard_map/reduce_scatter | solution.py:420
  266.5 8.1 psum.21
  291.4 17.2 %collective-permute-done.3.refs_1_ = bf16[1024,512]{1,0:T(8,128)(2,1)} collective-permute-done((bf16[1024,512]{1,0:T(8,128)(2,1)}, bf16[1024,512]{1,0:T(8,128)(2,1)}, u32[]{:S(2)}, u32[]{:S(2)}) %collective-permute-start.3) | collective-permute-done | bytes 1048608 | tf_op jit(solution)/shard_map/ppermute | solution.py:68
  308.6 19.9 %collective-permute-done.4.refs_2_ = bf16[1024,512]{1,0:T(8,128)(2,1)} collective-permute-done((bf16[1024,512]{1,0:T(8,128)(2,1)}, bf16[1024,512]{1,0:T(8,128)(2,1)}, u32[]{:S(2)}, u32[]{:S(2)}) %collective-permute-start.4) | collective-permute-done | bytes 1048608 | tf_op jit(solution)/shard_map/ppermute | solution.py:68
  328.6 6.2 join_columns.3
  334.7 26.9 %all-gather.14.cloned.1.call-done = bf16[4096,512]{1,0:T(8,128)(2,1)} async-done(((bf16[1024,512]{1,0:T(8,128)(2,1)}), bf16[4096,512]{1,0:T(8,128)(2,1)}) %all-gather.14.cloned.1.call-update) | async-done | bytes 4194320 | tf_op jit(solution)/shard_map/all_gather | solution.py:409
  365.2 8.0 all-to-all-start.4
  376.2 16.2 convert_bitcast_fusion.1
  392.5 7.4 copy.308
  399.9 99.9 %all-to-all-done.4 = bf16[4,4,352,256]{3,2,1,0:T(8,128)(2,1)} async-done(((bf16[4,4,352,256]{3,2,1,0:T(8,128)(2,1)}), bf16[4,4,352,256]{3,2,1,0:T(8,128)(2,1)}, u32[]{:S(2)}, u32[]{:S(2)}) %all-to-all-start.4) | async-done | bytes 2883616 | tf_op jit(solution)/shard_map/all_to_all | solution.py:428
  505.8 16.2 convert_bitcast_fusion
  522.0 7.3 copy.317
  543.3 17.2 %lay_out_weights.1 = (bf16[2,1408,2048]{2,1,0:T(8,128)(2,1)}, bf16[1408,2048]{1,0:T(8,128)(2,1)}) custom-call(s32[3]{0:T(128)S(1)} %pad_add_fusion.1.ids_ref, bf16[16,352,256]{2,1,0:T(8,128)(2,1)S(1)} %bitcast.388, bf16[16,352,256]{2,1,0:T(8,128)(2,1)} %bitcast.48.refs_1_, bf16[16,352,256]{2,1,0:T(8,128)(2,1)} %bitcast.50.refs_2_, ...), custom_call_target="tpu_custom_call" | custom-call | bytes 34603008 | tf_op jit(solution)/shard_map/lay_out_weights/pallas_call | solution.py:92
  561.6 36.0 %all-to-all-done.3 = bf16[4,2048,512]{2,1,0:T(8,128)(2,1)} async-done(((bf16[4,2048,512]{2,1,0:T(8,128)(2,1)}), bf16[4,2048,512]{2,1,0:T(8,128)(2,1)}, u32[]{:S(2)}, u32[]{:S(2)}) %all-to-all-start.3) | async-done | bytes 8388640 | tf_op jit(solution)/shard_map/all_to_all | solution.py:425
  597.6 11.5 copy.309
  609.1 6.5 all-to-all-start.5
  615.6 32.1 %fusion.125 = f32[2048,2816]{1,0:T(8,128)} fusion(bf16[2048,2048]{0,1:T(8,128)(2,1)} %bitcast.413, bf16[2816,2048]{1,0:T(8,128)(2,1)} %bitcast.507), kind=kOutput, calls=%fused_computation.293 | convolution fusion | flops 23622320128 | bytes 42991616 | tf_op jit(solution)/shard_map/dot_general | solution.py:30
  647.7 12.3 fusion.8
  662.5 18.0 %multiply_convert_fusion = bf16[2048,2048]{1,0:T(8,128)(2,1)} fusion(bf16[2048,1408]{1,0:T(8,128)(2,1)S(1)} %get-tuple-element.234, bf16[1408,2048]{1,0:T(8,128)(2,1)} %get-tuple-element.91, f32[2048]{0:T(1024)S(1)} %bitcast.479), kind=kOutput, calls=%fused_computation.6 | convolution fusion | flops 11819548672 | bytes 19931136 | tf_op jit(solution)/shard_map/dot_general | solution.py:26
  680.5 26.3 %all-to-all-done.5 = bf16[4,2048,512]{2,1,0:T(8,128)(2,1)} async-done(((bf16[4,2048,512]{2,1,0:T(8,128)(2,1)}), bf16[4,2048,512]{2,1,0:T(8,128)(2,1)}, u32[]{:S(2)}, u32[]{:S(2)}) %all-to-all-start.5) | async-done | bytes 8388640 | tf_op jit(solution)/shard_map/all_to_all | solution.py:425
  706.8 11.4 copy.318
  726.4 27.7 %multiply_convert_fusion.2 = (bf16[2048,1408]{1,0:T(8,128)(2,1)}, bf16[2048,1408]{1,0:T(8,128)(2,1)}, f32[2048]{0:T(1024)S(1)}) fusion(f32[2048,2816]{1,0:T(8,128)} %fusion.125, f32[2048]{0:T(1024)S(1)} %bitcast.480, bf16[2048,1408]{1,0:T(8,128)(2,1)} %copy-done.29, bf16[2048,2048]{0,1:T(8,128)(2,1)S(1)} %bitcast.416, bf16[1408,2048]{1,0:T(8,128)(2,1)} %get-tuple-element.91), kind=kOutput, calls=%fused_computation.17 | convolution fusion | flops 11860178944 | bytes 54542336 | tf_op jit(solution)/shard_map/dot_general | solution.py:30
  754.1 7.5 copy.406
  761.7 6.3 all-to-all-start.6
  774.6 8.4 copy.324
  782.9 11.7 fusion.126
  797.8 8.3 multiply_convert_fusion.5
  806.2 10.3 fusion.40
  816.5 28.5 %convolution_convert_fusion.3 = bf16[2048,2048]{1,0:T(8,128)(2,1)} fusion(bf16[2816,2048]{1,0:T(8,128)(2,1)} %bitcast.508, bf16[2048,1408]{1,0:T(8,128)(2,1)S(1)} %bitcast.428, bf16[2048,1408]{1,0:T(8,128)(2,1)S(1)} %bitcast.426), kind=kOutput, calls=%fused_computation.44 | convolution fusion | flops 23649583104 | bytes 31457280 | tf_op jit(solution)/shard_map/dot_general | solution.py:26
  859.7 12.3 bitcast_convert_fusion.1
  873.8 6.4 fusion.127
  881.1 7.4 copy.405
  894.6 17.9 %convolution_convert_fusion.2.out_ref = bf16[1408,2048]{1,0:T(8,128)(2,1)} fusion(bf16[2048,1408]{1,0:T(8,128)(2,1)} %get-tuple-element.101, bf16[2048,2048]{0,1:T(8,128)(2,1)} %bitcast.415), kind=kOutput, calls=%fused_computation.43 | convolution fusion | flops 11814043648 | bytes 19922944 | tf_op jit(solution)/shard_map/dot_general | solution.py:34
  912.5 32.1 %convolution_convert_fusion = bf16[2816,2048]{1,0:T(8,128)(2,1)} fusion(bf16[2048,2816]{1,0:T(8,128)(2,1)} %pad_maximum_fusion, bf16[2048,2048]{0,1:T(8,128)(2,1)} %bitcast.414), kind=kOutput, calls=%fused_computation.21 | convolution fusion | flops 23628087296 | bytes 31457280 | tf_op jit(solution)/shard_map/dot_general | solution.py:34
  952.7 33.1 %all-to-all-done.7 = bf16[4,2048,512]{2,1,0:T(8,128)(2,1)} async-done(((bf16[4,2048,512]{2,1,0:T(8,128)(2,1)}), bf16[4,2048,512]{2,1,0:T(8,128)(2,1)}, u32[]{:S(2)}, u32[]{:S(2)}) %all-to-all-start.7) | async-done | bytes 8388640 | tf_op jit(solution)/shard_map/all_to_all | solution.py:425
  985.7 12.1 bitcast_convert_fusion
  1005.1 7.7 maximum_bitcast_fusion.2
  1012.8 6.3 all-to-all-start.8
  1019.1 11.9 take_apart.1
  1047.1 63.7 %all-to-all-done.8 = bf16[4,2048,512]{2,1,0:T(8,128)(2,1)} async-done(((bf16[4,2048,512]{2,1,0:T(8,128)(2,1)}), bf16[4,2048,512]{2,1,0:T(8,128)(2,1)}, u32[]{:S(2)}, u32[]{:S(2)}) %all-to-all-start.8) | async-done | bytes 8388640 | tf_op jit(solution)/shard_map/all_to_all | solution.py:425
  1110.8 7.1 convert_reduce_fusion
  1125.7 8.1 psum.22
  1152.8 7.2 convolution_convert_fusion.1
  1164.2 38.9 %all-to-all-done.9 = bf16[4,4,352,256]{3,2,1,0:T(8,128)(2,1)S(1)} async-done(((bf16[4,4,352,256]{3,2,1,0:T(8,128)(2,1)}), bf16[4,4,352,256]{3,2,1,0:T(8,128)(2,1)S(1)}, u32[]{:S(2)}, u32[]{:S(2)}) %all-to-all-start.9) | async-done | bytes 2883616 | tf_op jit(solution)/shard_map/all_to_all | solution.py:428
  1204.7 8.4 all-to-all-start.10
  1223.8 21.6 %attend_back.1 = (bf16[1024,512]{1,0:T(8,128)(2,1)S(1)}, f32[1024,256]{1,0:T(8,128)S(1)}, bf16[1024,1024]{1,0:T(8,128)(2,1)S(1)}, f32[1024,256]{1,0:T(8,128)S(1)}) custom-call(s32[1]{0:T(128)} %copy.431.len_ref, bf16[1024,512]{1,0:T(8,128)(2,1)S(1)} %copy-done.1, bf16[1024,256]{1,0:T(8,128)(2,1)S(1)} %copy-done.5, bf16[1024,1024]{1,0:T(8,128)(2,1)S(1)} %copy-done.9, ...), custom_call_target="tpu_custom_call" | custom-call | flops 6710886400 | bytes 33554432 | tf_op jit(solution)/shard_map/attend_back/pallas_call | solution.py:324
  1247.7 16.7 %collective-permute-done.22.refs_2_ = bf16[1024,512]{1,0:T(8,128)(2,1)} collective-permute-done((bf16[1024,512]{1,0:T(8,128)(2,1)}, bf16[1024,512]{1,0:T(8,128)(2,1)}, u32[]{:S(2)}, u32[]{:S(2)}) %collective-permute-start.22) | collective-permute-done | bytes 1048608 | tf_op jit(solution)/shard_map/ppermute | solution.py:68
  1279.7 45.1 %all-to-all-done.10 = bf16[4,4,352,256]{3,2,1,0:T(8,128)(2,1)} async-done(((bf16[4,4,352,256]{3,2,1,0:T(8,128)(2,1)}), bf16[4,4,352,256]{3,2,1,0:T(8,128)(2,1)}, u32[]{:S(2)}, u32[]{:S(2)}) %all-to-all-start.10) | async-done | bytes 2883616 | tf_op jit(solution)/shard_map/all_to_all | solution.py:428
  1324.8 8.9 all-to-all-start.11
  1334.7 7.2 convolution_add_fusion
  1374.6 20.4 %collective-permute-done.25 = bf16[1024,512]{1,0:T(8,128)(2,1)} collective-permute-done((bf16[1024,512]{1,0:T(8,128)(2,1)}, bf16[1024,512]{1,0:T(8,128)(2,1)}, u32[]{:S(2)}, u32[]{:S(2)}) %collective-permute-start.25) | collective-permute-done | bytes 1048608 | tf_op jit(solution)/shard_map/ppermute | solution.py:68
  1398.1 16.2 all-to-all-done.11
  1431.1 6.2 all-to-all-start.12
  1437.2 97.3 %psum.23 = f32[8,128]{1,0:T(8,128)S(1)} all-reduce(f32[8,128]{1,0:T(8,128)S(1)} %bitcast.483), channel_id=1, replica_groups=mesh['dp'=8,'tensor'=4] {'tensor'}, use_global_device_ids=true, to_apply=%region_20.21 | all-reduce | flops 1024 | bytes 8192 | tf_op jit(solution)/shard_map/psum | solution.py:598
  1547.6 16.7 %collective-permute-done.27.refs_1_ = bf16[1024,512]{1,0:T(8,128)(2,1)S(1)} collective-permute-done((bf16[1024,512]{1,0:T(8,128)(2,1)}, bf16[1024,512]{1,0:T(8,128)(2,1)S(1)}, u32[]{:S(2)}, u32[]{:S(2)}) %collective-permute-start.27) | collective-permute-done | bytes 1048608 | tf_op jit(solution)/shard_map/ppermute | solution.py:68
  1564.3 19.2 %collective-permute-done.28.refs_2_ = bf16[1024,512]{1,0:T(8,128)(2,1)S(1)} collective-permute-done((bf16[1024,512]{1,0:T(8,128)(2,1)}, bf16[1024,512]{1,0:T(8,128)(2,1)S(1)}, u32[]{:S(2)}, u32[]{:S(2)}) %collective-permute-start.28) | collective-permute-done | bytes 1048608 | tf_op jit(solution)/shard_map/ppermute | solution.py:68
  1590.6 13.8 home_gradients.1
  (459 shorter events, 370.8 us)
Async XLA Ops:
  7.2 98.6 %all-gather.12.cloned.1.call-start = ((), (), s32[]{:S(2)}) async-start(), calls=%async_computation.24 | async-start | bytes 9879552 | tf_op jit(solution)/shard_map/all_gather | solution.py:489
  34.8 101.2 %all-to-all-start = ((bf16[4,4,3,352,256]{4,3,1,2,0:T(8,128)(2,1)}), bf16[4,4,3,352,256]{4,3,1,2,0:T(8,128)(2,1)}, u32[]{:S(2)}, u32[]{:S(2)}) async-start(bf16[4,4,3,352,256]{4,3,1,2,0:T(8,128)(2,1)} %copy.303), calls=%async_computation | async-start | bytes 17301504 | tf_op jit(solution)/shard_map/all_to_all | solution.py:425
  41.2 9.0 collective-permute-start
  42.9 7.4 collective-permute-start.1
  44.1 6.6 collective-permute-start.2
  49.1 113.1 %copy-start.67 = (f32[1024]{0:T(1024)}, f32[1024]{0:T(1024)S(1)}, u32[]{:S(2)}) copy-start(f32[1024]{0:T(1024)S(1)} %add_rsqrt_fusion.1) | copy-start | bytes 12292
  110.6 51.6 %copy-start.73 = (f32[8,1,256]{2,1,0:T(1,128)}, f32[8,1,256]{2,1,0:T(1,128)S(1)}, u32[]{:S(2)}) copy-start(f32[8,1,256]{2,1,0:T(1,128)S(1)} %get-tuple-element.242) | copy-start | bytes 24580
  143.3 68.5 %all-to-all-start.1 = ((bf16[4,4,352,256]{3,2,1,0:T(8,128)(2,1)}), bf16[4,4,352,256]{3,2,1,0:T(8,128)(2,1)S(1)}, u32[]{:S(2)}, u32[]{:S(2)}) async-start(bf16[4,4,352,256]{3,2,1,0:T(8,128)(2,1)} %copy.305), calls=%async_computation.1 | async-start | bytes 5767168 | tf_op jit(solution)/shard_map/all_to_all | solution.py:428
  148.6 115.9 %reduce-scatter.6.cloned.1.call-start = ((), (), s32[]{:S(2)}) async-start(), calls=%async_computation.18 | async-start | bytes 5242880 | tf_op jit(solution)/shard_map/reduce_scatter | solution.py:420
  215.4 66.7 %all-to-all-start.2 = ((bf16[4,4,352,256]{3,2,1,0:T(8,128)(2,1)}), bf16[4,4,352,256]{3,2,1,0:T(8,128)(2,1)}, u32[]{:S(2)}, u32[]{:S(2)}) async-start(bf16[4,4,352,256]{3,2,1,0:T(8,128)(2,1)} %copy.306), calls=%async_computation.3 | async-start | bytes 5767168 | tf_op jit(solution)/shard_map/all_to_all | solution.py:428
  220.8 140.8 %all-gather.14.cloned.1.call-start = ((), (), s32[]{:S(2)}) async-start(), calls=%async_computation.25 | async-start | bytes 5242880 | tf_op jit(solution)/shard_map/all_gather | solution.py:409
  220.9 67.4 %copy-start.69 = (f32[512]{0:T(512)}, f32[512]{0:T(512)S(1)}, u32[]{:S(2)}) copy-start(f32[512]{0:T(512)S(1)} %dynamic-slice_convert_fusion.3) | copy-start | bytes 6148
  282.1 223.7 %all-gather.16.cloned.1.call-start = ((), (), s32[]{:S(2)}) async-start(), calls=%async_computation.26 | async-start | bytes 5242880 | tf_op jit(solution)/shard_map/all_gather | solution.py:409
  282.1 26.5 %collective-permute-start.3 = (bf16[1024,512]{1,0:T(8,128)(2,1)}, bf16[1024,512]{1,0:T(8,128)(2,1)}, u32[]{:S(2)}, u32[]{:S(2)}) collective-permute-start(bf16[1024,512]{1,0:T(8,128)(2,1)} %multiply_convert_fusion.8.refs_0_), channel_id=1, source_target_pairs={{0,1},{1,0},{2,3},{3,2},{4,5},{5,4},{6,7},{7,6},{8,9},{9,8},{10,11... | collective-permute-start | bytes 3145736 | tf_op jit(solution)/shard_map/ppermute | solution.py:68
  283.1 45.5 %collective-permute-start.4 = (bf16[1024,512]{1,0:T(8,128)(2,1)}, bf16[1024,512]{1,0:T(8,128)(2,1)}, u32[]{:S(2)}, u32[]{:S(2)}) collective-permute-start(bf16[1024,512]{1,0:T(8,128)(2,1)} %multiply_convert_fusion.8.refs_0_), channel_id=1, source_target_pairs={{0,2},{1,3},{2,0},{3,1},{4,6},{5,7},{6,4},{7,5},{8,10},{9,11},{10,... | collective-permute-start | bytes 3145736 | tf_op jit(solution)/shard_map/ppermute | solution.py:68
  284.3 44.2 %collective-permute-start.5 = (bf16[1024,512]{1,0:T(8,128)(2,1)}, bf16[1024,512]{1,0:T(8,128)(2,1)}, u32[]{:S(2)}, u32[]{:S(2)}) collective-permute-start(bf16[1024,512]{1,0:T(8,128)(2,1)} %multiply_convert_fusion.8.refs_0_), channel_id=1, source_target_pairs={{0,3},{1,2},{2,1},{3,0},{4,7},{5,6},{6,5},{7,4},{8,11},{9,10},{10,... | collective-permute-start | bytes 3145736 | tf_op jit(solution)/shard_map/ppermute | solution.py:68
  365.2 134.5 %all-to-all-start.4 = ((bf16[4,4,352,256]{3,2,1,0:T(8,128)(2,1)}), bf16[4,4,352,256]{3,2,1,0:T(8,128)(2,1)}, u32[]{:S(2)}, u32[]{:S(2)}) async-start(bf16[4,4,352,256]{3,2,1,0:T(8,128)(2,1)} %copy.310), calls=%async_computation.5 | async-start | bytes 5767168 | tf_op jit(solution)/shard_map/all_to_all | solution.py:428
  376.2 165.6 %copy-start.80 = (s32[4,4,1024]{2,1,0:T(4,128)}, s32[4,4,1024]{2,1,0:T(4,128)S(1)}, u32[]{:S(2)}) copy-start(s32[4,4,1024]{2,1,0:T(4,128)S(1)} %fusion.44) | copy-start | bytes 196612
  499.7 97.9 %all-to-all-start.3 = ((bf16[4,2048,512]{2,1,0:T(8,128)(2,1)}), bf16[4,2048,512]{2,1,0:T(8,128)(2,1)}, u32[]{:S(2)}, u32[]{:S(2)}) async-start(bf16[4,2048,512]{2,1,0:T(8,128)(2,1)} %bitcast.389), calls=%async_computation.4 | async-start | bytes 16777216 | tf_op jit(solution)/shard_map/all_to_all | solution.py:425
  505.8 212.5 %all-gather.18.cloned.1.call-start = ((), (), s32[]{:S(2)}) async-start(), calls=%async_computation.27 | async-start | bytes 9732096 | tf_op jit(solution)/shard_map/all_gather | solution.py:617
  529.3 11.8 collective-permute-start.6
  529.4 12.5 collective-permute-start.8
  529.9 13.4 collective-permute-start.7
  535.0 25.4 %collective-permute-start.9 = (f32[8,128]{1,0:T(8,128)S(1)}, f32[8,128]{1,0:T(8,128)S(1)}, u32[]{:S(2)}, u32[]{:S(2)}) collective-permute-start(f32[8,128]{1,0:T(8,128)S(1)} %get-tuple-element.273), channel_id=1, source_target_pairs={{0,24},{4,28},{8,16},{12,20},{16,8},{20,12},{24,0},{28,4},{1,25},{... | collective-permute-start | bytes 12296 | tf_op jit(solution)/shard_map/ppermute | solution.py:73
  536.9 23.6 %collective-permute-start.10 = (f32[8,128]{1,0:T(8,128)S(1)}, f32[8,128]{1,0:T(8,128)S(1)}, u32[]{:S(2)}, u32[]{:S(2)}) collective-permute-start(f32[8,128]{1,0:T(8,128)S(1)} %get-tuple-element.272), channel_id=1, source_target_pairs={{0,16},{4,20},{8,24},{12,28},{16,0},{20,4},{24,8},{28,12},{1,17},{... | collective-permute-start | bytes 12296 | tf_op jit(solution)/shard_map/ppermute | solution.py:73
  541.1 19.3 %collective-permute-start.11 = (f32[8,128]{1,0:T(8,128)S(1)}, f32[8,128]{1,0:T(8,128)S(1)}, u32[]{:S(2)}, u32[]{:S(2)}) collective-permute-start(f32[8,128]{1,0:T(8,128)S(1)} %get-tuple-element.271), channel_id=1, source_target_pairs={{0,8},{4,12},{8,0},{12,4},{16,24},{20,28},{24,16},{28,20},{1,9},{5... | collective-permute-start | bytes 12296 | tf_op jit(solution)/shard_map/ppermute | solution.py:73
  609.1 97.8 %all-to-all-start.5 = ((bf16[4,2048,512]{2,1,0:T(8,128)(2,1)}), bf16[4,2048,512]{2,1,0:T(8,128)(2,1)}, u32[]{:S(2)}, u32[]{:S(2)}) async-start(bf16[4,2048,512]{2,1,0:T(8,128)(2,1)} %bitcast.390), calls=%async_computation.6 | async-start | bytes 16777216 | tf_op jit(solution)/shard_map/all_to_all | solution.py:425
  761.7 98.0 %all-to-all-start.6 = ((bf16[4,2048,512]{2,1,0:T(8,128)(2,1)}), bf16[4,2048,512]{2,1,0:T(8,128)(2,1)}, u32[]{:S(2)}, u32[]{:S(2)}) async-start(bf16[4,2048,512]{2,1,0:T(8,128)(2,1)} %bitcast.391), calls=%async_computation.7 | async-start | bytes 16777216 | tf_op jit(solution)/shard_map/all_to_all | solution.py:425
  768.0 181.9 %reduce-scatter.8.cloned.1.call-start = ((), (), s32[]{:S(2)}) async-start(), calls=%async_computation.19 | async-start | bytes 5242880 | tf_op jit(solution)/shard_map/reduce_scatter | solution.py:412
  769.5 80.5 %collective-permute-start.14 = (f32[8,128]{1,0:T(8,128)S(1)}, f32[8,128]{1,0:T(8,128)S(1)}, u32[]{:S(2)}, u32[]{:S(2)}) collective-permute-start(f32[8,128]{1,0:T(8,128)S(1)} %get-tuple-element.277), channel_id=1, source_target_pairs={{0,24},{4,28},{8,16},{12,20},{16,8},{20,12},{24,0},{28,4},{1,25},{... | collective-permute-start | bytes 12296 | tf_op jit(solution)/shard_map/ppermute | solution.py:73
  770.3 79.7 %collective-permute-start.13 = (f32[8,128]{1,0:T(8,128)S(1)}, f32[8,128]{1,0:T(8,128)S(1)}, u32[]{:S(2)}, u32[]{:S(2)}) collective-permute-start(f32[8,128]{1,0:T(8,128)S(1)} %get-tuple-element.278), channel_id=1, source_target_pairs={{0,16},{4,20},{8,24},{12,28},{16,0},{20,4},{24,8},{28,12},{1,17},{... | collective-permute-start | bytes 12296 | tf_op jit(solution)/shard_map/ppermute | solution.py:73
  774.6 75.5 %collective-permute-start.12 = (f32[8,128]{1,0:T(8,128)S(1)}, f32[8,128]{1,0:T(8,128)S(1)}, u32[]{:S(2)}, u32[]{:S(2)}) collective-permute-start(f32[8,128]{1,0:T(8,128)S(1)} %get-tuple-element.279), channel_id=1, source_target_pairs={{0,8},{4,12},{8,0},{12,4},{16,24},{20,28},{24,16},{28,20},{1,9},{5... | collective-permute-start | bytes 12296 | tf_op jit(solution)/shard_map/ppermute | solution.py:73
  850.0 30.1 %collective-permute-start.17 = (f32[4,8,128]{2,1,0:T(8,128)S(1)}, f32[4,8,128]{2,1,0:T(8,128)S(1)}, u32[]{:S(2)}, u32[]{:S(2)}) collective-permute-start(f32[4,8,128]{2,1,0:T(8,128)S(1)} %get-tuple-element.275), channel_id=1, source_target_pairs={{0,3},{1,2},{2,1},{3,0},{4,7},{5,6},{6,5},{7,4},{8,11},{9,10},{10,... | collective-permute-start | bytes 49160 | tf_op jit(solution)/shard_map/ppermute | solution.py:68
  851.6 28.6 %collective-permute-start.16 = (f32[4,8,128]{2,1,0:T(8,128)S(1)}, f32[4,8,128]{2,1,0:T(8,128)S(1)}, u32[]{:S(2)}, u32[]{:S(2)}) collective-permute-start(f32[4,8,128]{2,1,0:T(8,128)S(1)} %get-tuple-element.275), channel_id=1, source_target_pairs={{0,2},{1,3},{2,0},{3,1},{4,6},{5,7},{6,4},{7,5},{8,10},{9,11},{10,... | collective-permute-start | bytes 49160 | tf_op jit(solution)/shard_map/ppermute | solution.py:68
  851.7 28.5 %collective-permute-start.15 = (f32[4,8,128]{2,1,0:T(8,128)S(1)}, f32[4,8,128]{2,1,0:T(8,128)S(1)}, u32[]{:S(2)}, u32[]{:S(2)}) collective-permute-start(f32[4,8,128]{2,1,0:T(8,128)S(1)} %get-tuple-element.275), channel_id=1, source_target_pairs={{0,1},{1,0},{2,3},{3,2},{4,5},{5,4},{6,7},{7,6},{8,9},{9,8},{10,11... | collective-permute-start | bytes 49160 | tf_op jit(solution)/shard_map/ppermute | solution.py:68
  888.5 97.3 %all-to-all-start.7 = ((bf16[4,2048,512]{2,1,0:T(8,128)(2,1)}), bf16[4,2048,512]{2,1,0:T(8,128)(2,1)}, u32[]{:S(2)}, u32[]{:S(2)}) async-start(bf16[4,2048,512]{2,1,0:T(8,128)(2,1)} %bitcast.392), calls=%async_computation.8 | async-start | bytes 16777216 | tf_op jit(solution)/shard_map/all_to_all | solution.py:425
  894.6 223.3 %reduce-scatter.10.cloned.1.call-start = ((), (), s32[]{:S(2)}) async-start(), calls=%async_computation.20 | async-start | bytes 5242880 | tf_op jit(solution)/shard_map/reduce_scatter | solution.py:412
  1012.8 98.0 %all-to-all-start.8 = ((bf16[4,2048,512]{2,1,0:T(8,128)(2,1)}), bf16[4,2048,512]{2,1,0:T(8,128)(2,1)}, u32[]{:S(2)}, u32[]{:S(2)}) async-start(bf16[4,2048,512]{2,1,0:T(8,128)(2,1)} %maximum_bitcast_fusion.2), calls=%async_computation.10 | async-start | bytes 16777216 | tf_op jit(solution)/shard_map/all_to_all | solution.py:425
  1019.0 184.0 %all-gather.10.cloned.1.call-start = ((), (), s32[]{:S(2)}) async-start(), calls=%async_computation.21 | async-start | bytes 5242880 | tf_op jit(solution)/shard_map/all_gather | solution.py:417
  1031.0 5.3 collective-permute-start.18
  1031.1 9.4 collective-permute-start.19
  1031.6 13.0 collective-permute-start.20
  1047.1 72.5 %copy-start.20 = (bf16[1024,512]{1,0:T(8,128)(2,1)S(1)}, bf16[1024,512]{1,0:T(8,128)(2,1)}, u32[]{:S(2)}) copy-start(bf16[1024,512]{1,0:T(8,128)(2,1)} %reduce-scatter.6.cloned.1.call-done) | copy-start | bytes 3145732
  1047.1 72.5 %copy-start.66 = (f32[1024]{0:T(1024)S(1)}, f32[1024]{0:T(1024)}, u32[]{:S(2)}) copy-start(f32[1024]{0:T(1024)} %copy-done.65) | copy-start | bytes 12292
  1047.1 72.6 %copy-start.70 = (f32[512]{0:T(512)S(1)}, f32[512]{0:T(512)}, u32[]{:S(2)}) copy-start(f32[512]{0:T(512)} %copy-done.69) | copy-start | bytes 6148
  1138.4 64.7 %all-to-all-start.9 = ((bf16[4,4,352,256]{3,2,1,0:T(8,128)(2,1)}), bf16[4,4,352,256]{3,2,1,0:T(8,128)(2,1)S(1)}, u32[]{:S(2)}, u32[]{:S(2)}) async-start(bf16[4,4,352,256]{3,2,1,0:T(8,128)(2,1)} %bitcast.399), calls=%async_computation.12 | async-start | bytes 5767168 | tf_op jit(solution)/shard_map/all_to_all | solution.py:428
  1143.9 460.5 %reduce-scatter.14.cloned.1.call-start = ((), (), s32[]{:S(2)}) async-start(), calls=%async_computation.23 | async-start | bytes 9732096 | tf_op jit(solution)/shard_map/reduce_scatter | solution.py:775
  1204.7 120.1 %all-to-all-start.10 = ((bf16[4,4,352,256]{3,2,1,0:T(8,128)(2,1)}), bf16[4,4,352,256]{3,2,1,0:T(8,128)(2,1)}, u32[]{:S(2)}, u32[]{:S(2)}) async-start(bf16[4,4,352,256]{3,2,1,0:T(8,128)(2,1)} %bitcast.398), calls=%async_computation.13 | async-start | bytes 5767168 | tf_op jit(solution)/shard_map/all_to_all | solution.py:428
  1217.3 30.3 %collective-permute-start.21 = (bf16[1024,512]{1,0:T(8,128)(2,1)}, bf16[1024,512]{1,0:T(8,128)(2,1)}, u32[]{:S(2)}, u32[]{:S(2)}) collective-permute-start(bf16[1024,512]{1,0:T(8,128)(2,1)} %get-tuple-element.122.refs_0_), channel_id=1, source_target_pairs={{0,1},{1,0},{2,3},{3,2},{4,5},{5,4},{6,7},{7,6},{8,9},{9,8},{10,11... | collective-permute-start | bytes 3145736 | tf_op jit(solution)/shard_map/ppermute | solution.py:68
  1218.3 46.1 %collective-permute-start.22 = (bf16[1024,512]{1,0:T(8,128)(2,1)}, bf16[1024,512]{1,0:T(8,128)(2,1)}, u32[]{:S(2)}, u32[]{:S(2)}) collective-permute-start(bf16[1024,512]{1,0:T(8,128)(2,1)} %get-tuple-element.122.refs_0_), channel_id=1, source_target_pairs={{0,2},{1,3},{2,0},{3,1},{4,6},{5,7},{6,4},{7,5},{8,10},{9,11},{10,... | collective-permute-start | bytes 3145736 | tf_op jit(solution)/shard_map/ppermute | solution.py:68
  1219.5 44.9 %collective-permute-start.23 = (bf16[1024,512]{1,0:T(8,128)(2,1)}, bf16[1024,512]{1,0:T(8,128)(2,1)}, u32[]{:S(2)}, u32[]{:S(2)}) collective-permute-start(bf16[1024,512]{1,0:T(8,128)(2,1)} %get-tuple-element.122.refs_0_), channel_id=1, source_target_pairs={{0,3},{1,2},{2,1},{3,0},{4,7},{5,6},{6,5},{7,4},{8,11},{9,10},{10,... | collective-permute-start | bytes 3145736 | tf_op jit(solution)/shard_map/ppermute | solution.py:68
  1272.1 62.7 %copy-start.49 = (bf16[1024,512]{0,1:T(8,128)(2,1)}, bf16[1024,512]{0,1:T(8,128)(2,1)S(1)}, u32[]{:S(2)}) copy-start(bf16[1024,512]{0,1:T(8,128)(2,1)S(1)} %multiply_convert_fusion.7) | copy-start | bytes 3145732
  1324.8 89.5 %all-to-all-start.11 = ((bf16[4,4,352,256]{3,2,1,0:T(8,128)(2,1)}), bf16[4,4,352,256]{3,2,1,0:T(8,128)(2,1)}, u32[]{:S(2)}, u32[]{:S(2)}) async-start(bf16[4,4,352,256]{3,2,1,0:T(8,128)(2,1)} %bitcast.397), calls=%async_computation.14 | async-start | bytes 5767168 | tf_op jit(solution)/shard_map/all_to_all | solution.py:428
  1333.7 275.3 %reduce-scatter.12.cloned.1.call-start = ((), (), s32[]{:S(2)}) async-start(), calls=%async_computation.22 | async-start | bytes 9879552 | tf_op jit(solution)/shard_map/reduce_scatter | solution.py:775
  1347.3 27.3 %collective-permute-start.26 = (bf16[1024,512]{1,0:T(8,128)(2,1)}, bf16[1024,512]{1,0:T(8,128)(2,1)}, u32[]{:S(2)}, u32[]{:S(2)}) collective-permute-start(bf16[1024,512]{1,0:T(8,128)(2,1)} %get-tuple-element.247), channel_id=1, source_target_pairs={{0,3},{1,2},{2,1},{3,0},{4,7},{5,6},{6,5},{7,4},{8,11},{9,10},{10,... | collective-permute-start | bytes 3145736 | tf_op jit(solution)/shard_map/ppermute | solution.py:68
  1348.8 46.2 %collective-permute-start.25 = (bf16[1024,512]{1,0:T(8,128)(2,1)}, bf16[1024,512]{1,0:T(8,128)(2,1)}, u32[]{:S(2)}, u32[]{:S(2)}) collective-permute-start(bf16[1024,512]{1,0:T(8,128)(2,1)} %get-tuple-element.248), channel_id=1, source_target_pairs={{0,2},{1,3},{2,0},{3,1},{4,6},{5,7},{6,4},{7,5},{8,10},{9,11},{10,... | collective-permute-start | bytes 3145736 | tf_op jit(solution)/shard_map/ppermute | solution.py:68
  1349.4 45.6 %collective-permute-start.24 = (bf16[1024,512]{1,0:T(8,128)(2,1)}, bf16[1024,512]{1,0:T(8,128)(2,1)}, u32[]{:S(2)}, u32[]{:S(2)}) collective-permute-start(bf16[1024,512]{1,0:T(8,128)(2,1)} %get-tuple-element.246), channel_id=1, source_target_pairs={{0,1},{1,0},{2,3},{3,2},{4,5},{5,4},{6,7},{7,6},{8,9},{9,8},{10,11... | collective-permute-start | bytes 3145736 | tf_op jit(solution)/shard_map/ppermute | solution.py:68
  1431.1 159.5 %all-to-all-start.12 = ((bf16[4,3,4,352,256]{4,3,2,1,0:T(8,128)(2,1)}), bf16[4,3,4,352,256]{4,3,2,1,0:T(8,128)(2,1)}, u32[]{:S(2)}, u32[]{:S(2)}) async-start(bf16[4,3,4,352,256]{4,3,2,1,0:T(8,128)(2,1)} %maximum_bitcast_fusion.1), calls=%async_computation.16 | async-start | bytes 17301504 | tf_op jit(solution)/shard_map/all_to_all | solution.py:425
  1537.9 26.3 %collective-permute-start.27 = (bf16[1024,512]{1,0:T(8,128)(2,1)}, bf16[1024,512]{1,0:T(8,128)(2,1)S(1)}, u32[]{:S(2)}, u32[]{:S(2)}) collective-permute-start(bf16[1024,512]{1,0:T(8,128)(2,1)} %fusion.34.refs_0_), channel_id=1, source_target_pairs={{0,1},{1,0},{2,3},{3,2},{4,5},{5,4},{6,7},{7,6},{8,9},{9,8},{10,11... | collective-permute-start | bytes 3145736 | tf_op jit(solution)/shard_map/ppermute | solution.py:68
  1538.4 45.1 %collective-permute-start.28 = (bf16[1024,512]{1,0:T(8,128)(2,1)}, bf16[1024,512]{1,0:T(8,128)(2,1)S(1)}, u32[]{:S(2)}, u32[]{:S(2)}) collective-permute-start(bf16[1024,512]{1,0:T(8,128)(2,1)} %fusion.34.refs_0_), channel_id=1, source_target_pairs={{0,2},{1,3},{2,0},{3,1},{4,6},{5,7},{6,4},{7,5},{8,10},{9,11},{10,... | collective-permute-start | bytes 3145736 | tf_op jit(solution)/shard_map/ppermute | solution.py:68
  1539.9 43.5 %collective-permute-start.29 = (bf16[1024,512]{1,0:T(8,128)(2,1)}, bf16[1024,512]{1,0:T(8,128)(2,1)}, u32[]{:S(2)}, u32[]{:S(2)}) collective-permute-start(bf16[1024,512]{1,0:T(8,128)(2,1)} %fusion.34.refs_0_), channel_id=1, source_target_pairs={{0,3},{1,2},{2,1},{3,0},{4,7},{5,6},{6,5},{7,4},{8,11},{9,10},{10,... | collective-permute-start | bytes 3145736 | tf_op jit(solution)/shard_map/ppermute | solution.py:68
  1610.5 11.8 collective-permute-start.32
  1611.9 10.5 collective-permute-start.31
  1612.2 10.3 collective-permute-start.30
  (87 other events, 660.8 us)
Sparse Core Ops, SparseCore 0:
  19.6 86.0 all-gather.11
  211.9 52.5 reduce-scatter.5
  282.2 79.3 all-gather.13
  363.1 139.3 all-gather.15
  529.5 83.8 all-gather.17
  872.1 77.6 reduce-scatter.7
  998.0 77.4 reduce-scatter.9
  1138.5 53.7 all-gather.9
  1203.2 203.0 reduce-scatter.13
  1422.4 91.4 reduce-scatter.11

commit v6 on v5

--- a/solution.py
+++ b/solution.py
@@ -80,40 +80,37 @@
 
 def lay_out_weights(lay, ids, stacks, f_loc, d_loc, width):
     ffe = f_loc * lay.t
+    count = len(stacks) // lay.q
 
     def kernel(ids_ref, *refs):
-        sources, (in_ref, out_ref) = refs[: 3 * lay.q], refs[3 * lay.q :]
         for kc in range(lay.q):
             columns = pl.ds(pl.multiple_of((ids_ref[1] ^ kc) * d_loc, 128), d_loc)
-            for g in range(2):
-                in_ref[g, :, columns] = sources[3 * kc + g][0]
-            out_ref[:, columns] = sources[3 * kc + 2][0]
-
-    own_in, own_out = pl.pallas_call(
+            for g in range(count):
+                refs[-1][g, :, columns] = refs[count * kc + g][0]
+
+    own = pl.pallas_call(
         kernel,
-        out_shape=(
-            jax.ShapeDtypeStruct((2, ffe, width), BF16),
-            jax.ShapeDtypeStruct((ffe, width), BF16),
-        ),
+        out_shape=jax.ShapeDtypeStruct((count, ffe, width), BF16),
         grid_spec=pltpu.PrefetchScalarGridSpec(
             num_scalar_prefetch=1,
             grid=(lay.t, lay.z),
             in_specs=[
-                pl.BlockSpec((1, f_loc, d_loc), lambda kt, kz, ids: (kz * lay.t + kt, 0, 0))
+                pl.BlockSpec(
+                    (1, f_loc, d_loc), lambda kt, kz, ids: ((kz ^ ids[0]) * lay.t + kt, 0, 0)
+                )
             ]
-            * (3 * lay.q),
-            out_specs=(
-                pl.BlockSpec((2, f_loc, lay.q * d_loc), lambda kt, kz, ids: (0, kt, kz)),
-                pl.BlockSpec((f_loc, lay.q * d_loc), lambda kt, kz, ids: (kt, kz)),
+            * len(stacks),
+            out_specs=pl.BlockSpec(
+                (count, f_loc, lay.q * d_loc), lambda kt, kz, ids: (0, kt, kz)
             ),
         ),
         cost_estimate=pl.CostEstimate(
-            flops=0, bytes_accessed=12 * ffe * width, transcendentals=0
+            flops=0, bytes_accessed=4 * count * ffe * width, transcendentals=0
         ),
         compiler_params=pltpu.CompilerParams(vmem_limit_bytes=32 << 20),
         name="lay_out_weights",
     )(ids, *stacks)
-    return own_in.reshape(2 * ffe, width), own_out
+    return own.reshape(count * ffe, width)
 
 
 def take_apart(lay, ids, grad_in, grad_out, f_loc, d_loc, width):
@@ -565,7 +562,7 @@
     latent_all = dot_nt(normed_low, down_t)
     latent_all, by_column = lax.optimization_barrier((latent_all, by_column))
     by_column = jnp.transpose(by_column, (2, 1, 0, 3, 4))
-    by_plane = [swap_z(by_column[g]) for g in range(3)]
+    by_plane = [swap_z(by_column[g]) for g in range(2)]
     latent = latent_all[:, :LATENT]
     kv_inverse = inverse_rms(latent)
     latent_hat = latent * kv_inverse
@@ -608,22 +605,29 @@
     ffn_all, ffn_low, cot_ready = lax.optimization_barrier((ffn_all, ffn_low, cot_part))
     picked = pick_rows(ffn_all)
     expert_rows = send_out(picked)
-    cot_picked = pick_rows(gather_z(cot_ready))
     shared_pack = jnp.concatenate(
         [jnp.swapaxes(w_shared_in, 1, 2).reshape(-1, d_loc), w_shared_out], 0
     )
-    cot_picked, shared_pack = lax.optimization_barrier((cot_picked, shared_pack))
+    cot_all, last_column = lax.optimization_barrier((gather_z(cot_ready), by_column[2]))
+    by_plane.append(
+        jnp.stack(
+            [
+                lay.over_z(lax.dynamic_index_in_dim(last_column, me_z ^ k, 0, keepdims=False), k)
+                for k in range(nz)
+            ]
+        )
+    )
+    cot_picked, shared_pack = lax.optimization_barrier((pick_rows(cot_all), shared_pack))
     cot_rows = send_out(cot_picked)
     shared_all = lax.all_gather(shared_pack, "dp", axis=0, tiled=False)
-    pieces = [plane.reshape(nz * nt, f_loc, d_loc) for plane in by_plane]
-    own_in, own_out = lay_out_weights(
-        lay,
-        ids,
-        [lay.over_c(pieces[g], k) for k in range(nq) for g in range(3)],
-        f_loc,
-        d_loc,
-        width,
-    )
+
+    def own_weights(matrices, order):
+        pieces = [by_plane[g].reshape(nz * nt, f_loc, d_loc) for g in matrices]
+        stacks = [lay.over_c(piece, k) for k in range(nq) for piece in pieces]
+        return lay_out_weights(lay, order, stacks, f_loc, d_loc, width)
+
+    own_in = own_weights((0, 1), ids * jnp.array([0, 1, 1], jnp.int32))
+    own_out = own_weights((2,), ids)
     router_probs = jax.nn.softmax(dot_nt(ffn_low, router_t), axis=-1)
     probs_turned = jnp.transpose(router_probs).reshape(EXPERTS, -1, 128)
     own_probs = in_order(
@@ -729,10 +733,10 @@
             shared_grad_full,
         )
     )
-    shared_both = jnp.concatenate([shared_grad_full, shared_full], 0).astype(BF16)
-    shared_both = swap_t(jnp.swapaxes(shared_both.reshape(2 * rows, nt, part), 0, 1))
-    shared_both = jnp.sum(shared_both.astype(F32), axis=0)
-    shared_grad, shared_part = shared_both[:rows], shared_both[rows:]
+    shared_grad = swap_t(
+        jnp.swapaxes(shared_grad_full.astype(BF16).reshape(rows, nt, part), 0, 1)
+    )
+    shared_grad = jnp.sum(shared_grad.astype(F32), axis=0)
     grad_pieces = take_apart(lay, ids, grad_in_own, grad_out_own, f_loc, d_loc, width)
     routed_grad = scatter_z(combine(grad_parts)).astype(F32)
     grad_class = [
@@ -795,11 +799,9 @@
         heads,
         score_scale,
     )
-    output_part = lax.optimization_barrier((residual + routed + shared_part).astype(BF16))
-    query_turned_grad, output_parts = lax.optimization_barrier(
-        (query_turned_grad, [lay.over_t(output_part, k) for k in range(nt)])
-    )
-    output = join_columns(output_parts, me_t, nt)
+    query_turned_grad, grad_plane[1], shared_full = lax.optimization_barrier(
+        (query_turned_grad, grad_plane[1], shared_full)
+    )
     turned_first, turned_second = rotate_back(
         query_turned_grad[:, : heads * half], query_turned_grad[:, heads * half :], wide_cos, wide_sin
     )
@@ -820,20 +822,23 @@
         scaled_kv - latent_hat * jnp.mean(latent_hat * scaled_kv, axis=-1, keepdims=True)
     )
     down_grad = jnp.concatenate([latent_back, key_rope_part], -1).astype(BF16)
-    normed_full, grad_plane[1] = lax.optimization_barrier(
-        (dot(query_grad, query_t) + dot(down_grad, down_t), grad_plane[1])
-    )
-    normed_grad = scatter_t_direct(normed_full)
-    normed_grad, grad_plane[2] = lax.optimization_barrier((normed_grad, grad_plane[2]))
-    grad_home = swap_t(jnp.transpose(jnp.stack(grad_plane), (2, 0, 1, 3, 4)))
+    normed_full, shared_part = lax.optimization_barrier(
+        (dot(query_grad, query_t) + dot(down_grad, down_t), scatter_t_direct(shared_full))
+    )
+    output = gather_t_direct((residual + routed + shared_part).astype(BF16))
+    normed_grad, shared_sum, grad_plane[2] = lax.optimization_barrier(
+        (scatter_t_direct(normed_full), shared_sum, grad_plane[2])
+    )
     attn_hat = own_part(hidden).astype(F32) * attn_inverse
     scaled_in = lax.dynamic_slice_in_dim(attn_scale, me_t * part, part, 0) * normed_grad
     attn_gain_part = jnp.sum(normed_grad * attn_hat, axis=0)
     input_grad = residual_grad + attn_inverse * (
         scaled_in - attn_hat * row_mean(attn_hat * scaled_in)
     )
+    input_low, grad_plane = lax.optimization_barrier((input_grad.astype(BF16), grad_plane))
+    grad_home = swap_t(jnp.transpose(jnp.stack(grad_plane), (2, 0, 1, 3, 4)))
     grad_expert_in, grad_expert_out = home_gradients(lay, grad_home, f_loc, d_loc)
-    grad_hidden = gather_t_direct(input_grad.astype(BF16))
+    grad_hidden = gather_t_direct(input_low)
 
     def spread(values):
         return lax.dynamic_update_slice(

time: 1650 us -> 1690 us (1.024)
  waiting for transfers between devices: 640 us -> 764 us
  blocking collectives: 113 us -> 24 us
    ppermute x18 -> x21, waiting for transfers between devices: 111 us -> 278 us  [over_t(): return lax.ppermute(values, 'tensor', [(i, i ^ k) for i in range(self.t)])]
    all_to_all x7, waiting for transfers between devices: 186 us -> 86.5 us  [swap_t(): lax.all_to_all(values, 'tensor', split_axis=0, concat_axis=0, tiled=True)]
    ppermute x9 -> x12, waiting for transfers between devices: 1.48 us -> 96.5 us  [over_z(): lax.ppermute(values, 'dp', [(d, d ^ k * self.q) for d in range(self.dp)])]
    psum x3, blocking collectives: 113 us -> 24 us  [row_mean(): return lax.psum(partial, 'tensor').reshape(-1, 1) * (1.0 / width)]
    all_to_all x6 -> x5, waiting for transfers between devices: 204 us -> 122 us  [swap_z(): lax.all_to_all(values, 'dp', split_axis=0, concat_axis=0, axis_index_grou...]
    all_gather x2, waiting for transfers between devices: 26.9 us -> 74 us  [gather_z(): lax.all_gather(values, 'dp', axis=0, tiled=False, axis_index_groups=lay.z...]
    all_to_all x6 -> x5, starting transfers between devices: 41.6 us -> 35.3 us  [swap_z(): lax.all_to_all(values, 'dp', split_axis=0, concat_axis=0, axis_index_grou...]
    unnamed x214 -> x246, local copies, waits for them, and re-layouts: 50.3 us -> 45.9 us
  transfers between devices with their start and end apart: 56 -> 61, of which waited for: 29 -> 31; matrix products, arithmetic and copies ran while one was open for 32% -> 30% of each run, Pallas kernels for 6% -> 6%
where the time goes in v6:
time: 1690 us; the launch traced here: 1670 us
  waiting for transfers between devices  764 us (45%)
  matrix products  327 us (19%)
  local copies, waits for them, and re-layouts  192 us (11%)
  starting transfers between devices  130 us (8%)
  other arithmetic  112 us (7%)
  Pallas kernels  107 us (6%)
  blocking collectives  24 us (1%)
  between operations  17.1 us (1%)
    ppermute x21, waiting for transfers between devices, over_t(): return lax.ppermute(values, 'tensor', [(i, i ^ k) for i in range(self.t)])  278 us
    all_to_all x5, waiting for transfers between devices, swap_z(): lax.all_to_all(values, 'dp', split_axis=0, concat_axis=0, axis_index_grou...  122 us
    dot_general x9, matrix products, dot_nt(): lax.dot_general(a, b, (((1,), (1,)), ((), ())), preferred_element_type=F32)  103 us
    ppermute x12, waiting for transfers between devices, over_z(): lax.ppermute(values, 'dp', [(d, d ^ k * self.q) for d in range(self.dp)])  96.5 us
    all_to_all x7, waiting for transfers between devices, swap_t(): lax.all_to_all(values, 'tensor', split_axis=0, concat_axis=0, tiled=True)  86.5 us
    dot_general x9, matrix products, dot(): return jnp.dot(a, b, preferred_element_type=F32)  79.8 us
    dot_general x8, matrix products, dot_tn(): lax.dot_general(a, b, (((0,), (0,)), ((), ())), preferred_element_type=F32)  79.1 us
    all_gather x2, waiting for transfers between devices, gather_z(): lax.all_gather(values, 'dp', axis=0, tiled=False, axis_index_groups=lay.z...  74 us
  transfers between devices with their start and end apart: 61, of which 31 were waited for; matrix products, arithmetic and copies ran while one was open for 30% of the time, Pallas kernels for 6%

profile of v6, /device:TPU:10, one launch (start us, length us, event | category | flops | bytes accessed | tf_op | source)
XLA Modules:
  0.0 1672.1 jit_solution(4119426753570068442)
XLA Ops:
  20.2 6.9 maximum_bitcast_fusion
  27.1 8.3 copy.301
  35.4 6.5 all-to-all-start
  51.3 55.2 %all-gather.12.cloned.1.call-done = bf16[17152,256]{1,0:T(8,128)(2,1)} async-done(((bf16[2144,256]{1,0:T(8,128)(2,1)}), bf16[17152,256]{1,0:T(8,128)(2,1)}) %all-gather.12.cloned.1.call-update) | async-done | bytes 8781840 | tf_op jit(solution)/shard_map/all_gather | solution.py:486
  117.2 19.4 %all-to-all-done = bf16[4,4,3,352,256]{4,3,1,2,0:T(8,128)(2,1)} async-done(((bf16[4,4,3,352,256]{4,3,1,2,0:T(8,128)(2,1)}), bf16[4,4,3,352,256]{4,3,1,2,0:T(8,128)(2,1)}, u32[]{:S(2)}, u32[]{:S(2)}) %all-to-all-start) | async-done | bytes 8650784 | tf_op jit(solution)/shard_map/all_to_all | solution.py:422
  162.5 6.4 fusion.118
  190.7 14.6 attend.1
  221.7 43.0 %reduce-scatter.6.cloned.1.call-done = bf16[1024,512]{1,0:T(8,128)(2,1)} async-done(((bf16[1024,2048]{1,0:T(8,128)(2,1)}), bf16[1024,512]{1,0:T(8,128)(2,1)}) %reduce-scatter.6.cloned.1.call-update) | async-done | bytes 1048592 | tf_op jit(solution)/shard_map/reduce_scatter | solution.py:417
  266.7 8.1 psum.21
  292.4 17.2 %collective-permute-done.3.refs_1_ = bf16[1024,512]{1,0:T(8,128)(2,1)} collective-permute-done((bf16[1024,512]{1,0:T(8,128)(2,1)}, bf16[1024,512]{1,0:T(8,128)(2,1)}, u32[]{:S(2)}, u32[]{:S(2)}) %collective-permute-start.3) | collective-permute-done | bytes 1048608 | tf_op jit(solution)/shard_map/ppermute | solution.py:68
  309.7 20.0 %collective-permute-done.4.refs_2_ = bf16[1024,512]{1,0:T(8,128)(2,1)} collective-permute-done((bf16[1024,512]{1,0:T(8,128)(2,1)}, bf16[1024,512]{1,0:T(8,128)(2,1)}, u32[]{:S(2)}, u32[]{:S(2)}) %collective-permute-start.4) | collective-permute-done | bytes 1048608 | tf_op jit(solution)/shard_map/ppermute | solution.py:68
  335.8 26.5 %all-gather.14.cloned.1.call-done = bf16[4096,512]{1,0:T(8,128)(2,1)} async-done(((bf16[1024,512]{1,0:T(8,128)(2,1)}), bf16[4096,512]{1,0:T(8,128)(2,1)}) %all-gather.14.cloned.1.call-update) | async-done | bytes 4194320 | tf_op jit(solution)/shard_map/all_gather | solution.py:406
  363.1 16.2 convert_bitcast_fusion.1
  379.3 7.5 copy.306
  395.6 47.5 %all-gather.16.cloned.1.call-done = bf16[4096,512]{1,0:T(8,128)(2,1)} async-done(((bf16[1024,512]{1,0:T(8,128)(2,1)}), bf16[4096,512]{1,0:T(8,128)(2,1)}) %all-gather.16.cloned.1.call-update) | async-done | bytes 4194320 | tf_op jit(solution)/shard_map/all_gather | solution.py:406
  443.1 16.2 convert_bitcast_fusion
  459.3 7.4 copy.315
  468.3 14.1 lay_out_weights.2
  495.7 11.5 copy.307
  507.2 6.4 all-to-all-start.4
  513.7 63.1 %collective-permute-done.10 = bf16[4,352,256]{2,1,0:T(8,128)(2,1)S(1)} collective-permute-done((bf16[4,352,256]{2,1,0:T(8,128)(2,1)}, bf16[4,352,256]{2,1,0:T(8,128)(2,1)S(1)}, u32[]{:S(2)}, u32[]{:S(2)}) %collective-permute-start.10) | collective-permute-done | bytes 720928 | tf_op jit(solution)/shard_map/ppermute | solution.py:73
  576.7 31.9 %collective-permute-done.9 = bf16[4,352,256]{2,1,0:T(8,128)(2,1)} collective-permute-done((bf16[4,352,256]{2,1,0:T(8,128)(2,1)S(1)}, bf16[4,352,256]{2,1,0:T(8,128)(2,1)}, u32[]{:S(2)}, u32[]{:S(2)}) %collective-permute-start.9) | collective-permute-done | bytes 720928 | tf_op jit(solution)/shard_map/ppermute | solution.py:73
  610.4 32.2 %fusion.127 = f32[2048,2816]{1,0:T(8,128)} fusion(bf16[2048,2048]{0,1:T(8,128)(2,1)} %bitcast.432, bf16[2816,2048]{1,0:T(8,128)(2,1)} %bitcast.411), kind=kOutput, calls=%fused_computation.303 | convolution fusion | flops 23622320128 | bytes 42991616 | tf_op jit(solution)/shard_map/dot_general | solution.py:30
  642.6 12.3 fusion.8
  654.9 9.3 lay_out_weights.3
  666.8 15.1 multiply_convert_fusion
  681.9 11.6 copy.316
  702.7 29.5 %multiply_convert_fusion.2 = (bf16[2048,1408]{1,0:T(8,128)(2,1)}, bf16[2048,1408]{1,0:T(8,128)(2,1)}, f32[2048]{0:T(1024)S(1)}) fusion(f32[2048,2816]{1,0:T(8,128)} %fusion.127, f32[2048]{0:T(1024)S(1)} %bitcast.497, bf16[2048,1408]{1,0:T(8,128)(2,1)} %copy-done.35, bf16[2048,2048]{0,1:T(8,128)(2,1)} %bitcast.434, bf16[1,1408,2048]{2,1,0:T(8,128)(2,1)S(1)} %bitcast.404), kind=kOutput, calls=%fused_computation.16 | convolution fusion | flops 11860178944 | bytes 54542336 | tf_op jit(solution)/shard_map/dot_general | solution.py:30
  732.2 7.5 copy.401
  754.2 8.6 copy.322
  762.7 11.8 fusion.128
  776.8 7.8 multiply_convert_fusion.5
  784.6 10.3 fusion.42
  795.0 28.7 %convolution_convert_fusion.3 = bf16[2048,2048]{1,0:T(8,128)(2,1)} fusion(bf16[2816,2048]{1,0:T(8,128)(2,1)S(1)} %bitcast.414, bf16[2048,1408]{1,0:T(8,128)(2,1)} %get-tuple-element.244, bf16[2048,1408]{1,0:T(8,128)(2,1)} %get-tuple-element.243), kind=kOutput, calls=%fused_computation.43 | convolution fusion | flops 23649583104 | bytes 31457280 | tf_op jit(solution)/shard_map/dot_general | solution.py:26
  823.7 7.9 pad_maximum_fusion
  838.8 12.3 bitcast_convert_fusion.1
  851.1 7.1 fusion.129
  859.1 7.6 copy.400
  872.9 18.0 %convolution_convert_fusion.2.out_ref = bf16[1408,2048]{1,0:T(8,128)(2,1)} fusion(bf16[2048,1408]{1,0:T(8,128)(2,1)} %get-tuple-element.104, bf16[2048,2048]{0,1:T(8,128)(2,1)} %bitcast.435), kind=kOutput, calls=%fused_computation.42 | convolution fusion | flops 11814043648 | bytes 19922944 | tf_op jit(solution)/shard_map/dot_general | solution.py:34
  890.9 31.9 %convolution_convert_fusion = bf16[2816,2048]{1,0:T(8,128)(2,1)} fusion(bf16[2048,2816]{1,0:T(8,128)(2,1)} %pad_maximum_fusion, bf16[2048,2048]{0,1:T(8,128)(2,1)} %bitcast.433), kind=kOutput, calls=%fused_computation.20 | convolution fusion | flops 23628087296 | bytes 31457280 | tf_op jit(solution)/shard_map/dot_general | solution.py:34
  932.0 32.9 %all-to-all-done.6 = bf16[4,2048,512]{2,1,0:T(8,128)(2,1)} async-done(((bf16[4,2048,512]{2,1,0:T(8,128)(2,1)}), bf16[4,2048,512]{2,1,0:T(8,128)(2,1)}, u32[]{:S(2)}, u32[]{:S(2)}) %all-to-all-start.6) | async-done | bytes 8388640 | tf_op jit(solution)/shard_map/all_to_all | solution.py:422
  964.9 12.1 bitcast_convert_fusion
  977.1 15.0 take_apart.1
  1019.5 30.5 %all-to-all-done.7 = bf16[4,1024,512]{2,1,0:T(8,128)(2,1)} async-done(((bf16[4,1024,512]{2,1,0:T(8,128)(2,1)}), bf16[4,1024,512]{2,1,0:T(8,128)(2,1)}, u32[]{:S(2)}, u32[]{:S(2)}) %all-to-all-start.7) | async-done | bytes 4194336 | tf_op jit(solution)/shard_map/all_to_all | solution.py:422
  1059.9 8.0 psum.22
  1072.5 6.5 all-to-all-start.8
  1079.5 6.6 convolution_convert_fusion.5
  1088.7 7.2 convolution_convert_fusion.1
  1100.0 39.1 %all-to-all-done.8 = bf16[4,4,352,256]{3,2,1,0:T(8,128)(2,1)S(1)} async-done(((bf16[4,4,352,256]{3,2,1,0:T(8,128)(2,1)}), bf16[4,4,352,256]{3,2,1,0:T(8,128)(2,1)S(1)}, u32[]{:S(2)}, u32[]{:S(2)}) %all-to-all-start.8) | async-done | bytes 2883616 | tf_op jit(solution)/shard_map/all_to_all | solution.py:425
  1140.7 8.1 all-to-all-start.9
  1157.9 21.6 %attend_back.1 = (bf16[1024,512]{1,0:T(8,128)(2,1)S(1)}, f32[1024,256]{1,0:T(8,128)S(1)}, bf16[1024,1024]{1,0:T(8,128)(2,1)S(1)}, f32[1024,256]{1,0:T(8,128)S(1)}) custom-call(s32[1]{0:T(128)} %copy.425.len_ref, bf16[1024,512]{1,0:T(8,128)(2,1)S(1)} %copy-done.5, bf16[1024,256]{1,0:T(8,128)(2,1)S(1)} %copy-done.9, bf16[1024,1024]{1,0:T(8,128)(2,1)S(1)} %copy-done.11, ...), custom_call_target="tpu_custom_call" | custom-call | flops 6710886400 | bytes 33554432 | tf_op jit(solution)/shard_map/attend_back/pallas_call | solution.py:321
  1180.8 78.3 %all-to-all-done.9 = bf16[4,4,352,256]{3,2,1,0:T(8,128)(2,1)} async-done(((bf16[4,4,352,256]{3,2,1,0:T(8,128)(2,1)}), bf16[4,4,352,256]{3,2,1,0:T(8,128)(2,1)}, u32[]{:S(2)}, u32[]{:S(2)}) %all-to-all-start.9) | async-done | bytes 2883616 | tf_op jit(solution)/shard_map/all_to_all | solution.py:425
  1259.2 9.3 all-to-all-start.10
  1315.2 11.9 collective-permute-done.26
  1327.1 20.7 %collective-permute-done.25 = bf16[1024,512]{1,0:T(8,128)(2,1)} collective-permute-done((bf16[1024,512]{1,0:T(8,128)(2,1)}, bf16[1024,512]{1,0:T(8,128)(2,1)}, u32[]{:S(2)}, u32[]{:S(2)}) %collective-permute-start.25) | collective-permute-done | bytes 1048608 | tf_op jit(solution)/shard_map/ppermute | solution.py:68
  1363.0 16.6 collective-permute-done.32
  1379.6 21.1 %collective-permute-done.31 = bf16[1024,512]{1,0:T(8,128)(2,1)S(1)} collective-permute-done((bf16[1024,512]{1,0:T(8,128)(2,1)S(1)}, bf16[1024,512]{1,0:T(8,128)(2,1)S(1)}, u32[]{:S(2)}, u32[]{:S(2)}) %collective-permute-start.31) | collective-permute-done | bytes 1048608 | tf_op jit(solution)/shard_map/ppermute | solution.py:68
  1412.7 7.9 psum.23
  1435.1 8.3 all-to-all-start.11
  1448.9 111.6 %collective-permute-done.27.refs_1_ = bf16[1024,512]{1,0:T(8,128)(2,1)} collective-permute-done((bf16[1024,512]{1,0:T(8,128)(2,1)}, bf16[1024,512]{1,0:T(8,128)(2,1)}, u32[]{:S(2)}, u32[]{:S(2)}) %collective-permute-start.27) | collective-permute-done | bytes 1048608 | tf_op jit(solution)/shard_map/ppermute | solution.py:68
  1565.5 18.8 %collective-permute-done.28.refs_2_ = bf16[1024,512]{1,0:T(8,128)(2,1)} collective-permute-done((bf16[1024,512]{1,0:T(8,128)(2,1)}, bf16[1024,512]{1,0:T(8,128)(2,1)}, u32[]{:S(2)}, u32[]{:S(2)}) %collective-permute-start.28) | collective-permute-done | bytes 1048608 | tf_op jit(solution)/shard_map/ppermute | solution.py:68
  1590.7 14.9 collective-permute-done.33.refs_1_
  1606.8 19.1 %collective-permute-done.35.refs_3_ = bf16[1024,512]{1,0:T(8,128)(2,1)} collective-permute-done((bf16[1024,512]{1,0:T(8,128)(2,1)S(1)}, bf16[1024,512]{1,0:T(8,128)(2,1)}, u32[]{:S(2)}, u32[]{:S(2)}) %collective-permute-start.35) | collective-permute-done | bytes 1048608 | tf_op jit(solution)/shard_map/ppermute | solution.py:68
  1632.1 13.8 home_gradients.1
  (505 shorter events, 392.0 us)
Async XLA Ops:
  7.2 99.3 %all-gather.12.cloned.1.call-start = ((), (), s32[]{:S(2)}) async-start(), calls=%async_computation.23 | async-start | bytes 9879552 | tf_op jit(solution)/shard_map/all_gather | solution.py:486
  35.4 101.2 %all-to-all-start = ((bf16[4,4,3,352,256]{4,3,1,2,0:T(8,128)(2,1)}), bf16[4,4,3,352,256]{4,3,1,2,0:T(8,128)(2,1)}, u32[]{:S(2)}, u32[]{:S(2)}) async-start(bf16[4,4,3,352,256]{4,3,1,2,0:T(8,128)(2,1)} %copy.301), calls=%async_computation | async-start | bytes 17301504 | tf_op jit(solution)/shard_map/all_to_all | solution.py:422
  41.9 9.0 collective-permute-start
  43.5 7.4 collective-permute-start.1
  44.7 6.6 collective-permute-start.2
  49.7 112.8 %copy-start.75 = (f32[1024]{0:T(1024)}, f32[1024]{0:T(1024)S(1)}, u32[]{:S(2)}) copy-start(f32[1024]{0:T(1024)S(1)} %add_rsqrt_fusion.1) | copy-start | bytes 12292
  143.9 68.2 %all-to-all-start.1 = ((bf16[4,4,352,256]{3,2,1,0:T(8,128)(2,1)}), bf16[4,4,352,256]{3,2,1,0:T(8,128)(2,1)S(1)}, u32[]{:S(2)}, u32[]{:S(2)}) async-start(bf16[4,4,352,256]{3,2,1,0:T(8,128)(2,1)} %copy.303), calls=%async_computation.1 | async-start | bytes 5767168 | tf_op jit(solution)/shard_map/all_to_all | solution.py:425
  149.2 115.5 %reduce-scatter.6.cloned.1.call-start = ((), (), s32[]{:S(2)}) async-start(), calls=%async_computation.17 | async-start | bytes 5242880 | tf_op jit(solution)/shard_map/reduce_scatter | solution.py:417
  215.6 67.1 %all-to-all-start.2 = ((bf16[4,4,352,256]{3,2,1,0:T(8,128)(2,1)}), bf16[4,4,352,256]{3,2,1,0:T(8,128)(2,1)}, u32[]{:S(2)}, u32[]{:S(2)}) async-start(bf16[4,4,352,256]{3,2,1,0:T(8,128)(2,1)} %copy.304), calls=%async_computation.3 | async-start | bytes 5767168 | tf_op jit(solution)/shard_map/all_to_all | solution.py:425
  221.6 140.6 %all-gather.14.cloned.1.call-start = ((), (), s32[]{:S(2)}) async-start(), calls=%async_computation.24 | async-start | bytes 5242880 | tf_op jit(solution)/shard_map/all_gather | solution.py:406
  282.7 160.4 %all-gather.16.cloned.1.call-start = ((), (), s32[]{:S(2)}) async-start(), calls=%async_computation.25 | async-start | bytes 5242880 | tf_op jit(solution)/shard_map/all_gather | solution.py:406
  283.2 26.5 %collective-permute-start.3 = (bf16[1024,512]{1,0:T(8,128)(2,1)}, bf16[1024,512]{1,0:T(8,128)(2,1)}, u32[]{:S(2)}, u32[]{:S(2)}) collective-permute-start(bf16[1024,512]{1,0:T(8,128)(2,1)} %multiply_convert_fusion.8.refs_0_), channel_id=1, source_target_pairs={{0,1},{1,0},{2,3},{3,2},{4,5},{5,4},{6,7},{7,6},{8,9},{9,8},{10,11... | collective-permute-start | bytes 3145736 | tf_op jit(solution)/shard_map/ppermute | solution.py:68
  284.1 45.6 %collective-permute-start.4 = (bf16[1024,512]{1,0:T(8,128)(2,1)}, bf16[1024,512]{1,0:T(8,128)(2,1)}, u32[]{:S(2)}, u32[]{:S(2)}) collective-permute-start(bf16[1024,512]{1,0:T(8,128)(2,1)} %multiply_convert_fusion.8.refs_0_), channel_id=1, source_target_pairs={{0,2},{1,3},{2,0},{3,1},{4,6},{5,7},{6,4},{7,5},{8,10},{9,11},{10,... | collective-permute-start | bytes 3145736 | tf_op jit(solution)/shard_map/ppermute | solution.py:68
  285.4 44.3 %collective-permute-start.5 = (bf16[1024,512]{1,0:T(8,128)(2,1)}, bf16[1024,512]{1,0:T(8,128)(2,1)}, u32[]{:S(2)}, u32[]{:S(2)}) collective-permute-start(bf16[1024,512]{1,0:T(8,128)(2,1)} %multiply_convert_fusion.8.refs_0_), channel_id=1, source_target_pairs={{0,3},{1,2},{2,1},{3,0},{4,7},{5,6},{6,5},{7,4},{8,11},{9,10},{10,... | collective-permute-start | bytes 3145736 | tf_op jit(solution)/shard_map/ppermute | solution.py:68
  363.1 105.2 %copy-start.92 = (s32[4,4,1024]{2,1,0:T(4,128)}, s32[4,4,1024]{2,1,0:T(4,128)S(1)}, u32[]{:S(2)}) copy-start(s32[4,4,1024]{2,1,0:T(4,128)S(1)} %fusion.46) | copy-start | bytes 196612
  386.8 108.9 %all-to-all-start.3 = ((bf16[4,2048,512]{2,1,0:T(8,128)(2,1)}), bf16[4,2048,512]{2,1,0:T(8,128)(2,1)}, u32[]{:S(2)}, u32[]{:S(2)}) async-start(bf16[4,2048,512]{2,1,0:T(8,128)(2,1)} %bitcast.406), calls=%async_computation.4 | async-start | bytes 16777216 | tf_op jit(solution)/shard_map/all_to_all | solution.py:422
  392.9 300.5 %all-gather.18.cloned.1.call-start = ((), (), s32[]{:S(2)}) async-start(), calls=%async_computation.26 | async-start | bytes 9732096 | tf_op jit(solution)/shard_map/all_gather | solution.py:622
  395.1 73.3 %collective-permute-start.6 = (bf16[16,352,256]{2,1,0:T(8,128)(2,1)S(1)}, bf16[16,352,256]{2,1,0:T(8,128)(2,1)}, u32[]{:S(2)}, u32[]{:S(2)}) collective-permute-start(bf16[16,352,256]{2,1,0:T(8,128)(2,1)S(1)} %bitcast.399), channel_id=1, source_target_pairs={{0,4},{4,0},{8,12},{12,8},{16,20},{20,16},{24,28},{28,24},{1,5},{5... | collective-permute-start | bytes 8650760 | tf_op jit(solution)/shard_map/ppermute | solution.py:78
  395.1 73.3 %collective-permute-start.7 = (bf16[16,352,256]{2,1,0:T(8,128)(2,1)}, bf16[16,352,256]{2,1,0:T(8,128)(2,1)}, u32[]{:S(2)}, u32[]{:S(2)}) collective-permute-start(bf16[16,352,256]{2,1,0:T(8,128)(2,1)} %bitcast.48.refs_1_), channel_id=1, source_target_pairs={{0,4},{4,0},{8,12},{12,8},{16,20},{20,16},{24,28},{28,24},{1,5},{5... | collective-permute-start | bytes 8650760 | tf_op jit(solution)/shard_map/ppermute | solution.py:78
  483.8 10.8 collective-permute-start.12
  486.1 8.5 collective-permute-start.13
  489.1 5.5 collective-permute-start.14
  490.2 86.6 %collective-permute-start.10 = (bf16[4,352,256]{2,1,0:T(8,128)(2,1)}, bf16[4,352,256]{2,1,0:T(8,128)(2,1)S(1)}, u32[]{:S(2)}, u32[]{:S(2)}) collective-permute-start(bf16[4,352,256]{2,1,0:T(8,128)(2,1)} %get-tuple-element.267), channel_id=1, source_target_pairs={{0,24},{4,28},{8,16},{12,20},{16,8},{20,12},{24,0},{28,4},{1,25},{... | collective-permute-start | bytes 2162696 | tf_op jit(solution)/shard_map/ppermute | solution.py:73
  490.7 117.9 %collective-permute-start.9 = (bf16[4,352,256]{2,1,0:T(8,128)(2,1)S(1)}, bf16[4,352,256]{2,1,0:T(8,128)(2,1)}, u32[]{:S(2)}, u32[]{:S(2)}) collective-permute-start(bf16[4,352,256]{2,1,0:T(8,128)(2,1)S(1)} %get-tuple-element.268), channel_id=1, source_target_pairs={{0,16},{4,20},{8,24},{12,28},{16,0},{20,4},{24,8},{28,12},{1,17},{... | collective-permute-start | bytes 2162696 | tf_op jit(solution)/shard_map/ppermute | solution.py:73
  494.5 114.1 %collective-permute-start.8 = (bf16[4,352,256]{2,1,0:T(8,128)(2,1)S(1)}, bf16[4,352,256]{2,1,0:T(8,128)(2,1)}, u32[]{:S(2)}, u32[]{:S(2)}) collective-permute-start(bf16[4,352,256]{2,1,0:T(8,128)(2,1)S(1)} %get-tuple-element.269), channel_id=1, source_target_pairs={{0,8},{4,12},{8,0},{12,4},{16,24},{20,28},{24,16},{28,20},{1,9},{5... | collective-permute-start | bytes 2162696 | tf_op jit(solution)/shard_map/ppermute | solution.py:73
  507.2 174.6 %all-to-all-start.4 = ((bf16[4,2048,512]{2,1,0:T(8,128)(2,1)}), bf16[4,2048,512]{2,1,0:T(8,128)(2,1)}, u32[]{:S(2)}, u32[]{:S(2)}) async-start(bf16[4,2048,512]{2,1,0:T(8,128)(2,1)} %bitcast.405), calls=%async_computation.5 | async-start | bytes 16777216 | tf_op jit(solution)/shard_map/all_to_all | solution.py:422
  610.3 44.6 %collective-permute-start.11 = (bf16[16,352,256]{2,1,0:T(8,128)(2,1)S(1)}, bf16[16,352,256]{2,1,0:T(8,128)(2,1)}, u32[]{:S(2)}, u32[]{:S(2)}) collective-permute-start(bf16[16,352,256]{2,1,0:T(8,128)(2,1)S(1)} %bitcast.401), channel_id=1, source_target_pairs={{0,4},{4,0},{8,12},{12,8},{16,20},{20,16},{24,28},{28,24},{1,5},{5... | collective-permute-start | bytes 8650760 | tf_op jit(solution)/shard_map/ppermute | solution.py:78
  739.6 99.2 %all-to-all-start.5 = ((bf16[4,2048,512]{2,1,0:T(8,128)(2,1)}), bf16[4,2048,512]{2,1,0:T(8,128)(2,1)}, u32[]{:S(2)}, u32[]{:S(2)}) async-start(bf16[4,2048,512]{2,1,0:T(8,128)(2,1)} %bitcast.407), calls=%async_computation.6 | async-start | bytes 16777216 | tf_op jit(solution)/shard_map/all_to_all | solution.py:422
  745.7 183.5 %reduce-scatter.8.cloned.1.call-start = ((), (), s32[]{:S(2)}) async-start(), calls=%async_computation.18 | async-start | bytes 5242880 | tf_op jit(solution)/shard_map/reduce_scatter | solution.py:409
  747.2 84.4 %collective-permute-start.17 = (f32[8,128]{1,0:T(8,128)S(1)}, f32[8,128]{1,0:T(8,128)S(1)}, u32[]{:S(2)}, u32[]{:S(2)}) collective-permute-start(f32[8,128]{1,0:T(8,128)S(1)} %get-tuple-element.293), channel_id=1, source_target_pairs={{0,24},{4,28},{8,16},{12,20},{16,8},{20,12},{24,0},{28,4},{1,25},{... | collective-permute-start | bytes 12296 | tf_op jit(solution)/shard_map/ppermute | solution.py:73
  749.7 81.9 %collective-permute-start.16 = (f32[8,128]{1,0:T(8,128)S(1)}, f32[8,128]{1,0:T(8,128)S(1)}, u32[]{:S(2)}, u32[]{:S(2)}) collective-permute-start(f32[8,128]{1,0:T(8,128)S(1)} %get-tuple-element.294), channel_id=1, source_target_pairs={{0,16},{4,20},{8,24},{12,28},{16,0},{20,4},{24,8},{28,12},{1,17},{... | collective-permute-start | bytes 12296 | tf_op jit(solution)/shard_map/ppermute | solution.py:73
  754.2 77.4 %collective-permute-start.15 = (f32[8,128]{1,0:T(8,128)S(1)}, f32[8,128]{1,0:T(8,128)S(1)}, u32[]{:S(2)}, u32[]{:S(2)}) collective-permute-start(f32[8,128]{1,0:T(8,128)S(1)} %get-tuple-element.295), channel_id=1, source_target_pairs={{0,8},{4,12},{8,0},{12,4},{16,24},{20,28},{24,16},{28,20},{1,9},{5... | collective-permute-start | bytes 12296 | tf_op jit(solution)/shard_map/ppermute | solution.py:73
  831.6 26.6 %collective-permute-start.20 = (f32[4,8,128]{2,1,0:T(8,128)S(1)}, f32[4,8,128]{2,1,0:T(8,128)S(1)}, u32[]{:S(2)}, u32[]{:S(2)}) collective-permute-start(f32[4,8,128]{2,1,0:T(8,128)S(1)} %get-tuple-element.291), channel_id=1, source_target_pairs={{0,3},{1,2},{2,1},{3,0},{4,7},{5,6},{6,5},{7,4},{8,11},{9,10},{10,... | collective-permute-start | bytes 49160 | tf_op jit(solution)/shard_map/ppermute | solution.py:68
  833.2 25.1 %collective-permute-start.19 = (f32[4,8,128]{2,1,0:T(8,128)S(1)}, f32[4,8,128]{2,1,0:T(8,128)S(1)}, u32[]{:S(2)}, u32[]{:S(2)}) collective-permute-start(f32[4,8,128]{2,1,0:T(8,128)S(1)} %get-tuple-element.291), channel_id=1, source_target_pairs={{0,2},{1,3},{2,0},{3,1},{4,6},{5,7},{6,4},{7,5},{8,10},{9,11},{10,... | collective-permute-start | bytes 49160 | tf_op jit(solution)/shard_map/ppermute | solution.py:68
  833.3 25.0 %collective-permute-start.18 = (f32[4,8,128]{2,1,0:T(8,128)S(1)}, f32[4,8,128]{2,1,0:T(8,128)S(1)}, u32[]{:S(2)}, u32[]{:S(2)}) collective-permute-start(f32[4,8,128]{2,1,0:T(8,128)S(1)} %get-tuple-element.291), channel_id=1, source_target_pairs={{0,1},{1,0},{2,3},{3,2},{4,5},{5,4},{6,7},{7,6},{8,9},{9,8},{10,11... | collective-permute-start | bytes 49160 | tf_op jit(solution)/shard_map/ppermute | solution.py:68
  866.8 98.2 %all-to-all-start.6 = ((bf16[4,2048,512]{2,1,0:T(8,128)(2,1)}), bf16[4,2048,512]{2,1,0:T(8,128)(2,1)}, u32[]{:S(2)}, u32[]{:S(2)}) async-start(bf16[4,2048,512]{2,1,0:T(8,128)(2,1)} %bitcast.408), calls=%async_computation.7 | async-start | bytes 16777216 | tf_op jit(solution)/shard_map/all_to_all | solution.py:422
  872.9 181.7 %reduce-scatter.10.cloned.1.call-start = ((), (), s32[]{:S(2)}) async-start(), calls=%async_computation.19 | async-start | bytes 5242880 | tf_op jit(solution)/shard_map/reduce_scatter | solution.py:409
  993.7 12.0 collective-permute-start.21
  993.7 17.2 %collective-permute-start.22 = (bf16[16,352,256]{2,1,0:T(8,128)(2,1)}, bf16[16,352,256]{2,1,0:T(8,128)(2,1)}, u32[]{:S(2)}, u32[]{:S(2)}) collective-permute-start(bf16[16,352,256]{2,1,0:T(8,128)(2,1)} %get-tuple-element.115), channel_id=1, source_target_pairs={{0,4},{4,0},{8,12},{12,8},{16,20},{20,16},{24,28},{28,24},{1,5},{5... | collective-permute-start | bytes 8650760 | tf_op jit(solution)/shard_map/ppermute | solution.py:78
  994.2 21.0 %collective-permute-start.23 = (bf16[16,352,256]{2,1,0:T(8,128)(2,1)}, bf16[16,352,256]{2,1,0:T(8,128)(2,1)}, u32[]{:S(2)}, u32[]{:S(2)}) collective-permute-start(bf16[16,352,256]{2,1,0:T(8,128)(2,1)} %get-tuple-element.117), channel_id=1, source_target_pairs={{0,4},{4,0},{8,12},{12,8},{16,20},{20,16},{24,28},{28,24},{1,5},{5... | collective-permute-start | bytes 8650760 | tf_op jit(solution)/shard_map/ppermute | solution.py:78
  996.6 53.3 %all-to-all-start.7 = ((bf16[4,1024,512]{2,1,0:T(8,128)(2,1)}), bf16[4,1024,512]{2,1,0:T(8,128)(2,1)}, u32[]{:S(2)}, u32[]{:S(2)}) async-start(bf16[4,1024,512]{2,1,0:T(8,128)(2,1)} %bitcast.410), calls=%async_computation.9 | async-start | bytes 8388608 | tf_op jit(solution)/shard_map/all_to_all | solution.py:422
  1002.2 136.9 %all-gather.10.cloned.1.call-start = ((), (), s32[]{:S(2)}) async-start(), calls=%async_computation.20 | async-start | bytes 5242880 | tf_op jit(solution)/shard_map/all_gather | solution.py:414
  1072.5 66.6 %all-to-all-start.8 = ((bf16[4,4,352,256]{3,2,1,0:T(8,128)(2,1)}), bf16[4,4,352,256]{3,2,1,0:T(8,128)(2,1)S(1)}, u32[]{:S(2)}, u32[]{:S(2)}) async-start(bf16[4,4,352,256]{3,2,1,0:T(8,128)(2,1)} %bitcast.418), calls=%async_computation.11 | async-start | bytes 5767168 | tf_op jit(solution)/shard_map/all_to_all | solution.py:425
  1079.0 322.3 %reduce-scatter.12.cloned.1.call-start = ((), (), s32[]{:S(2)}) async-start(), calls=%async_computation.21 | async-start | bytes 9732096 | tf_op jit(solution)/shard_map/reduce_scatter | solution.py:779
  1140.7 118.4 %all-to-all-start.9 = ((bf16[4,4,352,256]{3,2,1,0:T(8,128)(2,1)}), bf16[4,4,352,256]{3,2,1,0:T(8,128)(2,1)}, u32[]{:S(2)}, u32[]{:S(2)}) async-start(bf16[4,4,352,256]{3,2,1,0:T(8,128)(2,1)} %bitcast.417), calls=%async_computation.12 | async-start | bytes 5767168 | tf_op jit(solution)/shard_map/all_to_all | solution.py:425
  1259.2 144.9 %all-to-all-start.10 = ((bf16[4,4,352,256]{3,2,1,0:T(8,128)(2,1)}), bf16[4,4,352,256]{3,2,1,0:T(8,128)(2,1)}, u32[]{:S(2)}, u32[]{:S(2)}) async-start(bf16[4,4,352,256]{3,2,1,0:T(8,128)(2,1)} %bitcast.416), calls=%async_computation.14 | async-start | bytes 5767168 | tf_op jit(solution)/shard_map/all_to_all | solution.py:425
  1268.4 377.5 %reduce-scatter.14.cloned.1.call-start = ((), (), s32[]{:S(2)}) async-start(), calls=%async_computation.22 | async-start | bytes 9879552 | tf_op jit(solution)/shard_map/reduce_scatter | solution.py:779
  1299.2 27.9 %collective-permute-start.26 = (bf16[1024,512]{1,0:T(8,128)(2,1)}, bf16[1024,512]{1,0:T(8,128)(2,1)}, u32[]{:S(2)}, u32[]{:S(2)}) collective-permute-start(bf16[1024,512]{1,0:T(8,128)(2,1)} %get-tuple-element.257), channel_id=1, source_target_pairs={{0,3},{1,2},{2,1},{3,0},{4,7},{5,6},{6,5},{7,4},{8,11},{9,10},{10,... | collective-permute-start | bytes 3145736 | tf_op jit(solution)/shard_map/ppermute | solution.py:68
  1302.6 45.1 %collective-permute-start.25 = (bf16[1024,512]{1,0:T(8,128)(2,1)}, bf16[1024,512]{1,0:T(8,128)(2,1)}, u32[]{:S(2)}, u32[]{:S(2)}) collective-permute-start(bf16[1024,512]{1,0:T(8,128)(2,1)} %get-tuple-element.258), channel_id=1, source_target_pairs={{0,2},{1,3},{2,0},{3,1},{4,6},{5,7},{6,4},{7,5},{8,10},{9,11},{10,... | collective-permute-start | bytes 3145736 | tf_op jit(solution)/shard_map/ppermute | solution.py:68
  1303.2 44.5 %collective-permute-start.24 = (bf16[1024,512]{1,0:T(8,128)(2,1)}, bf16[1024,512]{1,0:T(8,128)(2,1)}, u32[]{:S(2)}, u32[]{:S(2)}) collective-permute-start(bf16[1024,512]{1,0:T(8,128)(2,1)} %get-tuple-element.256), channel_id=1, source_target_pairs={{0,1},{1,0},{2,3},{3,2},{4,5},{5,4},{6,7},{7,6},{8,9},{9,8},{10,11... | collective-permute-start | bytes 3145736 | tf_op jit(solution)/shard_map/ppermute | solution.py:68
  1352.6 27.0 %collective-permute-start.32 = (bf16[1024,512]{1,0:T(8,128)(2,1)S(1)}, bf16[1024,512]{1,0:T(8,128)(2,1)S(1)}, u32[]{:S(2)}, u32[]{:S(2)}) collective-permute-start(bf16[1024,512]{1,0:T(8,128)(2,1)S(1)} %get-tuple-element.254), channel_id=1, source_target_pairs={{0,3},{1,2},{2,1},{3,0},{4,7},{5,6},{6,5},{7,4},{8,11},{9,10},{10,... | collective-permute-start | bytes 3145736 | tf_op jit(solution)/shard_map/ppermute | solution.py:68
  1354.5 46.2 %collective-permute-start.31 = (bf16[1024,512]{1,0:T(8,128)(2,1)S(1)}, bf16[1024,512]{1,0:T(8,128)(2,1)S(1)}, u32[]{:S(2)}, u32[]{:S(2)}) collective-permute-start(bf16[1024,512]{1,0:T(8,128)(2,1)S(1)} %get-tuple-element.255), channel_id=1, source_target_pairs={{0,2},{1,3},{2,0},{3,1},{4,6},{5,7},{6,4},{7,5},{8,10},{9,11},{10,... | collective-permute-start | bytes 3145736 | tf_op jit(solution)/shard_map/ppermute | solution.py:68
  1355.9 44.8 %collective-permute-start.30 = (bf16[1024,512]{1,0:T(8,128)(2,1)S(1)}, bf16[1024,512]{1,0:T(8,128)(2,1)S(1)}, u32[]{:S(2)}, u32[]{:S(2)}) collective-permute-start(bf16[1024,512]{1,0:T(8,128)(2,1)S(1)} %get-tuple-element.253), channel_id=1, source_target_pairs={{0,1},{1,0},{2,3},{3,2},{4,5},{5,4},{6,7},{7,6},{8,9},{9,8},{10,11... | collective-permute-start | bytes 3145736 | tf_op jit(solution)/shard_map/ppermute | solution.py:68
  1435.1 128.3 %copy-start.31 = (f32[2112,256]{1,0:T(8,128)S(1)}, f32[2112,256]{1,0:T(8,128)}, u32[]{:S(2)}) copy-start(f32[2112,256]{1,0:T(8,128)} %bitcast_convert_fusion.2) | copy-start | bytes 6488068
  1435.1 196.9 %all-to-all-start.11 = ((bf16[4,3,4,352,256]{4,3,2,1,0:T(8,128)(2,1)}), bf16[4,3,4,352,256]{4,3,2,1,0:T(8,128)(2,1)}, u32[]{:S(2)}, u32[]{:S(2)}) async-start(bf16[4,3,4,352,256]{4,3,2,1,0:T(8,128)(2,1)} %maximum_bitcast_fusion.1), calls=%async_computation.16 | async-start | bytes 17301504 | tf_op jit(solution)/shard_map/all_to_all | solution.py:422
  1443.4 117.1 %collective-permute-start.27 = (bf16[1024,512]{1,0:T(8,128)(2,1)}, bf16[1024,512]{1,0:T(8,128)(2,1)}, u32[]{:S(2)}, u32[]{:S(2)}) collective-permute-start(bf16[1024,512]{1,0:T(8,128)(2,1)} %get-tuple-element.261.refs_0_), channel_id=1, source_target_pairs={{0,1},{1,0},{2,3},{3,2},{4,5},{5,4},{6,7},{7,6},{8,9},{9,8},{10,11... | collective-permute-start | bytes 3145736 | tf_op jit(solution)/shard_map/ppermute | solution.py:68
  1443.5 140.8 %collective-permute-start.28 = (bf16[1024,512]{1,0:T(8,128)(2,1)}, bf16[1024,512]{1,0:T(8,128)(2,1)}, u32[]{:S(2)}, u32[]{:S(2)}) collective-permute-start(bf16[1024,512]{1,0:T(8,128)(2,1)} %get-tuple-element.261.refs_0_), channel_id=1, source_target_pairs={{0,2},{1,3},{2,0},{3,1},{4,6},{5,7},{6,4},{7,5},{8,10},{9,11},{10,... | collective-permute-start | bytes 3145736 | tf_op jit(solution)/shard_map/ppermute | solution.py:68
  1445.5 139.1 %collective-permute-start.29 = (bf16[1024,512]{1,0:T(8,128)(2,1)}, bf16[1024,512]{1,0:T(8,128)(2,1)}, u32[]{:S(2)}, u32[]{:S(2)}) collective-permute-start(bf16[1024,512]{1,0:T(8,128)(2,1)} %get-tuple-element.261.refs_0_), channel_id=1, source_target_pairs={{0,3},{1,2},{2,1},{3,0},{4,7},{5,6},{6,5},{7,4},{8,11},{9,10},{10,... | collective-permute-start | bytes 3145736 | tf_op jit(solution)/shard_map/ppermute | solution.py:68
  1446.9 158.6 %collective-permute-start.33 = (bf16[1024,512]{1,0:T(8,128)(2,1)S(1)}, bf16[1024,512]{1,0:T(8,128)(2,1)}, u32[]{:S(2)}, u32[]{:S(2)}) collective-permute-start(bf16[1024,512]{1,0:T(8,128)(2,1)S(1)} %copy-done.40), channel_id=1, source_target_pairs={{0,1},{1,0},{2,3},{3,2},{4,5},{5,4},{6,7},{7,6},{8,9},{9,8},{10,11... | collective-permute-start | bytes 3145736 | tf_op jit(solution)/shard_map/ppermute | solution.py:68
  1447.0 159.8 %collective-permute-start.34 = (bf16[1024,512]{1,0:T(8,128)(2,1)S(1)}, bf16[1024,512]{1,0:T(8,128)(2,1)}, u32[]{:S(2)}, u32[]{:S(2)}) collective-permute-start(bf16[1024,512]{1,0:T(8,128)(2,1)S(1)} %copy-done.40), channel_id=1, source_target_pairs={{0,2},{1,3},{2,0},{3,1},{4,6},{5,7},{6,4},{7,5},{8,10},{9,11},{10,... | collective-permute-start | bytes 3145736 | tf_op jit(solution)/shard_map/ppermute | solution.py:68
  1560.6 65.4 %collective-permute-start.35 = (bf16[1024,512]{1,0:T(8,128)(2,1)S(1)}, bf16[1024,512]{1,0:T(8,128)(2,1)}, u32[]{:S(2)}, u32[]{:S(2)}) collective-permute-start(bf16[1024,512]{1,0:T(8,128)(2,1)S(1)} %copy-done.40), channel_id=1, source_target_pairs={{0,3},{1,2},{2,1},{3,0},{4,7},{5,6},{6,5},{7,4},{8,11},{9,10},{10,... | collective-permute-start | bytes 3145736 | tf_op jit(solution)/shard_map/ppermute | solution.py:68
  1648.2 10.3 collective-permute-start.38
  1649.6 11.9 collective-permute-start.37
  1651.1 10.5 collective-permute-start.36
  (108 other events, 869.6 us)
Sparse Core Ops, SparseCore 0:
  20.3 86.0 all-gather.11
  212.2 52.5 reduce-scatter.5
  282.9 79.3 all-gather.13
  363.8 79.2 all-gather.15
  466.8 139.9 all-gather.17
  851.3 77.8 reduce-scatter.7
  977.2 77.3 reduce-scatter.9
  1072.7 53.0 all-gather.9
  1139.3 207.1 reduce-scatter.11
  1412.8 90.9 reduce-scatter.13

commit v7 on v6

--- a/solution.py
+++ b/solution.py
@@ -617,9 +617,6 @@
             ]
         )
     )
-    cot_picked, shared_pack = lax.optimization_barrier((pick_rows(cot_all), shared_pack))
-    cot_rows = send_out(cot_picked)
-    shared_all = lax.all_gather(shared_pack, "dp", axis=0, tiled=False)
 
     def own_weights(matrices, order):
         pieces = [by_plane[g].reshape(nz * nt, f_loc, d_loc) for g in matrices]
@@ -627,6 +624,11 @@
         return lay_out_weights(lay, order, stacks, f_loc, d_loc, width)
 
     own_in = own_weights((0, 1), ids * jnp.array([0, 1, 1], jnp.int32))
+    by_plane[2], shared_pack, cot_picked = lax.optimization_barrier(
+        (by_plane[2], shared_pack, pick_rows(cot_all))
+    )
+    cot_rows = send_out(cot_picked)
+    shared_all = lax.all_gather(shared_pack, "dp", axis=0, tiled=False)
     own_out = own_weights((2,), ids)
     router_probs = jax.nn.softmax(dot_nt(ffn_low, router_t), axis=-1)
     probs_turned = jnp.transpose(router_probs).reshape(EXPERTS, -1, 128)
@@ -785,7 +787,6 @@
     residual_low, shared_grads, grad_plane[0] = lax.optimization_barrier(
         (residual_low, shared_grads, grad_plane[0])
     )
-    shared_sum = sum_dp(shared_grads)
     grad_out_w = dot_tn(attended_low, residual_low)
     attended_grad = dot_nt(residual_low, out_w).astype(BF16)
     query_nope_grad, query_turned_grad, kv_grad, rope_grad = attend_back(
@@ -799,9 +800,10 @@
         heads,
         score_scale,
     )
-    query_turned_grad, grad_plane[1], shared_full = lax.optimization_barrier(
-        (query_turned_grad, grad_plane[1], shared_full)
-    )
+    query_turned_grad, grad_plane[1], shared_full, shared_grads = lax.optimization_barrier(
+        (query_turned_grad, grad_plane[1], shared_full, shared_grads)
+    )
+    shared_sum = sum_dp(shared_grads)
     turned_first, turned_second = rotate_back(
         query_turned_grad[:, : heads * half], query_turned_grad[:, heads * half :], wide_cos, wide_sin
     )
@@ -826,8 +828,8 @@
         (dot(query_grad, query_t) + dot(down_grad, down_t), scatter_t_direct(shared_full))
     )
     output = gather_t_direct((residual + routed + shared_part).astype(BF16))
-    normed_grad, shared_sum, grad_plane[2] = lax.optimization_barrier(
-        (scatter_t_direct(normed_full), shared_sum, grad_plane[2])
+    normed_grad, grad_plane[2] = lax.optimization_barrier(
+        (scatter_t_direct(normed_full), grad_plane[2])
     )
     attn_hat = own_part(hidden).astype(F32) * attn_inverse
     scaled_in = lax.dynamic_slice_in_dim(attn_scale, me_t * part, part, 0) * normed_grad

time: 1690 us -> 1580 us (0.935)
  waiting for transfers between devices: 764 us -> 645 us
    all_to_all x5, waiting for transfers between devices: 122 us -> 63.5 us  [swap_z(): lax.all_to_all(values, 'dp', split_axis=0, concat_axis=0, axis_index_grou...]
    ppermute x12, waiting for transfers between devices: 96.5 us -> 38.8 us  [over_z(): lax.ppermute(values, 'dp', [(d, d ^ k * self.q) for d in range(self.dp)])]
    reduce_scatter x2, waiting for transfers between devices: 8.01 us -> 40.3 us  [scatter_z(): lax.psum_scatter(values, 'dp', scatter_dimension=0, tiled=False, axis_ind...]
    ppermute x21, waiting for transfers between devices: 278 us -> 251 us  [over_t(): return lax.ppermute(values, 'tensor', [(i, i ^ k) for i in range(self.t)])]
    unnamed x246 -> x252, local copies, waits for them, and re-layouts: 45.9 us -> 45.3 us
  transfers between devices with their start and end apart: 61 -> 61, of which waited for: 31 -> 30; matrix products, arithmetic and copies ran while one was open for 30% -> 34% of each run, Pallas kernels for 6% -> 7%
where the time goes in v7:
time: 1580 us; the launch traced here: 1560 us
  waiting for transfers between devices  645 us (41%)
  matrix products  328 us (21%)
  local copies, waits for them, and re-layouts  197 us (12%)
  starting transfers between devices  125 us (8%)
  other arithmetic  112 us (7%)
  Pallas kernels  106 us (7%)
  blocking collectives  24.6 us (2%)
  between operations  17 us (1%)
    ppermute x21, waiting for transfers between devices, over_t(): return lax.ppermute(values, 'tensor', [(i, i ^ k) for i in range(self.t)])  251 us
    dot_general x9, matrix products, dot_nt(): lax.dot_general(a, b, (((1,), (1,)), ((), ())), preferred_element_type=F32)  104 us
    dot_general x9, matrix products, dot(): return jnp.dot(a, b, preferred_element_type=F32)  81.8 us
    all_to_all x7, waiting for transfers between devices, swap_t(): lax.all_to_all(values, 'tensor', split_axis=0, concat_axis=0, tiled=True)  78.6 us
    dot_general x8, matrix products, dot_tn(): lax.dot_general(a, b, (((0,), (0,)), ((), ())), preferred_element_type=F32)  78.2 us
    all_gather x2, waiting for transfers between devices, gather_z(): lax.all_gather(values, 'dp', axis=0, tiled=False, axis_index_groups=lay.z...  74.6 us
    all_to_all x5, waiting for transfers between devices, swap_z(): lax.all_to_all(values, 'dp', split_axis=0, concat_axis=0, axis_index_grou...  63.5 us
    all_gather x1, waiting for transfers between devices, body(): front = lax.all_gather(front_pack, 'dp', axis=0, tiled=False)  55.1 us
  transfers between devices with their start and end apart: 61, of which 30 were waited for; matrix products, arithmetic and copies ran while one was open for 34% of the time, Pallas kernels for 7%

profile of v7, /device:TPU:10, one launch (start us, length us, event | category | flops | bytes accessed | tf_op | source)
XLA Modules:
  0.0 1555.9 jit_solution(17752267335598584415)
XLA Ops:
  20.2 6.9 maximum_bitcast_fusion
  27.1 8.3 copy.301
  35.4 6.4 all-to-all-start
  51.4 55.1 %all-gather.12.cloned.1.call-done = bf16[17152,256]{1,0:T(8,128)(2,1)} async-done(((bf16[2144,256]{1,0:T(8,128)(2,1)}), bf16[17152,256]{1,0:T(8,128)(2,1)}) %all-gather.12.cloned.1.call-update) | async-done | bytes 8781840 | tf_op jit(solution)/shard_map/all_gather | solution.py:486
  117.3 19.4 %all-to-all-done = bf16[4,4,3,352,256]{4,3,1,2,0:T(8,128)(2,1)} async-done(((bf16[4,4,3,352,256]{4,3,1,2,0:T(8,128)(2,1)}), bf16[4,4,3,352,256]{4,3,1,2,0:T(8,128)(2,1)}, u32[]{:S(2)}, u32[]{:S(2)}) %all-to-all-start) | async-done | bytes 8650784 | tf_op jit(solution)/shard_map/all_to_all | solution.py:422
  162.5 6.5 fusion.118
  190.8 14.6 attend.1
  221.6 43.3 %reduce-scatter.6.cloned.1.call-done = bf16[1024,512]{1,0:T(8,128)(2,1)} async-done(((bf16[1024,2048]{1,0:T(8,128)(2,1)}), bf16[1024,512]{1,0:T(8,128)(2,1)}) %reduce-scatter.6.cloned.1.call-update) | async-done | bytes 1048592 | tf_op jit(solution)/shard_map/reduce_scatter | solution.py:417
  266.8 8.1 psum.21
  292.4 17.3 %collective-permute-done.3.refs_1_ = bf16[1024,512]{1,0:T(8,128)(2,1)} collective-permute-done((bf16[1024,512]{1,0:T(8,128)(2,1)}, bf16[1024,512]{1,0:T(8,128)(2,1)}, u32[]{:S(2)}, u32[]{:S(2)}) %collective-permute-start.3) | collective-permute-done | bytes 1048608 | tf_op jit(solution)/shard_map/ppermute | solution.py:68
  309.6 19.9 %collective-permute-done.4.refs_2_ = bf16[1024,512]{1,0:T(8,128)(2,1)} collective-permute-done((bf16[1024,512]{1,0:T(8,128)(2,1)}, bf16[1024,512]{1,0:T(8,128)(2,1)}, u32[]{:S(2)}, u32[]{:S(2)}) %collective-permute-start.4) | collective-permute-done | bytes 1048608 | tf_op jit(solution)/shard_map/ppermute | solution.py:68
  335.8 26.4 %all-gather.14.cloned.1.call-done = bf16[4096,512]{1,0:T(8,128)(2,1)} async-done(((bf16[1024,512]{1,0:T(8,128)(2,1)}), bf16[4096,512]{1,0:T(8,128)(2,1)}) %all-gather.14.cloned.1.call-update) | async-done | bytes 4194320 | tf_op jit(solution)/shard_map/all_gather | solution.py:406
  365.2 16.2 %convert_bitcast_fusion.1 = bf16[4,4,512,512]{3,2,0,1:T(8,128)(2,1)} fusion(s32[4,4,1024]{2,1,0:T(4,128)S(1)} %fusion.46, bf16[4,1024,512]{2,1,0:T(8,128)(2,1)} %bitcast.523), kind=kOutput, calls=%fused_computation.40 | convolution fusion | flops 8602517504 | bytes 12648448 | tf_op jit(solution)/shard_map/sepk,skd->espd/dot_general | solution.py:519
  381.5 7.4 copy.306
  394.9 48.2 %all-gather.16.cloned.1.call-done = bf16[4096,512]{1,0:T(8,128)(2,1)} async-done(((bf16[1024,512]{1,0:T(8,128)(2,1)}), bf16[4096,512]{1,0:T(8,128)(2,1)}) %all-gather.16.cloned.1.call-update) | async-done | bytes 4194320 | tf_op jit(solution)/shard_map/all_gather | solution.py:406
  451.4 14.4 convert_bitcast_fusion
  465.8 7.4 copy.309
  473.2 23.4 %collective-permute-done.10 = bf16[4,352,256]{2,1,0:T(8,128)(2,1)S(1)} collective-permute-done((bf16[4,352,256]{2,1,0:T(8,128)(2,1)}, bf16[4,352,256]{2,1,0:T(8,128)(2,1)S(1)}, u32[]{:S(2)}, u32[]{:S(2)}) %collective-permute-start.10) | collective-permute-done | bytes 720928 | tf_op jit(solution)/shard_map/ppermute | solution.py:73
  496.6 13.9 collective-permute-done.9
  524.1 13.5 lay_out_weights.2
  538.7 11.5 copy.307
  552.3 6.4 all-to-all-start.4
  558.7 32.4 %fusion.127 = f32[2048,2816]{1,0:T(8,128)} fusion(bf16[2048,2048]{0,1:T(8,128)(2,1)} %bitcast.430, bf16[2816,2048]{1,0:T(8,128)(2,1)} %bitcast.410), kind=kOutput, calls=%fused_computation.303 | convolution fusion | flops 23622320128 | bytes 42991616 | tf_op jit(solution)/shard_map/dot_general | solution.py:30
  591.1 12.3 fusion.8
  603.4 9.3 lay_out_weights.3
  615.2 15.1 multiply_convert_fusion
  630.3 21.1 %all-to-all-done.4 = bf16[4,2048,512]{2,1,0:T(8,128)(2,1)} async-done(((bf16[4,2048,512]{2,1,0:T(8,128)(2,1)}), bf16[4,2048,512]{2,1,0:T(8,128)(2,1)}, u32[]{:S(2)}, u32[]{:S(2)}) %all-to-all-start.4) | async-done | bytes 8388640 | tf_op jit(solution)/shard_map/all_to_all | solution.py:422
  651.4 11.6 copy.316
  672.3 29.5 %multiply_convert_fusion.2 = (bf16[2048,1408]{1,0:T(8,128)(2,1)}, bf16[2048,1408]{1,0:T(8,128)(2,1)}, f32[2048]{0:T(1024)S(1)}) fusion(f32[2048,2816]{1,0:T(8,128)} %fusion.127, f32[2048]{0:T(1024)S(1)} %bitcast.495, bf16[2048,1408]{1,0:T(8,128)(2,1)} %copy-done.35, bf16[2048,2048]{0,1:T(8,128)(2,1)} %bitcast.432, bf16[1,1408,2048]{2,1,0:T(8,128)(2,1)S(1)} %bitcast.403), kind=kOutput, calls=%fused_computation.16 | convolution fusion | flops 11860178944 | bytes 54542336 | tf_op jit(solution)/shard_map/dot_general | solution.py:30
  701.8 7.5 copy.401
  709.3 6.3 all-to-all-start.5
  721.4 8.7 copy.322
  730.1 11.8 fusion.128
  744.1 7.8 multiply_convert_fusion.5
  752.0 10.4 fusion.42
  762.4 28.9 %convolution_convert_fusion.3 = bf16[2048,2048]{1,0:T(8,128)(2,1)} fusion(bf16[2816,2048]{1,0:T(8,128)(2,1)S(1)} %bitcast.413, bf16[2048,1408]{1,0:T(8,128)(2,1)} %get-tuple-element.246, bf16[2048,1408]{1,0:T(8,128)(2,1)} %get-tuple-element.245), kind=kOutput, calls=%fused_computation.43 | convolution fusion | flops 23649583104 | bytes 31457280 | tf_op jit(solution)/shard_map/dot_general | solution.py:26
  791.4 7.9 pad_maximum_fusion
  808.0 12.3 bitcast_convert_fusion.1
  820.4 7.1 fusion.129
  828.3 7.4 copy.400
  841.9 17.9 %convolution_convert_fusion.2.out_ref = bf16[1408,2048]{1,0:T(8,128)(2,1)} fusion(bf16[2048,1408]{1,0:T(8,128)(2,1)} %get-tuple-element.106, bf16[2048,2048]{0,1:T(8,128)(2,1)} %bitcast.433), kind=kOutput, calls=%fused_computation.42 | convolution fusion | flops 11814043648 | bytes 19922944 | tf_op jit(solution)/shard_map/dot_general | solution.py:34
  859.8 31.8 %convolution_convert_fusion = bf16[2816,2048]{1,0:T(8,128)(2,1)} fusion(bf16[2048,2816]{1,0:T(8,128)(2,1)} %pad_maximum_fusion, bf16[2048,2048]{0,1:T(8,128)(2,1)} %bitcast.431), kind=kOutput, calls=%fused_computation.20 | convolution fusion | flops 23628087296 | bytes 31457280 | tf_op jit(solution)/shard_map/dot_general | solution.py:34
  900.5 32.9 %all-to-all-done.6 = bf16[4,2048,512]{2,1,0:T(8,128)(2,1)} async-done(((bf16[4,2048,512]{2,1,0:T(8,128)(2,1)}), bf16[4,2048,512]{2,1,0:T(8,128)(2,1)}, u32[]{:S(2)}, u32[]{:S(2)}) %all-to-all-start.6) | async-done | bytes 8388640 | tf_op jit(solution)/shard_map/all_to_all | solution.py:422
  933.3 12.1 bitcast_convert_fusion
  945.5 15.0 take_apart.1
  988.2 34.4 %reduce-scatter.10.cloned.1.call-done = bf16[1,1024,512]{2,1,0:T(8,128)(2,1)} async-done(((bf16[4,1024,512]{2,1,0:T(8,128)(2,1)}), bf16[1,1024,512]{2,1,0:T(8,128)(2,1)}) %reduce-scatter.10.cloned.1.call-update) | async-done | bytes 1048592 | tf_op jit(solution)/shard_map/reduce_scatter | solution.py:409
  1037.8 8.0 psum.22
  1050.5 42.2 %all-to-all-done.8 = bf16[4,4,352,256]{3,2,1,0:T(8,128)(2,1)} async-done(((bf16[4,4,352,256]{3,2,1,0:T(8,128)(2,1)}), bf16[4,4,352,256]{3,2,1,0:T(8,128)(2,1)}, u32[]{:S(2)}, u32[]{:S(2)}) %all-to-all-start.8) | async-done | bytes 2883616 | tf_op jit(solution)/shard_map/all_to_all | solution.py:425
  1092.6 8.3 all-to-all-start.9
  1109.1 7.3 convolution_convert_fusion.1
  1125.4 21.6 %attend_back.1 = (bf16[1024,512]{1,0:T(8,128)(2,1)S(1)}, f32[1024,256]{1,0:T(8,128)S(1)}, bf16[1024,1024]{1,0:T(8,128)(2,1)S(1)}, f32[1024,256]{1,0:T(8,128)S(1)}) custom-call(s32[1]{0:T(128)} %copy.425.len_ref, bf16[1024,512]{1,0:T(8,128)(2,1)S(1)} %copy-done.5, bf16[1024,256]{1,0:T(8,128)(2,1)S(1)} %copy-done.9, bf16[1024,1024]{1,0:T(8,128)(2,1)S(1)} %copy-done.11, ...), custom_call_target="tpu_custom_call" | custom-call | flops 6710886400 | bytes 33554432 | tf_op jit(solution)/shard_map/attend_back/pallas_call | solution.py:321
  1149.2 13.4 all-to-all-done.9
  1167.3 8.0 all-to-all-start.10
  1212.4 8.3 convolution_add_fusion
  1220.7 9.3 collective-permute-done.25
  1245.5 16.7 %collective-permute-done.32 = bf16[1024,512]{1,0:T(8,128)(2,1)S(1)} collective-permute-done((bf16[1024,512]{1,0:T(8,128)(2,1)S(1)}, bf16[1024,512]{1,0:T(8,128)(2,1)S(1)}, u32[]{:S(2)}, u32[]{:S(2)}) %collective-permute-start.32) | collective-permute-done | bytes 1048608 | tf_op jit(solution)/shard_map/ppermute | solution.py:68
  1262.2 21.3 %collective-permute-done.31 = bf16[1024,512]{1,0:T(8,128)(2,1)S(1)} collective-permute-done((bf16[1024,512]{1,0:T(8,128)(2,1)S(1)}, bf16[1024,512]{1,0:T(8,128)(2,1)S(1)}, u32[]{:S(2)}, u32[]{:S(2)}) %collective-permute-start.31) | collective-permute-done | bytes 1048608 | tf_op jit(solution)/shard_map/ppermute | solution.py:68
  1295.8 8.5 psum.23
  1319.9 8.6 all-to-all-start.11
  1334.0 111.5 %collective-permute-done.27.refs_1_ = bf16[1024,512]{1,0:T(8,128)(2,1)S(1)} collective-permute-done((bf16[1024,512]{1,0:T(8,128)(2,1)S(1)}, bf16[1024,512]{1,0:T(8,128)(2,1)S(1)}, u32[]{:S(2)}, u32[]{:S(2)}) %collective-permute-start.27) | collective-permute-done | bytes 1048608 | tf_op jit(solution)/shard_map/ppermute | solution.py:68
  1448.4 20.9 %collective-permute-done.28.refs_2_ = bf16[1024,512]{1,0:T(8,128)(2,1)S(1)} collective-permute-done((bf16[1024,512]{1,0:T(8,128)(2,1)S(1)}, bf16[1024,512]{1,0:T(8,128)(2,1)S(1)}, u32[]{:S(2)}, u32[]{:S(2)}) %collective-permute-start.28) | collective-permute-done | bytes 1048608 | tf_op jit(solution)/shard_map/ppermute | solution.py:68
  1476.5 14.0 collective-permute-done.33.refs_1_
  1491.9 16.4 %collective-permute-done.35.refs_3_ = bf16[1024,512]{1,0:T(8,128)(2,1)} collective-permute-done((bf16[1024,512]{1,0:T(8,128)(2,1)S(1)}, bf16[1024,512]{1,0:T(8,128)(2,1)}, u32[]{:S(2)}, u32[]{:S(2)}) %collective-permute-start.35) | collective-permute-done | bytes 1048608 | tf_op jit(solution)/shard_map/ppermute | solution.py:68
  1514.5 13.8 home_gradients.1
  (511 shorter events, 394.7 us)
Async XLA Ops:
  7.2 99.3 %all-gather.12.cloned.1.call-start = ((), (), s32[]{:S(2)}) async-start(), calls=%async_computation.23 | async-start | bytes 9879552 | tf_op jit(solution)/shard_map/all_gather | solution.py:486
  35.4 101.2 %all-to-all-start = ((bf16[4,4,3,352,256]{4,3,1,2,0:T(8,128)(2,1)}), bf16[4,4,3,352,256]{4,3,1,2,0:T(8,128)(2,1)}, u32[]{:S(2)}, u32[]{:S(2)}) async-start(bf16[4,4,3,352,256]{4,3,1,2,0:T(8,128)(2,1)} %copy.301), calls=%async_computation | async-start | bytes 17301504 | tf_op jit(solution)/shard_map/all_to_all | solution.py:422
  41.9 9.0 collective-permute-start
  43.5 7.4 collective-permute-start.1
  44.7 6.6 collective-permute-start.2
  49.8 112.7 %copy-start.75 = (f32[1024]{0:T(1024)}, f32[1024]{0:T(1024)S(1)}, u32[]{:S(2)}) copy-start(f32[1024]{0:T(1024)S(1)} %add_rsqrt_fusion.1) | copy-start | bytes 12292
  143.9 68.3 %all-to-all-start.1 = ((bf16[4,4,352,256]{3,2,1,0:T(8,128)(2,1)}), bf16[4,4,352,256]{3,2,1,0:T(8,128)(2,1)S(1)}, u32[]{:S(2)}, u32[]{:S(2)}) async-start(bf16[4,4,352,256]{3,2,1,0:T(8,128)(2,1)} %copy.303), calls=%async_computation.1 | async-start | bytes 5767168 | tf_op jit(solution)/shard_map/all_to_all | solution.py:425
  149.2 115.6 %reduce-scatter.6.cloned.1.call-start = ((), (), s32[]{:S(2)}) async-start(), calls=%async_computation.17 | async-start | bytes 5242880 | tf_op jit(solution)/shard_map/reduce_scatter | solution.py:417
  215.7 66.9 %all-to-all-start.2 = ((bf16[4,4,352,256]{3,2,1,0:T(8,128)(2,1)}), bf16[4,4,352,256]{3,2,1,0:T(8,128)(2,1)}, u32[]{:S(2)}, u32[]{:S(2)}) async-start(bf16[4,4,352,256]{3,2,1,0:T(8,128)(2,1)} %copy.304), calls=%async_computation.3 | async-start | bytes 5767168 | tf_op jit(solution)/shard_map/all_to_all | solution.py:425
  221.5 140.7 %all-gather.14.cloned.1.call-start = ((), (), s32[]{:S(2)}) async-start(), calls=%async_computation.24 | async-start | bytes 5242880 | tf_op jit(solution)/shard_map/all_gather | solution.py:406
  221.6 61.1 %copy-start.79 = (f32[512]{0:T(512)}, f32[512]{0:T(512)S(1)}, u32[]{:S(2)}) copy-start(f32[512]{0:T(512)S(1)} %dynamic-slice_convert_fusion.6) | copy-start | bytes 6148
  282.7 160.4 %all-gather.16.cloned.1.call-start = ((), (), s32[]{:S(2)}) async-start(), calls=%async_computation.25 | async-start | bytes 5242880 | tf_op jit(solution)/shard_map/all_gather | solution.py:406
  283.1 26.5 %collective-permute-start.3 = (bf16[1024,512]{1,0:T(8,128)(2,1)}, bf16[1024,512]{1,0:T(8,128)(2,1)}, u32[]{:S(2)}, u32[]{:S(2)}) collective-permute-start(bf16[1024,512]{1,0:T(8,128)(2,1)} %multiply_convert_fusion.8.refs_0_), channel_id=1, source_target_pairs={{0,1},{1,0},{2,3},{3,2},{4,5},{5,4},{6,7},{7,6},{8,9},{9,8},{10,11... | collective-permute-start | bytes 3145736 | tf_op jit(solution)/shard_map/ppermute | solution.py:68
  284.1 45.5 %collective-permute-start.4 = (bf16[1024,512]{1,0:T(8,128)(2,1)}, bf16[1024,512]{1,0:T(8,128)(2,1)}, u32[]{:S(2)}, u32[]{:S(2)}) collective-permute-start(bf16[1024,512]{1,0:T(8,128)(2,1)} %multiply_convert_fusion.8.refs_0_), channel_id=1, source_target_pairs={{0,2},{1,3},{2,0},{3,1},{4,6},{5,7},{6,4},{7,5},{8,10},{9,11},{10,... | collective-permute-start | bytes 3145736 | tf_op jit(solution)/shard_map/ppermute | solution.py:68
  285.3 44.2 %collective-permute-start.5 = (bf16[1024,512]{1,0:T(8,128)(2,1)}, bf16[1024,512]{1,0:T(8,128)(2,1)}, u32[]{:S(2)}, u32[]{:S(2)}) collective-permute-start(bf16[1024,512]{1,0:T(8,128)(2,1)} %multiply_convert_fusion.8.refs_0_), channel_id=1, source_target_pairs={{0,3},{1,2},{2,1},{3,0},{4,7},{5,6},{6,5},{7,4},{8,11},{9,10},{10,... | collective-permute-start | bytes 3145736 | tf_op jit(solution)/shard_map/ppermute | solution.py:68
  365.2 158.7 %copy-start.92 = (s32[4,4,1024]{2,1,0:T(4,128)}, s32[4,4,1024]{2,1,0:T(4,128)S(1)}, u32[]{:S(2)}) copy-start(s32[4,4,1024]{2,1,0:T(4,128)S(1)} %fusion.46) | copy-start | bytes 196612
  388.9 149.8 %all-to-all-start.3 = ((bf16[4,2048,512]{2,1,0:T(8,128)(2,1)}), bf16[4,2048,512]{2,1,0:T(8,128)(2,1)}, u32[]{:S(2)}, u32[]{:S(2)}) async-start(bf16[4,2048,512]{2,1,0:T(8,128)(2,1)} %bitcast.404), calls=%async_computation.4 | async-start | bytes 16777216 | tf_op jit(solution)/shard_map/all_to_all | solution.py:422
  394.9 268.1 %all-gather.18.cloned.1.call-start = ((), (), s32[]{:S(2)}) async-start(), calls=%async_computation.26 | async-start | bytes 9732096 | tf_op jit(solution)/shard_map/all_gather | solution.py:631
  446.0 50.5 %collective-permute-start.10 = (bf16[4,352,256]{2,1,0:T(8,128)(2,1)}, bf16[4,352,256]{2,1,0:T(8,128)(2,1)S(1)}, u32[]{:S(2)}, u32[]{:S(2)}) collective-permute-start(bf16[4,352,256]{2,1,0:T(8,128)(2,1)} %get-tuple-element.269), channel_id=1, source_target_pairs={{0,24},{4,28},{8,16},{12,20},{16,8},{20,12},{24,0},{28,4},{1,25},{... | collective-permute-start | bytes 2162696 | tf_op jit(solution)/shard_map/ppermute | solution.py:73
  448.5 62.0 %collective-permute-start.9 = (bf16[4,352,256]{2,1,0:T(8,128)(2,1)S(1)}, bf16[4,352,256]{2,1,0:T(8,128)(2,1)}, u32[]{:S(2)}, u32[]{:S(2)}) collective-permute-start(bf16[4,352,256]{2,1,0:T(8,128)(2,1)S(1)} %get-tuple-element.270), channel_id=1, source_target_pairs={{0,16},{4,20},{8,24},{12,28},{16,0},{20,4},{24,8},{28,12},{1,17},{... | collective-permute-start | bytes 2162696 | tf_op jit(solution)/shard_map/ppermute | solution.py:73
  451.4 59.0 %collective-permute-start.8 = (bf16[4,352,256]{2,1,0:T(8,128)(2,1)S(1)}, bf16[4,352,256]{2,1,0:T(8,128)(2,1)}, u32[]{:S(2)}, u32[]{:S(2)}) collective-permute-start(bf16[4,352,256]{2,1,0:T(8,128)(2,1)S(1)} %get-tuple-element.271), channel_id=1, source_target_pairs={{0,8},{4,12},{8,0},{12,4},{16,24},{20,28},{24,16},{28,20},{1,9},{5... | collective-permute-start | bytes 2162696 | tf_op jit(solution)/shard_map/ppermute | solution.py:73
  513.3 10.7 collective-permute-start.6
  513.4 10.6 collective-permute-start.7
  518.9 18.6 %collective-permute-start.12 = (f32[8,128]{1,0:T(8,128)S(1)}, f32[8,128]{1,0:T(8,128)S(1)}, u32[]{:S(2)}, u32[]{:S(2)}) collective-permute-start(f32[8,128]{1,0:T(8,128)S(1)} %get-tuple-element.291), channel_id=1, source_target_pairs={{0,24},{4,28},{8,16},{12,20},{16,8},{20,12},{24,0},{28,4},{1,25},{... | collective-permute-start | bytes 12296 | tf_op jit(solution)/shard_map/ppermute | solution.py:73
  519.3 18.3 %collective-permute-start.13 = (f32[8,128]{1,0:T(8,128)S(1)}, f32[8,128]{1,0:T(8,128)S(1)}, u32[]{:S(2)}, u32[]{:S(2)}) collective-permute-start(f32[8,128]{1,0:T(8,128)S(1)} %get-tuple-element.290), channel_id=1, source_target_pairs={{0,16},{4,20},{8,24},{12,28},{16,0},{20,4},{24,8},{28,12},{1,17},{... | collective-permute-start | bytes 12296 | tf_op jit(solution)/shard_map/ppermute | solution.py:73
  523.7 13.9 collective-permute-start.14
  552.2 51.1 %collective-permute-start.11 = (bf16[16,352,256]{2,1,0:T(8,128)(2,1)S(1)}, bf16[16,352,256]{2,1,0:T(8,128)(2,1)}, u32[]{:S(2)}, u32[]{:S(2)}) collective-permute-start(bf16[16,352,256]{2,1,0:T(8,128)(2,1)S(1)} %bitcast.400), channel_id=1, source_target_pairs={{0,4},{4,0},{8,12},{12,8},{16,20},{20,16},{24,28},{28,24},{1,5},{5... | collective-permute-start | bytes 8650760 | tf_op jit(solution)/shard_map/ppermute | solution.py:78
  552.3 99.1 %all-to-all-start.4 = ((bf16[4,2048,512]{2,1,0:T(8,128)(2,1)}), bf16[4,2048,512]{2,1,0:T(8,128)(2,1)}, u32[]{:S(2)}, u32[]{:S(2)}) async-start(bf16[4,2048,512]{2,1,0:T(8,128)(2,1)} %bitcast.405), calls=%async_computation.5 | async-start | bytes 16777216 | tf_op jit(solution)/shard_map/all_to_all | solution.py:422
  709.3 98.7 %all-to-all-start.5 = ((bf16[4,2048,512]{2,1,0:T(8,128)(2,1)}), bf16[4,2048,512]{2,1,0:T(8,128)(2,1)}, u32[]{:S(2)}, u32[]{:S(2)}) async-start(bf16[4,2048,512]{2,1,0:T(8,128)(2,1)} %bitcast.406), calls=%async_computation.6 | async-start | bytes 16777216 | tf_op jit(solution)/shard_map/all_to_all | solution.py:422
  715.6 182.0 %reduce-scatter.8.cloned.1.call-start = ((), (), s32[]{:S(2)}) async-start(), calls=%async_computation.18 | async-start | bytes 5242880 | tf_op jit(solution)/shard_map/reduce_scatter | solution.py:409
  717.1 82.1 %collective-permute-start.17 = (f32[8,128]{1,0:T(8,128)S(1)}, f32[8,128]{1,0:T(8,128)S(1)}, u32[]{:S(2)}, u32[]{:S(2)}) collective-permute-start(f32[8,128]{1,0:T(8,128)S(1)} %get-tuple-element.295), channel_id=1, source_target_pairs={{0,24},{4,28},{8,16},{12,20},{16,8},{20,12},{24,0},{28,4},{1,25},{... | collective-permute-start | bytes 12296 | tf_op jit(solution)/shard_map/ppermute | solution.py:73
  718.6 80.6 %collective-permute-start.16 = (f32[8,128]{1,0:T(8,128)S(1)}, f32[8,128]{1,0:T(8,128)S(1)}, u32[]{:S(2)}, u32[]{:S(2)}) collective-permute-start(f32[8,128]{1,0:T(8,128)S(1)} %get-tuple-element.296), channel_id=1, source_target_pairs={{0,16},{4,20},{8,24},{12,28},{16,0},{20,4},{24,8},{28,12},{1,17},{... | collective-permute-start | bytes 12296 | tf_op jit(solution)/shard_map/ppermute | solution.py:73
  720.9 78.3 %collective-permute-start.15 = (f32[8,128]{1,0:T(8,128)S(1)}, f32[8,128]{1,0:T(8,128)S(1)}, u32[]{:S(2)}, u32[]{:S(2)}) collective-permute-start(f32[8,128]{1,0:T(8,128)S(1)} %get-tuple-element.297), channel_id=1, source_target_pairs={{0,8},{4,12},{8,0},{12,4},{16,24},{20,28},{24,16},{28,20},{1,9},{5... | collective-permute-start | bytes 12296 | tf_op jit(solution)/shard_map/ppermute | solution.py:73
  799.2 28.2 %collective-permute-start.20 = (f32[4,8,128]{2,1,0:T(8,128)S(1)}, f32[4,8,128]{2,1,0:T(8,128)S(1)}, u32[]{:S(2)}, u32[]{:S(2)}) collective-permute-start(f32[4,8,128]{2,1,0:T(8,128)S(1)} %get-tuple-element.293), channel_id=1, source_target_pairs={{0,3},{1,2},{2,1},{3,0},{4,7},{5,6},{6,5},{7,4},{8,11},{9,10},{10,... | collective-permute-start | bytes 49160 | tf_op jit(solution)/shard_map/ppermute | solution.py:68
  800.8 26.6 %collective-permute-start.19 = (f32[4,8,128]{2,1,0:T(8,128)S(1)}, f32[4,8,128]{2,1,0:T(8,128)S(1)}, u32[]{:S(2)}, u32[]{:S(2)}) collective-permute-start(f32[4,8,128]{2,1,0:T(8,128)S(1)} %get-tuple-element.293), channel_id=1, source_target_pairs={{0,2},{1,3},{2,0},{3,1},{4,6},{5,7},{6,4},{7,5},{8,10},{9,11},{10,... | collective-permute-start | bytes 49160 | tf_op jit(solution)/shard_map/ppermute | solution.py:68
  800.9 26.6 %collective-permute-start.18 = (f32[4,8,128]{2,1,0:T(8,128)S(1)}, f32[4,8,128]{2,1,0:T(8,128)S(1)}, u32[]{:S(2)}, u32[]{:S(2)}) collective-permute-start(f32[4,8,128]{2,1,0:T(8,128)S(1)} %get-tuple-element.293), channel_id=1, source_target_pairs={{0,1},{1,0},{2,3},{3,2},{4,5},{5,4},{6,7},{7,6},{8,9},{9,8},{10,11... | collective-permute-start | bytes 49160 | tf_op jit(solution)/shard_map/ppermute | solution.py:68
  835.8 97.6 %all-to-all-start.6 = ((bf16[4,2048,512]{2,1,0:T(8,128)(2,1)}), bf16[4,2048,512]{2,1,0:T(8,128)(2,1)}, u32[]{:S(2)}, u32[]{:S(2)}) async-start(bf16[4,2048,512]{2,1,0:T(8,128)(2,1)} %bitcast.407), calls=%async_computation.7 | async-start | bytes 16777216 | tf_op jit(solution)/shard_map/all_to_all | solution.py:422
  841.9 180.7 %reduce-scatter.10.cloned.1.call-start = ((), (), s32[]{:S(2)}) async-start(), calls=%async_computation.19 | async-start | bytes 5242880 | tf_op jit(solution)/shard_map/reduce_scatter | solution.py:409
  962.1 12.1 collective-permute-start.21
  962.1 17.4 %collective-permute-start.22 = (bf16[16,352,256]{2,1,0:T(8,128)(2,1)}, bf16[16,352,256]{2,1,0:T(8,128)(2,1)}, u32[]{:S(2)}, u32[]{:S(2)}) collective-permute-start(bf16[16,352,256]{2,1,0:T(8,128)(2,1)} %get-tuple-element.117), channel_id=1, source_target_pairs={{0,4},{4,0},{8,12},{12,8},{16,20},{20,16},{24,28},{28,24},{1,5},{5... | collective-permute-start | bytes 8650760 | tf_op jit(solution)/shard_map/ppermute | solution.py:78
  962.6 21.3 %collective-permute-start.23 = (bf16[16,352,256]{2,1,0:T(8,128)(2,1)}, bf16[16,352,256]{2,1,0:T(8,128)(2,1)}, u32[]{:S(2)}, u32[]{:S(2)}) collective-permute-start(bf16[16,352,256]{2,1,0:T(8,128)(2,1)} %get-tuple-element.119), channel_id=1, source_target_pairs={{0,4},{4,0},{8,12},{12,8},{16,20},{20,16},{24,28},{28,24},{1,5},{5... | collective-permute-start | bytes 8650760 | tf_op jit(solution)/shard_map/ppermute | solution.py:78
  965.1 60.4 %all-to-all-start.7 = ((bf16[4,1024,512]{2,1,0:T(8,128)(2,1)}), bf16[4,1024,512]{2,1,0:T(8,128)(2,1)}, u32[]{:S(2)}, u32[]{:S(2)}) async-start(bf16[4,1024,512]{2,1,0:T(8,128)(2,1)} %bitcast.409), calls=%async_computation.9 | async-start | bytes 8388608 | tf_op jit(solution)/shard_map/all_to_all | solution.py:422
  1025.4 67.2 %all-to-all-start.8 = ((bf16[4,4,352,256]{3,2,1,0:T(8,128)(2,1)}), bf16[4,4,352,256]{3,2,1,0:T(8,128)(2,1)}, u32[]{:S(2)}, u32[]{:S(2)}) async-start(bf16[4,4,352,256]{3,2,1,0:T(8,128)(2,1)} %bitcast.116), calls=%async_computation.11 | async-start | bytes 5767168 | tf_op jit(solution)/shard_map/all_to_all | solution.py:425
  1030.6 90.0 %all-gather.10.cloned.1.call-start = ((), (), s32[]{:S(2)}) async-start(), calls=%async_computation.20 | async-start | bytes 5242880 | tf_op jit(solution)/shard_map/all_gather | solution.py:414
  1092.6 70.0 %all-to-all-start.9 = ((bf16[4,4,352,256]{3,2,1,0:T(8,128)(2,1)}), bf16[4,4,352,256]{3,2,1,0:T(8,128)(2,1)}, u32[]{:S(2)}, u32[]{:S(2)}) async-start(bf16[4,4,352,256]{3,2,1,0:T(8,128)(2,1)} %bitcast.416), calls=%async_computation.12 | async-start | bytes 5767168 | tf_op jit(solution)/shard_map/all_to_all | solution.py:425
  1100.9 427.4 %reduce-scatter.14.cloned.1.call-start = ((), (), s32[]{:S(2)}) async-start(), calls=%async_computation.22 | async-start | bytes 9732096 | tf_op jit(solution)/shard_map/reduce_scatter | solution.py:781
  1167.3 119.8 %all-to-all-start.10 = ((bf16[4,4,352,256]{3,2,1,0:T(8,128)(2,1)}), bf16[4,4,352,256]{3,2,1,0:T(8,128)(2,1)}, u32[]{:S(2)}, u32[]{:S(2)}) async-start(bf16[4,4,352,256]{3,2,1,0:T(8,128)(2,1)} %bitcast.415), calls=%async_computation.13 | async-start | bytes 5767168 | tf_op jit(solution)/shard_map/all_to_all | solution.py:425
  1175.3 356.4 %reduce-scatter.12.cloned.1.call-start = ((), (), s32[]{:S(2)}) async-start(), calls=%async_computation.21 | async-start | bytes 9879552 | tf_op jit(solution)/shard_map/reduce_scatter | solution.py:781
  1182.4 38.3 %collective-permute-start.26 = (bf16[1024,512]{1,0:T(8,128)(2,1)}, bf16[1024,512]{1,0:T(8,128)(2,1)}, u32[]{:S(2)}, u32[]{:S(2)}) collective-permute-start(bf16[1024,512]{1,0:T(8,128)(2,1)} %get-tuple-element.259), channel_id=1, source_target_pairs={{0,3},{1,2},{2,1},{3,0},{4,7},{5,6},{6,5},{7,4},{8,11},{9,10},{10,... | collective-permute-start | bytes 3145736 | tf_op jit(solution)/shard_map/ppermute | solution.py:68
  1183.9 46.1 %collective-permute-start.25 = (bf16[1024,512]{1,0:T(8,128)(2,1)}, bf16[1024,512]{1,0:T(8,128)(2,1)}, u32[]{:S(2)}, u32[]{:S(2)}) collective-permute-start(bf16[1024,512]{1,0:T(8,128)(2,1)} %get-tuple-element.260), channel_id=1, source_target_pairs={{0,2},{1,3},{2,0},{3,1},{4,6},{5,7},{6,4},{7,5},{8,10},{9,11},{10,... | collective-permute-start | bytes 3145736 | tf_op jit(solution)/shard_map/ppermute | solution.py:68
  1184.4 45.6 %collective-permute-start.24 = (bf16[1024,512]{1,0:T(8,128)(2,1)}, bf16[1024,512]{1,0:T(8,128)(2,1)}, u32[]{:S(2)}, u32[]{:S(2)}) collective-permute-start(bf16[1024,512]{1,0:T(8,128)(2,1)} %get-tuple-element.258), channel_id=1, source_target_pairs={{0,1},{1,0},{2,3},{3,2},{4,5},{5,4},{6,7},{7,6},{8,9},{9,8},{10,11... | collective-permute-start | bytes 3145736 | tf_op jit(solution)/shard_map/ppermute | solution.py:68
  1235.1 27.1 %collective-permute-start.32 = (bf16[1024,512]{1,0:T(8,128)(2,1)S(1)}, bf16[1024,512]{1,0:T(8,128)(2,1)S(1)}, u32[]{:S(2)}, u32[]{:S(2)}) collective-permute-start(bf16[1024,512]{1,0:T(8,128)(2,1)S(1)} %get-tuple-element.256), channel_id=1, source_target_pairs={{0,3},{1,2},{2,1},{3,0},{4,7},{5,6},{6,5},{7,4},{8,11},{9,10},{10,... | collective-permute-start | bytes 3145736 | tf_op jit(solution)/shard_map/ppermute | solution.py:68
  1236.7 46.9 %collective-permute-start.31 = (bf16[1024,512]{1,0:T(8,128)(2,1)S(1)}, bf16[1024,512]{1,0:T(8,128)(2,1)S(1)}, u32[]{:S(2)}, u32[]{:S(2)}) collective-permute-start(bf16[1024,512]{1,0:T(8,128)(2,1)S(1)} %get-tuple-element.257), channel_id=1, source_target_pairs={{0,2},{1,3},{2,0},{3,1},{4,6},{5,7},{6,4},{7,5},{8,10},{9,11},{10,... | collective-permute-start | bytes 3145736 | tf_op jit(solution)/shard_map/ppermute | solution.py:68
  1237.3 46.3 %collective-permute-start.30 = (bf16[1024,512]{1,0:T(8,128)(2,1)S(1)}, bf16[1024,512]{1,0:T(8,128)(2,1)S(1)}, u32[]{:S(2)}, u32[]{:S(2)}) collective-permute-start(bf16[1024,512]{1,0:T(8,128)(2,1)S(1)} %get-tuple-element.255), channel_id=1, source_target_pairs={{0,1},{1,0},{2,3},{3,2},{4,5},{5,4},{6,7},{7,6},{8,9},{9,8},{10,11... | collective-permute-start | bytes 3145736 | tf_op jit(solution)/shard_map/ppermute | solution.py:68
  1319.9 194.6 %all-to-all-start.11 = ((bf16[4,3,4,352,256]{4,3,2,1,0:T(8,128)(2,1)}), bf16[4,3,4,352,256]{4,3,2,1,0:T(8,128)(2,1)}, u32[]{:S(2)}, u32[]{:S(2)}) async-start(bf16[4,3,4,352,256]{4,3,2,1,0:T(8,128)(2,1)} %maximum_bitcast_fusion.1), calls=%async_computation.15 | async-start | bytes 17301504 | tf_op jit(solution)/shard_map/all_to_all | solution.py:422
  1328.5 117.0 %collective-permute-start.27 = (bf16[1024,512]{1,0:T(8,128)(2,1)S(1)}, bf16[1024,512]{1,0:T(8,128)(2,1)S(1)}, u32[]{:S(2)}, u32[]{:S(2)}) collective-permute-start(bf16[1024,512]{1,0:T(8,128)(2,1)S(1)} %copy-done.41), channel_id=1, source_target_pairs={{0,1},{1,0},{2,3},{3,2},{4,5},{5,4},{6,7},{7,6},{8,9},{9,8},{10,11... | collective-permute-start | bytes 3145736 | tf_op jit(solution)/shard_map/ppermute | solution.py:68
  1328.6 140.7 %collective-permute-start.28 = (bf16[1024,512]{1,0:T(8,128)(2,1)S(1)}, bf16[1024,512]{1,0:T(8,128)(2,1)S(1)}, u32[]{:S(2)}, u32[]{:S(2)}) collective-permute-start(bf16[1024,512]{1,0:T(8,128)(2,1)S(1)} %copy-done.41), channel_id=1, source_target_pairs={{0,2},{1,3},{2,0},{3,1},{4,6},{5,7},{6,4},{7,5},{8,10},{9,11},{10,... | collective-permute-start | bytes 3145736 | tf_op jit(solution)/shard_map/ppermute | solution.py:68
  1330.5 139.8 %collective-permute-start.29 = (bf16[1024,512]{1,0:T(8,128)(2,1)S(1)}, bf16[1024,512]{1,0:T(8,128)(2,1)}, u32[]{:S(2)}, u32[]{:S(2)}) collective-permute-start(bf16[1024,512]{1,0:T(8,128)(2,1)S(1)} %copy-done.41), channel_id=1, source_target_pairs={{0,3},{1,2},{2,1},{3,0},{4,7},{5,6},{6,5},{7,4},{8,11},{9,10},{10,... | collective-permute-start | bytes 3145736 | tf_op jit(solution)/shard_map/ppermute | solution.py:68
  1332.0 158.5 %collective-permute-start.33 = (bf16[1024,512]{1,0:T(8,128)(2,1)S(1)}, bf16[1024,512]{1,0:T(8,128)(2,1)S(1)}, u32[]{:S(2)}, u32[]{:S(2)}) collective-permute-start(bf16[1024,512]{1,0:T(8,128)(2,1)S(1)} %copy-done.40), channel_id=1, source_target_pairs={{0,1},{1,0},{2,3},{3,2},{4,5},{5,4},{6,7},{7,6},{8,9},{9,8},{10,11... | collective-permute-start | bytes 3145736 | tf_op jit(solution)/shard_map/ppermute | solution.py:68
  1332.1 159.8 %collective-permute-start.34 = (bf16[1024,512]{1,0:T(8,128)(2,1)S(1)}, bf16[1024,512]{1,0:T(8,128)(2,1)}, u32[]{:S(2)}, u32[]{:S(2)}) collective-permute-start(bf16[1024,512]{1,0:T(8,128)(2,1)S(1)} %copy-done.40), channel_id=1, source_target_pairs={{0,2},{1,3},{2,0},{3,1},{4,6},{5,7},{6,4},{7,5},{8,10},{9,11},{10,... | collective-permute-start | bytes 3145736 | tf_op jit(solution)/shard_map/ppermute | solution.py:68
  1445.5 62.8 %collective-permute-start.35 = (bf16[1024,512]{1,0:T(8,128)(2,1)S(1)}, bf16[1024,512]{1,0:T(8,128)(2,1)}, u32[]{:S(2)}, u32[]{:S(2)}) collective-permute-start(bf16[1024,512]{1,0:T(8,128)(2,1)S(1)} %copy-done.40), channel_id=1, source_target_pairs={{0,3},{1,2},{2,1},{3,0},{4,7},{5,6},{6,5},{7,4},{8,11},{9,10},{10,... | collective-permute-start | bytes 3145736 | tf_op jit(solution)/shard_map/ppermute | solution.py:68
  1534.0 9.0 collective-permute-start.38
  1535.5 9.8 collective-permute-start.37
  1537.0 8.3 collective-permute-start.36
  (111 other events, 882.8 us)
Sparse Core Ops, SparseCore 0:
  20.3 86.0 all-gather.11
  212.3 52.5 reduce-scatter.5
  282.8 79.3 all-gather.13
  363.7 79.3 all-gather.15
  513.5 83.8 all-gather.17
  820.5 77.1 reduce-scatter.7
  945.6 76.9 reduce-scatter.9
  1050.6 53.4 all-gather.9
  1162.8 149.8 reduce-scatter.13
  1314.9 93.8 reduce-scatter.11

commit v8 on v7

--- a/solution.py
+++ b/solution.py
@@ -145,29 +145,38 @@
     )(ids, grad_in.reshape(2, ffe, width), grad_out)
 
 
-def home_gradients(lay, pieces, f_loc, d_loc):
-    def kernel(piece_ref, in_ref, out_ref):
-        in_ref[0] = piece_ref[0, :2, 0].astype(F32)
-        out_ref[0] = piece_ref[0, 2, 0].astype(F32)
-
-    spec = pl.BlockSpec((1, 3, 1, f_loc, d_loc), lambda e: (e % lay.t, 0, e // lay.t, 0, 0))
+def home_gradients(lay, ids, parts, f_loc, d_loc):
+    def kernel(ids_ref, *refs):
+        sources, (in_ref, out_ref) = refs[: 3 * lay.t], refs[3 * lay.t :]
+        for k in range(lay.t):
+
+            @pl.when((pl.program_id(1) ^ ids_ref[2]) == k)
+            def _(k=k):
+                for g in range(2):
+                    in_ref[0, g] = sources[g * lay.t + k][0].astype(F32)
+                out_ref[0] = sources[2 * lay.t + k][0].astype(F32)
+
     grad_in, grad_out = pl.pallas_call(
         kernel,
         out_shape=(
             jax.ShapeDtypeStruct((EXPERTS, 2, f_loc, d_loc), F32),
             jax.ShapeDtypeStruct((EXPERTS, f_loc, d_loc), F32),
         ),
-        grid=(EXPERTS,),
-        in_specs=[spec],
-        out_specs=(
-            pl.BlockSpec((1, 2, f_loc, d_loc), lambda e: (e, 0, 0, 0)),
-            pl.BlockSpec((1, f_loc, d_loc), lambda e: (e, 0, 0)),
+        grid_spec=pltpu.PrefetchScalarGridSpec(
+            num_scalar_prefetch=1,
+            grid=(lay.z, lay.t),
+            in_specs=[pl.BlockSpec((1, f_loc, d_loc), lambda z, t, ids: (z, 0, 0))] * (3 * lay.t),
+            out_specs=(
+                pl.BlockSpec((1, 2, f_loc, d_loc), lambda z, t, ids: (z * lay.t + t, 0, 0, 0)),
+                pl.BlockSpec((1, f_loc, d_loc), lambda z, t, ids: (z * lay.t + t, 0, 0)),
+            ),
         ),
         cost_estimate=pl.CostEstimate(
             flops=0, bytes_accessed=18 * EXPERTS * f_loc * d_loc, transcendentals=0
         ),
+        compiler_params=pltpu.CompilerParams(vmem_limit_bytes=32 << 20),
         name="home_gradients",
-    )(pieces)
+    )(ids, *[piece for part in parts for piece in part])
     return jnp.swapaxes(grad_in, 2, 3), grad_out
 
 
@@ -603,12 +612,22 @@
     ffn_all = gather_z(ffn_part)
     ffn_low = gather_t_direct(ffn_part)
     ffn_all, ffn_low, cot_ready = lax.optimization_barrier((ffn_all, ffn_low, cot_part))
-    picked = pick_rows(ffn_all)
+    picked, by_plane[0], by_plane[1] = lax.optimization_barrier(
+        (pick_rows(ffn_all), by_plane[0], by_plane[1])
+    )
     expert_rows = send_out(picked)
     shared_pack = jnp.concatenate(
         [jnp.swapaxes(w_shared_in, 1, 2).reshape(-1, d_loc), w_shared_out], 0
     )
-    cot_all, last_column = lax.optimization_barrier((gather_z(cot_ready), by_column[2]))
+    def own_weights(matrices, order):
+        pieces = [by_plane[g].reshape(nz * nt, f_loc, d_loc) for g in matrices]
+        stacks = [lay.over_c(piece, k) for k in range(nq) for piece in pieces]
+        return lay_out_weights(lay, order, stacks, f_loc, d_loc, width)
+
+    own_in = own_weights((0, 1), ids * jnp.array([0, 1, 1], jnp.int32))
+    cot_all, last_column, own_in = lax.optimization_barrier(
+        (gather_z(cot_ready), by_column[2], own_in)
+    )
     by_plane.append(
         jnp.stack(
             [
@@ -618,12 +637,6 @@
         )
     )
 
-    def own_weights(matrices, order):
-        pieces = [by_plane[g].reshape(nz * nt, f_loc, d_loc) for g in matrices]
-        stacks = [lay.over_c(piece, k) for k in range(nq) for piece in pieces]
-        return lay_out_weights(lay, order, stacks, f_loc, d_loc, width)
-
-    own_in = own_weights((0, 1), ids * jnp.array([0, 1, 1], jnp.int32))
     by_plane[2], shared_pack, cot_picked = lax.optimization_barrier(
         (by_plane[2], shared_pack, pick_rows(cot_all))
     )
@@ -667,6 +680,7 @@
         1,
     ).astype(BF16)
     gated_active = (active.astype(F32) * gate_rows).astype(BF16)
+    out_parts, pre_low = lax.optimization_barrier((out_parts, pre_low))
     rows_grad = dot(pre_low, own_in).astype(BF16)
     rows_grad, out_parts = lax.optimization_barrier((rows_grad, out_parts))
     grad_parts = send_back(rows_grad)
@@ -800,8 +814,21 @@
         heads,
         score_scale,
     )
-    query_turned_grad, grad_plane[1], shared_full, shared_grads = lax.optimization_barrier(
-        (query_turned_grad, grad_plane[1], shared_full, shared_grads)
+    def to_columns(values):
+        return [
+            lay.over_t(lax.dynamic_index_in_dim(values, me_t ^ k, 1, keepdims=False), k)
+            for k in range(nt)
+        ]
+
+    grad_home = [to_columns(grad_plane[0]), None, None]
+    (
+        query_turned_grad,
+        grad_plane[1],
+        grad_home[0],
+        shared_full,
+        shared_grads,
+    ) = lax.optimization_barrier(
+        (query_turned_grad, grad_plane[1], grad_home[0], shared_full, shared_grads)
     )
     shared_sum = sum_dp(shared_grads)
     turned_first, turned_second = rotate_back(
@@ -828,8 +855,8 @@
         (dot(query_grad, query_t) + dot(down_grad, down_t), scatter_t_direct(shared_full))
     )
     output = gather_t_direct((residual + routed + shared_part).astype(BF16))
-    normed_grad, grad_plane[2] = lax.optimization_barrier(
-        (scatter_t_direct(normed_full), grad_plane[2])
+    normed_grad, grad_plane[2], grad_home[1] = lax.optimization_barrier(
+        (scatter_t_direct(normed_full), grad_plane[2], to_columns(grad_plane[1]))
     )
     attn_hat = own_part(hidden).astype(F32) * attn_inverse
     scaled_in = lax.dynamic_slice_in_dim(attn_scale, me_t * part, part, 0) * normed_grad
@@ -837,9 +864,9 @@
     input_grad = residual_grad + attn_inverse * (
         scaled_in - attn_hat * row_mean(attn_hat * scaled_in)
     )
-    input_low, grad_plane = lax.optimization_barrier((input_grad.astype(BF16), grad_plane))
-    grad_home = swap_t(jnp.transpose(jnp.stack(grad_plane), (2, 0, 1, 3, 4)))
-    grad_expert_in, grad_expert_out = home_gradients(lay, grad_home, f_loc, d_loc)
+    input_low, grad_plane[2] = lax.optimization_barrier((input_grad.astype(BF16), grad_plane[2]))
+    grad_home[2] = to_columns(grad_plane[2])
+    grad_expert_in, grad_expert_out = home_gradients(lay, ids, grad_home, f_loc, d_loc)
     grad_hidden = gather_t_direct(input_low)
 
     def spread(values):

time: 1580 us -> 1510 us (0.956)
  waiting for transfers between devices: 645 us -> 592 us
    ppermute x21 -> x30, waiting for transfers between devices: 251 us -> 212 us  [over_t(): return lax.ppermute(values, 'tensor', [(i, i ^ k) for i in range(self.t)])]
    all_to_all x7 -> x6, waiting for transfers between devices: 78.6 us -> 90.5 us  [swap_t(): lax.all_to_all(values, 'tensor', split_axis=0, concat_axis=0, tiled=True)]
    ppermute x21 -> x30, starting transfers between devices: 26 us -> 36.8 us  [over_t(): return lax.ppermute(values, 'tensor', [(i, i ^ k) for i in range(self.t)])]
    all_to_all x7 -> x6, starting transfers between devices: 45.9 us -> 37.3 us  [swap_t(): lax.all_to_all(values, 'tensor', split_axis=0, concat_axis=0, tiled=True)]
    unnamed x252 -> x254, local copies, waits for them, and re-layouts: 45.3 us -> 47.3 us
  transfers between devices with their start and end apart: 61 -> 69, of which waited for: 30 -> 39; matrix products, arithmetic and copies ran while one was open for 34% -> 37% of each run, Pallas kernels for 7% -> 7%
where the time goes in v8:
time: 1510 us; the launch traced here: 1500 us
  waiting for transfers between devices  592 us (39%)
  matrix products  322 us (21%)
  local copies, waits for them, and re-layouts  200 us (13%)
  starting transfers between devices  127 us (8%)
  other arithmetic  110 us (7%)
  Pallas kernels  106 us (7%)
  blocking collectives  24.3 us (2%)
  between operations  16.9 us (1%)
    ppermute x30, waiting for transfers between devices, over_t(): return lax.ppermute(values, 'tensor', [(i, i ^ k) for i in range(self.t)])  212 us
    dot_general x9, matrix products, dot_nt(): lax.dot_general(a, b, (((1,), (1,)), ((), ())), preferred_element_type=F32)  99.5 us
    all_to_all x6, waiting for transfers between devices, swap_t(): lax.all_to_all(values, 'tensor', split_axis=0, concat_axis=0, tiled=True)  90.5 us
    dot_general x9, matrix products, dot(): return jnp.dot(a, b, preferred_element_type=F32)  79.7 us
    dot_general x8, matrix products, dot_tn(): lax.dot_general(a, b, (((0,), (0,)), ((), ())), preferred_element_type=F32)  78.5 us
    all_gather x2, waiting for transfers between devices, gather_z(): lax.all_gather(values, 'dp', axis=0, tiled=False, axis_index_groups=lay.z...  59.9 us
    all_gather x1, waiting for transfers between devices, body(): front = lax.all_gather(front_pack, 'dp', axis=0, tiled=False)  55.1 us
    all_to_all x5, waiting for transfers between devices, swap_z(): lax.all_to_all(values, 'dp', split_axis=0, concat_axis=0, axis_index_grou...  52.5 us
  transfers between devices with their start and end apart: 69, of which 39 were waited for; matrix products, arithmetic and copies ran while one was open for 37% of the time, Pallas kernels for 7%

profile of v8, /device:TPU:10, one launch (start us, length us, event | category | flops | bytes accessed | tf_op | source)
XLA Modules:
  0.0 1498.0 jit_solution(6261555589824080590)
XLA Ops:
  20.2 6.9 maximum_bitcast_fusion
  27.1 8.3 copy.295
  35.4 6.5 all-to-all-start
  51.3 55.1 %all-gather.12.cloned.1.call-done = bf16[17152,256]{1,0:T(8,128)(2,1)} async-done(((bf16[2144,256]{1,0:T(8,128)(2,1)}), bf16[17152,256]{1,0:T(8,128)(2,1)}) %all-gather.12.cloned.1.call-update) | async-done | bytes 8781840 | tf_op jit(solution)/shard_map/all_gather | solution.py:495
  117.3 19.3 %all-to-all-done = bf16[4,4,3,352,256]{4,3,1,2,0:T(8,128)(2,1)} async-done(((bf16[4,4,3,352,256]{4,3,1,2,0:T(8,128)(2,1)}), bf16[4,4,3,352,256]{4,3,1,2,0:T(8,128)(2,1)}, u32[]{:S(2)}, u32[]{:S(2)}) %all-to-all-start) | async-done | bytes 8650784 | tf_op jit(solution)/shard_map/all_to_all | solution.py:431
  162.4 6.4 fusion.118
  190.7 14.7 attend.1
  221.7 43.1 %reduce-scatter.6.cloned.1.call-done = bf16[1024,512]{1,0:T(8,128)(2,1)} async-done(((bf16[1024,2048]{1,0:T(8,128)(2,1)}), bf16[1024,512]{1,0:T(8,128)(2,1)}) %reduce-scatter.6.cloned.1.call-update) | async-done | bytes 1048592 | tf_op jit(solution)/shard_map/reduce_scatter | solution.py:426
  266.8 8.1 psum.21
  292.5 17.2 %collective-permute-done.3.refs_1_ = bf16[1024,512]{1,0:T(8,128)(2,1)} collective-permute-done((bf16[1024,512]{1,0:T(8,128)(2,1)}, bf16[1024,512]{1,0:T(8,128)(2,1)}, u32[]{:S(2)}, u32[]{:S(2)}) %collective-permute-start.3) | collective-permute-done | bytes 1048608 | tf_op jit(solution)/shard_map/ppermute | solution.py:68
  309.7 19.9 %collective-permute-done.4.refs_2_ = bf16[1024,512]{1,0:T(8,128)(2,1)} collective-permute-done((bf16[1024,512]{1,0:T(8,128)(2,1)}, bf16[1024,512]{1,0:T(8,128)(2,1)}, u32[]{:S(2)}, u32[]{:S(2)}) %collective-permute-start.4) | collective-permute-done | bytes 1048608 | tf_op jit(solution)/shard_map/ppermute | solution.py:68
  335.8 26.5 %all-gather.14.cloned.1.call-done = bf16[4096,512]{1,0:T(8,128)(2,1)} async-done(((bf16[1024,512]{1,0:T(8,128)(2,1)}), bf16[4096,512]{1,0:T(8,128)(2,1)}) %all-gather.14.cloned.1.call-update) | async-done | bytes 4194320 | tf_op jit(solution)/shard_map/all_gather | solution.py:415
  363.1 16.2 %convert_bitcast_fusion.1 = bf16[4,4,512,512]{3,2,0,1:T(8,128)(2,1)} fusion(s32[4,4,1024]{2,1,0:T(4,128)S(1)} %fusion.46, bf16[4,1024,512]{2,1,0:T(8,128)(2,1)} %bitcast.537), kind=kOutput, calls=%fused_computation.39 | convolution fusion | flops 8602517504 | bytes 12648448 | tf_op jit(solution)/shard_map/sepk,skd->espd/dot_general | solution.py:528
  379.3 7.5 copy.300
  396.6 13.1 lay_out_weights.2
  409.7 33.4 %all-gather.16.cloned.1.call-done = bf16[4096,512]{1,0:T(8,128)(2,1)} async-done(((bf16[1024,512]{1,0:T(8,128)(2,1)}), bf16[4096,512]{1,0:T(8,128)(2,1)}) %all-gather.16.cloned.1.call-update) | async-done | bytes 4194320 | tf_op jit(solution)/shard_map/all_gather | solution.py:415
  450.7 14.4 convert_bitcast_fusion
  465.1 7.5 copy.303
  472.6 23.1 %collective-permute-done.10 = bf16[4,352,256]{2,1,0:T(8,128)(2,1)S(1)} collective-permute-done((bf16[4,352,256]{2,1,0:T(8,128)(2,1)S(1)}, bf16[4,352,256]{2,1,0:T(8,128)(2,1)S(1)}, u32[]{:S(2)}, u32[]{:S(2)}) %collective-permute-start.10) | collective-permute-done | bytes 720928 | tf_op jit(solution)/shard_map/ppermute | solution.py:73
  495.6 13.9 collective-permute-done.9
  526.2 11.5 copy.301
  539.8 6.4 all-to-all-start.4
  546.2 32.3 %fusion.127 = f32[2048,2816]{1,0:T(8,128)} fusion(bf16[2048,2048]{0,1:T(8,128)(2,1)} %bitcast.437, bf16[2816,2048]{1,0:T(8,128)(2,1)} %bitcast.422), kind=kOutput, calls=%fused_computation.311 | convolution fusion | flops 23622320128 | bytes 42991616 | tf_op jit(solution)/shard_map/dot_general | solution.py:30
  578.5 12.3 fusion.8
  590.8 9.3 lay_out_weights.3
  602.6 15.0 %multiply_convert_fusion = bf16[2048,2048]{1,0:T(8,128)(2,1)} fusion(bf16[2048,1408]{1,0:T(8,128)(2,1)S(1)} %get-tuple-element.266, f32[2048]{0:T(1024)S(1)} %bitcast.507, bf16[1,1408,2048]{2,1,0:T(8,128)(2,1)S(1)} %lay_out_weights.3), kind=kOutput, calls=%fused_computation.5 | convolution fusion | flops 11819548672 | bytes 19931136 | tf_op jit(solution)/shard_map/dot_general | solution.py:26
  617.7 21.2 %all-to-all-done.4 = bf16[4,2048,512]{2,1,0:T(8,128)(2,1)} async-done(((bf16[4,2048,512]{2,1,0:T(8,128)(2,1)}), bf16[4,2048,512]{2,1,0:T(8,128)(2,1)}, u32[]{:S(2)}, u32[]{:S(2)}) %all-to-all-start.4) | async-done | bytes 8388640 | tf_op jit(solution)/shard_map/all_to_all | solution.py:431
  638.9 11.5 copy.310
  657.9 7.4 copy.389
  665.3 6.4 all-to-all-start.5
  671.7 28.3 %multiply_convert_fusion.2 = (bf16[2048,1408]{1,0:T(8,128)(2,1)}, bf16[2048,1408]{1,0:T(8,128)(2,1)}, f32[2048]{0:T(1024)S(1)}) fusion(f32[2048,2816]{1,0:T(8,128)} %fusion.127, f32[2048]{0:T(1024)S(1)} %bitcast.508, bf16[2048,1408]{1,0:T(8,128)(2,1)} %copy-done.36, bf16[2048,2048]{0,1:T(8,128)(2,1)} %bitcast.439, bf16[1,1408,2048]{2,1,0:T(8,128)(2,1)} %copy-done), kind=kOutput, calls=%fused_computation.16 | convolution fusion | flops 11860178944 | bytes 54542336 | tf_op jit(solution)/shard_map/dot_general | solution.py:30
  705.3 8.3 copy.316
  716.8 9.3 fusion.128
  732.1 8.4 fusion.42
  749.3 14.7 all-to-all-done.5
  764.1 31.2 %convolution_convert_fusion.3 = bf16[2048,2048]{1,0:T(8,128)(2,1)} fusion(bf16[2048,2816]{1,0:T(8,128)(2,1)} %pad_maximum_fusion, bf16[2816,2048]{1,0:T(8,128)(2,1)} %bitcast.423), kind=kOutput, calls=%fused_computation.42 | convolution fusion | flops 23626514432 | bytes 31457280 | tf_op jit(solution)/shard_map/dot_general | solution.py:26
  795.3 12.2 bitcast_convert_fusion.1
  809.3 7.2 fusion.129
  817.5 7.4 copy.388
  831.0 18.0 %convolution_convert_fusion.2.out_ref = bf16[1408,2048]{1,0:T(8,128)(2,1)} fusion(bf16[2048,1408]{1,0:T(8,128)(2,1)} %get-tuple-element.124, bf16[2048,2048]{0,1:T(8,128)(2,1)} %bitcast.440), kind=kOutput, calls=%fused_computation.41 | convolution fusion | flops 11814043648 | bytes 19922944 | tf_op jit(solution)/shard_map/dot_general | solution.py:34
  849.0 31.8 %convolution_convert_fusion = bf16[2816,2048]{1,0:T(8,128)(2,1)} fusion(bf16[2048,2816]{1,0:T(8,128)(2,1)} %pad_maximum_fusion, bf16[2048,2048]{0,1:T(8,128)(2,1)} %bitcast.438), kind=kOutput, calls=%fused_computation.20 | convolution fusion | flops 23628087296 | bytes 31457280 | tf_op jit(solution)/shard_map/dot_general | solution.py:34
  886.6 35.2 %all-to-all-done.6 = bf16[4,2048,512]{2,1,0:T(8,128)(2,1)} async-done(((bf16[4,2048,512]{2,1,0:T(8,128)(2,1)}), bf16[4,2048,512]{2,1,0:T(8,128)(2,1)}, u32[]{:S(2)}, u32[]{:S(2)}) %all-to-all-start.6) | async-done | bytes 8388640 | tf_op jit(solution)/shard_map/all_to_all | solution.py:431
  921.9 12.1 bitcast_convert_fusion
  934.0 15.5 %take_apart.1 = (bf16[16,352,256]{2,1,0:T(8,128)(2,1)S(1)}, bf16[16,352,256]{2,1,0:T(8,128)(2,1)S(1)}, bf16[16,352,256]{2,1,0:T(8,128)(2,1)S(1)}, bf16[16,352,25...) custom-call(s32[3]{0:T(128)S(1)} %get-tuple-element.268.ids_ref, ...), custom_call_target="tpu_custom_call" | custom-call | bytes 34603008 | tf_op jit(solution)/shard_map/take_apart/pallas_call | solution.py:128
  977.3 33.1 %reduce-scatter.10.cloned.1.call-done = bf16[1,1024,512]{2,1,0:T(8,128)(2,1)} async-done(((bf16[4,1024,512]{2,1,0:T(8,128)(2,1)}), bf16[1,1024,512]{2,1,0:T(8,128)(2,1)}) %reduce-scatter.10.cloned.1.call-update) | async-done | bytes 1048592 | tf_op jit(solution)/shard_map/reduce_scatter | solution.py:418
  1026.3 8.0 psum.22
  1039.0 41.5 %all-to-all-done.8 = bf16[4,4,352,256]{3,2,1,0:T(8,128)(2,1)} async-done(((bf16[4,4,352,256]{3,2,1,0:T(8,128)(2,1)}), bf16[4,4,352,256]{3,2,1,0:T(8,128)(2,1)}, u32[]{:S(2)}, u32[]{:S(2)}) %all-to-all-start.8) | async-done | bytes 2883616 | tf_op jit(solution)/shard_map/all_to_all | solution.py:434
  1080.4 8.3 all-to-all-start.9
  1097.0 7.4 convolution_convert_fusion.1
  1120.3 21.8 %attend_back.1 = (bf16[1024,512]{1,0:T(8,128)(2,1)S(1)}, f32[1024,256]{1,0:T(8,128)S(1)}, bf16[1024,1024]{1,0:T(8,128)(2,1)S(1)}, f32[1024,256]{1,0:T(8,128)S(1)}) custom-call(s32[1]{0:T(128)} %copy.410.len_ref, bf16[1024,512]{1,0:T(8,128)(2,1)S(1)} %copy-done.5, bf16[1024,256]{1,0:T(8,128)(2,1)S(1)} %copy-done.9, bf16[1024,1024]{1,0:T(8,128)(2,1)S(1)} %copy-done.13, ...), custom_call_target="tpu_custom_call" | custom-call | flops 6710886400 | bytes 33554432 | tf_op jit(solution)/shard_map/attend_back/pallas_call | solution.py:330
  1156.0 8.1 all-to-all-start.10
  1195.7 11.5 collective-permute-done.29
  1207.2 20.2 %collective-permute-done.28 = bf16[1024,512]{1,0:T(8,128)(2,1)S(1)} collective-permute-done((bf16[1024,512]{1,0:T(8,128)(2,1)S(1)}, bf16[1024,512]{1,0:T(8,128)(2,1)S(1)}, u32[]{:S(2)}, u32[]{:S(2)}) %collective-permute-start.28) | collective-permute-done | bytes 1048608 | tf_op jit(solution)/shard_map/ppermute | solution.py:68
  1250.5 9.4 collective-permute-done.35
  1267.0 14.5 collective-permute-done.34
  1286.2 10.8 collective-permute-done.36.refs_5_
  1297.8 14.6 collective-permute-done.38.refs_7_
  1322.2 8.2 psum.23
  1344.9 33.0 %collective-permute-done.45.refs_9_ = bf16[4,352,256]{2,1,0:T(8,128)(2,1)S(1)} collective-permute-done((bf16[4,352,256]{2,1,0:T(8,128)(2,1)S(1)}, bf16[4,352,256]{2,1,0:T(8,128)(2,1)S(1)}, u32[]{:S(2)}, u32[]{:S(2)}) %collective-permute-start.45) | collective-permute-done | bytes 720928 | tf_op jit(solution)/shard_map/ppermute | solution.py:68
  1380.8 13.5 collective-permute-done.47.refs_11_
  1398.3 13.5 home_gradients.1
  1411.8 7.4 collective-permute-done.31.refs_2_
  1426.4 12.1 collective-permute-done.39.refs_1_
  1438.5 23.1 %collective-permute-done.40.refs_2_ = bf16[1024,512]{1,0:T(8,128)(2,1)} collective-permute-done((bf16[1024,512]{1,0:T(8,128)(2,1)}, bf16[1024,512]{1,0:T(8,128)(2,1)}, u32[]{:S(2)}, u32[]{:S(2)}) %collective-permute-start.40) | collective-permute-done | bytes 1048608 | tf_op jit(solution)/shard_map/ppermute | solution.py:68
  (528 shorter events, 426.7 us)
Async XLA Ops:
  7.2 99.3 %all-gather.12.cloned.1.call-start = ((), (), s32[]{:S(2)}) async-start(), calls=%async_computation.22 | async-start | bytes 9879552 | tf_op jit(solution)/shard_map/all_gather | solution.py:495
  35.4 101.3 %all-to-all-start = ((bf16[4,4,3,352,256]{4,3,1,2,0:T(8,128)(2,1)}), bf16[4,4,3,352,256]{4,3,1,2,0:T(8,128)(2,1)}, u32[]{:S(2)}, u32[]{:S(2)}) async-start(bf16[4,4,3,352,256]{4,3,1,2,0:T(8,128)(2,1)} %copy.295), calls=%async_computation | async-start | bytes 17301504 | tf_op jit(solution)/shard_map/all_to_all | solution.py:431
  41.9 9.0 collective-permute-start
  143.9 68.2 %all-to-all-start.1 = ((bf16[4,4,352,256]{3,2,1,0:T(8,128)(2,1)}), bf16[4,4,352,256]{3,2,1,0:T(8,128)(2,1)S(1)}, u32[]{:S(2)}, u32[]{:S(2)}) async-start(bf16[4,4,352,256]{3,2,1,0:T(8,128)(2,1)} %copy.297), calls=%async_computation.1 | async-start | bytes 5767168 | tf_op jit(solution)/shard_map/all_to_all | solution.py:434
  149.2 115.6 %reduce-scatter.6.cloned.1.call-start = ((), (), s32[]{:S(2)}) async-start(), calls=%async_computation.16 | async-start | bytes 5242880 | tf_op jit(solution)/shard_map/reduce_scatter | solution.py:426
  215.7 67.0 %all-to-all-start.2 = ((bf16[4,4,352,256]{3,2,1,0:T(8,128)(2,1)}), bf16[4,4,352,256]{3,2,1,0:T(8,128)(2,1)}, u32[]{:S(2)}, u32[]{:S(2)}) async-start(bf16[4,4,352,256]{3,2,1,0:T(8,128)(2,1)} %copy.298), calls=%async_computation.3 | async-start | bytes 5767168 | tf_op jit(solution)/shard_map/all_to_all | solution.py:434
  221.6 140.7 %all-gather.14.cloned.1.call-start = ((), (), s32[]{:S(2)}) async-start(), calls=%async_computation.23 | async-start | bytes 5242880 | tf_op jit(solution)/shard_map/all_gather | solution.py:415
  282.7 160.4 %all-gather.16.cloned.1.call-start = ((), (), s32[]{:S(2)}) async-start(), calls=%async_computation.24 | async-start | bytes 5242880 | tf_op jit(solution)/shard_map/all_gather | solution.py:415
  283.2 26.5 %collective-permute-start.3 = (bf16[1024,512]{1,0:T(8,128)(2,1)}, bf16[1024,512]{1,0:T(8,128)(2,1)}, u32[]{:S(2)}, u32[]{:S(2)}) collective-permute-start(bf16[1024,512]{1,0:T(8,128)(2,1)} %multiply_convert_fusion.8.refs_0_), channel_id=1, source_target_pairs={{0,1},{1,0},{2,3},{3,2},{4,5},{5,4},{6,7},{7,6},{8,9},{9,8},{10,11... | collective-permute-start | bytes 3145736 | tf_op jit(solution)/shard_map/ppermute | solution.py:68
  284.1 45.5 %collective-permute-start.4 = (bf16[1024,512]{1,0:T(8,128)(2,1)}, bf16[1024,512]{1,0:T(8,128)(2,1)}, u32[]{:S(2)}, u32[]{:S(2)}) collective-permute-start(bf16[1024,512]{1,0:T(8,128)(2,1)} %multiply_convert_fusion.8.refs_0_), channel_id=1, source_target_pairs={{0,2},{1,3},{2,0},{3,1},{4,6},{5,7},{6,4},{7,5},{8,10},{9,11},{10,... | collective-permute-start | bytes 3145736 | tf_op jit(solution)/shard_map/ppermute | solution.py:68
  285.4 44.2 %collective-permute-start.5 = (bf16[1024,512]{1,0:T(8,128)(2,1)}, bf16[1024,512]{1,0:T(8,128)(2,1)}, u32[]{:S(2)}, u32[]{:S(2)}) collective-permute-start(bf16[1024,512]{1,0:T(8,128)(2,1)} %multiply_convert_fusion.8.refs_0_), channel_id=1, source_target_pairs={{0,3},{1,2},{2,1},{3,0},{4,7},{5,6},{6,5},{7,4},{8,11},{9,10},{10,... | collective-permute-start | bytes 3145736 | tf_op jit(solution)/shard_map/ppermute | solution.py:68
  386.8 9.5 collective-permute-start.6
  386.8 9.7 collective-permute-start.7
  389.6 136.6 %all-to-all-start.3 = ((bf16[4,2048,512]{2,1,0:T(8,128)(2,1)}), bf16[4,2048,512]{2,1,0:T(8,128)(2,1)}, u32[]{:S(2)}, u32[]{:S(2)}) async-start(bf16[4,2048,512]{2,1,0:T(8,128)(2,1)} %bitcast.416), calls=%async_computation.4 | async-start | bytes 16777216 | tf_op jit(solution)/shard_map/all_to_all | solution.py:431
  395.5 254.8 %all-gather.18.cloned.1.call-start = ((), (), s32[]{:S(2)}) async-start(), calls=%async_computation.25 | async-start | bytes 9732096 | tf_op jit(solution)/shard_map/all_gather | solution.py:644
  445.2 50.4 %collective-permute-start.10 = (bf16[4,352,256]{2,1,0:T(8,128)(2,1)S(1)}, bf16[4,352,256]{2,1,0:T(8,128)(2,1)S(1)}, u32[]{:S(2)}, u32[]{:S(2)}) collective-permute-start(bf16[4,352,256]{2,1,0:T(8,128)(2,1)S(1)} %get-tuple-element.305), channel_id=1, source_target_pairs={{0,24},{4,28},{8,16},{12,20},{16,8},{20,12},{24,0},{28,4},{1,25},{... | collective-permute-start | bytes 2162696 | tf_op jit(solution)/shard_map/ppermute | solution.py:73
  447.8 61.7 %collective-permute-start.9 = (bf16[4,352,256]{2,1,0:T(8,128)(2,1)S(1)}, bf16[4,352,256]{2,1,0:T(8,128)(2,1)S(1)}, u32[]{:S(2)}, u32[]{:S(2)}) collective-permute-start(bf16[4,352,256]{2,1,0:T(8,128)(2,1)S(1)} %get-tuple-element.306), channel_id=1, source_target_pairs={{0,16},{4,20},{8,24},{12,28},{16,0},{20,4},{24,8},{28,12},{1,17},{... | collective-permute-start | bytes 2162696 | tf_op jit(solution)/shard_map/ppermute | solution.py:73
  450.7 58.8 %collective-permute-start.8 = (bf16[4,352,256]{2,1,0:T(8,128)(2,1)S(1)}, bf16[4,352,256]{2,1,0:T(8,128)(2,1)S(1)}, u32[]{:S(2)}, u32[]{:S(2)}) collective-permute-start(bf16[4,352,256]{2,1,0:T(8,128)(2,1)S(1)} %get-tuple-element.307), channel_id=1, source_target_pairs={{0,8},{4,12},{8,0},{12,4},{16,24},{20,28},{24,16},{28,20},{1,9},{5... | collective-permute-start | bytes 2162696 | tf_op jit(solution)/shard_map/ppermute | solution.py:73
  539.7 51.2 %collective-permute-start.11 = (bf16[16,352,256]{2,1,0:T(8,128)(2,1)S(1)}, bf16[16,352,256]{2,1,0:T(8,128)(2,1)}, u32[]{:S(2)}, u32[]{:S(2)}) collective-permute-start(bf16[16,352,256]{2,1,0:T(8,128)(2,1)S(1)} %bitcast.414), channel_id=1, source_target_pairs={{0,4},{4,0},{8,12},{12,8},{16,20},{20,16},{24,28},{28,24},{1,5},{5... | collective-permute-start | bytes 8650760 | tf_op jit(solution)/shard_map/ppermute | solution.py:78
  539.8 99.1 %all-to-all-start.4 = ((bf16[4,2048,512]{2,1,0:T(8,128)(2,1)}), bf16[4,2048,512]{2,1,0:T(8,128)(2,1)}, u32[]{:S(2)}, u32[]{:S(2)}) async-start(bf16[4,2048,512]{2,1,0:T(8,128)(2,1)} %bitcast.417), calls=%async_computation.5 | async-start | bytes 16777216 | tf_op jit(solution)/shard_map/all_to_all | solution.py:431
  665.3 98.8 %all-to-all-start.5 = ((bf16[4,2048,512]{2,1,0:T(8,128)(2,1)}), bf16[4,2048,512]{2,1,0:T(8,128)(2,1)}, u32[]{:S(2)}, u32[]{:S(2)}) async-start(bf16[4,2048,512]{2,1,0:T(8,128)(2,1)} %bitcast.418), calls=%async_computation.6 | async-start | bytes 16777216 | tf_op jit(solution)/shard_map/all_to_all | solution.py:431
  671.7 212.1 %reduce-scatter.8.cloned.1.call-start = ((), (), s32[]{:S(2)}) async-start(), calls=%async_computation.17 | async-start | bytes 5242880 | tf_op jit(solution)/shard_map/reduce_scatter | solution.py:418
  701.5 44.2 %collective-permute-start.17 = (f32[8,128]{1,0:T(8,128)S(1)}, f32[8,128]{1,0:T(8,128)S(1)}, u32[]{:S(2)}, u32[]{:S(2)}) collective-permute-start(f32[8,128]{1,0:T(8,128)S(1)} %get-tuple-element.331), channel_id=1, source_target_pairs={{0,24},{4,28},{8,16},{12,20},{16,8},{20,12},{24,0},{28,4},{1,25},{... | collective-permute-start | bytes 12296 | tf_op jit(solution)/shard_map/ppermute | solution.py:73
  703.4 42.4 %collective-permute-start.16 = (f32[8,128]{1,0:T(8,128)S(1)}, f32[8,128]{1,0:T(8,128)S(1)}, u32[]{:S(2)}, u32[]{:S(2)}) collective-permute-start(f32[8,128]{1,0:T(8,128)S(1)} %get-tuple-element.332), channel_id=1, source_target_pairs={{0,16},{4,20},{8,24},{12,28},{16,0},{20,4},{24,8},{28,12},{1,17},{... | collective-permute-start | bytes 12296 | tf_op jit(solution)/shard_map/ppermute | solution.py:73
  705.3 40.4 %collective-permute-start.15 = (f32[8,128]{1,0:T(8,128)S(1)}, f32[8,128]{1,0:T(8,128)S(1)}, u32[]{:S(2)}, u32[]{:S(2)}) collective-permute-start(f32[8,128]{1,0:T(8,128)S(1)} %get-tuple-element.333), channel_id=1, source_target_pairs={{0,8},{4,12},{8,0},{12,4},{16,24},{20,28},{24,16},{28,20},{1,9},{5... | collective-permute-start | bytes 12296 | tf_op jit(solution)/shard_map/ppermute | solution.py:73
  745.8 70.8 %collective-permute-start.20 = (f32[4,8,128]{2,1,0:T(8,128)S(1)}, f32[4,8,128]{2,1,0:T(8,128)S(1)}, u32[]{:S(2)}, u32[]{:S(2)}) collective-permute-start(f32[4,8,128]{2,1,0:T(8,128)S(1)} %get-tuple-element.329), channel_id=1, source_target_pairs={{0,3},{1,2},{2,1},{3,0},{4,7},{5,6},{6,5},{7,4},{8,11},{9,10},{10,... | collective-permute-start | bytes 49160 | tf_op jit(solution)/shard_map/ppermute | solution.py:68
  747.3 69.3 %collective-permute-start.19 = (f32[4,8,128]{2,1,0:T(8,128)S(1)}, f32[4,8,128]{2,1,0:T(8,128)S(1)}, u32[]{:S(2)}, u32[]{:S(2)}) collective-permute-start(f32[4,8,128]{2,1,0:T(8,128)S(1)} %get-tuple-element.329), channel_id=1, source_target_pairs={{0,2},{1,3},{2,0},{3,1},{4,6},{5,7},{6,4},{7,5},{8,10},{9,11},{10,... | collective-permute-start | bytes 49160 | tf_op jit(solution)/shard_map/ppermute | solution.py:68
  747.4 69.1 %collective-permute-start.18 = (f32[4,8,128]{2,1,0:T(8,128)S(1)}, f32[4,8,128]{2,1,0:T(8,128)S(1)}, u32[]{:S(2)}, u32[]{:S(2)}) collective-permute-start(f32[4,8,128]{2,1,0:T(8,128)S(1)} %get-tuple-element.329), channel_id=1, source_target_pairs={{0,1},{1,0},{2,3},{3,2},{4,5},{5,4},{6,7},{7,6},{8,9},{9,8},{10,11... | collective-permute-start | bytes 49160 | tf_op jit(solution)/shard_map/ppermute | solution.py:68
  824.9 97.0 %all-to-all-start.6 = ((bf16[4,2048,512]{2,1,0:T(8,128)(2,1)}), bf16[4,2048,512]{2,1,0:T(8,128)(2,1)}, u32[]{:S(2)}, u32[]{:S(2)}) async-start(bf16[4,2048,512]{2,1,0:T(8,128)(2,1)} %bitcast.419), calls=%async_computation.7 | async-start | bytes 16777216 | tf_op jit(solution)/shard_map/all_to_all | solution.py:431
  831.0 179.3 %reduce-scatter.10.cloned.1.call-start = ((), (), s32[]{:S(2)}) async-start(), calls=%async_computation.18 | async-start | bytes 5242880 | tf_op jit(solution)/shard_map/reduce_scatter | solution.py:418
  951.2 12.1 collective-permute-start.21
  951.2 17.4 %collective-permute-start.22 = (bf16[16,352,256]{2,1,0:T(8,128)(2,1)}, bf16[16,352,256]{2,1,0:T(8,128)(2,1)}, u32[]{:S(2)}, u32[]{:S(2)}) collective-permute-start(bf16[16,352,256]{2,1,0:T(8,128)(2,1)} %get-tuple-element.135), channel_id=1, source_target_pairs={{0,4},{4,0},{8,12},{12,8},{16,20},{20,16},{24,28},{28,24},{1,5},{5... | collective-permute-start | bytes 8650760 | tf_op jit(solution)/shard_map/ppermute | solution.py:78
  951.7 21.3 %collective-permute-start.23 = (bf16[16,352,256]{2,1,0:T(8,128)(2,1)}, bf16[16,352,256]{2,1,0:T(8,128)(2,1)}, u32[]{:S(2)}, u32[]{:S(2)}) collective-permute-start(bf16[16,352,256]{2,1,0:T(8,128)(2,1)} %get-tuple-element.137), channel_id=1, source_target_pairs={{0,4},{4,0},{8,12},{12,8},{16,20},{20,16},{24,28},{28,24},{1,5},{5... | collective-permute-start | bytes 8650760 | tf_op jit(solution)/shard_map/ppermute | solution.py:78
  954.1 59.1 %all-to-all-start.7 = ((bf16[4,1024,512]{2,1,0:T(8,128)(2,1)}), bf16[4,1024,512]{2,1,0:T(8,128)(2,1)}, u32[]{:S(2)}, u32[]{:S(2)}) async-start(bf16[4,1024,512]{2,1,0:T(8,128)(2,1)} %bitcast.421), calls=%async_computation.9 | async-start | bytes 8388608 | tf_op jit(solution)/shard_map/all_to_all | solution.py:431
  1013.3 67.2 %all-to-all-start.8 = ((bf16[4,4,352,256]{3,2,1,0:T(8,128)(2,1)}), bf16[4,4,352,256]{3,2,1,0:T(8,128)(2,1)}, u32[]{:S(2)}, u32[]{:S(2)}) async-start(bf16[4,4,352,256]{3,2,1,0:T(8,128)(2,1)} %bitcast.116), calls=%async_computation.11 | async-start | bytes 5767168 | tf_op jit(solution)/shard_map/all_to_all | solution.py:434
  1018.4 90.1 %all-gather.10.cloned.1.call-start = ((), (), s32[]{:S(2)}) async-start(), calls=%async_computation.19 | async-start | bytes 5242880 | tf_op jit(solution)/shard_map/all_gather | solution.py:423
  1080.4 70.1 %all-to-all-start.9 = ((bf16[4,4,352,256]{3,2,1,0:T(8,128)(2,1)}), bf16[4,4,352,256]{3,2,1,0:T(8,128)(2,1)}, u32[]{:S(2)}, u32[]{:S(2)}) async-start(bf16[4,4,352,256]{3,2,1,0:T(8,128)(2,1)} %bitcast.426), calls=%async_computation.12 | async-start | bytes 5767168 | tf_op jit(solution)/shard_map/all_to_all | solution.py:434
  1088.8 379.0 %reduce-scatter.14.cloned.1.call-start = ((), (), s32[]{:S(2)}) async-start(), calls=%async_computation.21 | async-start | bytes 9732096 | tf_op jit(solution)/shard_map/reduce_scatter | solution.py:795
  1111.8 38.7 %collective-permute-start.24 = (bf16[4,352,256]{2,1,0:T(8,128)(2,1)}, bf16[4,352,256]{2,1,0:T(8,128)(2,1)S(1)}, u32[]{:S(2)}, u32[]{:S(2)}) collective-permute-start(bf16[4,352,256]{2,1,0:T(8,128)(2,1)} %get-tuple-element.302), channel_id=1, source_target_pairs={{0,1},{1,0},{2,3},{3,2},{4,5},{5,4},{6,7},{7,6},{8,9},{9,8},{10,11... | collective-permute-start | bytes 2162696 | tf_op jit(solution)/shard_map/ppermute | solution.py:68
  1112.4 38.2 %collective-permute-start.25 = (bf16[4,352,256]{2,1,0:T(8,128)(2,1)}, bf16[4,352,256]{2,1,0:T(8,128)(2,1)}, u32[]{:S(2)}, u32[]{:S(2)}) collective-permute-start(bf16[4,352,256]{2,1,0:T(8,128)(2,1)} %get-tuple-element.301), channel_id=1, source_target_pairs={{0,2},{1,3},{2,0},{3,1},{4,6},{5,7},{6,4},{7,5},{8,10},{9,11},{10,... | collective-permute-start | bytes 2162696 | tf_op jit(solution)/shard_map/ppermute | solution.py:68
  1113.9 36.7 %collective-permute-start.26 = (bf16[4,352,256]{2,1,0:T(8,128)(2,1)}, bf16[4,352,256]{2,1,0:T(8,128)(2,1)}, u32[]{:S(2)}, u32[]{:S(2)}) collective-permute-start(bf16[4,352,256]{2,1,0:T(8,128)(2,1)} %get-tuple-element.300), channel_id=1, source_target_pairs={{0,3},{1,2},{2,1},{3,0},{4,7},{5,6},{6,5},{7,4},{8,11},{9,10},{10,... | collective-permute-start | bytes 2162696 | tf_op jit(solution)/shard_map/ppermute | solution.py:68
  1156.0 130.2 %all-to-all-start.10 = ((bf16[4,4,352,256]{3,2,1,0:T(8,128)(2,1)}), bf16[4,4,352,256]{3,2,1,0:T(8,128)(2,1)}, u32[]{:S(2)}, u32[]{:S(2)}) async-start(bf16[4,4,352,256]{3,2,1,0:T(8,128)(2,1)} %bitcast.425), calls=%async_computation.13 | async-start | bytes 5767168 | tf_op jit(solution)/shard_map/all_to_all | solution.py:434
  1164.1 307.1 %reduce-scatter.12.cloned.1.call-start = ((), (), s32[]{:S(2)}) async-start(), calls=%async_computation.20 | async-start | bytes 9879552 | tf_op jit(solution)/shard_map/reduce_scatter | solution.py:795
  1180.1 27.1 %collective-permute-start.29 = (bf16[1024,512]{1,0:T(8,128)(2,1)S(1)}, bf16[1024,512]{1,0:T(8,128)(2,1)S(1)}, u32[]{:S(2)}, u32[]{:S(2)}) collective-permute-start(bf16[1024,512]{1,0:T(8,128)(2,1)S(1)} %get-tuple-element.283), channel_id=1, source_target_pairs={{0,3},{1,2},{2,1},{3,0},{4,7},{5,6},{6,5},{7,4},{8,11},{9,10},{10,... | collective-permute-start | bytes 3145736 | tf_op jit(solution)/shard_map/ppermute | solution.py:68
  1181.7 45.8 %collective-permute-start.28 = (bf16[1024,512]{1,0:T(8,128)(2,1)S(1)}, bf16[1024,512]{1,0:T(8,128)(2,1)S(1)}, u32[]{:S(2)}, u32[]{:S(2)}) collective-permute-start(bf16[1024,512]{1,0:T(8,128)(2,1)S(1)} %get-tuple-element.284), channel_id=1, source_target_pairs={{0,2},{1,3},{2,0},{3,1},{4,6},{5,7},{6,4},{7,5},{8,10},{9,11},{10,... | collective-permute-start | bytes 3145736 | tf_op jit(solution)/shard_map/ppermute | solution.py:68
  1182.2 45.3 %collective-permute-start.27 = (bf16[1024,512]{1,0:T(8,128)(2,1)S(1)}, bf16[1024,512]{1,0:T(8,128)(2,1)}, u32[]{:S(2)}, u32[]{:S(2)}) collective-permute-start(bf16[1024,512]{1,0:T(8,128)(2,1)S(1)} %get-tuple-element.282), channel_id=1, source_target_pairs={{0,1},{1,0},{2,3},{3,2},{4,5},{5,4},{6,7},{7,6},{8,9},{9,8},{10,11... | collective-permute-start | bytes 3145736 | tf_op jit(solution)/shard_map/ppermute | solution.py:68
  1232.7 27.3 %collective-permute-start.35 = (bf16[1024,512]{1,0:T(8,128)(2,1)}, bf16[1024,512]{1,0:T(8,128)(2,1)}, u32[]{:S(2)}, u32[]{:S(2)}) collective-permute-start(bf16[1024,512]{1,0:T(8,128)(2,1)} %get-tuple-element.280), channel_id=1, source_target_pairs={{0,3},{1,2},{2,1},{3,0},{4,7},{5,6},{6,5},{7,4},{8,11},{9,10},{10,... | collective-permute-start | bytes 3145736 | tf_op jit(solution)/shard_map/ppermute | solution.py:68
  1241.6 39.9 %collective-permute-start.34 = (bf16[1024,512]{1,0:T(8,128)(2,1)}, bf16[1024,512]{1,0:T(8,128)(2,1)}, u32[]{:S(2)}, u32[]{:S(2)}) collective-permute-start(bf16[1024,512]{1,0:T(8,128)(2,1)} %get-tuple-element.281), channel_id=1, source_target_pairs={{0,2},{1,3},{2,0},{3,1},{4,6},{5,7},{6,4},{7,5},{8,10},{9,11},{10,... | collective-permute-start | bytes 3145736 | tf_op jit(solution)/shard_map/ppermute | solution.py:68
  1242.3 39.3 %collective-permute-start.33 = (bf16[1024,512]{1,0:T(8,128)(2,1)}, bf16[1024,512]{1,0:T(8,128)(2,1)}, u32[]{:S(2)}, u32[]{:S(2)}) collective-permute-start(bf16[1024,512]{1,0:T(8,128)(2,1)} %get-tuple-element.279), channel_id=1, source_target_pairs={{0,1},{1,0},{2,3},{3,2},{4,5},{5,4},{6,7},{7,6},{8,9},{9,8},{10,11... | collective-permute-start | bytes 3145736 | tf_op jit(solution)/shard_map/ppermute | solution.py:68
  1248.6 48.4 %collective-permute-start.36 = (bf16[4,352,256]{2,1,0:T(8,128)(2,1)}, bf16[4,352,256]{2,1,0:T(8,128)(2,1)S(1)}, u32[]{:S(2)}, u32[]{:S(2)}) collective-permute-start(bf16[4,352,256]{2,1,0:T(8,128)(2,1)} %get-tuple-element.298), channel_id=1, source_target_pairs={{0,1},{1,0},{2,3},{3,2},{4,5},{5,4},{6,7},{7,6},{8,9},{9,8},{10,11... | collective-permute-start | bytes 2162696 | tf_op jit(solution)/shard_map/ppermute | solution.py:68
  1249.3 48.5 %collective-permute-start.37 = (bf16[4,352,256]{2,1,0:T(8,128)(2,1)}, bf16[4,352,256]{2,1,0:T(8,128)(2,1)}, u32[]{:S(2)}, u32[]{:S(2)}) collective-permute-start(bf16[4,352,256]{2,1,0:T(8,128)(2,1)} %get-tuple-element.297), channel_id=1, source_target_pairs={{0,2},{1,3},{2,0},{3,1},{4,6},{5,7},{6,4},{7,5},{8,10},{9,11},{10,... | collective-permute-start | bytes 2162696 | tf_op jit(solution)/shard_map/ppermute | solution.py:68
  1259.9 52.4 %collective-permute-start.38 = (bf16[4,352,256]{2,1,0:T(8,128)(2,1)}, bf16[4,352,256]{2,1,0:T(8,128)(2,1)}, u32[]{:S(2)}, u32[]{:S(2)}) collective-permute-start(bf16[4,352,256]{2,1,0:T(8,128)(2,1)} %get-tuple-element.296), channel_id=1, source_target_pairs={{0,3},{1,2},{2,1},{3,0},{4,7},{5,6},{6,5},{7,4},{8,11},{9,10},{10,... | collective-permute-start | bytes 2162696 | tf_op jit(solution)/shard_map/ppermute | solution.py:68
  1336.4 58.6 %collective-permute-start.30 = (bf16[1024,512]{1,0:T(8,128)(2,1)S(1)}, bf16[1024,512]{1,0:T(8,128)(2,1)S(1)}, u32[]{:S(2)}, u32[]{:S(2)}) collective-permute-start(bf16[1024,512]{1,0:T(8,128)(2,1)S(1)} %get-tuple-element.287.refs_0_), channel_id=1, source_target_pairs={{0,1},{1,0},{2,3},{3,2},{4,5},{5,4},{6,7},{7,6},{8,9},{9,8},{10,11... | collective-permute-start | bytes 3145736 | tf_op jit(solution)/shard_map/ppermute | solution.py:68
  1339.9 38.0 %collective-permute-start.45 = (bf16[4,352,256]{2,1,0:T(8,128)(2,1)S(1)}, bf16[4,352,256]{2,1,0:T(8,128)(2,1)S(1)}, u32[]{:S(2)}, u32[]{:S(2)}) collective-permute-start(bf16[4,352,256]{2,1,0:T(8,128)(2,1)S(1)} %get-tuple-element.294), channel_id=1, source_target_pairs={{0,1},{1,0},{2,3},{3,2},{4,5},{5,4},{6,7},{7,6},{8,9},{9,8},{10,11... | collective-permute-start | bytes 2162696 | tf_op jit(solution)/shard_map/ppermute | solution.py:68
  1340.5 39.8 %collective-permute-start.46 = (bf16[4,352,256]{2,1,0:T(8,128)(2,1)S(1)}, bf16[4,352,256]{2,1,0:T(8,128)(2,1)S(1)}, u32[]{:S(2)}, u32[]{:S(2)}) collective-permute-start(bf16[4,352,256]{2,1,0:T(8,128)(2,1)S(1)} %get-tuple-element.293), channel_id=1, source_target_pairs={{0,2},{1,3},{2,0},{3,1},{4,6},{5,7},{6,4},{7,5},{8,10},{9,11},{10,... | collective-permute-start | bytes 2162696 | tf_op jit(solution)/shard_map/ppermute | solution.py:68
  1341.9 52.4 %collective-permute-start.47 = (bf16[4,352,256]{2,1,0:T(8,128)(2,1)S(1)}, bf16[4,352,256]{2,1,0:T(8,128)(2,1)S(1)}, u32[]{:S(2)}, u32[]{:S(2)}) collective-permute-start(bf16[4,352,256]{2,1,0:T(8,128)(2,1)S(1)} %get-tuple-element.292), channel_id=1, source_target_pairs={{0,3},{1,2},{2,1},{3,0},{4,7},{5,6},{6,5},{7,4},{8,11},{9,10},{10,... | collective-permute-start | bytes 2162696 | tf_op jit(solution)/shard_map/ppermute | solution.py:68
  1343.4 75.8 %collective-permute-start.31 = (bf16[1024,512]{1,0:T(8,128)(2,1)S(1)}, bf16[1024,512]{1,0:T(8,128)(2,1)S(1)}, u32[]{:S(2)}, u32[]{:S(2)}) collective-permute-start(bf16[1024,512]{1,0:T(8,128)(2,1)S(1)} %get-tuple-element.287.refs_0_), channel_id=1, source_target_pairs={{0,2},{1,3},{2,0},{3,1},{4,6},{5,7},{6,4},{7,5},{8,10},{9,11},{10,... | collective-permute-start | bytes 3145736 | tf_op jit(solution)/shard_map/ppermute | solution.py:68
  1377.9 42.3 %collective-permute-start.32 = (bf16[1024,512]{1,0:T(8,128)(2,1)S(1)}, bf16[1024,512]{1,0:T(8,128)(2,1)}, u32[]{:S(2)}, u32[]{:S(2)}) collective-permute-start(bf16[1024,512]{1,0:T(8,128)(2,1)S(1)} %get-tuple-element.287.refs_0_), channel_id=1, source_target_pairs={{0,3},{1,2},{2,1},{3,0},{4,7},{5,6},{6,5},{7,4},{8,11},{9,10},{10,... | collective-permute-start | bytes 3145736 | tf_op jit(solution)/shard_map/ppermute | solution.py:68
  1380.3 58.1 %collective-permute-start.39 = (bf16[1024,512]{1,0:T(8,128)(2,1)}, bf16[1024,512]{1,0:T(8,128)(2,1)}, u32[]{:S(2)}, u32[]{:S(2)}) collective-permute-start(bf16[1024,512]{1,0:T(8,128)(2,1)} %get-tuple-element.159.refs_0_), channel_id=1, source_target_pairs={{0,1},{1,0},{2,3},{3,2},{4,5},{5,4},{6,7},{7,6},{8,9},{9,8},{10,11... | collective-permute-start | bytes 3145736 | tf_op jit(solution)/shard_map/ppermute | solution.py:68
  1394.3 67.2 %collective-permute-start.40 = (bf16[1024,512]{1,0:T(8,128)(2,1)}, bf16[1024,512]{1,0:T(8,128)(2,1)}, u32[]{:S(2)}, u32[]{:S(2)}) collective-permute-start(bf16[1024,512]{1,0:T(8,128)(2,1)} %get-tuple-element.159.refs_0_), channel_id=1, source_target_pairs={{0,2},{1,3},{2,0},{3,1},{4,6},{5,7},{6,4},{7,5},{8,10},{9,11},{10,... | collective-permute-start | bytes 3145736 | tf_op jit(solution)/shard_map/ppermute | solution.py:68
  1395.9 65.6 %collective-permute-start.41 = (bf16[1024,512]{1,0:T(8,128)(2,1)}, bf16[1024,512]{1,0:T(8,128)(2,1)}, u32[]{:S(2)}, u32[]{:S(2)}) collective-permute-start(bf16[1024,512]{1,0:T(8,128)(2,1)} %get-tuple-element.159.refs_0_), channel_id=1, source_target_pairs={{0,3},{1,2},{2,1},{3,0},{4,7},{5,6},{6,5},{7,4},{8,11},{9,10},{10,... | collective-permute-start | bytes 3145736 | tf_op jit(solution)/shard_map/ppermute | solution.py:68
  1473.5 11.0 collective-permute-start.44
  1475.1 12.4 collective-permute-start.43
  1475.6 11.8 collective-permute-start.42
  (120 other events, 1908.6 us)
Sparse Core Ops, SparseCore 0:
  20.3 86.0 all-gather.11
  212.2 52.5 reduce-scatter.5
  282.9 79.3 all-gather.13
  363.8 79.2 all-gather.15
  511.4 83.6 all-gather.17
  807.6 76.1 reduce-scatter.7
  934.1 76.1 reduce-scatter.9
  1039.1 53.4 all-gather.9
  1150.7 150.0 reduce-scatter.13
  1322.3 90.5 reduce-scatter.11

commit v9 on v8

--- a/solution.py
+++ b/solution.py
@@ -680,35 +680,6 @@
         1,
     ).astype(BF16)
     gated_active = (active.astype(F32) * gate_rows).astype(BF16)
-    out_parts, pre_low = lax.optimization_barrier((out_parts, pre_low))
-    rows_grad = dot(pre_low, own_in).astype(BF16)
-    rows_grad, out_parts = lax.optimization_barrier((rows_grad, out_parts))
-    grad_parts = send_back(rows_grad)
-    routed, pre_low, gated_active = lax.optimization_barrier(
-        (combine(out_parts), pre_low, gated_active)
-    )
-    routed = scatter_z(routed).astype(F32)
-    token_grad = jnp.sum(jnp.where(own_place, gate_grad[:, :, None], 0.0), axis=1)
-    token_grad = token_grad.reshape(nz, -1, 128)
-    token_plane = jnp.stack(
-        [
-            lay.over_z(lax.dynamic_index_in_dim(token_grad, me_z ^ k, 0, keepdims=False), k)
-            for k in range(nz)
-        ]
-    )
-    token_home = jnp.stack([lay.over_t(token_plane, k) for k in range(nt)])
-    experts = jnp.arange(EXPERTS, dtype=jnp.int32)
-    came_from = (me_t ^ (experts % nt)) * nz + (me_z ^ (experts // nt))
-    probs_grad = lax.dot_general(
-        token_home.reshape(EXPERTS, rows),
-        (experts[:, None] == came_from[None, :]).astype(F32),
-        (((0,), (0,)), ((), ())),
-        precision=lax.Precision.HIGHEST,
-        preferred_element_type=F32,
-    )
-
-    grad_in_own = dot_tn(pre_low, expert_rows).astype(BF16)
-    grad_out_own = dot_tn(gated_active, cot_rows).astype(BF16)
     ffs = w_shared_out.shape[0]
     shared_in = jnp.swapaxes(shared_all[:, : 2 * ffs], 0, 1).reshape(2 * ffs, width)
     shared_out = jnp.swapaxes(shared_all[:, 2 * ffs :], 0, 1).reshape(ffs, width)
@@ -730,24 +701,44 @@
     grad_shared_out = dot_tn(shared_act, cot_low)
     shared_grad_full = dot(shared_pre_grad, shared_in)
 
+    out_parts, pre_low, shared_full = lax.optimization_barrier((out_parts, pre_low, shared_full))
+    rows_grad = dot(pre_low, own_in).astype(BF16)
+    rows_grad, out_parts = lax.optimization_barrier((rows_grad, out_parts))
+    grad_parts = send_back(rows_grad)
+    routed, pre_low, gated_active, shared_part = lax.optimization_barrier(
+        (combine(out_parts), pre_low, gated_active, scatter_t(shared_full))
+    )
+    routed = scatter_z(routed).astype(F32)
+    token_grad = jnp.sum(jnp.where(own_place, gate_grad[:, :, None], 0.0), axis=1)
+    token_grad = token_grad.reshape(nz, -1, 128)
+    token_plane = jnp.stack(
+        [
+            lay.over_z(lax.dynamic_index_in_dim(token_grad, me_z ^ k, 0, keepdims=False), k)
+            for k in range(nz)
+        ]
+    )
+    token_home = jnp.stack([lay.over_t(token_plane, k) for k in range(nt)])
+    experts = jnp.arange(EXPERTS, dtype=jnp.int32)
+    came_from = (me_t ^ (experts % nt)) * nz + (me_z ^ (experts // nt))
+    probs_grad = lax.dot_general(
+        token_home.reshape(EXPERTS, rows),
+        (experts[:, None] == came_from[None, :]).astype(F32),
+        (((0,), (0,)), ((), ())),
+        precision=lax.Precision.HIGHEST,
+        preferred_element_type=F32,
+    )
+
+    grad_in_own = dot_tn(pre_low, expert_rows).astype(BF16)
+    grad_out_own = dot_tn(gated_active, cot_rows).astype(BF16)
     (
         grad_parts,
         grad_in_own,
         grad_out_own,
         routed,
         probs_grad,
-        shared_full,
         shared_grad_full,
     ) = lax.optimization_barrier(
-        (
-            grad_parts,
-            grad_in_own,
-            grad_out_own,
-            routed,
-            probs_grad,
-            shared_full,
-            shared_grad_full,
-        )
+        (grad_parts, grad_in_own, grad_out_own, routed, probs_grad, shared_grad_full)
     )
     shared_grad = swap_t(
         jnp.swapaxes(shared_grad_full.astype(BF16).reshape(rows, nt, part), 0, 1)
@@ -798,8 +789,9 @@
         return jnp.swapaxes(values.astype(BF16).reshape(-1, ndp, d_loc), 0, 1)
 
     shared_grads = jnp.concatenate([by_owner(grad_shared_in), by_owner(grad_shared_out)], 1)
-    residual_low, shared_grads, grad_plane[0] = lax.optimization_barrier(
-        (residual_low, shared_grads, grad_plane[0])
+    output_part = lax.optimization_barrier((residual + routed + shared_part).astype(BF16))
+    residual_low, shared_grads, grad_plane[0], output_part = lax.optimization_barrier(
+        (residual_low, shared_grads, grad_plane[0], output_part)
     )
     grad_out_w = dot_tn(attended_low, residual_low)
     attended_grad = dot_nt(residual_low, out_w).astype(BF16)
@@ -821,14 +813,8 @@
         ]
 
     grad_home = [to_columns(grad_plane[0]), None, None]
-    (
-        query_turned_grad,
-        grad_plane[1],
-        grad_home[0],
-        shared_full,
-        shared_grads,
-    ) = lax.optimization_barrier(
-        (query_turned_grad, grad_plane[1], grad_home[0], shared_full, shared_grads)
+    query_turned_grad, grad_plane[1], grad_home[0], shared_grads = lax.optimization_barrier(
+        (query_turned_grad, grad_plane[1], grad_home[0], shared_grads)
     )
     shared_sum = sum_dp(shared_grads)
     turned_first, turned_second = rotate_back(
@@ -851,10 +837,9 @@
         scaled_kv - latent_hat * jnp.mean(latent_hat * scaled_kv, axis=-1, keepdims=True)
     )
     down_grad = jnp.concatenate([latent_back, key_rope_part], -1).astype(BF16)
-    normed_full, shared_part = lax.optimization_barrier(
-        (dot(query_grad, query_t) + dot(down_grad, down_t), scatter_t_direct(shared_full))
-    )
-    output = gather_t_direct((residual + routed + shared_part).astype(BF16))
+    normed_full, output = lax.optimization_barrier(
+        (dot(query_grad, query_t) + dot(down_grad, down_t), gather_t(output_part))
+    )
     normed_grad, grad_plane[2], grad_home[1] = lax.optimization_barrier(
         (scatter_t_direct(normed_full), grad_plane[2], to_columns(grad_plane[1]))
     )
@@ -864,7 +849,9 @@
     input_grad = residual_grad + attn_inverse * (
         scaled_in - attn_hat * row_mean(attn_hat * scaled_in)
     )
-    input_low, grad_plane[2] = lax.optimization_barrier((input_grad.astype(BF16), grad_plane[2]))
+    input_low, grad_plane[2], query_grad, kv_grad, down_grad = lax.optimization_barrier(
+        (input_grad.astype(BF16), grad_plane[2], query_grad, kv_grad, down_grad)
+    )
     grad_home[2] = to_columns(grad_plane[2])
     grad_expert_in, grad_expert_out = home_gradients(lay, ids, grad_home, f_loc, d_loc)
     grad_hidden = gather_t_direct(input_low)
@@ -877,12 +864,14 @@
     kv_gain_row = jnp.pad(
         grad_kv_gain.reshape(ndp, lat_loc), ((0, 0), (0, d_loc - lat_loc))
     ).reshape(1, width)
-    gain_grads = jnp.concatenate([spread(attn_gain_part), spread(ffn_gain_part), kv_gain_row], 0)
+    gain_grads = jnp.concatenate([spread(ffn_gain_part), kv_gain_row], 0)
+    attn_sum_all = lax.psum(spread(attn_gain_part).reshape(-1, 128), ("dp", "tensor"))
+    attn_gain_grad = lax.dynamic_slice_in_dim(attn_sum_all.reshape(-1), me_dp * d_loc, d_loc, 0)
     front_sum = sum_dp(
         jnp.concatenate(
             [
                 by_owner(dot_tn(down_grad, normed_low)),
-                by_owner(jnp.pad(gain_grads, ((0, 13), (0, 0)))),
+                by_owner(jnp.pad(gain_grads, ((0, 14), (0, 0)))),
                 by_owner(router_part),
                 by_owner(dot_tn(query_grad, normed_low)),
                 by_owner(grad_out_w),
@@ -899,13 +888,13 @@
     return (
         output,
         grad_hidden,
-        own_sum[down_rows],
+        attn_gain_grad,
         jnp.transpose(by_head(front_sum[at : at + q_rows])),
         jnp.transpose(own_sum[:down_rows]),
-        own_sum[down_rows + 2, :lat_loc],
+        own_sum[down_rows + 1, :lat_loc],
         front_sum[at + q_rows + out_rows :].reshape(w_kv_up.shape),
         front_sum[at + q_rows : at + q_rows + out_rows],
-        own_sum[down_rows + 1],
+        own_sum[down_rows],
         jnp.transpose(front_sum[down_rows + EXPERTS : at]),
         grad_expert_in,
         grad_expert_out,

time: 1510 us -> 1520 us (level)
  blocking collectives: 24.3 us -> 118 us
  waiting for transfers between devices: 592 us -> 514 us
    ppermute x30 -> x24, waiting for transfers between devices: 212 us -> 82.3 us  [over_t(): return lax.ppermute(values, 'tensor', [(i, i ^ k) for i in range(self.t)])]
    psum x0 -> x1, blocking collectives: none -> 91 us  [body(): lax.psum(spread(attn_gain_part).reshape(-1, 128), ('dp', 'tensor'))]
    all_to_all x5, waiting for transfers between devices: 52.5 us -> 94.5 us  [swap_z(): lax.all_to_all(values, 'dp', split_axis=0, concat_axis=0, axis_index_grou...]
    all_to_all x6, waiting for transfers between devices: 90.5 us -> 132 us  [swap_t(): lax.all_to_all(values, 'tensor', split_axis=0, concat_axis=0, tiled=True)]
    reduce_scatter x2, waiting for transfers between devices: 36.1 us -> 0.44 us  [scatter_z(): lax.psum_scatter(values, 'dp', scatter_dimension=0, tiled=False, axis_ind...]
    ppermute x30 -> x24, starting transfers between devices: 36.8 us -> 28.5 us  [over_t(): return lax.ppermute(values, 'tensor', [(i, i ^ k) for i in range(self.t)])]
    unnamed x254 -> x249, local copies, waits for them, and re-layouts: 47.3 us -> 48.6 us
    reduce_scatter x1 -> x2, waiting for transfers between devices: 43.1 us -> 43.5 us  [scatter_t(): lax.psum_scatter(values.astype(BF16), 'tensor', scatter_dimension=1, tile...]
  transfers between devices with their start and end apart: 69 -> 65, of which waited for: 39 -> 32; matrix products, arithmetic and copies ran while one was open for 37% -> 36% of each run, Pallas kernels for 7% -> 7%
where the time goes in v9:
time: 1520 us; the launch traced here: 1510 us
  waiting for transfers between devices  514 us (34%)
  matrix products  321 us (21%)
  local copies, waits for them, and re-layouts  206 us (14%)
  starting transfers between devices  119 us (8%)
  blocking collectives  118 us (8%)
  other arithmetic  113 us (7%)
  Pallas kernels  100 us (7%)
  between operations  16.7 us (1%)
    all_to_all x6, waiting for transfers between devices, swap_t(): lax.all_to_all(values, 'tensor', split_axis=0, concat_axis=0, tiled=True)  132 us
    dot_general x9, matrix products, dot_nt(): lax.dot_general(a, b, (((1,), (1,)), ((), ())), preferred_element_type=F32)  100 us
    all_to_all x5, waiting for transfers between devices, swap_z(): lax.all_to_all(values, 'dp', split_axis=0, concat_axis=0, axis_index_grou...  94.5 us
    psum x1, blocking collectives, body(): lax.psum(spread(attn_gain_part).reshape(-1, 128), ('dp', 'tensor'))  91 us
    ppermute x24, waiting for transfers between devices, over_t(): return lax.ppermute(values, 'tensor', [(i, i ^ k) for i in range(self.t)])  82.3 us
    dot_general x8, matrix products, dot_tn(): lax.dot_general(a, b, (((0,), (0,)), ((), ())), preferred_element_type=F32)  80.6 us
    dot_general x9, matrix products, dot(): return jnp.dot(a, b, preferred_element_type=F32)  78.5 us
    all_gather x2, waiting for transfers between devices, gather_z(): lax.all_gather(values, 'dp', axis=0, tiled=False, axis_index_groups=lay.z...  59.8 us
  transfers between devices with their start and end apart: 65, of which 32 were waited for; matrix products, arithmetic and copies ran while one was open for 36% of the time, Pallas kernels for 7%

profile of v9, /device:TPU:10, one launch (start us, length us, event | category | flops | bytes accessed | tf_op | source)
XLA Modules:
  0.0 1507.3 jit_solution(4104375822792895385)
XLA Ops:
  20.2 6.9 maximum_bitcast_fusion
  27.1 8.3 copy.295
  35.5 6.4 all-to-all-start
  51.4 55.1 %all-gather.15.cloned.1.call-done = bf16[17152,256]{1,0:T(8,128)(2,1)} async-done(((bf16[2144,256]{1,0:T(8,128)(2,1)}), bf16[17152,256]{1,0:T(8,128)(2,1)}) %all-gather.15.cloned.1.call-update) | async-done | bytes 8781840 | tf_op jit(solution)/shard_map/all_gather | solution.py:495
  117.2 19.5 %all-to-all-done = bf16[4,4,3,352,256]{4,3,1,2,0:T(8,128)(2,1)} async-done(((bf16[4,4,3,352,256]{4,3,1,2,0:T(8,128)(2,1)}), bf16[4,4,3,352,256]{4,3,1,2,0:T(8,128)(2,1)}, u32[]{:S(2)}, u32[]{:S(2)}) %all-to-all-start) | async-done | bytes 8650784 | tf_op jit(solution)/shard_map/all_to_all | solution.py:431
  166.1 6.4 fusion.112
  190.9 14.6 attend.1
  221.5 43.5 %reduce-scatter.7.cloned.1.call-done = bf16[1024,512]{1,0:T(8,128)(2,1)} async-done(((bf16[1024,2048]{1,0:T(8,128)(2,1)}), bf16[1024,512]{1,0:T(8,128)(2,1)}) %reduce-scatter.7.cloned.1.call-update) | async-done | bytes 1048592 | tf_op jit(solution)/shard_map/reduce_scatter | solution.py:426
  267.0 8.1 psum.28
  292.4 17.3 %collective-permute-done.3.refs_1_ = bf16[1024,512]{1,0:T(8,128)(2,1)} collective-permute-done((bf16[1024,512]{1,0:T(8,128)(2,1)}, bf16[1024,512]{1,0:T(8,128)(2,1)}, u32[]{:S(2)}, u32[]{:S(2)}) %collective-permute-start.3) | collective-permute-done | bytes 1048608 | tf_op jit(solution)/shard_map/ppermute | solution.py:68
  309.6 19.9 %collective-permute-done.4.refs_2_ = bf16[1024,512]{1,0:T(8,128)(2,1)} collective-permute-done((bf16[1024,512]{1,0:T(8,128)(2,1)}, bf16[1024,512]{1,0:T(8,128)(2,1)}, u32[]{:S(2)}, u32[]{:S(2)}) %collective-permute-start.4) | collective-permute-done | bytes 1048608 | tf_op jit(solution)/shard_map/ppermute | solution.py:68
  329.6 6.2 join_columns.2
  335.7 26.5 %all-gather.17.cloned.1.call-done = bf16[4096,512]{1,0:T(8,128)(2,1)} async-done(((bf16[1024,512]{1,0:T(8,128)(2,1)}), bf16[4096,512]{1,0:T(8,128)(2,1)}) %all-gather.17.cloned.1.call-update) | async-done | bytes 4194320 | tf_op jit(solution)/shard_map/all_gather | solution.py:415
  363.0 16.2 %convert_bitcast_fusion.1 = bf16[4,4,512,512]{3,2,0,1:T(8,128)(2,1)} fusion(s32[4,4,1024]{2,1,0:T(4,128)S(1)} %fusion.46, bf16[4,1024,512]{2,1,0:T(8,128)(2,1)} %bitcast.527), kind=kOutput, calls=%fused_computation.39 | convolution fusion | flops 8602517504 | bytes 12648448 | tf_op jit(solution)/shard_map/sepk,skd->espd/dot_general | solution.py:528
  379.3 7.6 copy.300
  396.6 13.1 lay_out_weights.2
  409.7 33.3 %all-gather.19.cloned.1.call-done = bf16[4096,512]{1,0:T(8,128)(2,1)} async-done(((bf16[1024,512]{1,0:T(8,128)(2,1)}), bf16[4096,512]{1,0:T(8,128)(2,1)}) %all-gather.19.cloned.1.call-update) | async-done | bytes 4194320 | tf_op jit(solution)/shard_map/all_gather | solution.py:415
  450.6 14.3 convert_bitcast_fusion
  465.0 7.4 copy.303
  472.4 23.2 %collective-permute-done.10 = bf16[4,352,256]{2,1,0:T(8,128)(2,1)S(1)} collective-permute-done((bf16[4,352,256]{2,1,0:T(8,128)(2,1)S(1)}, bf16[4,352,256]{2,1,0:T(8,128)(2,1)S(1)}, u32[]{:S(2)}, u32[]{:S(2)}) %collective-permute-start.10) | collective-permute-done | bytes 720928 | tf_op jit(solution)/shard_map/ppermute | solution.py:73
  495.6 13.9 collective-permute-done.9
  525.6 11.5 copy.301
  539.2 6.4 all-to-all-start.4
  545.6 32.4 %fusion.120 = f32[2048,2816]{1,0:T(8,128)} fusion(bf16[2048,2048]{0,1:T(8,128)(2,1)} %bitcast.437, bf16[2816,2048]{1,0:T(8,128)(2,1)} %bitcast.422), kind=kOutput, calls=%fused_computation.299 | convolution fusion | flops 23622320128 | bytes 42991616 | tf_op jit(solution)/shard_map/dot_general | solution.py:30
  577.9 12.3 fusion.8
  590.3 9.3 lay_out_weights.3
  602.0 15.0 multiply_convert_fusion
  617.1 21.2 %all-to-all-done.4 = bf16[4,2048,512]{2,1,0:T(8,128)(2,1)} async-done(((bf16[4,2048,512]{2,1,0:T(8,128)(2,1)}), bf16[4,2048,512]{2,1,0:T(8,128)(2,1)}, u32[]{:S(2)}, u32[]{:S(2)}) %all-to-all-start.4) | async-done | bytes 8388640 | tf_op jit(solution)/shard_map/all_to_all | solution.py:431
  638.3 11.5 copy.310
  657.3 7.4 copy.389
  664.7 6.6 all-to-all-start.5
  671.4 8.2 copy.313
  679.6 10.4 fusion.121
  703.0 27.4 %multiply_convert_fusion.2 = (bf16[2048,1408]{1,0:T(8,128)(2,1)S(1)}, bf16[2048,1408]{1,0:T(8,128)(2,1)}, f32[2048]{0:T(1024)S(1)}) fusion(f32[2048,2816]{1,0:T(8,128)} %fusion.120, f32[2048]{0:T(1024)S(1)} %bitcast.500, bf16[2048,1408]{1,0:T(8,128)(2,1)} %copy-done.37, bf16[2048,2048]{0,1:T(8,128)(2,1)} %bitcast.439, bf16[1,1408,2048]{2,1,0:T(8,128)(2,1)} %copy-done), kind=kOutput, calls=%fused_computation.16 | convolution fusion | flops 11860178944 | bytes 54542336 | tf_op jit(solution)/shard_map/dot_general | solution.py:30
  730.3 7.9 pad_maximum_fusion
  738.2 25.1 %all-to-all-done.5 = bf16[4,2048,512]{2,1,0:T(8,128)(2,1)} async-done(((bf16[4,2048,512]{2,1,0:T(8,128)(2,1)}), bf16[4,2048,512]{2,1,0:T(8,128)(2,1)}, u32[]{:S(2)}, u32[]{:S(2)}) %all-to-all-start.5) | async-done | bytes 8388640 | tf_op jit(solution)/shard_map/all_to_all | solution.py:431
  775.9 31.6 %convolution_convert_fusion.3 = bf16[2048,2048]{1,0:T(8,128)(2,1)} fusion(bf16[2048,2816]{1,0:T(8,128)(2,1)} %pad_maximum_fusion, bf16[2816,2048]{1,0:T(8,128)(2,1)} %bitcast.423), kind=kOutput, calls=%fused_computation.42 | convolution fusion | flops 23626514432 | bytes 31457280 | tf_op jit(solution)/shard_map/dot_general | solution.py:26
  807.6 12.2 bitcast_convert_fusion.1
  822.8 11.0 fusion.42
  834.7 7.6 copy.388
  842.3 6.4 all-to-all-start.6
  848.7 17.9 %convolution_convert_fusion.2.out_ref = bf16[1408,2048]{1,0:T(8,128)(2,1)} fusion(bf16[2048,1408]{1,0:T(8,128)(2,1)} %get-tuple-element.130, bf16[2048,2048]{0,1:T(8,128)(2,1)} %bitcast.440), kind=kOutput, calls=%fused_computation.41 | convolution fusion | flops 11814043648 | bytes 19922944 | tf_op jit(solution)/shard_map/dot_general | solution.py:34
  866.6 31.6 %convolution_convert_fusion = bf16[2816,2048]{1,0:T(8,128)(2,1)} fusion(bf16[2048,2816]{1,0:T(8,128)(2,1)} %pad_maximum_fusion, bf16[2048,2048]{0,1:T(8,128)(2,1)} %bitcast.438), kind=kOutput, calls=%fused_computation.20 | convolution fusion | flops 23628087296 | bytes 31457280 | tf_op jit(solution)/shard_map/dot_general | solution.py:34
  901.5 35.8 %all-to-all-done.6 = bf16[4,2048,512]{2,1,0:T(8,128)(2,1)} async-done(((bf16[4,2048,512]{2,1,0:T(8,128)(2,1)}), bf16[4,2048,512]{2,1,0:T(8,128)(2,1)}, u32[]{:S(2)}, u32[]{:S(2)}) %all-to-all-start.6) | async-done | bytes 8388640 | tf_op jit(solution)/shard_map/all_to_all | solution.py:431
  937.3 12.1 bitcast_convert_fusion
  949.4 15.1 %take_apart.1 = (bf16[16,352,256]{2,1,0:T(8,128)(2,1)S(1)}, bf16[16,352,256]{2,1,0:T(8,128)(2,1)S(1)}, bf16[16,352,256]{2,1,0:T(8,128)(2,1)S(1)}, bf16[16,352,25...) custom-call(s32[3]{0:T(128)S(1)} %get-tuple-element.276.ids_ref, ...), custom_call_target="tpu_custom_call" | custom-call | bytes 34603008 | tf_op jit(solution)/shard_map/take_apart/pallas_call | solution.py:128
  992.4 30.1 %all-to-all-done.7 = bf16[4,1024,512]{2,1,0:T(8,128)(2,1)} async-done(((bf16[4,1024,512]{2,1,0:T(8,128)(2,1)}), bf16[4,1024,512]{2,1,0:T(8,128)(2,1)}, u32[]{:S(2)}, u32[]{:S(2)}) %all-to-all-start.7) | async-done | bytes 4194336 | tf_op jit(solution)/shard_map/all_to_all | solution.py:431
  1033.9 8.0 psum.29
  1051.9 6.1 convolution_convert_fusion.5
  1060.8 7.2 convolution_convert_fusion.1
  1072.1 39.4 %all-to-all-done.8 = bf16[4,4,352,256]{3,2,1,0:T(8,128)(2,1)S(1)} async-done(((bf16[4,4,352,256]{3,2,1,0:T(8,128)(2,1)}), bf16[4,4,352,256]{3,2,1,0:T(8,128)(2,1)S(1)}, u32[]{:S(2)}, u32[]{:S(2)}) %all-to-all-start.8) | async-done | bytes 2883616 | tf_op jit(solution)/shard_map/all_to_all | solution.py:434
  1113.1 7.8 all-to-all-start.9
  1133.4 21.6 %attend_back.1 = (bf16[1024,512]{1,0:T(8,128)(2,1)S(1)}, f32[1024,256]{1,0:T(8,128)S(1)}, bf16[1024,1024]{1,0:T(8,128)(2,1)S(1)}, f32[1024,256]{1,0:T(8,128)S(1)}) custom-call(s32[1]{0:T(128)} %copy.410.len_ref, bf16[1024,512]{1,0:T(8,128)(2,1)S(1)} %copy-done.5, bf16[1024,256]{1,0:T(8,128)(2,1)S(1)} %copy-done.12, bf16[1024,1024]{1,0:T(8,128)(2,1)S(1)} %copy-done.16, ...), custom_call_target="tpu_custom_call" | custom-call | flops 6710886400 | bytes 33554432 | tf_op jit(solution)/shard_map/attend_back/pallas_call | solution.py:330
  1157.3 25.0 %all-to-all-done.9 = bf16[4,4,352,256]{3,2,1,0:T(8,128)(2,1)} async-done(((bf16[4,4,352,256]{3,2,1,0:T(8,128)(2,1)}), bf16[4,4,352,256]{3,2,1,0:T(8,128)(2,1)}, u32[]{:S(2)}, u32[]{:S(2)}) %all-to-all-start.9) | async-done | bytes 2883616 | tf_op jit(solution)/shard_map/all_to_all | solution.py:434
  1183.1 8.0 all-to-all-start.10
  1207.4 6.3 convolution_add_fusion
  1238.7 7.2 collective-permute-done.29
  1250.7 14.8 collective-permute-done.28
  1271.6 25.4 %all-to-all-done.10 = bf16[4,4,352,256]{3,2,1,0:T(8,128)(2,1)} async-done(((bf16[4,4,352,256]{3,2,1,0:T(8,128)(2,1)}), bf16[4,4,352,256]{3,2,1,0:T(8,128)(2,1)}, u32[]{:S(2)}, u32[]{:S(2)}) %all-to-all-start.10) | async-done | bytes 2883616 | tf_op jit(solution)/shard_map/all_to_all | solution.py:434
  1299.5 10.5 psum.30
  1344.7 14.3 collective-permute-done.39.refs_9_
  1360.7 91.0 %psum.31 = f32[2048]{0:T(1024)S(1)} all-reduce(f32[2048]{0:T(1024)S(1)} %dynamic_update_slice.8), channel_id=1, replica_groups=mesh['dp'=8,'tensor'=4] {'dp','tensor'}, use_global_device_ids=true, to_apply=%region_23.24 | all-reduce | flops 2048 | bytes 16384 | tf_op jit(solution)/shard_map/psum | solution.py:868
  1453.4 14.1 home_gradients.1
  1467.6 6.2 join_columns.3
  (515 shorter events, 386.0 us)
Async XLA Ops:
  7.2 99.3 %all-gather.15.cloned.1.call-start = ((), (), s32[]{:S(2)}) async-start(), calls=%async_computation.25 | async-start | bytes 9879552 | tf_op jit(solution)/shard_map/all_gather | solution.py:495
  35.5 101.2 %all-to-all-start = ((bf16[4,4,3,352,256]{4,3,1,2,0:T(8,128)(2,1)}), bf16[4,4,3,352,256]{4,3,1,2,0:T(8,128)(2,1)}, u32[]{:S(2)}, u32[]{:S(2)}) async-start(bf16[4,4,3,352,256]{4,3,1,2,0:T(8,128)(2,1)} %copy.295), calls=%async_computation | async-start | bytes 17301504 | tf_op jit(solution)/shard_map/all_to_all | solution.py:431
  41.9 9.0 collective-permute-start
  43.5 7.4 collective-permute-start.1
  44.7 6.6 collective-permute-start.2
  143.9 68.4 %all-to-all-start.1 = ((bf16[4,4,352,256]{3,2,1,0:T(8,128)(2,1)}), bf16[4,4,352,256]{3,2,1,0:T(8,128)(2,1)S(1)}, u32[]{:S(2)}, u32[]{:S(2)}) async-start(bf16[4,4,352,256]{3,2,1,0:T(8,128)(2,1)} %copy.297), calls=%async_computation.1 | async-start | bytes 5767168 | tf_op jit(solution)/shard_map/all_to_all | solution.py:434
  149.3 115.8 %reduce-scatter.7.cloned.1.call-start = ((), (), s32[]{:S(2)}) async-start(), calls=%async_computation.17 | async-start | bytes 5242880 | tf_op jit(solution)/shard_map/reduce_scatter | solution.py:426
  215.9 66.8 %all-to-all-start.2 = ((bf16[4,4,352,256]{3,2,1,0:T(8,128)(2,1)}), bf16[4,4,352,256]{3,2,1,0:T(8,128)(2,1)}, u32[]{:S(2)}, u32[]{:S(2)}) async-start(bf16[4,4,352,256]{3,2,1,0:T(8,128)(2,1)} %copy.298), calls=%async_computation.3 | async-start | bytes 5767168 | tf_op jit(solution)/shard_map/all_to_all | solution.py:434
  221.4 140.8 %all-gather.17.cloned.1.call-start = ((), (), s32[]{:S(2)}) async-start(), calls=%async_computation.26 | async-start | bytes 5242880 | tf_op jit(solution)/shard_map/all_gather | solution.py:415
  282.7 160.4 %all-gather.19.cloned.1.call-start = ((), (), s32[]{:S(2)}) async-start(), calls=%async_computation.27 | async-start | bytes 5242880 | tf_op jit(solution)/shard_map/all_gather | solution.py:415
  283.2 26.5 %collective-permute-start.3 = (bf16[1024,512]{1,0:T(8,128)(2,1)}, bf16[1024,512]{1,0:T(8,128)(2,1)}, u32[]{:S(2)}, u32[]{:S(2)}) collective-permute-start(bf16[1024,512]{1,0:T(8,128)(2,1)} %multiply_convert_fusion.8.refs_0_), channel_id=1, source_target_pairs={{0,1},{1,0},{2,3},{3,2},{4,5},{5,4},{6,7},{7,6},{8,9},{9,8},{10,11... | collective-permute-start | bytes 3145736 | tf_op jit(solution)/shard_map/ppermute | solution.py:68
  284.1 45.5 %collective-permute-start.4 = (bf16[1024,512]{1,0:T(8,128)(2,1)}, bf16[1024,512]{1,0:T(8,128)(2,1)}, u32[]{:S(2)}, u32[]{:S(2)}) collective-permute-start(bf16[1024,512]{1,0:T(8,128)(2,1)} %multiply_convert_fusion.8.refs_0_), channel_id=1, source_target_pairs={{0,2},{1,3},{2,0},{3,1},{4,6},{5,7},{6,4},{7,5},{8,10},{9,11},{10,... | collective-permute-start | bytes 3145736 | tf_op jit(solution)/shard_map/ppermute | solution.py:68
  285.3 44.2 %collective-permute-start.5 = (bf16[1024,512]{1,0:T(8,128)(2,1)}, bf16[1024,512]{1,0:T(8,128)(2,1)}, u32[]{:S(2)}, u32[]{:S(2)}) collective-permute-start(bf16[1024,512]{1,0:T(8,128)(2,1)} %multiply_convert_fusion.8.refs_0_), channel_id=1, source_target_pairs={{0,3},{1,2},{2,1},{3,0},{4,7},{5,6},{6,5},{7,4},{8,11},{9,10},{10,... | collective-permute-start | bytes 3145736 | tf_op jit(solution)/shard_map/ppermute | solution.py:68
  386.8 9.5 collective-permute-start.6
  386.9 9.7 collective-permute-start.7
  389.6 136.0 %all-to-all-start.3 = ((bf16[4,2048,512]{2,1,0:T(8,128)(2,1)}), bf16[4,2048,512]{2,1,0:T(8,128)(2,1)}, u32[]{:S(2)}, u32[]{:S(2)}) async-start(bf16[4,2048,512]{2,1,0:T(8,128)(2,1)} %bitcast.416), calls=%async_computation.4 | async-start | bytes 16777216 | tf_op jit(solution)/shard_map/all_to_all | solution.py:431
  395.6 254.2 %all-gather.21.cloned.1.call-start = ((), (), s32[]{:S(2)}) async-start(), calls=%async_computation.28 | async-start | bytes 9732096 | tf_op jit(solution)/shard_map/all_gather | solution.py:644
  445.2 50.4 %collective-permute-start.10 = (bf16[4,352,256]{2,1,0:T(8,128)(2,1)S(1)}, bf16[4,352,256]{2,1,0:T(8,128)(2,1)S(1)}, u32[]{:S(2)}, u32[]{:S(2)}) collective-permute-start(bf16[4,352,256]{2,1,0:T(8,128)(2,1)S(1)} %get-tuple-element.309), channel_id=1, source_target_pairs={{0,24},{4,28},{8,16},{12,20},{16,8},{20,12},{24,0},{28,4},{1,25},{... | collective-permute-start | bytes 2162696 | tf_op jit(solution)/shard_map/ppermute | solution.py:73
  447.7 61.7 %collective-permute-start.9 = (bf16[4,352,256]{2,1,0:T(8,128)(2,1)S(1)}, bf16[4,352,256]{2,1,0:T(8,128)(2,1)S(1)}, u32[]{:S(2)}, u32[]{:S(2)}) collective-permute-start(bf16[4,352,256]{2,1,0:T(8,128)(2,1)S(1)} %get-tuple-element.310), channel_id=1, source_target_pairs={{0,16},{4,20},{8,24},{12,28},{16,0},{20,4},{24,8},{28,12},{1,17},{... | collective-permute-start | bytes 2162696 | tf_op jit(solution)/shard_map/ppermute | solution.py:73
  450.6 58.8 %collective-permute-start.8 = (bf16[4,352,256]{2,1,0:T(8,128)(2,1)S(1)}, bf16[4,352,256]{2,1,0:T(8,128)(2,1)S(1)}, u32[]{:S(2)}, u32[]{:S(2)}) collective-permute-start(bf16[4,352,256]{2,1,0:T(8,128)(2,1)S(1)} %get-tuple-element.311), channel_id=1, source_target_pairs={{0,8},{4,12},{8,0},{12,4},{16,24},{20,28},{24,16},{28,20},{1,9},{5... | collective-permute-start | bytes 2162696 | tf_op jit(solution)/shard_map/ppermute | solution.py:73
  516.3 5.0 collective-permute-start.12
  516.6 5.9 collective-permute-start.13
  520.9 3.6 collective-permute-start.14
  539.1 51.1 %collective-permute-start.11 = (bf16[16,352,256]{2,1,0:T(8,128)(2,1)S(1)}, bf16[16,352,256]{2,1,0:T(8,128)(2,1)}, u32[]{:S(2)}, u32[]{:S(2)}) collective-permute-start(bf16[16,352,256]{2,1,0:T(8,128)(2,1)S(1)} %bitcast.414), channel_id=1, source_target_pairs={{0,4},{4,0},{8,12},{12,8},{16,20},{20,16},{24,28},{28,24},{1,5},{5... | collective-permute-start | bytes 8650760 | tf_op jit(solution)/shard_map/ppermute | solution.py:78
  539.2 99.1 %all-to-all-start.4 = ((bf16[4,2048,512]{2,1,0:T(8,128)(2,1)}), bf16[4,2048,512]{2,1,0:T(8,128)(2,1)}, u32[]{:S(2)}, u32[]{:S(2)}) async-start(bf16[4,2048,512]{2,1,0:T(8,128)(2,1)} %bitcast.417), calls=%async_computation.5 | async-start | bytes 16777216 | tf_op jit(solution)/shard_map/all_to_all | solution.py:431
  664.7 98.6 %all-to-all-start.5 = ((bf16[4,2048,512]{2,1,0:T(8,128)(2,1)}), bf16[4,2048,512]{2,1,0:T(8,128)(2,1)}, u32[]{:S(2)}, u32[]{:S(2)}) async-start(bf16[4,2048,512]{2,1,0:T(8,128)(2,1)} %bitcast.418), calls=%async_computation.6 | async-start | bytes 16777216 | tf_op jit(solution)/shard_map/all_to_all | solution.py:431
  671.4 148.4 %reduce-scatter.9.cloned.1.call-start = ((), (), s32[]{:S(2)}) async-start(), calls=%async_computation.18 | async-start | bytes 5242880 | tf_op jit(solution)/shard_map/reduce_scatter | solution.py:426
  763.3 135.3 %reduce-scatter.11.cloned.1.call-start = ((), (), s32[]{:S(2)}) async-start(), calls=%async_computation.19 | async-start | bytes 5242880 | tf_op jit(solution)/shard_map/reduce_scatter | solution.py:418
  765.0 3.8 collective-permute-start.17
  767.1 4.5 collective-permute-start.16
  772.5 61.3 %collective-permute-start.20 = (f32[4,8,128]{2,1,0:T(8,128)S(1)}, f32[4,8,128]{2,1,0:T(8,128)S(1)}, u32[]{:S(2)}, u32[]{:S(2)}) collective-permute-start(f32[4,8,128]{2,1,0:T(8,128)S(1)} %get-tuple-element.331), channel_id=1, source_target_pairs={{0,3},{1,2},{2,1},{3,0},{4,7},{5,6},{6,5},{7,4},{8,11},{9,10},{10,... | collective-permute-start | bytes 49160 | tf_op jit(solution)/shard_map/ppermute | solution.py:68
  774.0 59.8 %collective-permute-start.19 = (f32[4,8,128]{2,1,0:T(8,128)S(1)}, f32[4,8,128]{2,1,0:T(8,128)S(1)}, u32[]{:S(2)}, u32[]{:S(2)}) collective-permute-start(f32[4,8,128]{2,1,0:T(8,128)S(1)} %get-tuple-element.331), channel_id=1, source_target_pairs={{0,2},{1,3},{2,0},{3,1},{4,6},{5,7},{6,4},{7,5},{8,10},{9,11},{10,... | collective-permute-start | bytes 49160 | tf_op jit(solution)/shard_map/ppermute | solution.py:68
  774.5 59.3 %collective-permute-start.18 = (f32[4,8,128]{2,1,0:T(8,128)S(1)}, f32[4,8,128]{2,1,0:T(8,128)S(1)}, u32[]{:S(2)}, u32[]{:S(2)}) collective-permute-start(f32[4,8,128]{2,1,0:T(8,128)S(1)} %get-tuple-element.331), channel_id=1, source_target_pairs={{0,1},{1,0},{2,3},{3,2},{4,5},{5,4},{6,7},{7,6},{8,9},{9,8},{10,11... | collective-permute-start | bytes 49160 | tf_op jit(solution)/shard_map/ppermute | solution.py:68
  842.3 95.0 %all-to-all-start.6 = ((bf16[4,2048,512]{2,1,0:T(8,128)(2,1)}), bf16[4,2048,512]{2,1,0:T(8,128)(2,1)}, u32[]{:S(2)}, u32[]{:S(2)}) async-start(bf16[4,2048,512]{2,1,0:T(8,128)(2,1)} %bitcast.419), calls=%async_computation.7 | async-start | bytes 16777216 | tf_op jit(solution)/shard_map/all_to_all | solution.py:431
  848.7 178.1 %reduce-scatter.13.cloned.1.call-start = ((), (), s32[]{:S(2)}) async-start(), calls=%async_computation.20 | async-start | bytes 5242880 | tf_op jit(solution)/shard_map/reduce_scatter | solution.py:418
  966.2 12.1 collective-permute-start.21
  966.2 17.4 %collective-permute-start.22 = (bf16[16,352,256]{2,1,0:T(8,128)(2,1)}, bf16[16,352,256]{2,1,0:T(8,128)(2,1)}, u32[]{:S(2)}, u32[]{:S(2)}) collective-permute-start(bf16[16,352,256]{2,1,0:T(8,128)(2,1)} %get-tuple-element.139), channel_id=1, source_target_pairs={{0,4},{4,0},{8,12},{12,8},{16,20},{20,16},{24,28},{28,24},{1,5},{5... | collective-permute-start | bytes 8650760 | tf_op jit(solution)/shard_map/ppermute | solution.py:78
  966.7 21.3 %collective-permute-start.23 = (bf16[16,352,256]{2,1,0:T(8,128)(2,1)}, bf16[16,352,256]{2,1,0:T(8,128)(2,1)}, u32[]{:S(2)}, u32[]{:S(2)}) collective-permute-start(bf16[16,352,256]{2,1,0:T(8,128)(2,1)} %get-tuple-element.141), channel_id=1, source_target_pairs={{0,4},{4,0},{8,12},{12,8},{16,20},{20,16},{24,28},{28,24},{1,5},{5... | collective-permute-start | bytes 8650760 | tf_op jit(solution)/shard_map/ppermute | solution.py:78
  969.1 53.3 %all-to-all-start.7 = ((bf16[4,1024,512]{2,1,0:T(8,128)(2,1)}), bf16[4,1024,512]{2,1,0:T(8,128)(2,1)}, u32[]{:S(2)}, u32[]{:S(2)}) async-start(bf16[4,1024,512]{2,1,0:T(8,128)(2,1)} %bitcast.421), calls=%async_computation.10 | async-start | bytes 8388608 | tf_op jit(solution)/shard_map/all_to_all | solution.py:431
  974.7 136.9 %all-gather.11.cloned.1.call-start = ((), (), s32[]{:S(2)}) async-start(), calls=%async_computation.21 | async-start | bytes 5242880 | tf_op jit(solution)/shard_map/all_gather | solution.py:423
  1046.7 64.9 %all-to-all-start.8 = ((bf16[4,4,352,256]{3,2,1,0:T(8,128)(2,1)}), bf16[4,4,352,256]{3,2,1,0:T(8,128)(2,1)S(1)}, u32[]{:S(2)}, u32[]{:S(2)}) async-start(bf16[4,4,352,256]{3,2,1,0:T(8,128)(2,1)} %bitcast.426), calls=%async_computation.12 | async-start | bytes 5767168 | tf_op jit(solution)/shard_map/all_to_all | solution.py:434
  1051.7 161.9 %all-gather.13.cloned.1.call-start = ((), (), s32[]{:S(2)}) async-start(), calls=%async_computation.22 | async-start | bytes 5242880 | tf_op jit(solution)/shard_map/all_gather | solution.py:423
  1113.1 69.1 %all-to-all-start.9 = ((bf16[4,4,352,256]{3,2,1,0:T(8,128)(2,1)}), bf16[4,4,352,256]{3,2,1,0:T(8,128)(2,1)}, u32[]{:S(2)}, u32[]{:S(2)}) async-start(bf16[4,4,352,256]{3,2,1,0:T(8,128)(2,1)} %bitcast.117), calls=%async_computation.13 | async-start | bytes 5767168 | tf_op jit(solution)/shard_map/all_to_all | solution.py:434
  1121.0 352.7 %reduce-scatter.17.cloned.1.call-start = ((), (), s32[]{:S(2)}) async-start(), calls=%async_computation.24 | async-start | bytes 9732096 | tf_op jit(solution)/shard_map/reduce_scatter | solution.py:786
  1124.8 57.5 %collective-permute-start.24 = (bf16[4,352,256]{2,1,0:T(8,128)(2,1)}, bf16[4,352,256]{2,1,0:T(8,128)(2,1)S(1)}, u32[]{:S(2)}, u32[]{:S(2)}) collective-permute-start(bf16[4,352,256]{2,1,0:T(8,128)(2,1)} %get-tuple-element.306), channel_id=1, source_target_pairs={{0,1},{1,0},{2,3},{3,2},{4,5},{5,4},{6,7},{7,6},{8,9},{9,8},{10,11... | collective-permute-start | bytes 2162696 | tf_op jit(solution)/shard_map/ppermute | solution.py:68
  1126.0 56.3 %collective-permute-start.25 = (bf16[4,352,256]{2,1,0:T(8,128)(2,1)}, bf16[4,352,256]{2,1,0:T(8,128)(2,1)}, u32[]{:S(2)}, u32[]{:S(2)}) collective-permute-start(bf16[4,352,256]{2,1,0:T(8,128)(2,1)} %get-tuple-element.305), channel_id=1, source_target_pairs={{0,2},{1,3},{2,0},{3,1},{4,6},{5,7},{6,4},{7,5},{8,10},{9,11},{10,... | collective-permute-start | bytes 2162696 | tf_op jit(solution)/shard_map/ppermute | solution.py:68
  1127.3 54.9 %collective-permute-start.26 = (bf16[4,352,256]{2,1,0:T(8,128)(2,1)}, bf16[4,352,256]{2,1,0:T(8,128)(2,1)}, u32[]{:S(2)}, u32[]{:S(2)}) collective-permute-start(bf16[4,352,256]{2,1,0:T(8,128)(2,1)} %get-tuple-element.304), channel_id=1, source_target_pairs={{0,3},{1,2},{2,1},{3,0},{4,7},{5,6},{6,5},{7,4},{8,11},{9,10},{10,... | collective-permute-start | bytes 2162696 | tf_op jit(solution)/shard_map/ppermute | solution.py:68
  1183.1 113.9 %all-to-all-start.10 = ((bf16[4,4,352,256]{3,2,1,0:T(8,128)(2,1)}), bf16[4,4,352,256]{3,2,1,0:T(8,128)(2,1)}, u32[]{:S(2)}, u32[]{:S(2)}) async-start(bf16[4,4,352,256]{3,2,1,0:T(8,128)(2,1)} %bitcast.425), calls=%async_computation.14 | async-start | bytes 5767168 | tf_op jit(solution)/shard_map/all_to_all | solution.py:434
  1191.0 286.2 %reduce-scatter.15.cloned.1.call-start = ((), (), s32[]{:S(2)}) async-start(), calls=%async_computation.23 | async-start | bytes 9879552 | tf_op jit(solution)/shard_map/reduce_scatter | solution.py:786
  1218.5 27.4 %collective-permute-start.29 = (bf16[1024,512]{1,0:T(8,128)(2,1)}, bf16[1024,512]{1,0:T(8,128)(2,1)}, u32[]{:S(2)}, u32[]{:S(2)}) collective-permute-start(bf16[1024,512]{1,0:T(8,128)(2,1)} %get-tuple-element.288), channel_id=1, source_target_pairs={{0,3},{1,2},{2,1},{3,0},{4,7},{5,6},{6,5},{7,4},{8,11},{9,10},{10,... | collective-permute-start | bytes 3145736 | tf_op jit(solution)/shard_map/ppermute | solution.py:68
  1225.3 40.2 %collective-permute-start.28 = (bf16[1024,512]{1,0:T(8,128)(2,1)}, bf16[1024,512]{1,0:T(8,128)(2,1)S(1)}, u32[]{:S(2)}, u32[]{:S(2)}) collective-permute-start(bf16[1024,512]{1,0:T(8,128)(2,1)} %get-tuple-element.289), channel_id=1, source_target_pairs={{0,2},{1,3},{2,0},{3,1},{4,6},{5,7},{6,4},{7,5},{8,10},{9,11},{10,... | collective-permute-start | bytes 3145736 | tf_op jit(solution)/shard_map/ppermute | solution.py:68
  1226.1 41.6 %collective-permute-start.27 = (bf16[1024,512]{1,0:T(8,128)(2,1)}, bf16[1024,512]{1,0:T(8,128)(2,1)S(1)}, u32[]{:S(2)}, u32[]{:S(2)}) collective-permute-start(bf16[1024,512]{1,0:T(8,128)(2,1)} %get-tuple-element.287), channel_id=1, source_target_pairs={{0,1},{1,0},{2,3},{3,2},{4,5},{5,4},{6,7},{7,6},{8,9},{9,8},{10,11... | collective-permute-start | bytes 3145736 | tf_op jit(solution)/shard_map/ppermute | solution.py:68
  1235.7 61.3 %collective-permute-start.30 = (bf16[4,352,256]{2,1,0:T(8,128)(2,1)}, bf16[4,352,256]{2,1,0:T(8,128)(2,1)}, u32[]{:S(2)}, u32[]{:S(2)}) collective-permute-start(bf16[4,352,256]{2,1,0:T(8,128)(2,1)} %get-tuple-element.302), channel_id=1, source_target_pairs={{0,1},{1,0},{2,3},{3,2},{4,5},{5,4},{6,7},{7,6},{8,9},{9,8},{10,11... | collective-permute-start | bytes 2162696 | tf_op jit(solution)/shard_map/ppermute | solution.py:68
  1237.3 59.7 %collective-permute-start.31 = (bf16[4,352,256]{2,1,0:T(8,128)(2,1)}, bf16[4,352,256]{2,1,0:T(8,128)(2,1)}, u32[]{:S(2)}, u32[]{:S(2)}) collective-permute-start(bf16[4,352,256]{2,1,0:T(8,128)(2,1)} %get-tuple-element.301), channel_id=1, source_target_pairs={{0,2},{1,3},{2,0},{3,1},{4,6},{5,7},{6,4},{7,5},{8,10},{9,11},{10,... | collective-permute-start | bytes 2162696 | tf_op jit(solution)/shard_map/ppermute | solution.py:68
  1245.9 51.1 %collective-permute-start.32 = (bf16[4,352,256]{2,1,0:T(8,128)(2,1)}, bf16[4,352,256]{2,1,0:T(8,128)(2,1)}, u32[]{:S(2)}, u32[]{:S(2)}) collective-permute-start(bf16[4,352,256]{2,1,0:T(8,128)(2,1)} %get-tuple-element.300), channel_id=1, source_target_pairs={{0,3},{1,2},{2,1},{3,0},{4,7},{5,6},{6,5},{7,4},{8,11},{9,10},{10,... | collective-permute-start | bytes 2162696 | tf_op jit(solution)/shard_map/ppermute | solution.py:68
  1339.8 19.1 %collective-permute-start.39 = (bf16[4,352,256]{2,1,0:T(8,128)(2,1)S(1)}, bf16[4,352,256]{2,1,0:T(8,128)(2,1)S(1)}, u32[]{:S(2)}, u32[]{:S(2)}) collective-permute-start(bf16[4,352,256]{2,1,0:T(8,128)(2,1)S(1)} %get-tuple-element.298), channel_id=1, source_target_pairs={{0,1},{1,0},{2,3},{3,2},{4,5},{5,4},{6,7},{7,6},{8,9},{9,8},{10,11... | collective-permute-start | bytes 2162696 | tf_op jit(solution)/shard_map/ppermute | solution.py:68
  1339.8 127.7 %collective-permute-start.33 = (bf16[1024,512]{1,0:T(8,128)(2,1)}, bf16[1024,512]{1,0:T(8,128)(2,1)}, u32[]{:S(2)}, u32[]{:S(2)}) collective-permute-start(bf16[1024,512]{1,0:T(8,128)(2,1)} %fusion.38.refs_0_), channel_id=1, source_target_pairs={{0,1},{1,0},{2,3},{3,2},{4,5},{5,4},{6,7},{7,6},{8,9},{9,8},{10,11... | collective-permute-start | bytes 3145736 | tf_op jit(solution)/shard_map/ppermute | solution.py:68
  1341.9 125.7 %collective-permute-start.34 = (bf16[1024,512]{1,0:T(8,128)(2,1)}, bf16[1024,512]{1,0:T(8,128)(2,1)}, u32[]{:S(2)}, u32[]{:S(2)}) collective-permute-start(bf16[1024,512]{1,0:T(8,128)(2,1)} %fusion.38.refs_0_), channel_id=1, source_target_pairs={{0,2},{1,3},{2,0},{3,1},{4,6},{5,7},{6,4},{7,5},{8,10},{9,11},{10,... | collective-permute-start | bytes 3145736 | tf_op jit(solution)/shard_map/ppermute | solution.py:68
  1343.2 124.4 %collective-permute-start.35 = (bf16[1024,512]{1,0:T(8,128)(2,1)}, bf16[1024,512]{1,0:T(8,128)(2,1)}, u32[]{:S(2)}, u32[]{:S(2)}) collective-permute-start(bf16[1024,512]{1,0:T(8,128)(2,1)} %fusion.38.refs_0_), channel_id=1, source_target_pairs={{0,3},{1,2},{2,1},{3,0},{4,7},{5,6},{6,5},{7,4},{8,11},{9,10},{10,... | collective-permute-start | bytes 3145736 | tf_op jit(solution)/shard_map/ppermute | solution.py:68
  1343.4 108.9 %collective-permute-start.40 = (bf16[4,352,256]{2,1,0:T(8,128)(2,1)}, bf16[4,352,256]{2,1,0:T(8,128)(2,1)}, u32[]{:S(2)}, u32[]{:S(2)}) collective-permute-start(bf16[4,352,256]{2,1,0:T(8,128)(2,1)} %get-tuple-element.297), channel_id=1, source_target_pairs={{0,2},{1,3},{2,0},{3,1},{4,6},{5,7},{6,4},{7,5},{8,10},{9,11},{10,... | collective-permute-start | bytes 2162696 | tf_op jit(solution)/shard_map/ppermute | solution.py:68
  1359.8 92.5 %collective-permute-start.41 = (bf16[4,352,256]{2,1,0:T(8,128)(2,1)}, bf16[4,352,256]{2,1,0:T(8,128)(2,1)}, u32[]{:S(2)}, u32[]{:S(2)}) collective-permute-start(bf16[4,352,256]{2,1,0:T(8,128)(2,1)} %get-tuple-element.296), channel_id=1, source_target_pairs={{0,3},{1,2},{2,1},{3,0},{4,7},{5,6},{6,5},{7,4},{8,11},{9,10},{10,... | collective-permute-start | bytes 2162696 | tf_op jit(solution)/shard_map/ppermute | solution.py:68
  1479.5 11.3 collective-permute-start.38
  1481.0 14.1 collective-permute-start.37
  1481.0 14.1 collective-permute-start.36
  (113 other events, 1767.0 us)
Sparse Core Ops, SparseCore 0:
  20.3 86.0 all-gather.14
  212.4 52.5 reduce-scatter.6
  282.8 79.3 all-gather.16
  363.7 79.2 all-gather.18
  511.4 83.6 all-gather.20
  763.4 52.8 reduce-scatter.8
  822.9 75.6 reduce-scatter.10
  949.5 76.7 reduce-scatter.12
  1046.8 53.3 all-gather.10
  1111.7 77.3 all-gather.12
  1191.5 140.3 reduce-scatter.16
  1336.9 92.1 reduce-scatter.14

commit v10 on v9

--- a/solution.py
+++ b/solution.py
@@ -840,8 +840,13 @@
     normed_full, output = lax.optimization_barrier(
         (dot(query_grad, query_t) + dot(down_grad, down_t), gather_t(output_part))
     )
+    pieces = [lay.over_t(part_for(normed_full, k).astype(BF16), k) for k in range(1, nt)]
+    pieces[0], query_grad, kv_grad, down_grad = lax.optimization_barrier(
+        (pieces[0], query_grad, kv_grad, down_grad)
+    )
+    normed_grad = part_for(normed_full, 0) + sum(piece.astype(F32) for piece in pieces)
     normed_grad, grad_plane[2], grad_home[1] = lax.optimization_barrier(
-        (scatter_t_direct(normed_full), grad_plane[2], to_columns(grad_plane[1]))
+        (normed_grad, grad_plane[2], to_columns(grad_plane[1]))
     )
     attn_hat = own_part(hidden).astype(F32) * attn_inverse
     scaled_in = lax.dynamic_slice_in_dim(attn_scale, me_t * part, part, 0) * normed_grad
@@ -849,9 +854,7 @@
     input_grad = residual_grad + attn_inverse * (
         scaled_in - attn_hat * row_mean(attn_hat * scaled_in)
     )
-    input_low, grad_plane[2], query_grad, kv_grad, down_grad = lax.optimization_barrier(
-        (input_grad.astype(BF16), grad_plane[2], query_grad, kv_grad, down_grad)
-    )
+    input_low, grad_plane[2] = lax.optimization_barrier((input_grad.astype(BF16), grad_plane[2]))
     grad_home[2] = to_columns(grad_plane[2])
     grad_expert_in, grad_expert_out = home_gradients(lay, ids, grad_home, f_loc, d_loc)
     grad_hidden = gather_t_direct(input_low)
@@ -864,14 +867,12 @@
     kv_gain_row = jnp.pad(
         grad_kv_gain.reshape(ndp, lat_loc), ((0, 0), (0, d_loc - lat_loc))
     ).reshape(1, width)
-    gain_grads = jnp.concatenate([spread(ffn_gain_part), kv_gain_row], 0)
-    attn_sum_all = lax.psum(spread(attn_gain_part).reshape(-1, 128), ("dp", "tensor"))
-    attn_gain_grad = lax.dynamic_slice_in_dim(attn_sum_all.reshape(-1), me_dp * d_loc, d_loc, 0)
+    gain_grads = jnp.concatenate([spread(attn_gain_part), spread(ffn_gain_part), kv_gain_row], 0)
     front_sum = sum_dp(
         jnp.concatenate(
             [
                 by_owner(dot_tn(down_grad, normed_low)),
-                by_owner(jnp.pad(gain_grads, ((0, 14), (0, 0)))),
+                by_owner(jnp.pad(gain_grads, ((0, 13), (0, 0)))),
                 by_owner(router_part),
                 by_owner(dot_tn(query_grad, normed_low)),
                 by_owner(grad_out_w),
@@ -888,13 +889,13 @@
     return (
         output,
         grad_hidden,
-        attn_gain_grad,
+        own_sum[down_rows],
         jnp.transpose(by_head(front_sum[at : at + q_rows])),
         jnp.transpose(own_sum[:down_rows]),
-        own_sum[down_rows + 1, :lat_loc],
+        own_sum[down_rows + 2, :lat_loc],
         front_sum[at + q_rows + out_rows :].reshape(w_kv_up.shape),
         front_sum[at + q_rows : at + q_rows + out_rows],
-        own_sum[down_rows],
+        own_sum[down_rows + 1],
         jnp.transpose(front_sum[down_rows + EXPERTS : at]),
         grad_expert_in,
         grad_expert_out,

time: 1520 us -> 1480 us (0.974)
  blocking collectives: 118 us -> 24.9 us
  waiting for transfers between devices: 514 us -> 569 us
    psum x1 -> x0, blocking collectives: 91 us -> none  [body(): lax.psum(spread(attn_gain_part).reshape(-1, 128), ('dp', 'tensor'))]
    ppermute x24, waiting for transfers between devices: 82.3 us -> 145 us  [over_t(): return lax.ppermute(values, 'tensor', [(i, i ^ k) for i in range(self.t)])]
    unnamed x249 -> x245, local copies, waits for them, and re-layouts: 48.6 us -> 47.4 us
  transfers between devices with their start and end apart: 65 -> 65, of which waited for: 32 -> 33; matrix products, arithmetic and copies ran while one was open for 36% -> 37% of each run, Pallas kernels for 7% -> 7%
where the time goes in v10:
time: 1480 us; the launch traced here: 1470 us
  waiting for transfers between devices  569 us (38%)
  matrix products  322 us (22%)
  local copies, waits for them, and re-layouts  203 us (14%)
  starting transfers between devices  120 us (8%)
  other arithmetic  114 us (8%)
  Pallas kernels  100 us (7%)
  blocking collectives  24.9 us (2%)
  between operations  16.7 us (1%)
    ppermute x24, waiting for transfers between devices, over_t(): return lax.ppermute(values, 'tensor', [(i, i ^ k) for i in range(self.t)])  145 us
    all_to_all x6, waiting for transfers between devices, swap_t(): lax.all_to_all(values, 'tensor', split_axis=0, concat_axis=0, tiled=True)  132 us
    dot_general x9, matrix products, dot_nt(): lax.dot_general(a, b, (((1,), (1,)), ((), ())), preferred_element_type=F32)  99.6 us
    all_to_all x5, waiting for transfers between devices, swap_z(): lax.all_to_all(values, 'dp', split_axis=0, concat_axis=0, axis_index_grou...  87.4 us
    dot_general x8, matrix products, dot_tn(): lax.dot_general(a, b, (((0,), (0,)), ((), ())), preferred_element_type=F32)  82.3 us
    dot_general x9, matrix products, dot(): return jnp.dot(a, b, preferred_element_type=F32)  78.5 us
    all_gather x2, waiting for transfers between devices, gather_z(): lax.all_gather(values, 'dp', axis=0, tiled=False, axis_index_groups=lay.z...  59.7 us
    all_gather x1, waiting for transfers between devices, body(): front = lax.all_gather(front_pack, 'dp', axis=0, tiled=False)  55.1 us
  transfers between devices with their start and end apart: 65, of which 33 were waited for; matrix products, arithmetic and copies ran while one was open for 37% of the time, Pallas kernels for 7%

profile of v10, /device:TPU:10, one launch (start us, length us, event | category | flops | bytes accessed | tf_op | source)
XLA Modules:
  0.0 1469.8 jit_solution(14627526113781259555)
XLA Ops:
  20.2 6.9 maximum_bitcast_fusion
  27.1 8.3 copy.295
  35.5 6.5 all-to-all-start
  51.4 55.1 %all-gather.15.cloned.1.call-done = bf16[17152,256]{1,0:T(8,128)(2,1)} async-done(((bf16[2144,256]{1,0:T(8,128)(2,1)}), bf16[17152,256]{1,0:T(8,128)(2,1)}) %all-gather.15.cloned.1.call-update) | async-done | bytes 8781840 | tf_op jit(solution)/shard_map/all_gather | solution.py:495
  117.2 19.5 %all-to-all-done = bf16[4,4,3,352,256]{4,3,1,2,0:T(8,128)(2,1)} async-done(((bf16[4,4,3,352,256]{4,3,1,2,0:T(8,128)(2,1)}), bf16[4,4,3,352,256]{4,3,1,2,0:T(8,128)(2,1)}, u32[]{:S(2)}, u32[]{:S(2)}) %all-to-all-start) | async-done | bytes 8650784 | tf_op jit(solution)/shard_map/all_to_all | solution.py:431
  166.1 6.4 fusion.114
  191.0 14.6 attend.1
  221.5 43.6 %reduce-scatter.7.cloned.1.call-done = bf16[1024,512]{1,0:T(8,128)(2,1)} async-done(((bf16[1024,2048]{1,0:T(8,128)(2,1)}), bf16[1024,512]{1,0:T(8,128)(2,1)}) %reduce-scatter.7.cloned.1.call-update) | async-done | bytes 1048592 | tf_op jit(solution)/shard_map/reduce_scatter | solution.py:426
  267.0 8.1 psum.21
  292.4 17.3 %collective-permute-done.3.refs_1_ = bf16[1024,512]{1,0:T(8,128)(2,1)} collective-permute-done((bf16[1024,512]{1,0:T(8,128)(2,1)}, bf16[1024,512]{1,0:T(8,128)(2,1)}, u32[]{:S(2)}, u32[]{:S(2)}) %collective-permute-start.3) | collective-permute-done | bytes 1048608 | tf_op jit(solution)/shard_map/ppermute | solution.py:68
  309.6 19.9 %collective-permute-done.4.refs_2_ = bf16[1024,512]{1,0:T(8,128)(2,1)} collective-permute-done((bf16[1024,512]{1,0:T(8,128)(2,1)}, bf16[1024,512]{1,0:T(8,128)(2,1)}, u32[]{:S(2)}, u32[]{:S(2)}) %collective-permute-start.4) | collective-permute-done | bytes 1048608 | tf_op jit(solution)/shard_map/ppermute | solution.py:68
  329.6 6.2 join_columns.2
  335.8 26.5 %all-gather.17.cloned.1.call-done = bf16[4096,512]{1,0:T(8,128)(2,1)} async-done(((bf16[1024,512]{1,0:T(8,128)(2,1)}), bf16[4096,512]{1,0:T(8,128)(2,1)}) %all-gather.17.cloned.1.call-update) | async-done | bytes 4194320 | tf_op jit(solution)/shard_map/all_gather | solution.py:415
  363.1 16.2 %convert_bitcast_fusion.1 = bf16[4,4,512,512]{3,2,0,1:T(8,128)(2,1)} fusion(s32[4,4,1024]{2,1,0:T(4,128)S(1)} %fusion.46, bf16[4,1024,512]{2,1,0:T(8,128)(2,1)} %bitcast.531), kind=kOutput, calls=%fused_computation.39 | convolution fusion | flops 8602517504 | bytes 12648448 | tf_op jit(solution)/shard_map/sepk,skd->espd/dot_general | solution.py:528
  379.3 7.6 copy.300
  396.6 13.2 lay_out_weights.2
  409.8 33.2 %all-gather.19.cloned.1.call-done = bf16[4096,512]{1,0:T(8,128)(2,1)} async-done(((bf16[1024,512]{1,0:T(8,128)(2,1)}), bf16[4096,512]{1,0:T(8,128)(2,1)}) %all-gather.19.cloned.1.call-update) | async-done | bytes 4194320 | tf_op jit(solution)/shard_map/all_gather | solution.py:415
  450.6 14.3 convert_bitcast_fusion
  465.0 7.4 copy.303
  472.4 23.2 %collective-permute-done.10 = bf16[4,352,256]{2,1,0:T(8,128)(2,1)S(1)} collective-permute-done((bf16[4,352,256]{2,1,0:T(8,128)(2,1)S(1)}, bf16[4,352,256]{2,1,0:T(8,128)(2,1)S(1)}, u32[]{:S(2)}, u32[]{:S(2)}) %collective-permute-start.10) | collective-permute-done | bytes 720928 | tf_op jit(solution)/shard_map/ppermute | solution.py:73
  495.6 13.9 collective-permute-done.9
  525.7 11.5 copy.301
  539.2 6.4 all-to-all-start.4
  545.6 32.3 %fusion.123 = f32[2048,2816]{1,0:T(8,128)} fusion(bf16[2048,2048]{0,1:T(8,128)(2,1)} %bitcast.439, bf16[2816,2048]{1,0:T(8,128)(2,1)} %bitcast.424), kind=kOutput, calls=%fused_computation.303 | convolution fusion | flops 23622320128 | bytes 42991616 | tf_op jit(solution)/shard_map/dot_general | solution.py:30
  577.9 12.3 fusion.8
  590.3 9.3 lay_out_weights.3
  602.0 15.0 %multiply_convert_fusion = bf16[2048,2048]{1,0:T(8,128)(2,1)} fusion(bf16[2048,1408]{1,0:T(8,128)(2,1)S(1)} %get-tuple-element.276, f32[2048]{0:T(1024)S(1)} %bitcast.501, bf16[1,1408,2048]{2,1,0:T(8,128)(2,1)S(1)} %lay_out_weights.3), kind=kOutput, calls=%fused_computation.5 | convolution fusion | flops 11819548672 | bytes 19931136 | tf_op jit(solution)/shard_map/dot_general | solution.py:26
  617.1 21.2 %all-to-all-done.4 = bf16[4,2048,512]{2,1,0:T(8,128)(2,1)} async-done(((bf16[4,2048,512]{2,1,0:T(8,128)(2,1)}), bf16[4,2048,512]{2,1,0:T(8,128)(2,1)}, u32[]{:S(2)}, u32[]{:S(2)}) %all-to-all-start.4) | async-done | bytes 8388640 | tf_op jit(solution)/shard_map/all_to_all | solution.py:431
  638.3 11.5 copy.310
  657.3 7.4 copy.389
  664.7 6.6 all-to-all-start.5
  671.4 8.2 copy.313
  679.6 10.4 fusion.124
  702.9 27.3 %multiply_convert_fusion.2 = (bf16[2048,1408]{1,0:T(8,128)(2,1)S(1)}, bf16[2048,1408]{1,0:T(8,128)(2,1)}, f32[2048]{0:T(1024)S(1)}) fusion(f32[2048,2816]{1,0:T(8,128)} %fusion.123, f32[2048]{0:T(1024)S(1)} %bitcast.502, bf16[2048,1408]{1,0:T(8,128)(2,1)} %copy-done.34, bf16[2048,2048]{0,1:T(8,128)(2,1)} %bitcast.441, bf16[1,1408,2048]{2,1,0:T(8,128)(2,1)} %copy-done), kind=kOutput, calls=%fused_computation.16 | convolution fusion | flops 11860178944 | bytes 54542336 | tf_op jit(solution)/shard_map/dot_general | solution.py:30
  730.3 7.9 pad_maximum_fusion
  738.2 25.1 %all-to-all-done.5 = bf16[4,2048,512]{2,1,0:T(8,128)(2,1)} async-done(((bf16[4,2048,512]{2,1,0:T(8,128)(2,1)}), bf16[4,2048,512]{2,1,0:T(8,128)(2,1)}, u32[]{:S(2)}, u32[]{:S(2)}) %all-to-all-start.5) | async-done | bytes 8388640 | tf_op jit(solution)/shard_map/all_to_all | solution.py:431
  776.0 31.6 %convolution_convert_fusion.3 = bf16[2048,2048]{1,0:T(8,128)(2,1)} fusion(bf16[2048,2816]{1,0:T(8,128)(2,1)} %pad_maximum_fusion, bf16[2816,2048]{1,0:T(8,128)(2,1)} %bitcast.425), kind=kOutput, calls=%fused_computation.42 | convolution fusion | flops 23626514432 | bytes 31457280 | tf_op jit(solution)/shard_map/dot_general | solution.py:26
  807.6 12.2 bitcast_convert_fusion.1
  822.8 11.0 fusion.42
  834.7 7.6 copy.388
  842.3 6.4 all-to-all-start.6
  848.7 17.9 %convolution_convert_fusion.2.out_ref = bf16[1408,2048]{1,0:T(8,128)(2,1)} fusion(bf16[2048,1408]{1,0:T(8,128)(2,1)} %get-tuple-element.131, bf16[2048,2048]{0,1:T(8,128)(2,1)} %bitcast.442), kind=kOutput, calls=%fused_computation.41 | convolution fusion | flops 11814043648 | bytes 19922944 | tf_op jit(solution)/shard_map/dot_general | solution.py:34
  866.6 31.6 %convolution_convert_fusion = bf16[2816,2048]{1,0:T(8,128)(2,1)} fusion(bf16[2048,2816]{1,0:T(8,128)(2,1)} %pad_maximum_fusion, bf16[2048,2048]{0,1:T(8,128)(2,1)} %bitcast.440), kind=kOutput, calls=%fused_computation.20 | convolution fusion | flops 23628087296 | bytes 31457280 | tf_op jit(solution)/shard_map/dot_general | solution.py:34
  901.5 35.8 %all-to-all-done.6 = bf16[4,2048,512]{2,1,0:T(8,128)(2,1)} async-done(((bf16[4,2048,512]{2,1,0:T(8,128)(2,1)}), bf16[4,2048,512]{2,1,0:T(8,128)(2,1)}, u32[]{:S(2)}, u32[]{:S(2)}) %all-to-all-start.6) | async-done | bytes 8388640 | tf_op jit(solution)/shard_map/all_to_all | solution.py:431
  937.3 12.1 bitcast_convert_fusion
  949.5 15.1 %take_apart.1 = (bf16[16,352,256]{2,1,0:T(8,128)(2,1)S(1)}, bf16[16,352,256]{2,1,0:T(8,128)(2,1)S(1)}, bf16[16,352,256]{2,1,0:T(8,128)(2,1)S(1)}, bf16[16,352,25...) custom-call(s32[3]{0:T(128)S(1)} %get-tuple-element.278.ids_ref, ...), custom_call_target="tpu_custom_call" | custom-call | bytes 34603008 | tf_op jit(solution)/shard_map/take_apart/pallas_call | solution.py:128
  992.4 30.1 %all-to-all-done.7 = bf16[4,1024,512]{2,1,0:T(8,128)(2,1)} async-done(((bf16[4,1024,512]{2,1,0:T(8,128)(2,1)}), bf16[4,1024,512]{2,1,0:T(8,128)(2,1)}, u32[]{:S(2)}, u32[]{:S(2)}) %all-to-all-start.7) | async-done | bytes 4194336 | tf_op jit(solution)/shard_map/all_to_all | solution.py:431
  1033.9 8.0 psum.22
  1051.9 6.1 convolution_convert_fusion.5
  1060.8 7.2 convolution_convert_fusion.1
  1072.1 39.5 %all-to-all-done.8 = bf16[4,4,352,256]{3,2,1,0:T(8,128)(2,1)S(1)} async-done(((bf16[4,4,352,256]{3,2,1,0:T(8,128)(2,1)}), bf16[4,4,352,256]{3,2,1,0:T(8,128)(2,1)S(1)}, u32[]{:S(2)}, u32[]{:S(2)}) %all-to-all-start.8) | async-done | bytes 2883616 | tf_op jit(solution)/shard_map/all_to_all | solution.py:434
  1113.2 7.8 all-to-all-start.9
  1133.4 21.6 %attend_back.1 = (bf16[1024,512]{1,0:T(8,128)(2,1)S(1)}, f32[1024,256]{1,0:T(8,128)S(1)}, bf16[1024,1024]{1,0:T(8,128)(2,1)S(1)}, f32[1024,256]{1,0:T(8,128)S(1)}) custom-call(s32[1]{0:T(128)} %copy.411.len_ref, bf16[1024,512]{1,0:T(8,128)(2,1)S(1)} %copy-done.5, bf16[1024,256]{1,0:T(8,128)(2,1)S(1)} %copy-done.10, bf16[1024,1024]{1,0:T(8,128)(2,1)S(1)} %copy-done.14, ...), custom_call_target="tpu_custom_call" | custom-call | flops 6710886400 | bytes 33554432 | tf_op jit(solution)/shard_map/attend_back/pallas_call | solution.py:330
  1157.3 25.0 %all-to-all-done.9 = bf16[4,4,352,256]{3,2,1,0:T(8,128)(2,1)} async-done(((bf16[4,4,352,256]{3,2,1,0:T(8,128)(2,1)}), bf16[4,4,352,256]{3,2,1,0:T(8,128)(2,1)}, u32[]{:S(2)}, u32[]{:S(2)}) %all-to-all-start.9) | async-done | bytes 2883616 | tf_op jit(solution)/shard_map/all_to_all | solution.py:434
  1183.1 7.9 all-to-all-start.10
  1208.3 6.3 convolution_add_fusion
  1238.5 7.4 collective-permute-done.27
  1250.4 18.7 %collective-permute-done.29 = bf16[1024,512]{1,0:T(8,128)(2,1)S(1)} collective-permute-done((bf16[1024,512]{1,0:T(8,128)(2,1)}, bf16[1024,512]{1,0:T(8,128)(2,1)S(1)}, u32[]{:S(2)}, u32[]{:S(2)}) %collective-permute-start.29) | collective-permute-done | bytes 1048608 | tf_op jit(solution)/shard_map/ppermute | solution.py:68
  1278.6 18.4 %all-to-all-done.10 = bf16[4,4,352,256]{3,2,1,0:T(8,128)(2,1)} async-done(((bf16[4,4,352,256]{3,2,1,0:T(8,128)(2,1)}), bf16[4,4,352,256]{3,2,1,0:T(8,128)(2,1)}, u32[]{:S(2)}, u32[]{:S(2)}) %all-to-all-start.10) | async-done | bytes 2883616 | tf_op jit(solution)/shard_map/all_to_all | solution.py:434
  1329.2 8.8 psum.23
  1349.1 13.4 collective-permute-done.39.refs_9_
  1364.2 54.5 %collective-permute-done.40.refs_10_ = bf16[4,352,256]{2,1,0:T(8,128)(2,1)S(1)} collective-permute-done((bf16[4,352,256]{2,1,0:T(8,128)(2,1)S(1)}, bf16[4,352,256]{2,1,0:T(8,128)(2,1)S(1)}, u32[]{:S(2)}, u32[]{:S(2)}) %collective-permute-start.40) | collective-permute-done | bytes 720928 | tf_op jit(solution)/shard_map/ppermute | solution.py:68
  1418.6 13.8 home_gradients.1
  1434.4 6.1 join_columns.3
  (509 shorter events, 390.9 us)
Async XLA Ops:
  7.2 99.3 %all-gather.15.cloned.1.call-start = ((), (), s32[]{:S(2)}) async-start(), calls=%async_computation.25 | async-start | bytes 9879552 | tf_op jit(solution)/shard_map/all_gather | solution.py:495
  35.5 101.2 %all-to-all-start = ((bf16[4,4,3,352,256]{4,3,1,2,0:T(8,128)(2,1)}), bf16[4,4,3,352,256]{4,3,1,2,0:T(8,128)(2,1)}, u32[]{:S(2)}, u32[]{:S(2)}) async-start(bf16[4,4,3,352,256]{4,3,1,2,0:T(8,128)(2,1)} %copy.295), calls=%async_computation | async-start | bytes 17301504 | tf_op jit(solution)/shard_map/all_to_all | solution.py:431
  41.9 9.0 collective-permute-start
  43.5 7.4 collective-permute-start.1
  44.7 6.6 collective-permute-start.2
  143.9 68.4 %all-to-all-start.1 = ((bf16[4,4,352,256]{3,2,1,0:T(8,128)(2,1)}), bf16[4,4,352,256]{3,2,1,0:T(8,128)(2,1)S(1)}, u32[]{:S(2)}, u32[]{:S(2)}) async-start(bf16[4,4,352,256]{3,2,1,0:T(8,128)(2,1)} %copy.297), calls=%async_computation.1 | async-start | bytes 5767168 | tf_op jit(solution)/shard_map/all_to_all | solution.py:434
  149.3 115.8 %reduce-scatter.7.cloned.1.call-start = ((), (), s32[]{:S(2)}) async-start(), calls=%async_computation.17 | async-start | bytes 5242880 | tf_op jit(solution)/shard_map/reduce_scatter | solution.py:426
  216.0 66.7 %all-to-all-start.2 = ((bf16[4,4,352,256]{3,2,1,0:T(8,128)(2,1)}), bf16[4,4,352,256]{3,2,1,0:T(8,128)(2,1)}, u32[]{:S(2)}, u32[]{:S(2)}) async-start(bf16[4,4,352,256]{3,2,1,0:T(8,128)(2,1)} %copy.298), calls=%async_computation.3 | async-start | bytes 5767168 | tf_op jit(solution)/shard_map/all_to_all | solution.py:434
  221.4 140.8 %all-gather.17.cloned.1.call-start = ((), (), s32[]{:S(2)}) async-start(), calls=%async_computation.26 | async-start | bytes 5242880 | tf_op jit(solution)/shard_map/all_gather | solution.py:415
  282.7 160.4 %all-gather.19.cloned.1.call-start = ((), (), s32[]{:S(2)}) async-start(), calls=%async_computation.27 | async-start | bytes 5242880 | tf_op jit(solution)/shard_map/all_gather | solution.py:415
  283.2 26.5 %collective-permute-start.3 = (bf16[1024,512]{1,0:T(8,128)(2,1)}, bf16[1024,512]{1,0:T(8,128)(2,1)}, u32[]{:S(2)}, u32[]{:S(2)}) collective-permute-start(bf16[1024,512]{1,0:T(8,128)(2,1)} %multiply_convert_fusion.8.refs_0_), channel_id=1, source_target_pairs={{0,1},{1,0},{2,3},{3,2},{4,5},{5,4},{6,7},{7,6},{8,9},{9,8},{10,11... | collective-permute-start | bytes 3145736 | tf_op jit(solution)/shard_map/ppermute | solution.py:68
  284.1 45.5 %collective-permute-start.4 = (bf16[1024,512]{1,0:T(8,128)(2,1)}, bf16[1024,512]{1,0:T(8,128)(2,1)}, u32[]{:S(2)}, u32[]{:S(2)}) collective-permute-start(bf16[1024,512]{1,0:T(8,128)(2,1)} %multiply_convert_fusion.8.refs_0_), channel_id=1, source_target_pairs={{0,2},{1,3},{2,0},{3,1},{4,6},{5,7},{6,4},{7,5},{8,10},{9,11},{10,... | collective-permute-start | bytes 3145736 | tf_op jit(solution)/shard_map/ppermute | solution.py:68
  285.4 44.2 %collective-permute-start.5 = (bf16[1024,512]{1,0:T(8,128)(2,1)}, bf16[1024,512]{1,0:T(8,128)(2,1)}, u32[]{:S(2)}, u32[]{:S(2)}) collective-permute-start(bf16[1024,512]{1,0:T(8,128)(2,1)} %multiply_convert_fusion.8.refs_0_), channel_id=1, source_target_pairs={{0,3},{1,2},{2,1},{3,0},{4,7},{5,6},{6,5},{7,4},{8,11},{9,10},{10,... | collective-permute-start | bytes 3145736 | tf_op jit(solution)/shard_map/ppermute | solution.py:68
  386.9 9.5 collective-permute-start.6
  386.9 9.7 collective-permute-start.7
  389.6 136.0 %all-to-all-start.3 = ((bf16[4,2048,512]{2,1,0:T(8,128)(2,1)}), bf16[4,2048,512]{2,1,0:T(8,128)(2,1)}, u32[]{:S(2)}, u32[]{:S(2)}) async-start(bf16[4,2048,512]{2,1,0:T(8,128)(2,1)} %bitcast.418), calls=%async_computation.4 | async-start | bytes 16777216 | tf_op jit(solution)/shard_map/all_to_all | solution.py:431
  395.6 254.1 %all-gather.21.cloned.1.call-start = ((), (), s32[]{:S(2)}) async-start(), calls=%async_computation.28 | async-start | bytes 9732096 | tf_op jit(solution)/shard_map/all_gather | solution.py:644
  445.2 50.4 %collective-permute-start.10 = (bf16[4,352,256]{2,1,0:T(8,128)(2,1)S(1)}, bf16[4,352,256]{2,1,0:T(8,128)(2,1)S(1)}, u32[]{:S(2)}, u32[]{:S(2)}) collective-permute-start(bf16[4,352,256]{2,1,0:T(8,128)(2,1)S(1)} %get-tuple-element.311), channel_id=1, source_target_pairs={{0,24},{4,28},{8,16},{12,20},{16,8},{20,12},{24,0},{28,4},{1,25},{... | collective-permute-start | bytes 2162696 | tf_op jit(solution)/shard_map/ppermute | solution.py:73
  447.7 61.7 %collective-permute-start.9 = (bf16[4,352,256]{2,1,0:T(8,128)(2,1)S(1)}, bf16[4,352,256]{2,1,0:T(8,128)(2,1)S(1)}, u32[]{:S(2)}, u32[]{:S(2)}) collective-permute-start(bf16[4,352,256]{2,1,0:T(8,128)(2,1)S(1)} %get-tuple-element.312), channel_id=1, source_target_pairs={{0,16},{4,20},{8,24},{12,28},{16,0},{20,4},{24,8},{28,12},{1,17},{... | collective-permute-start | bytes 2162696 | tf_op jit(solution)/shard_map/ppermute | solution.py:73
  450.6 58.8 %collective-permute-start.8 = (bf16[4,352,256]{2,1,0:T(8,128)(2,1)S(1)}, bf16[4,352,256]{2,1,0:T(8,128)(2,1)S(1)}, u32[]{:S(2)}, u32[]{:S(2)}) collective-permute-start(bf16[4,352,256]{2,1,0:T(8,128)(2,1)S(1)} %get-tuple-element.313), channel_id=1, source_target_pairs={{0,8},{4,12},{8,0},{12,4},{16,24},{20,28},{24,16},{28,20},{1,9},{5... | collective-permute-start | bytes 2162696 | tf_op jit(solution)/shard_map/ppermute | solution.py:73
  516.3 5.0 collective-permute-start.12
  516.6 5.9 collective-permute-start.13
  520.9 3.6 collective-permute-start.14
  539.1 51.1 %collective-permute-start.11 = (bf16[16,352,256]{2,1,0:T(8,128)(2,1)S(1)}, bf16[16,352,256]{2,1,0:T(8,128)(2,1)}, u32[]{:S(2)}, u32[]{:S(2)}) collective-permute-start(bf16[16,352,256]{2,1,0:T(8,128)(2,1)S(1)} %bitcast.416), channel_id=1, source_target_pairs={{0,4},{4,0},{8,12},{12,8},{16,20},{20,16},{24,28},{28,24},{1,5},{5... | collective-permute-start | bytes 8650760 | tf_op jit(solution)/shard_map/ppermute | solution.py:78
  539.2 99.1 %all-to-all-start.4 = ((bf16[4,2048,512]{2,1,0:T(8,128)(2,1)}), bf16[4,2048,512]{2,1,0:T(8,128)(2,1)}, u32[]{:S(2)}, u32[]{:S(2)}) async-start(bf16[4,2048,512]{2,1,0:T(8,128)(2,1)} %bitcast.419), calls=%async_computation.5 | async-start | bytes 16777216 | tf_op jit(solution)/shard_map/all_to_all | solution.py:431
  664.7 98.5 %all-to-all-start.5 = ((bf16[4,2048,512]{2,1,0:T(8,128)(2,1)}), bf16[4,2048,512]{2,1,0:T(8,128)(2,1)}, u32[]{:S(2)}, u32[]{:S(2)}) async-start(bf16[4,2048,512]{2,1,0:T(8,128)(2,1)} %bitcast.420), calls=%async_computation.6 | async-start | bytes 16777216 | tf_op jit(solution)/shard_map/all_to_all | solution.py:431
  671.4 148.4 %reduce-scatter.9.cloned.1.call-start = ((), (), s32[]{:S(2)}) async-start(), calls=%async_computation.18 | async-start | bytes 5242880 | tf_op jit(solution)/shard_map/reduce_scatter | solution.py:426
  763.3 135.3 %reduce-scatter.11.cloned.1.call-start = ((), (), s32[]{:S(2)}) async-start(), calls=%async_computation.19 | async-start | bytes 5242880 | tf_op jit(solution)/shard_map/reduce_scatter | solution.py:418
  765.0 3.8 collective-permute-start.17
  767.1 4.5 collective-permute-start.16
  772.5 61.3 %collective-permute-start.20 = (f32[4,8,128]{2,1,0:T(8,128)S(1)}, f32[4,8,128]{2,1,0:T(8,128)S(1)}, u32[]{:S(2)}, u32[]{:S(2)}) collective-permute-start(f32[4,8,128]{2,1,0:T(8,128)S(1)} %get-tuple-element.335), channel_id=1, source_target_pairs={{0,3},{1,2},{2,1},{3,0},{4,7},{5,6},{6,5},{7,4},{8,11},{9,10},{10,... | collective-permute-start | bytes 49160 | tf_op jit(solution)/shard_map/ppermute | solution.py:68
  774.0 59.8 %collective-permute-start.19 = (f32[4,8,128]{2,1,0:T(8,128)S(1)}, f32[4,8,128]{2,1,0:T(8,128)S(1)}, u32[]{:S(2)}, u32[]{:S(2)}) collective-permute-start(f32[4,8,128]{2,1,0:T(8,128)S(1)} %get-tuple-element.335), channel_id=1, source_target_pairs={{0,2},{1,3},{2,0},{3,1},{4,6},{5,7},{6,4},{7,5},{8,10},{9,11},{10,... | collective-permute-start | bytes 49160 | tf_op jit(solution)/shard_map/ppermute | solution.py:68
  774.5 59.3 %collective-permute-start.18 = (f32[4,8,128]{2,1,0:T(8,128)S(1)}, f32[4,8,128]{2,1,0:T(8,128)S(1)}, u32[]{:S(2)}, u32[]{:S(2)}) collective-permute-start(f32[4,8,128]{2,1,0:T(8,128)S(1)} %get-tuple-element.335), channel_id=1, source_target_pairs={{0,1},{1,0},{2,3},{3,2},{4,5},{5,4},{6,7},{7,6},{8,9},{9,8},{10,11... | collective-permute-start | bytes 49160 | tf_op jit(solution)/shard_map/ppermute | solution.py:68
  842.3 95.0 %all-to-all-start.6 = ((bf16[4,2048,512]{2,1,0:T(8,128)(2,1)}), bf16[4,2048,512]{2,1,0:T(8,128)(2,1)}, u32[]{:S(2)}, u32[]{:S(2)}) async-start(bf16[4,2048,512]{2,1,0:T(8,128)(2,1)} %bitcast.421), calls=%async_computation.7 | async-start | bytes 16777216 | tf_op jit(solution)/shard_map/all_to_all | solution.py:431
  848.7 178.2 %reduce-scatter.13.cloned.1.call-start = ((), (), s32[]{:S(2)}) async-start(), calls=%async_computation.20 | async-start | bytes 5242880 | tf_op jit(solution)/shard_map/reduce_scatter | solution.py:418
  966.2 12.2 collective-permute-start.21
  966.2 17.5 %collective-permute-start.22 = (bf16[16,352,256]{2,1,0:T(8,128)(2,1)}, bf16[16,352,256]{2,1,0:T(8,128)(2,1)}, u32[]{:S(2)}, u32[]{:S(2)}) collective-permute-start(bf16[16,352,256]{2,1,0:T(8,128)(2,1)} %get-tuple-element.140), channel_id=1, source_target_pairs={{0,4},{4,0},{8,12},{12,8},{16,20},{20,16},{24,28},{28,24},{1,5},{5... | collective-permute-start | bytes 8650760 | tf_op jit(solution)/shard_map/ppermute | solution.py:78
  966.7 21.4 %collective-permute-start.23 = (bf16[16,352,256]{2,1,0:T(8,128)(2,1)}, bf16[16,352,256]{2,1,0:T(8,128)(2,1)}, u32[]{:S(2)}, u32[]{:S(2)}) collective-permute-start(bf16[16,352,256]{2,1,0:T(8,128)(2,1)} %get-tuple-element.142), channel_id=1, source_target_pairs={{0,4},{4,0},{8,12},{12,8},{16,20},{20,16},{24,28},{28,24},{1,5},{5... | collective-permute-start | bytes 8650760 | tf_op jit(solution)/shard_map/ppermute | solution.py:78
  969.1 53.4 %all-to-all-start.7 = ((bf16[4,1024,512]{2,1,0:T(8,128)(2,1)}), bf16[4,1024,512]{2,1,0:T(8,128)(2,1)}, u32[]{:S(2)}, u32[]{:S(2)}) async-start(bf16[4,1024,512]{2,1,0:T(8,128)(2,1)} %bitcast.423), calls=%async_computation.10 | async-start | bytes 8388608 | tf_op jit(solution)/shard_map/all_to_all | solution.py:431
  974.7 136.9 %all-gather.11.cloned.1.call-start = ((), (), s32[]{:S(2)}) async-start(), calls=%async_computation.21 | async-start | bytes 5242880 | tf_op jit(solution)/shard_map/all_gather | solution.py:423
  1046.7 64.9 %all-to-all-start.8 = ((bf16[4,4,352,256]{3,2,1,0:T(8,128)(2,1)}), bf16[4,4,352,256]{3,2,1,0:T(8,128)(2,1)S(1)}, u32[]{:S(2)}, u32[]{:S(2)}) async-start(bf16[4,4,352,256]{3,2,1,0:T(8,128)(2,1)} %bitcast.428), calls=%async_computation.12 | async-start | bytes 5767168 | tf_op jit(solution)/shard_map/all_to_all | solution.py:434
  1051.7 162.8 %all-gather.13.cloned.1.call-start = ((), (), s32[]{:S(2)}) async-start(), calls=%async_computation.22 | async-start | bytes 5242880 | tf_op jit(solution)/shard_map/all_gather | solution.py:423
  1113.2 69.1 %all-to-all-start.9 = ((bf16[4,4,352,256]{3,2,1,0:T(8,128)(2,1)}), bf16[4,4,352,256]{3,2,1,0:T(8,128)(2,1)}, u32[]{:S(2)}, u32[]{:S(2)}) async-start(bf16[4,4,352,256]{3,2,1,0:T(8,128)(2,1)} %bitcast.117), calls=%async_computation.13 | async-start | bytes 5767168 | tf_op jit(solution)/shard_map/all_to_all | solution.py:434
  1121.0 319.5 %reduce-scatter.17.cloned.1.call-start = ((), (), s32[]{:S(2)}) async-start(), calls=%async_computation.24 | async-start | bytes 9732096 | tf_op jit(solution)/shard_map/reduce_scatter | solution.py:786
  1124.8 57.5 %collective-permute-start.24 = (bf16[4,352,256]{2,1,0:T(8,128)(2,1)}, bf16[4,352,256]{2,1,0:T(8,128)(2,1)S(1)}, u32[]{:S(2)}, u32[]{:S(2)}) collective-permute-start(bf16[4,352,256]{2,1,0:T(8,128)(2,1)} %get-tuple-element.308), channel_id=1, source_target_pairs={{0,1},{1,0},{2,3},{3,2},{4,5},{5,4},{6,7},{7,6},{8,9},{9,8},{10,11... | collective-permute-start | bytes 2162696 | tf_op jit(solution)/shard_map/ppermute | solution.py:68
  1126.0 56.3 %collective-permute-start.25 = (bf16[4,352,256]{2,1,0:T(8,128)(2,1)}, bf16[4,352,256]{2,1,0:T(8,128)(2,1)}, u32[]{:S(2)}, u32[]{:S(2)}) collective-permute-start(bf16[4,352,256]{2,1,0:T(8,128)(2,1)} %get-tuple-element.307), channel_id=1, source_target_pairs={{0,2},{1,3},{2,0},{3,1},{4,6},{5,7},{6,4},{7,5},{8,10},{9,11},{10,... | collective-permute-start | bytes 2162696 | tf_op jit(solution)/shard_map/ppermute | solution.py:68
  1127.4 54.9 %collective-permute-start.26 = (bf16[4,352,256]{2,1,0:T(8,128)(2,1)}, bf16[4,352,256]{2,1,0:T(8,128)(2,1)}, u32[]{:S(2)}, u32[]{:S(2)}) collective-permute-start(bf16[4,352,256]{2,1,0:T(8,128)(2,1)} %get-tuple-element.306), channel_id=1, source_target_pairs={{0,3},{1,2},{2,1},{3,0},{4,7},{5,6},{6,5},{7,4},{8,11},{9,10},{10,... | collective-permute-start | bytes 2162696 | tf_op jit(solution)/shard_map/ppermute | solution.py:68
  1183.1 113.9 %all-to-all-start.10 = ((bf16[4,4,352,256]{3,2,1,0:T(8,128)(2,1)}), bf16[4,4,352,256]{3,2,1,0:T(8,128)(2,1)}, u32[]{:S(2)}, u32[]{:S(2)}) async-start(bf16[4,4,352,256]{3,2,1,0:T(8,128)(2,1)} %bitcast.427), calls=%async_computation.14 | async-start | bytes 5767168 | tf_op jit(solution)/shard_map/all_to_all | solution.py:434
  1191.1 252.9 %reduce-scatter.15.cloned.1.call-start = ((), (), s32[]{:S(2)}) async-start(), calls=%async_computation.23 | async-start | bytes 9879552 | tf_op jit(solution)/shard_map/reduce_scatter | solution.py:786
  1219.5 26.4 %collective-permute-start.27 = (bf16[1024,512]{1,0:T(8,128)(2,1)}, bf16[1024,512]{1,0:T(8,128)(2,1)}, u32[]{:S(2)}, u32[]{:S(2)}) collective-permute-start(bf16[1024,512]{1,0:T(8,128)(2,1)} %get-tuple-element.289), channel_id=1, source_target_pairs={{0,1},{1,0},{2,3},{3,2},{4,5},{5,4},{6,7},{7,6},{8,9},{9,8},{10,11... | collective-permute-start | bytes 3145736 | tf_op jit(solution)/shard_map/ppermute | solution.py:68
  1224.5 44.6 %collective-permute-start.29 = (bf16[1024,512]{1,0:T(8,128)(2,1)}, bf16[1024,512]{1,0:T(8,128)(2,1)S(1)}, u32[]{:S(2)}, u32[]{:S(2)}) collective-permute-start(bf16[1024,512]{1,0:T(8,128)(2,1)} %get-tuple-element.290), channel_id=1, source_target_pairs={{0,3},{1,2},{2,1},{3,0},{4,7},{5,6},{6,5},{7,4},{8,11},{9,10},{10,... | collective-permute-start | bytes 3145736 | tf_op jit(solution)/shard_map/ppermute | solution.py:68
  1226.0 48.8 %collective-permute-start.28 = (bf16[1024,512]{1,0:T(8,128)(2,1)}, bf16[1024,512]{1,0:T(8,128)(2,1)S(1)}, u32[]{:S(2)}, u32[]{:S(2)}) collective-permute-start(bf16[1024,512]{1,0:T(8,128)(2,1)} %get-tuple-element.291), channel_id=1, source_target_pairs={{0,2},{1,3},{2,0},{3,1},{4,6},{5,7},{6,4},{7,5},{8,10},{9,11},{10,... | collective-permute-start | bytes 3145736 | tf_op jit(solution)/shard_map/ppermute | solution.py:68
  1235.9 61.1 %collective-permute-start.30 = (bf16[4,352,256]{2,1,0:T(8,128)(2,1)}, bf16[4,352,256]{2,1,0:T(8,128)(2,1)}, u32[]{:S(2)}, u32[]{:S(2)}) collective-permute-start(bf16[4,352,256]{2,1,0:T(8,128)(2,1)} %get-tuple-element.304), channel_id=1, source_target_pairs={{0,1},{1,0},{2,3},{3,2},{4,5},{5,4},{6,7},{7,6},{8,9},{9,8},{10,11... | collective-permute-start | bytes 2162696 | tf_op jit(solution)/shard_map/ppermute | solution.py:68
  1237.2 65.6 %collective-permute-start.31 = (bf16[4,352,256]{2,1,0:T(8,128)(2,1)}, bf16[4,352,256]{2,1,0:T(8,128)(2,1)}, u32[]{:S(2)}, u32[]{:S(2)}) collective-permute-start(bf16[4,352,256]{2,1,0:T(8,128)(2,1)} %get-tuple-element.303), channel_id=1, source_target_pairs={{0,2},{1,3},{2,0},{3,1},{4,6},{5,7},{6,4},{7,5},{8,10},{9,11},{10,... | collective-permute-start | bytes 2162696 | tf_op jit(solution)/shard_map/ppermute | solution.py:68
  1245.9 56.9 %collective-permute-start.32 = (bf16[4,352,256]{2,1,0:T(8,128)(2,1)}, bf16[4,352,256]{2,1,0:T(8,128)(2,1)}, u32[]{:S(2)}, u32[]{:S(2)}) collective-permute-start(bf16[4,352,256]{2,1,0:T(8,128)(2,1)} %get-tuple-element.302), channel_id=1, source_target_pairs={{0,3},{1,2},{2,1},{3,0},{4,7},{5,6},{6,5},{7,4},{8,11},{9,10},{10,... | collective-permute-start | bytes 2162696 | tf_op jit(solution)/shard_map/ppermute | solution.py:68
  1343.4 19.1 %collective-permute-start.39 = (bf16[4,352,256]{2,1,0:T(8,128)(2,1)S(1)}, bf16[4,352,256]{2,1,0:T(8,128)(2,1)S(1)}, u32[]{:S(2)}, u32[]{:S(2)}) collective-permute-start(bf16[4,352,256]{2,1,0:T(8,128)(2,1)S(1)} %get-tuple-element.300), channel_id=1, source_target_pairs={{0,1},{1,0},{2,3},{3,2},{4,5},{5,4},{6,7},{7,6},{8,9},{9,8},{10,11... | collective-permute-start | bytes 2162696 | tf_op jit(solution)/shard_map/ppermute | solution.py:68
  1344.3 88.1 %collective-permute-start.33 = (bf16[1024,512]{1,0:T(8,128)(2,1)S(1)}, bf16[1024,512]{1,0:T(8,128)(2,1)S(1)}, u32[]{:S(2)}, u32[]{:S(2)}) collective-permute-start(bf16[1024,512]{1,0:T(8,128)(2,1)S(1)} %fusion.38.refs_0_), channel_id=1, source_target_pairs={{0,1},{1,0},{2,3},{3,2},{4,5},{5,4},{6,7},{7,6},{8,9},{9,8},{10,11... | collective-permute-start | bytes 3145736 | tf_op jit(solution)/shard_map/ppermute | solution.py:68
  1345.5 87.0 %collective-permute-start.34 = (bf16[1024,512]{1,0:T(8,128)(2,1)S(1)}, bf16[1024,512]{1,0:T(8,128)(2,1)S(1)}, u32[]{:S(2)}, u32[]{:S(2)}) collective-permute-start(bf16[1024,512]{1,0:T(8,128)(2,1)S(1)} %fusion.38.refs_0_), channel_id=1, source_target_pairs={{0,2},{1,3},{2,0},{3,1},{4,6},{5,7},{6,4},{7,5},{8,10},{9,11},{10,... | collective-permute-start | bytes 3145736 | tf_op jit(solution)/shard_map/ppermute | solution.py:68
  1346.3 88.1 %collective-permute-start.35 = (bf16[1024,512]{1,0:T(8,128)(2,1)S(1)}, bf16[1024,512]{1,0:T(8,128)(2,1)}, u32[]{:S(2)}, u32[]{:S(2)}) collective-permute-start(bf16[1024,512]{1,0:T(8,128)(2,1)S(1)} %fusion.38.refs_0_), channel_id=1, source_target_pairs={{0,3},{1,2},{2,1},{3,0},{4,7},{5,6},{6,5},{7,4},{8,11},{9,10},{10,... | collective-permute-start | bytes 3145736 | tf_op jit(solution)/shard_map/ppermute | solution.py:68
  1347.8 70.8 %collective-permute-start.40 = (bf16[4,352,256]{2,1,0:T(8,128)(2,1)S(1)}, bf16[4,352,256]{2,1,0:T(8,128)(2,1)S(1)}, u32[]{:S(2)}, u32[]{:S(2)}) collective-permute-start(bf16[4,352,256]{2,1,0:T(8,128)(2,1)S(1)} %get-tuple-element.299), channel_id=1, source_target_pairs={{0,2},{1,3},{2,0},{3,1},{4,6},{5,7},{6,4},{7,5},{8,10},{9,11},{10,... | collective-permute-start | bytes 2162696 | tf_op jit(solution)/shard_map/ppermute | solution.py:68
  1362.5 56.1 %collective-permute-start.41 = (bf16[4,352,256]{2,1,0:T(8,128)(2,1)S(1)}, bf16[4,352,256]{2,1,0:T(8,128)(2,1)S(1)}, u32[]{:S(2)}, u32[]{:S(2)}) collective-permute-start(bf16[4,352,256]{2,1,0:T(8,128)(2,1)S(1)} %get-tuple-element.298), channel_id=1, source_target_pairs={{0,3},{1,2},{2,1},{3,0},{4,7},{5,6},{6,5},{7,4},{8,11},{9,10},{10,... | collective-permute-start | bytes 2162696 | tf_op jit(solution)/shard_map/ppermute | solution.py:68
  1446.2 9.0 collective-permute-start.38
  1448.0 9.5 collective-permute-start.37
  1448.6 8.9 collective-permute-start.36
  (111 other events, 1867.8 us)
Sparse Core Ops, SparseCore 0:
  20.3 86.0 all-gather.14
  212.5 52.5 reduce-scatter.6
  282.8 79.3 all-gather.16
  363.7 79.2 all-gather.18
  511.4 83.6 all-gather.20
  763.4 52.8 reduce-scatter.8
  822.9 75.6 reduce-scatter.10
  949.6 76.7 reduce-scatter.12
  1046.9 53.2 all-gather.10
  1111.8 77.3 all-gather.12
  1191.5 140.3 reduce-scatter.16
  1334.1 94.0 reduce-scatter.14

commit v11 on v10

--- a/solution.py
+++ b/solution.py
@@ -419,6 +419,12 @@
             values, "dp", scatter_dimension=0, tiled=False, axis_index_groups=lay.z_groups
         )
 
+    def sum_dp(values):
+        return lax.psum_scatter(values, "dp", scatter_dimension=0, tiled=False).astype(F32)
+
+    def by_owner(values):
+        return jnp.swapaxes(values.astype(BF16).reshape(-1, ndp, d_loc), 0, 1)
+
     def gather_t(values):
         return lax.all_gather(values, "tensor", axis=1, tiled=True)
 
@@ -669,17 +675,6 @@
     rows_out = (dot(active, own_out) * gate_rows).astype(BF16)
     rows_out, cot_rows, shared_all = lax.optimization_barrier((rows_out, cot_rows, shared_all))
     out_parts = send_back(rows_out)
-    active_grad_raw = dot_nt(cot_rows, own_out)
-    gate_grad = jnp.sum(active.astype(F32) * active_grad_raw, axis=-1).reshape(nz, CAP)
-    active_grad = active_grad_raw * gate_rows
-    pre_low = jnp.concatenate(
-        [
-            active_grad * up_pre * gate_sig * (1.0 + gate_pre * (1.0 - gate_sig)),
-            active_grad * gate_silu,
-        ],
-        1,
-    ).astype(BF16)
-    gated_active = (active.astype(F32) * gate_rows).astype(BF16)
     ffs = w_shared_out.shape[0]
     shared_in = jnp.swapaxes(shared_all[:, : 2 * ffs], 0, 1).reshape(2 * ffs, width)
     shared_out = jnp.swapaxes(shared_all[:, 2 * ffs :], 0, 1).reshape(ffs, width)
@@ -700,13 +695,28 @@
     grad_shared_in = dot_tn(shared_pre_grad, ffn_low)
     grad_shared_out = dot_tn(shared_act, cot_low)
     shared_grad_full = dot(shared_pre_grad, shared_in)
-
+    shared_pack, cot_rows = lax.optimization_barrier(
+        (jnp.concatenate([by_owner(grad_shared_in), by_owner(grad_shared_out)], 1), cot_rows)
+    )
+    shared_full, shared_sum = lax.optimization_barrier((shared_full, sum_dp(shared_pack)))
+
+    active_grad_raw = dot_nt(cot_rows, own_out)
+    gate_grad = jnp.sum(active.astype(F32) * active_grad_raw, axis=-1).reshape(nz, CAP)
+    active_grad = active_grad_raw * gate_rows
+    pre_low = jnp.concatenate(
+        [
+            active_grad * up_pre * gate_sig * (1.0 + gate_pre * (1.0 - gate_sig)),
+            active_grad * gate_silu,
+        ],
+        1,
+    ).astype(BF16)
+    gated_active = (active.astype(F32) * gate_rows).astype(BF16)
     out_parts, pre_low, shared_full = lax.optimization_barrier((out_parts, pre_low, shared_full))
     rows_grad = dot(pre_low, own_in).astype(BF16)
     rows_grad, out_parts = lax.optimization_barrier((rows_grad, out_parts))
     grad_parts = send_back(rows_grad)
-    routed, pre_low, gated_active, shared_part = lax.optimization_barrier(
-        (combine(out_parts), pre_low, gated_active, scatter_t(shared_full))
+    routed, pre_low, gated_active = lax.optimization_barrier(
+        (combine(out_parts), pre_low, gated_active)
     )
     routed = scatter_z(routed).astype(F32)
     token_grad = jnp.sum(jnp.where(own_place, gate_grad[:, :, None], 0.0), axis=1)
@@ -730,15 +740,11 @@
 
     grad_in_own = dot_tn(pre_low, expert_rows).astype(BF16)
     grad_out_own = dot_tn(gated_active, cot_rows).astype(BF16)
-    (
-        grad_parts,
-        grad_in_own,
-        grad_out_own,
-        routed,
-        probs_grad,
-        shared_grad_full,
-    ) = lax.optimization_barrier(
-        (grad_parts, grad_in_own, grad_out_own, routed, probs_grad, shared_grad_full)
+    grad_parts, grad_in_own, grad_out_own, probs_grad = lax.optimization_barrier(
+        (grad_parts, grad_in_own, grad_out_own, probs_grad)
+    )
+    routed, shared_part, shared_grad_full = lax.optimization_barrier(
+        (routed, scatter_t(shared_full), shared_grad_full)
     )
     shared_grad = swap_t(
         jnp.swapaxes(shared_grad_full.astype(BF16).reshape(rows, nt, part), 0, 1)
@@ -782,16 +788,9 @@
     )
     residual_low = gather_t(residual_grad.astype(BF16))
 
-    def sum_dp(values):
-        return lax.psum_scatter(values, "dp", scatter_dimension=0, tiled=False).astype(F32)
-
-    def by_owner(values):
-        return jnp.swapaxes(values.astype(BF16).reshape(-1, ndp, d_loc), 0, 1)
-
-    shared_grads = jnp.concatenate([by_owner(grad_shared_in), by_owner(grad_shared_out)], 1)
     output_part = lax.optimization_barrier((residual + routed + shared_part).astype(BF16))
-    residual_low, shared_grads, grad_plane[0], output_part = lax.optimization_barrier(
-        (residual_low, shared_grads, grad_plane[0], output_part)
+    residual_low, grad_plane[0], output_part = lax.optimization_barrier(
+        (residual_low, grad_plane[0], output_part)
     )
     grad_out_w = dot_tn(attended_low, residual_low)
     attended_grad = dot_nt(residual_low, out_w).astype(BF16)
@@ -813,10 +812,9 @@
         ]
 
     grad_home = [to_columns(grad_plane[0]), None, None]
-    query_turned_grad, grad_plane[1], grad_home[0], shared_grads = lax.optimization_barrier(
-        (query_turned_grad, grad_plane[1], grad_home[0], shared_grads)
-    )
-    shared_sum = sum_dp(shared_grads)
+    query_turned_grad, grad_plane[1], grad_home[0] = lax.optimization_barrier(
+        (query_turned_grad, grad_plane[1], grad_home[0])
+    )
     turned_first, turned_second = rotate_back(
         query_turned_grad[:, : heads * half], query_turned_grad[:, heads * half :], wide_cos, wide_sin
     )

time: 1480 us -> 1510 us (1.020)
  blocking collectives: 24.9 us -> 92.1 us
  waiting for transfers between devices: 569 us -> 542 us
    all_to_all x5 -> x4, waiting for transfers between devices: 87.4 us -> 16.7 us  [swap_z(): lax.all_to_all(values, 'dp', split_axis=0, concat_axis=0, axis_index_grou...]
    all_to_all x0 -> x1, blocking collectives: none -> 67 us  [swap_z(): lax.all_to_all(values, 'dp', split_axis=0, concat_axis=0, axis_index_grou...]
    reduce_scatter x2, waiting for transfers between devices: 0.01 us -> 34.5 us  [sum_dp(): lax.psum_scatter(values, 'dp', scatter_dimension=0, tiled=False).astype(F32)]
    ppermute x24, waiting for transfers between devices: 145 us -> 170 us  [over_t(): return lax.ppermute(values, 'tensor', [(i, i ^ k) for i in range(self.t)])]
    all_to_all x5 -> x4, starting transfers between devices: 31.6 us -> 27.5 us  [swap_z(): lax.all_to_all(values, 'dp', split_axis=0, concat_axis=0, axis_index_grou...]
    unnamed x245 -> x233, local copies, waits for them, and re-layouts: 47.4 us -> 45.7 us
  transfers between devices with their start and end apart: 65 -> 64, of which waited for: 33 -> 34; matrix products, arithmetic and copies ran while one was open for 37% -> 34% of each run, Pallas kernels for 7% -> 7%
where the time goes in v11:
time: 1510 us; the launch traced here: 1500 us
  waiting for transfers between devices  542 us (36%)
  matrix products  316 us (21%)
  local copies, waits for them, and re-layouts  201 us (13%)
  starting transfers between devices  114 us (8%)
  other arithmetic  114 us (8%)
  Pallas kernels  99.3 us (7%)
  blocking collectives  92.1 us (6%)
  between operations  16.7 us (1%)
    ppermute x24, waiting for transfers between devices, over_t(): return lax.ppermute(values, 'tensor', [(i, i ^ k) for i in range(self.t)])  170 us
    all_to_all x6, waiting for transfers between devices, swap_t(): lax.all_to_all(values, 'tensor', split_axis=0, concat_axis=0, tiled=True)  117 us
    dot_general x9, matrix products, dot_nt(): lax.dot_general(a, b, (((1,), (1,)), ((), ())), preferred_element_type=F32)  95.3 us
    dot_general x9, matrix products, dot(): return jnp.dot(a, b, preferred_element_type=F32)  80.3 us
    dot_general x8, matrix products, dot_tn(): lax.dot_general(a, b, (((0,), (0,)), ((), ())), preferred_element_type=F32)  76.9 us
    all_to_all x1, blocking collectives, swap_z(): lax.all_to_all(values, 'dp', split_axis=0, concat_axis=0, axis_index_grou...  67 us
    all_gather x2, waiting for transfers between devices, gather_z(): lax.all_gather(values, 'dp', axis=0, tiled=False, axis_index_groups=lay.z...  59.3 us
    all_gather x1, waiting for transfers between devices, body(): front = lax.all_gather(front_pack, 'dp', axis=0, tiled=False)  53.6 us
  transfers between devices with their start and end apart: 64, of which 34 were waited for; matrix products, arithmetic and copies ran while one was open for 34% of the time, Pallas kernels for 7%

profile of v11, /device:TPU:10, one launch (start us, length us, event | category | flops | bytes accessed | tf_op | source)
XLA Modules:
  0.0 1495.9 jit_solution(14608700949598170088)
XLA Ops:
  21.2 6.9 maximum_bitcast_fusion
  28.0 8.4 copy.295
  36.4 6.5 all-to-all-start
  53.7 53.6 %all-gather.15.cloned.1.call-done = bf16[17152,256]{1,0:T(8,128)(2,1)} async-done(((bf16[2144,256]{1,0:T(8,128)(2,1)}), bf16[17152,256]{1,0:T(8,128)(2,1)}) %all-gather.15.cloned.1.call-update) | async-done | bytes 8781840 | tf_op jit(solution)/shard_map/all_gather | solution.py:501
  118.1 19.6 %all-to-all-done = bf16[4,4,3,352,256]{4,3,1,2,0:T(8,128)(2,1)} async-done(((bf16[4,4,3,352,256]{4,3,1,2,0:T(8,128)(2,1)}), bf16[4,4,3,352,256]{4,3,1,2,0:T(8,128)(2,1)}, u32[]{:S(2)}, u32[]{:S(2)}) %all-to-all-start) | async-done | bytes 8650784 | tf_op jit(solution)/shard_map/all_to_all | solution.py:437
  178.0 6.5 fusion.114
  189.7 14.6 attend.1
  214.6 7.8 all-to-all-start.2
  222.5 42.2 %reduce-scatter.7.cloned.1.call-done = bf16[1024,512]{1,0:T(8,128)(2,1)} async-done(((bf16[1024,2048]{1,0:T(8,128)(2,1)}), bf16[1024,512]{1,0:T(8,128)(2,1)}) %reduce-scatter.7.cloned.1.call-update) | async-done | bytes 1048592 | tf_op jit(solution)/shard_map/reduce_scatter | solution.py:432
  266.6 8.1 psum.21
  277.6 6.2 all-to-all-done.2
  293.3 18.2 %collective-permute-done.5.refs_3_ = bf16[1024,512]{1,0:T(8,128)(2,1)} collective-permute-done((bf16[1024,512]{1,0:T(8,128)(2,1)}, bf16[1024,512]{1,0:T(8,128)(2,1)}, u32[]{:S(2)}, u32[]{:S(2)}) %collective-permute-start.5) | collective-permute-done | bytes 1048608 | tf_op jit(solution)/shard_map/ppermute | solution.py:68
  311.5 19.7 %collective-permute-done.4.refs_2_ = bf16[1024,512]{1,0:T(8,128)(2,1)} collective-permute-done((bf16[1024,512]{1,0:T(8,128)(2,1)}, bf16[1024,512]{1,0:T(8,128)(2,1)}, u32[]{:S(2)}, u32[]{:S(2)}) %collective-permute-start.4) | collective-permute-done | bytes 1048608 | tf_op jit(solution)/shard_map/ppermute | solution.py:68
  337.3 26.1 %all-gather.17.cloned.1.call-done = bf16[4096,512]{1,0:T(8,128)(2,1)} async-done(((bf16[1024,512]{1,0:T(8,128)(2,1)}), bf16[4096,512]{1,0:T(8,128)(2,1)}) %all-gather.17.cloned.1.call-update) | async-done | bytes 4194320 | tf_op jit(solution)/shard_map/all_gather | solution.py:415
  364.2 16.2 %convert_bitcast_fusion.1 = bf16[4,4,512,512]{3,2,0,1:T(8,128)(2,1)} fusion(s32[4,4,1024]{2,1,0:T(4,128)S(1)} %fusion.46, bf16[4,1024,512]{2,1,0:T(8,128)(2,1)} %bitcast.532), kind=kOutput, calls=%fused_computation.39 | convolution fusion | flops 8602517504 | bytes 12648448 | tf_op jit(solution)/shard_map/sepk,skd->espd/dot_general | solution.py:534
  380.5 7.6 copy.300
  397.8 13.2 lay_out_weights.2
  411.0 33.3 %all-gather.19.cloned.1.call-done = bf16[4096,512]{1,0:T(8,128)(2,1)} async-done(((bf16[1024,512]{1,0:T(8,128)(2,1)}), bf16[4096,512]{1,0:T(8,128)(2,1)}) %all-gather.19.cloned.1.call-update) | async-done | bytes 4194320 | tf_op jit(solution)/shard_map/all_gather | solution.py:415
  451.8 14.4 convert_bitcast_fusion
  466.2 7.4 copy.303
  473.6 23.2 %collective-permute-done.10 = bf16[4,352,256]{2,1,0:T(8,128)(2,1)S(1)} collective-permute-done((bf16[4,352,256]{2,1,0:T(8,128)(2,1)S(1)}, bf16[4,352,256]{2,1,0:T(8,128)(2,1)S(1)}, u32[]{:S(2)}, u32[]{:S(2)}) %collective-permute-start.10) | collective-permute-done | bytes 720928 | tf_op jit(solution)/shard_map/ppermute | solution.py:73
  496.8 13.9 collective-permute-done.9
  525.7 11.5 copy.301
  539.2 6.5 all-to-all-start.4
  545.7 32.3 %fusion.123 = f32[2048,2816]{1,0:T(8,128)} fusion(bf16[2048,2048]{0,1:T(8,128)(2,1)} %bitcast.440, bf16[2816,2048]{1,0:T(8,128)(2,1)} %bitcast.425), kind=kOutput, calls=%fused_computation.303 | convolution fusion | flops 23622320128 | bytes 42991616 | tf_op jit(solution)/shard_map/dot_general | solution.py:30
  578.1 12.3 fusion.8
  590.4 9.3 lay_out_weights.3
  602.2 15.1 %multiply_convert_fusion = bf16[2048,2048]{1,0:T(8,128)(2,1)} fusion(bf16[2048,1408]{1,0:T(8,128)(2,1)S(1)} %get-tuple-element.280, f32[2048]{0:T(1024)S(1)} %bitcast.502, bf16[1,1408,2048]{2,1,0:T(8,128)(2,1)S(1)} %lay_out_weights.3), kind=kOutput, calls=%fused_computation.5 | convolution fusion | flops 11819548672 | bytes 19931136 | tf_op jit(solution)/shard_map/dot_general | solution.py:26
  617.3 18.4 %all-to-all-done.4 = bf16[4,2048,512]{2,1,0:T(8,128)(2,1)} async-done(((bf16[4,2048,512]{2,1,0:T(8,128)(2,1)}), bf16[4,2048,512]{2,1,0:T(8,128)(2,1)}, u32[]{:S(2)}, u32[]{:S(2)}) %all-to-all-start.4) | async-done | bytes 8388640 | tf_op jit(solution)/shard_map/all_to_all | solution.py:437
  635.8 11.4 copy.310
  654.8 8.6 copy.313
  666.7 9.0 fusion.124
  683.5 7.8 convolution_convert_fusion.1
  695.4 7.4 copy.389
  702.9 6.5 all-to-all-start.5
  709.4 6.5 fusion.125
  715.9 27.5 %multiply_convert_fusion.2 = (bf16[2048,1408]{1,0:T(8,128)(2,1)S(1)}, bf16[2048,1408]{1,0:T(8,128)(2,1)}, f32[2048]{0:T(1024)S(1)}) fusion(f32[2048,2816]{1,0:T(8,128)} %fusion.123, f32[2048]{0:T(1024)S(1)} %bitcast.503, bf16[2048,1408]{1,0:T(8,128)(2,1)} %copy-done.32, bf16[2048,2048]{0,1:T(8,128)(2,1)} %bitcast.442, bf16[1,1408,2048]{2,1,0:T(8,128)(2,1)} %copy-done), kind=kOutput, calls=%fused_computation.16 | convolution fusion | flops 11860178944 | bytes 54542336 | tf_op jit(solution)/shard_map/dot_general | solution.py:30
  743.4 8.0 pad_maximum_fusion
  751.4 34.5 %reduce-scatter.9.cloned.1.call-done = bf16[1,2112,256]{2,1,0:T(8,128)(2,1)} async-done(((bf16[8,2112,256]{2,1,0:T(8,128)(2,1)}), bf16[1,2112,256]{2,1,0:T(8,128)(2,1)}) %reduce-scatter.9.cloned.1.call-update) | async-done | bytes 1081360 | tf_op jit(solution)/shard_map/reduce_scatter | solution.py:423
  788.6 12.0 all-to-all-done.5
  819.8 31.9 %convolution_convert_fusion.3 = bf16[2048,2048]{1,0:T(8,128)(2,1)} fusion(bf16[2048,2816]{1,0:T(8,128)(2,1)} %pad_maximum_fusion, bf16[2816,2048]{1,0:T(8,128)(2,1)} %bitcast.426), kind=kOutput, calls=%fused_computation.42 | convolution fusion | flops 23626514432 | bytes 31457280 | tf_op jit(solution)/shard_map/dot_general | solution.py:26
  851.8 7.6 copy.388
  859.4 12.1 bitcast_convert_fusion.1
  878.4 18.4 %convolution_convert_fusion.2.out_ref = bf16[1408,2048]{1,0:T(8,128)(2,1)} fusion(bf16[2048,1408]{1,0:T(8,128)(2,1)} %get-tuple-element.138, bf16[2048,2048]{0,1:T(8,128)(2,1)} %bitcast.443), kind=kOutput, calls=%fused_computation.41 | convolution fusion | flops 11814043648 | bytes 19922944 | tf_op jit(solution)/shard_map/dot_general | solution.py:34
  896.8 31.7 %convolution_convert_fusion = bf16[2816,2048]{1,0:T(8,128)(2,1)} fusion(bf16[2048,2816]{1,0:T(8,128)(2,1)} %pad_maximum_fusion, bf16[2048,2048]{0,1:T(8,128)(2,1)} %bitcast.441), kind=kOutput, calls=%fused_computation.20 | convolution fusion | flops 23628087296 | bytes 31457280 | tf_op jit(solution)/shard_map/dot_general | solution.py:34
  928.5 36.4 %all-to-all-done.7 = bf16[4,2048,512]{2,1,0:T(8,128)(2,1)} async-done(((bf16[4,2048,512]{2,1,0:T(8,128)(2,1)}), bf16[4,2048,512]{2,1,0:T(8,128)(2,1)}, u32[]{:S(2)}, u32[]{:S(2)}) %all-to-all-start.7) | async-done | bytes 8388640 | tf_op jit(solution)/shard_map/all_to_all | solution.py:437
  964.8 12.2 bitcast_convert_fusion
  977.1 14.8 take_apart.1
  995.5 11.2 fusion.41
  1039.9 30.5 %all-to-all-done.6 = bf16[4,1024,512]{2,1,0:T(8,128)(2,1)} async-done(((bf16[4,1024,512]{2,1,0:T(8,128)(2,1)}), bf16[4,1024,512]{2,1,0:T(8,128)(2,1)}, u32[]{:S(2)}, u32[]{:S(2)}) %all-to-all-start.6) | async-done | bytes 4194336 | tf_op jit(solution)/shard_map/all_to_all | solution.py:437
  1081.3 8.0 psum.22
  1094.1 67.0 %all_to_all.55 = bf16[4,4,352,256]{3,2,1,0:T(8,128)(2,1)} all-to-all(bf16[4,4,352,256]{3,2,1,0:T(8,128)(2,1)} %bitcast.429), channel_id=1, replica_groups={{0,8,16,24},{4,12,20,28},{1,9,17,25},{5,13,21,29},{2,10,18,26},{6,14,22..., dimensions={0} | all-to-all | bytes 5767168 | tf_op jit(solution)/shard_map/all_to_all | solution.py:440
  1161.0 6.4 all-to-all-start.9
  1182.9 21.6 %attend_back.1 = (bf16[1024,512]{1,0:T(8,128)(2,1)S(1)}, f32[1024,256]{1,0:T(8,128)S(1)}, bf16[1024,1024]{1,0:T(8,128)(2,1)S(1)}, f32[1024,256]{1,0:T(8,128)S(1)}) custom-call(s32[1]{0:T(128)} %copy.411.len_ref, bf16[1024,512]{1,0:T(8,128)(2,1)S(1)} %copy-done.5, bf16[1024,256]{1,0:T(8,128)(2,1)S(1)} %copy-done.10, bf16[1024,1024]{1,0:T(8,128)(2,1)S(1)} %copy-done.14, ...), custom_call_target="tpu_custom_call" | custom-call | flops 6710886400 | bytes 33554432 | tf_op jit(solution)/shard_map/attend_back/pallas_call | solution.py:330
  1217.6 10.5 all-to-all-done.9
  1228.1 7.9 all-to-all-start.10
  1270.8 9.5 collective-permute-done.27
  1286.2 17.2 %collective-permute-done.29 = bf16[1024,512]{1,0:T(8,128)(2,1)} collective-permute-done((bf16[1024,512]{1,0:T(8,128)(2,1)}, bf16[1024,512]{1,0:T(8,128)(2,1)}, u32[]{:S(2)}, u32[]{:S(2)}) %collective-permute-start.29) | collective-permute-done | bytes 1048608 | tf_op jit(solution)/shard_map/ppermute | solution.py:68
  1303.4 17.4 %collective-permute-done.28 = bf16[1024,512]{1,0:T(8,128)(2,1)} collective-permute-done((bf16[1024,512]{1,0:T(8,128)(2,1)}, bf16[1024,512]{1,0:T(8,128)(2,1)}, u32[]{:S(2)}, u32[]{:S(2)}) %collective-permute-start.28) | collective-permute-done | bytes 1048608 | tf_op jit(solution)/shard_map/ppermute | solution.py:68
  1325.2 8.2 collective-permute-done.31.refs_6_
  1353.8 9.1 psum.23
  1374.4 14.1 collective-permute-done.41.refs_11_
  1391.6 51.5 %collective-permute-done.40.refs_10_ = bf16[4,352,256]{2,1,0:T(8,128)(2,1)S(1)} collective-permute-done((bf16[4,352,256]{2,1,0:T(8,128)(2,1)S(1)}, bf16[4,352,256]{2,1,0:T(8,128)(2,1)S(1)}, u32[]{:S(2)}, u32[]{:S(2)}) %collective-permute-start.40) | collective-permute-done | bytes 720928 | tf_op jit(solution)/shard_map/ppermute | solution.py:68
  1443.1 13.5 home_gradients.1
  (496 shorter events, 392.6 us)
Async XLA Ops:
  7.2 100.1 %all-gather.15.cloned.1.call-start = ((), (), s32[]{:S(2)}) async-start(), calls=%async_computation.25 | async-start | bytes 9879552 | tf_op jit(solution)/shard_map/all_gather | solution.py:501
  36.4 101.2 %all-to-all-start = ((bf16[4,4,3,352,256]{4,3,1,2,0:T(8,128)(2,1)}), bf16[4,4,3,352,256]{4,3,1,2,0:T(8,128)(2,1)}, u32[]{:S(2)}, u32[]{:S(2)}) async-start(bf16[4,4,3,352,256]{4,3,1,2,0:T(8,128)(2,1)} %copy.295), calls=%async_computation | async-start | bytes 17301504 | tf_op jit(solution)/shard_map/all_to_all | solution.py:437
  42.9 7.3 collective-permute-start.2
  43.0 7.2 collective-permute-start.1
  46.0 7.7 collective-permute-start
  144.9 66.1 %all-to-all-start.1 = ((bf16[4,4,352,256]{3,2,1,0:T(8,128)(2,1)}), bf16[4,4,352,256]{3,2,1,0:T(8,128)(2,1)S(1)}, u32[]{:S(2)}, u32[]{:S(2)}) async-start(bf16[4,4,352,256]{3,2,1,0:T(8,128)(2,1)} %copy.297), calls=%async_computation.1 | async-start | bytes 5767168 | tf_op jit(solution)/shard_map/all_to_all | solution.py:440
  150.2 114.4 %reduce-scatter.7.cloned.1.call-start = ((), (), s32[]{:S(2)}) async-start(), calls=%async_computation.17 | async-start | bytes 5242880 | tf_op jit(solution)/shard_map/reduce_scatter | solution.py:432
  214.6 69.2 %all-to-all-start.2 = ((bf16[4,4,352,256]{3,2,1,0:T(8,128)(2,1)}), bf16[4,4,352,256]{3,2,1,0:T(8,128)(2,1)}, u32[]{:S(2)}, u32[]{:S(2)}) async-start(bf16[4,4,352,256]{3,2,1,0:T(8,128)(2,1)} %copy.298), calls=%async_computation.3 | async-start | bytes 5767168 | tf_op jit(solution)/shard_map/all_to_all | solution.py:440
  222.4 141.0 %all-gather.17.cloned.1.call-start = ((), (), s32[]{:S(2)}) async-start(), calls=%async_computation.26 | async-start | bytes 5242880 | tf_op jit(solution)/shard_map/all_gather | solution.py:415
  283.9 160.4 %all-gather.19.cloned.1.call-start = ((), (), s32[]{:S(2)}) async-start(), calls=%async_computation.27 | async-start | bytes 5242880 | tf_op jit(solution)/shard_map/all_gather | solution.py:415
  284.1 27.4 %collective-permute-start.5 = (bf16[1024,512]{1,0:T(8,128)(2,1)}, bf16[1024,512]{1,0:T(8,128)(2,1)}, u32[]{:S(2)}, u32[]{:S(2)}) collective-permute-start(bf16[1024,512]{1,0:T(8,128)(2,1)} %multiply_convert_fusion.8.refs_0_), channel_id=1, source_target_pairs={{0,3},{1,2},{2,1},{3,0},{4,7},{5,6},{6,5},{7,4},{8,11},{9,10},{10,... | collective-permute-start | bytes 3145736 | tf_op jit(solution)/shard_map/ppermute | solution.py:68
  285.7 45.4 %collective-permute-start.4 = (bf16[1024,512]{1,0:T(8,128)(2,1)}, bf16[1024,512]{1,0:T(8,128)(2,1)}, u32[]{:S(2)}, u32[]{:S(2)}) collective-permute-start(bf16[1024,512]{1,0:T(8,128)(2,1)} %multiply_convert_fusion.8.refs_0_), channel_id=1, source_target_pairs={{0,2},{1,3},{2,0},{3,1},{4,6},{5,7},{6,4},{7,5},{8,10},{9,11},{10,... | collective-permute-start | bytes 3145736 | tf_op jit(solution)/shard_map/ppermute | solution.py:68
  286.5 44.6 %collective-permute-start.3 = (bf16[1024,512]{1,0:T(8,128)(2,1)}, bf16[1024,512]{1,0:T(8,128)(2,1)}, u32[]{:S(2)}, u32[]{:S(2)}) collective-permute-start(bf16[1024,512]{1,0:T(8,128)(2,1)} %multiply_convert_fusion.8.refs_0_), channel_id=1, source_target_pairs={{0,1},{1,0},{2,3},{3,2},{4,5},{5,4},{6,7},{7,6},{8,9},{9,8},{10,11... | collective-permute-start | bytes 3145736 | tf_op jit(solution)/shard_map/ppermute | solution.py:68
  388.0 9.5 collective-permute-start.6
  388.0 9.7 collective-permute-start.7
  390.8 134.9 %all-to-all-start.3 = ((bf16[4,2048,512]{2,1,0:T(8,128)(2,1)}), bf16[4,2048,512]{2,1,0:T(8,128)(2,1)}, u32[]{:S(2)}, u32[]{:S(2)}) async-start(bf16[4,2048,512]{2,1,0:T(8,128)(2,1)} %bitcast.419), calls=%async_computation.4 | async-start | bytes 16777216 | tf_op jit(solution)/shard_map/all_to_all | solution.py:437
  396.8 250.5 %all-gather.21.cloned.1.call-start = ((), (), s32[]{:S(2)}) async-start(), calls=%async_computation.28 | async-start | bytes 9732096 | tf_op jit(solution)/shard_map/all_gather | solution.py:650
  446.4 50.4 %collective-permute-start.10 = (bf16[4,352,256]{2,1,0:T(8,128)(2,1)S(1)}, bf16[4,352,256]{2,1,0:T(8,128)(2,1)S(1)}, u32[]{:S(2)}, u32[]{:S(2)}) collective-permute-start(bf16[4,352,256]{2,1,0:T(8,128)(2,1)S(1)} %get-tuple-element.315), channel_id=1, source_target_pairs={{0,24},{4,28},{8,16},{12,20},{16,8},{20,12},{24,0},{28,4},{1,25},{... | collective-permute-start | bytes 2162696 | tf_op jit(solution)/shard_map/ppermute | solution.py:73
  448.9 61.7 %collective-permute-start.9 = (bf16[4,352,256]{2,1,0:T(8,128)(2,1)S(1)}, bf16[4,352,256]{2,1,0:T(8,128)(2,1)S(1)}, u32[]{:S(2)}, u32[]{:S(2)}) collective-permute-start(bf16[4,352,256]{2,1,0:T(8,128)(2,1)S(1)} %get-tuple-element.316), channel_id=1, source_target_pairs={{0,16},{4,20},{8,24},{12,28},{16,0},{20,4},{24,8},{28,12},{1,17},{... | collective-permute-start | bytes 2162696 | tf_op jit(solution)/shard_map/ppermute | solution.py:73
  451.8 58.8 %collective-permute-start.8 = (bf16[4,352,256]{2,1,0:T(8,128)(2,1)S(1)}, bf16[4,352,256]{2,1,0:T(8,128)(2,1)S(1)}, u32[]{:S(2)}, u32[]{:S(2)}) collective-permute-start(bf16[4,352,256]{2,1,0:T(8,128)(2,1)S(1)} %get-tuple-element.317), channel_id=1, source_target_pairs={{0,8},{4,12},{8,0},{12,4},{16,24},{20,28},{24,16},{28,20},{1,9},{5... | collective-permute-start | bytes 2162696 | tf_op jit(solution)/shard_map/ppermute | solution.py:73
  517.5 4.1 collective-permute-start.14
  519.7 4.5 collective-permute-start.13
  521.0 3.6 collective-permute-start.12
  539.2 96.5 %all-to-all-start.4 = ((bf16[4,2048,512]{2,1,0:T(8,128)(2,1)}), bf16[4,2048,512]{2,1,0:T(8,128)(2,1)}, u32[]{:S(2)}, u32[]{:S(2)}) async-start(bf16[4,2048,512]{2,1,0:T(8,128)(2,1)} %bitcast.420), calls=%async_computation.5 | async-start | bytes 16777216 | tf_op jit(solution)/shard_map/all_to_all | solution.py:437
  545.7 240.2 %reduce-scatter.9.cloned.1.call-start = ((), (), s32[]{:S(2)}) async-start(), calls=%async_computation.18 | async-start | bytes 9732096 | tf_op jit(solution)/shard_map/reduce_scatter | solution.py:423
  545.7 44.6 %collective-permute-start.11 = (bf16[16,352,256]{2,1,0:T(8,128)(2,1)S(1)}, bf16[16,352,256]{2,1,0:T(8,128)(2,1)}, u32[]{:S(2)}, u32[]{:S(2)}) collective-permute-start(bf16[16,352,256]{2,1,0:T(8,128)(2,1)S(1)} %bitcast.417), channel_id=1, source_target_pairs={{0,4},{4,0},{8,12},{12,8},{16,20},{20,16},{24,28},{28,24},{1,5},{5... | collective-permute-start | bytes 8650760 | tf_op jit(solution)/shard_map/ppermute | solution.py:78
  702.9 97.8 %all-to-all-start.5 = ((bf16[4,2048,512]{2,1,0:T(8,128)(2,1)}), bf16[4,2048,512]{2,1,0:T(8,128)(2,1)}, u32[]{:S(2)}, u32[]{:S(2)}) async-start(bf16[4,2048,512]{2,1,0:T(8,128)(2,1)} %bitcast.421), calls=%async_computation.6 | async-start | bytes 16777216 | tf_op jit(solution)/shard_map/all_to_all | solution.py:437
  709.4 297.4 %reduce-scatter.13.cloned.1.call-start = ((), (), s32[]{:S(2)}) async-start(), calls=%async_computation.20 | async-start | bytes 5242880 | tf_op jit(solution)/shard_map/reduce_scatter | solution.py:432
  802.2 6.1 collective-permute-start.17
  803.6 6.3 collective-permute-start.16
  808.3 3.6 collective-permute-start.15
  811.9 4.1 collective-permute-start.19
  812.5 4.1 collective-permute-start.18
  814.0 5.0 collective-permute-start.20
  871.5 93.3 %all-to-all-start.7 = ((bf16[4,2048,512]{2,1,0:T(8,128)(2,1)}), bf16[4,2048,512]{2,1,0:T(8,128)(2,1)}, u32[]{:S(2)}, u32[]{:S(2)}) async-start(bf16[4,2048,512]{2,1,0:T(8,128)(2,1)} %bitcast.422), calls=%async_computation.11 | async-start | bytes 16777216 | tf_op jit(solution)/shard_map/all_to_all | solution.py:437
  877.6 132.0 %reduce-scatter.11.cloned.1.call-start = ((), (), s32[]{:S(2)}) async-start(), calls=%async_computation.19 | async-start | bytes 5242880 | tf_op jit(solution)/shard_map/reduce_scatter | solution.py:418
  878.3 196.5 %reduce-scatter.15.cloned.1.call-start = ((), (), s32[]{:S(2)}) async-start(), calls=%async_computation.21 | async-start | bytes 5242880 | tf_op jit(solution)/shard_map/reduce_scatter | solution.py:418
  995.0 30.8 %collective-permute-start.21 = (bf16[16,352,256]{2,1,0:T(8,128)(2,1)}, bf16[16,352,256]{2,1,0:T(8,128)(2,1)}, u32[]{:S(2)}, u32[]{:S(2)}) collective-permute-start(bf16[16,352,256]{2,1,0:T(8,128)(2,1)} %get-tuple-element.143), channel_id=1, source_target_pairs={{0,4},{4,0},{8,12},{12,8},{16,20},{20,16},{24,28},{28,24},{1,5},{5... | collective-permute-start | bytes 8650760 | tf_op jit(solution)/shard_map/ppermute | solution.py:78
  995.0 36.2 %collective-permute-start.22 = (bf16[16,352,256]{2,1,0:T(8,128)(2,1)}, bf16[16,352,256]{2,1,0:T(8,128)(2,1)}, u32[]{:S(2)}, u32[]{:S(2)}) collective-permute-start(bf16[16,352,256]{2,1,0:T(8,128)(2,1)} %get-tuple-element.145), channel_id=1, source_target_pairs={{0,4},{4,0},{8,12},{12,8},{16,20},{20,16},{24,28},{28,24},{1,5},{5... | collective-permute-start | bytes 8650760 | tf_op jit(solution)/shard_map/ppermute | solution.py:78
  1006.7 28.8 %collective-permute-start.23 = (bf16[16,352,256]{2,1,0:T(8,128)(2,1)}, bf16[16,352,256]{2,1,0:T(8,128)(2,1)}, u32[]{:S(2)}, u32[]{:S(2)}) collective-permute-start(bf16[16,352,256]{2,1,0:T(8,128)(2,1)} %get-tuple-element.147), channel_id=1, source_target_pairs={{0,4},{4,0},{8,12},{12,8},{16,20},{20,16},{24,28},{28,24},{1,5},{5... | collective-permute-start | bytes 8650760 | tf_op jit(solution)/shard_map/ppermute | solution.py:78
  1017.0 53.4 %all-to-all-start.6 = ((bf16[4,1024,512]{2,1,0:T(8,128)(2,1)}), bf16[4,1024,512]{2,1,0:T(8,128)(2,1)}, u32[]{:S(2)}, u32[]{:S(2)}) async-start(bf16[4,1024,512]{2,1,0:T(8,128)(2,1)} %bitcast.424), calls=%async_computation.10 | async-start | bytes 8388608 | tf_op jit(solution)/shard_map/all_to_all | solution.py:437
  1022.6 145.3 %all-gather.11.cloned.1.call-start = ((), (), s32[]{:S(2)}) async-start(), calls=%async_computation.22 | async-start | bytes 5242880 | tf_op jit(solution)/shard_map/all_gather | solution.py:429
  1161.0 67.0 %all-to-all-start.9 = ((bf16[4,4,352,256]{3,2,1,0:T(8,128)(2,1)}), bf16[4,4,352,256]{3,2,1,0:T(8,128)(2,1)}, u32[]{:S(2)}, u32[]{:S(2)}) async-start(bf16[4,4,352,256]{3,2,1,0:T(8,128)(2,1)} %bitcast.118), calls=%async_computation.14 | async-start | bytes 5767168 | tf_op jit(solution)/shard_map/all_to_all | solution.py:440
  1167.4 81.6 %all-gather.13.cloned.1.call-start = ((), (), s32[]{:S(2)}) async-start(), calls=%async_computation.23 | async-start | bytes 5242880 | tf_op jit(solution)/shard_map/all_gather | solution.py:429
  1177.0 61.9 %collective-permute-start.26 = (bf16[4,352,256]{2,1,0:T(8,128)(2,1)}, bf16[4,352,256]{2,1,0:T(8,128)(2,1)}, u32[]{:S(2)}, u32[]{:S(2)}) collective-permute-start(bf16[4,352,256]{2,1,0:T(8,128)(2,1)} %get-tuple-element.310), channel_id=1, source_target_pairs={{0,3},{1,2},{2,1},{3,0},{4,7},{5,6},{6,5},{7,4},{8,11},{9,10},{10,... | collective-permute-start | bytes 2162696 | tf_op jit(solution)/shard_map/ppermute | solution.py:68
  1179.0 59.8 %collective-permute-start.25 = (bf16[4,352,256]{2,1,0:T(8,128)(2,1)}, bf16[4,352,256]{2,1,0:T(8,128)(2,1)}, u32[]{:S(2)}, u32[]{:S(2)}) collective-permute-start(bf16[4,352,256]{2,1,0:T(8,128)(2,1)} %get-tuple-element.311), channel_id=1, source_target_pairs={{0,2},{1,3},{2,0},{3,1},{4,6},{5,7},{6,4},{7,5},{8,10},{9,11},{10,... | collective-permute-start | bytes 2162696 | tf_op jit(solution)/shard_map/ppermute | solution.py:68
  1179.6 59.3 %collective-permute-start.24 = (bf16[4,352,256]{2,1,0:T(8,128)(2,1)}, bf16[4,352,256]{2,1,0:T(8,128)(2,1)}, u32[]{:S(2)}, u32[]{:S(2)}) collective-permute-start(bf16[4,352,256]{2,1,0:T(8,128)(2,1)} %get-tuple-element.312), channel_id=1, source_target_pairs={{0,1},{1,0},{2,3},{3,2},{4,5},{5,4},{6,7},{7,6},{8,9},{9,8},{10,11... | collective-permute-start | bytes 2162696 | tf_op jit(solution)/shard_map/ppermute | solution.py:68
  1228.1 97.1 %all-to-all-start.10 = ((bf16[4,4,352,256]{3,2,1,0:T(8,128)(2,1)}), bf16[4,4,352,256]{3,2,1,0:T(8,128)(2,1)}, u32[]{:S(2)}, u32[]{:S(2)}) async-start(bf16[4,4,352,256]{3,2,1,0:T(8,128)(2,1)} %bitcast.428), calls=%async_computation.15 | async-start | bytes 5767168 | tf_op jit(solution)/shard_map/all_to_all | solution.py:440
  1236.0 228.7 %reduce-scatter.17.cloned.1.call-start = ((), (), s32[]{:S(2)}) async-start(), calls=%async_computation.24 | async-start | bytes 9879552 | tf_op jit(solution)/shard_map/reduce_scatter | solution.py:423
  1253.8 26.4 %collective-permute-start.27 = (bf16[1024,512]{1,0:T(8,128)(2,1)}, bf16[1024,512]{1,0:T(8,128)(2,1)}, u32[]{:S(2)}, u32[]{:S(2)}) collective-permute-start(bf16[1024,512]{1,0:T(8,128)(2,1)} %get-tuple-element.293), channel_id=1, source_target_pairs={{0,1},{1,0},{2,3},{3,2},{4,5},{5,4},{6,7},{7,6},{8,9},{9,8},{10,11... | collective-permute-start | bytes 3145736 | tf_op jit(solution)/shard_map/ppermute | solution.py:68
  1255.0 48.4 %collective-permute-start.29 = (bf16[1024,512]{1,0:T(8,128)(2,1)}, bf16[1024,512]{1,0:T(8,128)(2,1)}, u32[]{:S(2)}, u32[]{:S(2)}) collective-permute-start(bf16[1024,512]{1,0:T(8,128)(2,1)} %get-tuple-element.294), channel_id=1, source_target_pairs={{0,3},{1,2},{2,1},{3,0},{4,7},{5,6},{6,5},{7,4},{8,11},{9,10},{10,... | collective-permute-start | bytes 3145736 | tf_op jit(solution)/shard_map/ppermute | solution.py:68
  1256.4 64.3 %collective-permute-start.28 = (bf16[1024,512]{1,0:T(8,128)(2,1)}, bf16[1024,512]{1,0:T(8,128)(2,1)}, u32[]{:S(2)}, u32[]{:S(2)}) collective-permute-start(bf16[1024,512]{1,0:T(8,128)(2,1)} %get-tuple-element.295), channel_id=1, source_target_pairs={{0,2},{1,3},{2,0},{3,1},{4,6},{5,7},{6,4},{7,5},{8,10},{9,11},{10,... | collective-permute-start | bytes 3145736 | tf_op jit(solution)/shard_map/ppermute | solution.py:68
  1266.9 58.3 %collective-permute-start.32 = (bf16[4,352,256]{2,1,0:T(8,128)(2,1)}, bf16[4,352,256]{2,1,0:T(8,128)(2,1)S(1)}, u32[]{:S(2)}, u32[]{:S(2)}) collective-permute-start(bf16[4,352,256]{2,1,0:T(8,128)(2,1)} %get-tuple-element.306), channel_id=1, source_target_pairs={{0,3},{1,2},{2,1},{3,0},{4,7},{5,6},{6,5},{7,4},{8,11},{9,10},{10,... | collective-permute-start | bytes 2162696 | tf_op jit(solution)/shard_map/ppermute | solution.py:68
  1268.9 64.5 %collective-permute-start.31 = (bf16[4,352,256]{2,1,0:T(8,128)(2,1)}, bf16[4,352,256]{2,1,0:T(8,128)(2,1)}, u32[]{:S(2)}, u32[]{:S(2)}) collective-permute-start(bf16[4,352,256]{2,1,0:T(8,128)(2,1)} %get-tuple-element.307), channel_id=1, source_target_pairs={{0,2},{1,3},{2,0},{3,1},{4,6},{5,7},{6,4},{7,5},{8,10},{9,11},{10,... | collective-permute-start | bytes 2162696 | tf_op jit(solution)/shard_map/ppermute | solution.py:68
  1280.2 53.2 %collective-permute-start.30 = (bf16[4,352,256]{2,1,0:T(8,128)(2,1)}, bf16[4,352,256]{2,1,0:T(8,128)(2,1)S(1)}, u32[]{:S(2)}, u32[]{:S(2)}) collective-permute-start(bf16[4,352,256]{2,1,0:T(8,128)(2,1)} %get-tuple-element.308), channel_id=1, source_target_pairs={{0,1},{1,0},{2,3},{3,2},{4,5},{5,4},{6,7},{7,6},{8,9},{9,8},{10,11... | collective-permute-start | bytes 2162696 | tf_op jit(solution)/shard_map/ppermute | solution.py:68
  1368.4 20.1 %collective-permute-start.41 = (bf16[4,352,256]{2,1,0:T(8,128)(2,1)S(1)}, bf16[4,352,256]{2,1,0:T(8,128)(2,1)S(1)}, u32[]{:S(2)}, u32[]{:S(2)}) collective-permute-start(bf16[4,352,256]{2,1,0:T(8,128)(2,1)S(1)} %get-tuple-element.302), channel_id=1, source_target_pairs={{0,3},{1,2},{2,1},{3,0},{4,7},{5,6},{6,5},{7,4},{8,11},{9,10},{10,... | collective-permute-start | bytes 2162696 | tf_op jit(solution)/shard_map/ppermute | solution.py:68
  1370.0 86.6 %collective-permute-start.35 = (bf16[1024,512]{1,0:T(8,128)(2,1)S(1)}, bf16[1024,512]{1,0:T(8,128)(2,1)S(1)}, u32[]{:S(2)}, u32[]{:S(2)}) collective-permute-start(bf16[1024,512]{1,0:T(8,128)(2,1)S(1)} %fusion.38.refs_0_), channel_id=1, source_target_pairs={{0,3},{1,2},{2,1},{3,0},{4,7},{5,6},{6,5},{7,4},{8,11},{9,10},{10,... | collective-permute-start | bytes 3145736 | tf_op jit(solution)/shard_map/ppermute | solution.py:68
  1371.4 85.2 %collective-permute-start.34 = (bf16[1024,512]{1,0:T(8,128)(2,1)S(1)}, bf16[1024,512]{1,0:T(8,128)(2,1)S(1)}, u32[]{:S(2)}, u32[]{:S(2)}) collective-permute-start(bf16[1024,512]{1,0:T(8,128)(2,1)S(1)} %fusion.38.refs_0_), channel_id=1, source_target_pairs={{0,2},{1,3},{2,0},{3,1},{4,6},{5,7},{6,4},{7,5},{8,10},{9,11},{10,... | collective-permute-start | bytes 3145736 | tf_op jit(solution)/shard_map/ppermute | solution.py:68
  1372.0 86.6 %collective-permute-start.33 = (bf16[1024,512]{1,0:T(8,128)(2,1)S(1)}, bf16[1024,512]{1,0:T(8,128)(2,1)}, u32[]{:S(2)}, u32[]{:S(2)}) collective-permute-start(bf16[1024,512]{1,0:T(8,128)(2,1)S(1)} %fusion.38.refs_0_), channel_id=1, source_target_pairs={{0,1},{1,0},{2,3},{3,2},{4,5},{5,4},{6,7},{7,6},{8,9},{9,8},{10,11... | collective-permute-start | bytes 3145736 | tf_op jit(solution)/shard_map/ppermute | solution.py:68
  1373.5 69.6 %collective-permute-start.40 = (bf16[4,352,256]{2,1,0:T(8,128)(2,1)S(1)}, bf16[4,352,256]{2,1,0:T(8,128)(2,1)S(1)}, u32[]{:S(2)}, u32[]{:S(2)}) collective-permute-start(bf16[4,352,256]{2,1,0:T(8,128)(2,1)S(1)} %get-tuple-element.303), channel_id=1, source_target_pairs={{0,2},{1,3},{2,0},{3,1},{4,6},{5,7},{6,4},{7,5},{8,10},{9,11},{10,... | collective-permute-start | bytes 2162696 | tf_op jit(solution)/shard_map/ppermute | solution.py:68
  1388.5 54.6 %collective-permute-start.39 = (bf16[4,352,256]{2,1,0:T(8,128)(2,1)S(1)}, bf16[4,352,256]{2,1,0:T(8,128)(2,1)S(1)}, u32[]{:S(2)}, u32[]{:S(2)}) collective-permute-start(bf16[4,352,256]{2,1,0:T(8,128)(2,1)S(1)} %get-tuple-element.304), channel_id=1, source_target_pairs={{0,1},{1,0},{2,3},{3,2},{4,5},{5,4},{6,7},{7,6},{8,9},{9,8},{10,11... | collective-permute-start | bytes 2162696 | tf_op jit(solution)/shard_map/ppermute | solution.py:68
  1466.9 11.1 collective-permute-start.38
  1468.6 15.0 %collective-permute-start.37 = (bf16[592,256]{1,0:T(8,128)(2,1)S(1)}, bf16[592,256]{1,0:T(8,128)(2,1)}, u32[]{:S(2)}, u32[]{:S(2)}) collective-permute-start(bf16[592,256]{1,0:T(8,128)(2,1)S(1)} %fusion.49), channel_id=1, source_target_pairs={{0,2},{1,3},{2,0},{3,1},{4,6},{5,7},{6,4},{7,5},{8,10},{9,11},{10,... | collective-permute-start | bytes 909320 | tf_op jit(solution)/shard_map/ppermute | solution.py:68
  1469.7 13.9 collective-permute-start.36
  (104 other events, 1846.4 us)
Sparse Core Ops, SparseCore 0:
  21.3 86.0 all-gather.14
  211.2 53.4 reduce-scatter.6
  284.0 79.4 all-gather.16
  364.9 79.2 all-gather.18
  512.5 83.6 all-gather.20
  695.6 90.2 reduce-scatter.8
  800.8 54.0 reduce-scatter.12
  880.7 75.9 reduce-scatter.10
  977.2 75.5 reduce-scatter.14
  1094.2 52.4 all-gather.10
  1170.1 77.6 all-gather.12
  1354.0 90.7 reduce-scatter.16

commit v12 on v10

--- a/solution.py
+++ b/solution.py
@@ -699,12 +699,13 @@
     ).astype(BF16)
     grad_shared_in = dot_tn(shared_pre_grad, ffn_low)
     grad_shared_out = dot_tn(shared_act, cot_low)
-    shared_grad_full = dot(shared_pre_grad, shared_in)
 
     out_parts, pre_low, shared_full = lax.optimization_barrier((out_parts, pre_low, shared_full))
     rows_grad = dot(pre_low, own_in).astype(BF16)
     rows_grad, out_parts = lax.optimization_barrier((rows_grad, out_parts))
     grad_parts = send_back(rows_grad)
+    rows_grad, shared_late = lax.optimization_barrier((rows_grad, shared_pre_grad))
+    shared_grad_full = dot(shared_late, shared_in)
     routed, pre_low, gated_active, shared_part = lax.optimization_barrier(
         (combine(out_parts), pre_low, gated_active, scatter_t(shared_full))
     )
@@ -730,20 +731,16 @@
 
     grad_in_own = dot_tn(pre_low, expert_rows).astype(BF16)
     grad_out_own = dot_tn(gated_active, cot_rows).astype(BF16)
-    (
-        grad_parts,
-        grad_in_own,
-        grad_out_own,
-        routed,
-        probs_grad,
-        shared_grad_full,
-    ) = lax.optimization_barrier(
-        (grad_parts, grad_in_own, grad_out_own, routed, probs_grad, shared_grad_full)
-    )
-    shared_grad = swap_t(
-        jnp.swapaxes(shared_grad_full.astype(BF16).reshape(rows, nt, part), 0, 1)
-    )
-    shared_grad = jnp.sum(shared_grad.astype(F32), axis=0)
+    grad_parts, grad_in_own, grad_out_own, probs_grad, shared_grad_full = lax.optimization_barrier(
+        (grad_parts, grad_in_own, grad_out_own, probs_grad, shared_grad_full)
+    )
+    routed, shared_ready = lax.optimization_barrier(
+        (
+            routed,
+            jnp.swapaxes(shared_grad_full.astype(BF16).reshape(rows, nt, part), 0, 1),
+        )
+    )
+    shared_grad = jnp.sum(swap_t(shared_ready).astype(F32), axis=0)
     grad_pieces = take_apart(lay, ids, grad_in_own, grad_out_own, f_loc, d_loc, width)
     routed_grad = scatter_z(combine(grad_parts)).astype(F32)
     grad_class = [

time: 1480 us -> 1480 us (level)
  waiting for transfers between devices: 569 us -> 551 us
    all_to_all x6, waiting for transfers between devices: 132 us -> 62.1 us  [swap_t(): lax.all_to_all(values, 'tensor', split_axis=0, concat_axis=0, tiled=True)]
    reduce_scatter x2, waiting for transfers between devices: 0.39 us -> 52.6 us  [scatter_z(): lax.psum_scatter(values, 'dp', scatter_dimension=0, tiled=False, axis_ind...]
    unnamed x245 -> x247, local copies, waits for them, and re-layouts: 47.4 us -> 48.2 us
  transfers between devices with their start and end apart: 65 -> 65, of which waited for: 33 -> 34; matrix products, arithmetic and copies ran while one was open for 37% -> 39% of each run, Pallas kernels for 7% -> 7%
where the time goes in v12:
time: 1480 us; the launch traced here: 1460 us
  waiting for transfers between devices  551 us (37%)
  matrix products  321 us (22%)
  local copies, waits for them, and re-layouts  204 us (14%)
  starting transfers between devices  126 us (9%)
  other arithmetic  118 us (8%)
  Pallas kernels  100 us (7%)
  blocking collectives  25.1 us (2%)
  between operations  17 us (1%)
    ppermute x24, waiting for transfers between devices, over_t(): return lax.ppermute(values, 'tensor', [(i, i ^ k) for i in range(self.t)])  146 us
    dot_general x9, matrix products, dot_nt(): lax.dot_general(a, b, (((1,), (1,)), ((), ())), preferred_element_type=F32)  99.8 us
    all_to_all x5, waiting for transfers between devices, swap_z(): lax.all_to_all(values, 'dp', split_axis=0, concat_axis=0, axis_index_grou...  88.9 us
    dot_general x8, matrix products, dot_tn(): lax.dot_general(a, b, (((0,), (0,)), ((), ())), preferred_element_type=F32)  81.9 us
    dot_general x9, matrix products, dot(): return jnp.dot(a, b, preferred_element_type=F32)  77.9 us
    all_to_all x6, waiting for transfers between devices, swap_t(): lax.all_to_all(values, 'tensor', split_axis=0, concat_axis=0, tiled=True)  62.1 us
    all_gather x2, waiting for transfers between devices, gather_z(): lax.all_gather(values, 'dp', axis=0, tiled=False, axis_index_groups=lay.z...  59.7 us
    all_gather x1, waiting for transfers between devices, body(): front = lax.all_gather(front_pack, 'dp', axis=0, tiled=False)  55.1 us
  transfers between devices with their start and end apart: 65, of which 34 were waited for; matrix products, arithmetic and copies ran while one was open for 39% of the time, Pallas kernels for 7%

profile of v12, /device:TPU:10, one launch (start us, length us, event | category | flops | bytes accessed | tf_op | source)
XLA Modules:
  0.0 1462.9 jit_solution(8926024843604065921)
XLA Ops:
  20.2 6.9 maximum_bitcast_fusion
  27.1 8.3 copy.295
  35.4 6.5 all-to-all-start
  51.4 55.1 %all-gather.15.cloned.1.call-done = bf16[17152,256]{1,0:T(8,128)(2,1)} async-done(((bf16[2144,256]{1,0:T(8,128)(2,1)}), bf16[17152,256]{1,0:T(8,128)(2,1)}) %all-gather.15.cloned.1.call-update) | async-done | bytes 8781840 | tf_op jit(solution)/shard_map/all_gather | solution.py:495
  117.2 19.5 %all-to-all-done = bf16[4,4,3,352,256]{4,3,1,2,0:T(8,128)(2,1)} async-done(((bf16[4,4,3,352,256]{4,3,1,2,0:T(8,128)(2,1)}), bf16[4,4,3,352,256]{4,3,1,2,0:T(8,128)(2,1)}, u32[]{:S(2)}, u32[]{:S(2)}) %all-to-all-start) | async-done | bytes 8650784 | tf_op jit(solution)/shard_map/all_to_all | solution.py:431
  165.9 6.4 fusion.111
  190.7 14.6 attend.1
  221.7 43.2 %reduce-scatter.7.cloned.1.call-done = bf16[1024,512]{1,0:T(8,128)(2,1)} async-done(((bf16[1024,2048]{1,0:T(8,128)(2,1)}), bf16[1024,512]{1,0:T(8,128)(2,1)}) %reduce-scatter.7.cloned.1.call-update) | async-done | bytes 1048592 | tf_op jit(solution)/shard_map/reduce_scatter | solution.py:426
  266.8 8.1 psum.21
  292.4 17.3 %collective-permute-done.3.refs_1_ = bf16[1024,512]{1,0:T(8,128)(2,1)} collective-permute-done((bf16[1024,512]{1,0:T(8,128)(2,1)}, bf16[1024,512]{1,0:T(8,128)(2,1)}, u32[]{:S(2)}, u32[]{:S(2)}) %collective-permute-start.3) | collective-permute-done | bytes 1048608 | tf_op jit(solution)/shard_map/ppermute | solution.py:68
  309.6 20.0 %collective-permute-done.4.refs_2_ = bf16[1024,512]{1,0:T(8,128)(2,1)} collective-permute-done((bf16[1024,512]{1,0:T(8,128)(2,1)}, bf16[1024,512]{1,0:T(8,128)(2,1)}, u32[]{:S(2)}, u32[]{:S(2)}) %collective-permute-start.4) | collective-permute-done | bytes 1048608 | tf_op jit(solution)/shard_map/ppermute | solution.py:68
  329.6 6.2 join_columns.2
  335.8 26.4 %all-gather.17.cloned.1.call-done = bf16[4096,512]{1,0:T(8,128)(2,1)} async-done(((bf16[1024,512]{1,0:T(8,128)(2,1)}), bf16[4096,512]{1,0:T(8,128)(2,1)}) %all-gather.17.cloned.1.call-update) | async-done | bytes 4194320 | tf_op jit(solution)/shard_map/all_gather | solution.py:415
  363.0 16.2 %convert_bitcast_fusion.1 = bf16[4,4,512,512]{3,2,0,1:T(8,128)(2,1)} fusion(s32[4,4,1024]{2,1,0:T(4,128)S(1)} %fusion.45, bf16[4,1024,512]{2,1,0:T(8,128)(2,1)} %bitcast.533), kind=kOutput, calls=%fused_computation.39 | convolution fusion | flops 8602517504 | bytes 12648448 | tf_op jit(solution)/shard_map/sepk,skd->espd/dot_general | solution.py:528
  379.3 7.6 copy.300
  396.6 13.2 lay_out_weights.2
  409.8 33.2 %all-gather.19.cloned.1.call-done = bf16[4096,512]{1,0:T(8,128)(2,1)} async-done(((bf16[1024,512]{1,0:T(8,128)(2,1)}), bf16[4096,512]{1,0:T(8,128)(2,1)}) %all-gather.19.cloned.1.call-update) | async-done | bytes 4194320 | tf_op jit(solution)/shard_map/all_gather | solution.py:415
  450.6 14.3 convert_bitcast_fusion
  465.0 7.4 copy.303
  472.4 23.1 %collective-permute-done.10 = bf16[4,352,256]{2,1,0:T(8,128)(2,1)S(1)} collective-permute-done((bf16[4,352,256]{2,1,0:T(8,128)(2,1)S(1)}, bf16[4,352,256]{2,1,0:T(8,128)(2,1)S(1)}, u32[]{:S(2)}, u32[]{:S(2)}) %collective-permute-start.10) | collective-permute-done | bytes 720928 | tf_op jit(solution)/shard_map/ppermute | solution.py:73
  495.6 13.9 collective-permute-done.9
  526.1 11.5 copy.301
  539.7 6.4 all-to-all-start.4
  546.2 32.4 %fusion.120 = f32[2048,2816]{1,0:T(8,128)} fusion(bf16[2048,2048]{0,1:T(8,128)(2,1)} %bitcast.441, bf16[2816,2048]{1,0:T(8,128)(2,1)} %bitcast.426), kind=kOutput, calls=%fused_computation.300 | convolution fusion | flops 23622320128 | bytes 42991616 | tf_op jit(solution)/shard_map/dot_general | solution.py:30
  578.5 12.3 fusion.8
  590.8 9.3 lay_out_weights.3
  602.6 15.1 %multiply_convert_fusion = bf16[2048,2048]{1,0:T(8,128)(2,1)} fusion(bf16[2048,1408]{1,0:T(8,128)(2,1)S(1)} %get-tuple-element.280, f32[2048]{0:T(1024)S(1)} %bitcast.503, bf16[1,1408,2048]{2,1,0:T(8,128)(2,1)S(1)} %lay_out_weights.3), kind=kOutput, calls=%fused_computation.5 | convolution fusion | flops 11819548672 | bytes 19931136 | tf_op jit(solution)/shard_map/dot_general | solution.py:26
  617.7 21.2 %all-to-all-done.4 = bf16[4,2048,512]{2,1,0:T(8,128)(2,1)} async-done(((bf16[4,2048,512]{2,1,0:T(8,128)(2,1)}), bf16[4,2048,512]{2,1,0:T(8,128)(2,1)}, u32[]{:S(2)}, u32[]{:S(2)}) %all-to-all-start.4) | async-done | bytes 8388640 | tf_op jit(solution)/shard_map/all_to_all | solution.py:431
  638.9 11.4 copy.310
  650.3 7.4 copy.389
  657.7 6.2 all-to-all-start.5
  664.1 28.0 %multiply_convert_fusion.2 = (bf16[2048,1408]{1,0:T(8,128)(2,1)}, bf16[2048,1408]{1,0:T(8,128)(2,1)}, f32[2048]{0:T(1024)S(1)}) fusion(f32[2048,2816]{1,0:T(8,128)} %fusion.120, f32[2048]{0:T(1024)S(1)} %bitcast.504, bf16[2048,1408]{1,0:T(8,128)(2,1)} %copy-done.36, bf16[2048,2048]{0,1:T(8,128)(2,1)} %bitcast.443, bf16[1,1408,2048]{2,1,0:T(8,128)(2,1)} %copy-done), kind=kOutput, calls=%fused_computation.16 | convolution fusion | flops 11860178944 | bytes 54542336 | tf_op jit(solution)/shard_map/dot_general | solution.py:30
  697.5 8.2 copy.313
  713.8 10.1 pad_maximum_fusion
  723.9 9.3 fusion.121
  733.3 6.2 multiply_convert_fusion.5
  757.2 31.3 %convolution_convert_fusion.3 = bf16[2048,2048]{1,0:T(8,128)(2,1)} fusion(bf16[2048,2816]{1,0:T(8,128)(2,1)} %pad_maximum_fusion, bf16[2816,2048]{1,0:T(8,128)(2,1)} %bitcast.427), kind=kOutput, calls=%fused_computation.42 | convolution fusion | flops 23626514432 | bytes 31457280 | tf_op jit(solution)/shard_map/dot_general | solution.py:26
  788.5 7.7 copy.388
  796.2 7.5 all-to-all-start.6
  803.7 12.3 bitcast_convert_fusion.1
  816.0 11.0 fusion.123
  829.9 18.0 %convolution_convert_fusion.2.out_ref = bf16[1408,2048]{1,0:T(8,128)(2,1)} fusion(bf16[2048,1408]{1,0:T(8,128)(2,1)} %get-tuple-element.134, bf16[2048,2048]{0,1:T(8,128)(2,1)} %bitcast.444), kind=kOutput, calls=%fused_computation.41 | convolution fusion | flops 11814043648 | bytes 19922944 | tf_op jit(solution)/shard_map/dot_general | solution.py:34
  848.0 31.7 %convolution_convert_fusion = bf16[2816,2048]{1,0:T(8,128)(2,1)} fusion(bf16[2048,2816]{1,0:T(8,128)(2,1)} %pad_maximum_fusion, bf16[2048,2048]{0,1:T(8,128)(2,1)} %bitcast.442), kind=kOutput, calls=%fused_computation.20 | convolution fusion | flops 23628087296 | bytes 31457280 | tf_op jit(solution)/shard_map/dot_general | solution.py:34
  879.6 17.2 %all-to-all-done.6 = bf16[4,2048,512]{2,1,0:T(8,128)(2,1)} async-done(((bf16[4,2048,512]{2,1,0:T(8,128)(2,1)}), bf16[4,2048,512]{2,1,0:T(8,128)(2,1)}, u32[]{:S(2)}, u32[]{:S(2)}) %all-to-all-start.6) | async-done | bytes 8388640 | tf_op jit(solution)/shard_map/all_to_all | solution.py:431
  896.8 12.2 bitcast_convert_fusion
  909.0 15.4 %take_apart.1 = (bf16[16,352,256]{2,1,0:T(8,128)(2,1)S(1)}, bf16[16,352,256]{2,1,0:T(8,128)(2,1)S(1)}, bf16[16,352,256]{2,1,0:T(8,128)(2,1)S(1)}, bf16[16,352,25...) custom-call(s32[3]{0:T(128)S(1)} %get-tuple-element.282.ids_ref, ...), custom_call_target="tpu_custom_call" | custom-call | bytes 34603008 | tf_op jit(solution)/shard_map/take_apart/pallas_call | solution.py:128
  938.8 11.8 all-to-all-start.7
  968.3 47.3 %reduce-scatter.13.cloned.1.call-done = bf16[1,1024,512]{2,1,0:T(8,128)(2,1)} async-done(((bf16[4,1024,512]{2,1,0:T(8,128)(2,1)}), bf16[1,1024,512]{2,1,0:T(8,128)(2,1)}) %reduce-scatter.13.cloned.1.call-update) | async-done | bytes 1048592 | tf_op jit(solution)/shard_map/reduce_scatter | solution.py:418
  1026.4 8.0 psum.22
  1044.0 6.1 convolution_convert_fusion.5
  1052.4 6.5 convolution_convert_fusion.1
  1063.0 40.9 %all-to-all-done.8 = bf16[4,4,352,256]{3,2,1,0:T(8,128)(2,1)S(1)} async-done(((bf16[4,4,352,256]{3,2,1,0:T(8,128)(2,1)}), bf16[4,4,352,256]{3,2,1,0:T(8,128)(2,1)S(1)}, u32[]{:S(2)}, u32[]{:S(2)}) %all-to-all-start.8) | async-done | bytes 2883616 | tf_op jit(solution)/shard_map/all_to_all | solution.py:434
  1105.5 7.9 all-to-all-start.9
  1126.0 21.6 %attend_back.1 = (bf16[1024,512]{1,0:T(8,128)(2,1)S(1)}, f32[1024,256]{1,0:T(8,128)S(1)}, bf16[1024,1024]{1,0:T(8,128)(2,1)S(1)}, f32[1024,256]{1,0:T(8,128)S(1)}) custom-call(s32[1]{0:T(128)} %copy.411.len_ref, bf16[1024,512]{1,0:T(8,128)(2,1)S(1)} %copy-done.5, bf16[1024,256]{1,0:T(8,128)(2,1)S(1)} %copy-done.10, bf16[1024,1024]{1,0:T(8,128)(2,1)S(1)} %copy-done.14, ...), custom_call_target="tpu_custom_call" | custom-call | flops 6710886400 | bytes 33554432 | tf_op jit(solution)/shard_map/attend_back/pallas_call | solution.py:330
  1149.8 24.8 %all-to-all-done.9 = bf16[4,4,352,256]{3,2,1,0:T(8,128)(2,1)} async-done(((bf16[4,4,352,256]{3,2,1,0:T(8,128)(2,1)}), bf16[4,4,352,256]{3,2,1,0:T(8,128)(2,1)}, u32[]{:S(2)}, u32[]{:S(2)}) %all-to-all-start.9) | async-done | bytes 2883616 | tf_op jit(solution)/shard_map/all_to_all | solution.py:434
  1175.7 7.8 all-to-all-start.10
  1230.8 7.3 collective-permute-done.27
  1242.7 18.7 %collective-permute-done.29 = bf16[1024,512]{1,0:T(8,128)(2,1)S(1)} collective-permute-done((bf16[1024,512]{1,0:T(8,128)(2,1)}, bf16[1024,512]{1,0:T(8,128)(2,1)S(1)}, u32[]{:S(2)}, u32[]{:S(2)}) %collective-permute-start.29) | collective-permute-done | bytes 1048608 | tf_op jit(solution)/shard_map/ppermute | solution.py:68
  1271.0 18.3 %all-to-all-done.10 = bf16[4,4,352,256]{3,2,1,0:T(8,128)(2,1)} async-done(((bf16[4,4,352,256]{3,2,1,0:T(8,128)(2,1)}), bf16[4,4,352,256]{3,2,1,0:T(8,128)(2,1)}, u32[]{:S(2)}, u32[]{:S(2)}) %all-to-all-start.10) | async-done | bytes 2883616 | tf_op jit(solution)/shard_map/all_to_all | solution.py:434
  1321.6 9.0 psum.23
  1341.6 13.6 collective-permute-done.39.refs_9_
  1356.6 54.9 %collective-permute-done.40.refs_10_ = bf16[4,352,256]{2,1,0:T(8,128)(2,1)S(1)} collective-permute-done((bf16[4,352,256]{2,1,0:T(8,128)(2,1)S(1)}, bf16[4,352,256]{2,1,0:T(8,128)(2,1)S(1)}, u32[]{:S(2)}, u32[]{:S(2)}) %collective-permute-start.40) | collective-permute-done | bytes 720928 | tf_op jit(solution)/shard_map/ppermute | solution.py:68
  1411.5 13.7 home_gradients.1
  1427.2 6.1 join_columns.3
  (512 shorter events, 394.8 us)
Async XLA Ops:
  7.2 99.3 %all-gather.15.cloned.1.call-start = ((), (), s32[]{:S(2)}) async-start(), calls=%async_computation.25 | async-start | bytes 9879552 | tf_op jit(solution)/shard_map/all_gather | solution.py:495
  35.4 101.2 %all-to-all-start = ((bf16[4,4,3,352,256]{4,3,1,2,0:T(8,128)(2,1)}), bf16[4,4,3,352,256]{4,3,1,2,0:T(8,128)(2,1)}, u32[]{:S(2)}, u32[]{:S(2)}) async-start(bf16[4,4,3,352,256]{4,3,1,2,0:T(8,128)(2,1)} %copy.295), calls=%async_computation | async-start | bytes 17301504 | tf_op jit(solution)/shard_map/all_to_all | solution.py:431
  41.9 9.0 collective-permute-start
  43.5 7.4 collective-permute-start.1
  44.7 6.6 collective-permute-start.2
  143.9 68.1 %all-to-all-start.1 = ((bf16[4,4,352,256]{3,2,1,0:T(8,128)(2,1)}), bf16[4,4,352,256]{3,2,1,0:T(8,128)(2,1)S(1)}, u32[]{:S(2)}, u32[]{:S(2)}) async-start(bf16[4,4,352,256]{3,2,1,0:T(8,128)(2,1)} %copy.297), calls=%async_computation.1 | async-start | bytes 5767168 | tf_op jit(solution)/shard_map/all_to_all | solution.py:434
  149.3 115.6 %reduce-scatter.7.cloned.1.call-start = ((), (), s32[]{:S(2)}) async-start(), calls=%async_computation.17 | async-start | bytes 5242880 | tf_op jit(solution)/shard_map/reduce_scatter | solution.py:426
  215.7 67.0 %all-to-all-start.2 = ((bf16[4,4,352,256]{3,2,1,0:T(8,128)(2,1)}), bf16[4,4,352,256]{3,2,1,0:T(8,128)(2,1)}, u32[]{:S(2)}, u32[]{:S(2)}) async-start(bf16[4,4,352,256]{3,2,1,0:T(8,128)(2,1)} %copy.298), calls=%async_computation.3 | async-start | bytes 5767168 | tf_op jit(solution)/shard_map/all_to_all | solution.py:434
  221.6 140.7 %all-gather.17.cloned.1.call-start = ((), (), s32[]{:S(2)}) async-start(), calls=%async_computation.26 | async-start | bytes 5242880 | tf_op jit(solution)/shard_map/all_gather | solution.py:415
  282.7 160.4 %all-gather.19.cloned.1.call-start = ((), (), s32[]{:S(2)}) async-start(), calls=%async_computation.27 | async-start | bytes 5242880 | tf_op jit(solution)/shard_map/all_gather | solution.py:415
  283.2 26.5 %collective-permute-start.3 = (bf16[1024,512]{1,0:T(8,128)(2,1)}, bf16[1024,512]{1,0:T(8,128)(2,1)}, u32[]{:S(2)}, u32[]{:S(2)}) collective-permute-start(bf16[1024,512]{1,0:T(8,128)(2,1)} %multiply_convert_fusion.8.refs_0_), channel_id=1, source_target_pairs={{0,1},{1,0},{2,3},{3,2},{4,5},{5,4},{6,7},{7,6},{8,9},{9,8},{10,11... | collective-permute-start | bytes 3145736 | tf_op jit(solution)/shard_map/ppermute | solution.py:68
  284.1 45.5 %collective-permute-start.4 = (bf16[1024,512]{1,0:T(8,128)(2,1)}, bf16[1024,512]{1,0:T(8,128)(2,1)}, u32[]{:S(2)}, u32[]{:S(2)}) collective-permute-start(bf16[1024,512]{1,0:T(8,128)(2,1)} %multiply_convert_fusion.8.refs_0_), channel_id=1, source_target_pairs={{0,2},{1,3},{2,0},{3,1},{4,6},{5,7},{6,4},{7,5},{8,10},{9,11},{10,... | collective-permute-start | bytes 3145736 | tf_op jit(solution)/shard_map/ppermute | solution.py:68
  285.3 44.3 %collective-permute-start.5 = (bf16[1024,512]{1,0:T(8,128)(2,1)}, bf16[1024,512]{1,0:T(8,128)(2,1)}, u32[]{:S(2)}, u32[]{:S(2)}) collective-permute-start(bf16[1024,512]{1,0:T(8,128)(2,1)} %multiply_convert_fusion.8.refs_0_), channel_id=1, source_target_pairs={{0,3},{1,2},{2,1},{3,0},{4,7},{5,6},{6,5},{7,4},{8,11},{9,10},{10,... | collective-permute-start | bytes 3145736 | tf_op jit(solution)/shard_map/ppermute | solution.py:68
  386.9 9.5 collective-permute-start.6
  386.9 9.7 collective-permute-start.7
  389.6 136.5 %all-to-all-start.3 = ((bf16[4,2048,512]{2,1,0:T(8,128)(2,1)}), bf16[4,2048,512]{2,1,0:T(8,128)(2,1)}, u32[]{:S(2)}, u32[]{:S(2)}) async-start(bf16[4,2048,512]{2,1,0:T(8,128)(2,1)} %bitcast.420), calls=%async_computation.4 | async-start | bytes 16777216 | tf_op jit(solution)/shard_map/all_to_all | solution.py:431
  395.6 254.7 %all-gather.21.cloned.1.call-start = ((), (), s32[]{:S(2)}) async-start(), calls=%async_computation.28 | async-start | bytes 9732096 | tf_op jit(solution)/shard_map/all_gather | solution.py:644
  445.2 50.4 %collective-permute-start.10 = (bf16[4,352,256]{2,1,0:T(8,128)(2,1)S(1)}, bf16[4,352,256]{2,1,0:T(8,128)(2,1)S(1)}, u32[]{:S(2)}, u32[]{:S(2)}) collective-permute-start(bf16[4,352,256]{2,1,0:T(8,128)(2,1)S(1)} %get-tuple-element.315), channel_id=1, source_target_pairs={{0,24},{4,28},{8,16},{12,20},{16,8},{20,12},{24,0},{28,4},{1,25},{... | collective-permute-start | bytes 2162696 | tf_op jit(solution)/shard_map/ppermute | solution.py:73
  447.7 61.7 %collective-permute-start.9 = (bf16[4,352,256]{2,1,0:T(8,128)(2,1)S(1)}, bf16[4,352,256]{2,1,0:T(8,128)(2,1)S(1)}, u32[]{:S(2)}, u32[]{:S(2)}) collective-permute-start(bf16[4,352,256]{2,1,0:T(8,128)(2,1)S(1)} %get-tuple-element.316), channel_id=1, source_target_pairs={{0,16},{4,20},{8,24},{12,28},{16,0},{20,4},{24,8},{28,12},{1,17},{... | collective-permute-start | bytes 2162696 | tf_op jit(solution)/shard_map/ppermute | solution.py:73
  450.6 58.8 %collective-permute-start.8 = (bf16[4,352,256]{2,1,0:T(8,128)(2,1)S(1)}, bf16[4,352,256]{2,1,0:T(8,128)(2,1)S(1)}, u32[]{:S(2)}, u32[]{:S(2)}) collective-permute-start(bf16[4,352,256]{2,1,0:T(8,128)(2,1)S(1)} %get-tuple-element.317), channel_id=1, source_target_pairs={{0,8},{4,12},{8,0},{12,4},{16,24},{20,28},{24,16},{28,20},{1,9},{5... | collective-permute-start | bytes 2162696 | tf_op jit(solution)/shard_map/ppermute | solution.py:73
  516.8 5.0 collective-permute-start.12
  517.1 5.9 collective-permute-start.13
  539.7 51.2 %collective-permute-start.11 = (bf16[16,352,256]{2,1,0:T(8,128)(2,1)S(1)}, bf16[16,352,256]{2,1,0:T(8,128)(2,1)}, u32[]{:S(2)}, u32[]{:S(2)}) collective-permute-start(bf16[16,352,256]{2,1,0:T(8,128)(2,1)S(1)} %bitcast.418), channel_id=1, source_target_pairs={{0,4},{4,0},{8,12},{12,8},{16,20},{20,16},{24,28},{28,24},{1,5},{5... | collective-permute-start | bytes 8650760 | tf_op jit(solution)/shard_map/ppermute | solution.py:78
  539.7 99.1 %all-to-all-start.4 = ((bf16[4,2048,512]{2,1,0:T(8,128)(2,1)}), bf16[4,2048,512]{2,1,0:T(8,128)(2,1)}, u32[]{:S(2)}, u32[]{:S(2)}) async-start(bf16[4,2048,512]{2,1,0:T(8,128)(2,1)} %bitcast.421), calls=%async_computation.5 | async-start | bytes 16777216 | tf_op jit(solution)/shard_map/all_to_all | solution.py:431
  657.7 98.5 %all-to-all-start.5 = ((bf16[4,2048,512]{2,1,0:T(8,128)(2,1)}), bf16[4,2048,512]{2,1,0:T(8,128)(2,1)}, u32[]{:S(2)}, u32[]{:S(2)}) async-start(bf16[4,2048,512]{2,1,0:T(8,128)(2,1)} %bitcast.422), calls=%async_computation.6 | async-start | bytes 16777216 | tf_op jit(solution)/shard_map/all_to_all | solution.py:431
  663.9 163.1 %reduce-scatter.9.cloned.1.call-start = ((), (), s32[]{:S(2)}) async-start(), calls=%async_computation.18 | async-start | bytes 5242880 | tf_op jit(solution)/shard_map/reduce_scatter | solution.py:426
  710.0 35.6 %collective-permute-start.17 = (f32[8,128]{1,0:T(8,128)S(1)}, f32[8,128]{1,0:T(8,128)S(1)}, u32[]{:S(2)}, u32[]{:S(2)}) collective-permute-start(f32[8,128]{1,0:T(8,128)S(1)} %get-tuple-element.341), channel_id=1, source_target_pairs={{0,24},{4,28},{8,16},{12,20},{16,8},{20,12},{24,0},{28,4},{1,25},{... | collective-permute-start | bytes 12296 | tf_op jit(solution)/shard_map/ppermute | solution.py:73
  711.8 33.8 %collective-permute-start.16 = (f32[8,128]{1,0:T(8,128)S(1)}, f32[8,128]{1,0:T(8,128)S(1)}, u32[]{:S(2)}, u32[]{:S(2)}) collective-permute-start(f32[8,128]{1,0:T(8,128)S(1)} %get-tuple-element.342), channel_id=1, source_target_pairs={{0,16},{4,20},{8,24},{12,28},{16,0},{20,4},{24,8},{28,12},{1,17},{... | collective-permute-start | bytes 12296 | tf_op jit(solution)/shard_map/ppermute | solution.py:73
  713.8 31.9 %collective-permute-start.15 = (f32[8,128]{1,0:T(8,128)S(1)}, f32[8,128]{1,0:T(8,128)S(1)}, u32[]{:S(2)}, u32[]{:S(2)}) collective-permute-start(f32[8,128]{1,0:T(8,128)S(1)} %get-tuple-element.343), channel_id=1, source_target_pairs={{0,8},{4,12},{8,0},{12,4},{16,24},{20,28},{24,16},{28,20},{1,9},{5... | collective-permute-start | bytes 12296 | tf_op jit(solution)/shard_map/ppermute | solution.py:73
  745.7 10.6 collective-permute-start.20
  747.2 9.2 collective-permute-start.19
  747.3 9.1 collective-permute-start.18
  796.2 100.7 %all-to-all-start.6 = ((bf16[4,2048,512]{2,1,0:T(8,128)(2,1)}), bf16[4,2048,512]{2,1,0:T(8,128)(2,1)}, u32[]{:S(2)}, u32[]{:S(2)}) async-start(bf16[4,2048,512]{2,1,0:T(8,128)(2,1)} %bitcast.423), calls=%async_computation.9 | async-start | bytes 16777216 | tf_op jit(solution)/shard_map/all_to_all | solution.py:431
  803.7 132.3 %reduce-scatter.11.cloned.1.call-start = ((), (), s32[]{:S(2)}) async-start(), calls=%async_computation.19 | async-start | bytes 5242880 | tf_op jit(solution)/shard_map/reduce_scatter | solution.py:418
  829.9 185.8 %reduce-scatter.13.cloned.1.call-start = ((), (), s32[]{:S(2)}) async-start(), calls=%async_computation.20 | async-start | bytes 5242880 | tf_op jit(solution)/shard_map/reduce_scatter | solution.py:418
  927.7 26.5 %collective-permute-start.21 = (bf16[16,352,256]{2,1,0:T(8,128)(2,1)}, bf16[16,352,256]{2,1,0:T(8,128)(2,1)}, u32[]{:S(2)}, u32[]{:S(2)}) collective-permute-start(bf16[16,352,256]{2,1,0:T(8,128)(2,1)} %get-tuple-element.142), channel_id=1, source_target_pairs={{0,4},{4,0},{8,12},{12,8},{16,20},{20,16},{24,28},{28,24},{1,5},{5... | collective-permute-start | bytes 8650760 | tf_op jit(solution)/shard_map/ppermute | solution.py:78
  927.7 31.8 %collective-permute-start.22 = (bf16[16,352,256]{2,1,0:T(8,128)(2,1)}, bf16[16,352,256]{2,1,0:T(8,128)(2,1)}, u32[]{:S(2)}, u32[]{:S(2)}) collective-permute-start(bf16[16,352,256]{2,1,0:T(8,128)(2,1)} %get-tuple-element.144), channel_id=1, source_target_pairs={{0,4},{4,0},{8,12},{12,8},{16,20},{20,16},{24,28},{28,24},{1,5},{5... | collective-permute-start | bytes 8650760 | tf_op jit(solution)/shard_map/ppermute | solution.py:78
  928.2 35.7 %collective-permute-start.23 = (bf16[16,352,256]{2,1,0:T(8,128)(2,1)}, bf16[16,352,256]{2,1,0:T(8,128)(2,1)}, u32[]{:S(2)}, u32[]{:S(2)}) collective-permute-start(bf16[16,352,256]{2,1,0:T(8,128)(2,1)} %get-tuple-element.146), channel_id=1, source_target_pairs={{0,4},{4,0},{8,12},{12,8},{16,20},{20,16},{24,28},{28,24},{1,5},{5... | collective-permute-start | bytes 8650760 | tf_op jit(solution)/shard_map/ppermute | solution.py:78
  938.8 79.6 %all-to-all-start.7 = ((bf16[4,1024,512]{2,1,0:T(8,128)(2,1)}), bf16[4,1024,512]{2,1,0:T(8,128)(2,1)}, u32[]{:S(2)}, u32[]{:S(2)}) async-start(bf16[4,1024,512]{2,1,0:T(8,128)(2,1)} %bitcast.425), calls=%async_computation.10 | async-start | bytes 8388608 | tf_op jit(solution)/shard_map/all_to_all | solution.py:431
  950.7 153.3 %all-gather.11.cloned.1.call-start = ((), (), s32[]{:S(2)}) async-start(), calls=%async_computation.21 | async-start | bytes 5242880 | tf_op jit(solution)/shard_map/all_gather | solution.py:423
  1039.3 64.7 %all-to-all-start.8 = ((bf16[4,4,352,256]{3,2,1,0:T(8,128)(2,1)}), bf16[4,4,352,256]{3,2,1,0:T(8,128)(2,1)S(1)}, u32[]{:S(2)}, u32[]{:S(2)}) async-start(bf16[4,4,352,256]{3,2,1,0:T(8,128)(2,1)} %bitcast.430), calls=%async_computation.12 | async-start | bytes 5767168 | tf_op jit(solution)/shard_map/all_to_all | solution.py:434
  1044.0 162.9 %all-gather.13.cloned.1.call-start = ((), (), s32[]{:S(2)}) async-start(), calls=%async_computation.22 | async-start | bytes 5242880 | tf_op jit(solution)/shard_map/all_gather | solution.py:423
  1105.5 69.2 %all-to-all-start.9 = ((bf16[4,4,352,256]{3,2,1,0:T(8,128)(2,1)}), bf16[4,4,352,256]{3,2,1,0:T(8,128)(2,1)}, u32[]{:S(2)}, u32[]{:S(2)}) async-start(bf16[4,4,352,256]{3,2,1,0:T(8,128)(2,1)} %bitcast.117), calls=%async_computation.13 | async-start | bytes 5767168 | tf_op jit(solution)/shard_map/all_to_all | solution.py:434
  1113.4 320.0 %reduce-scatter.17.cloned.1.call-start = ((), (), s32[]{:S(2)}) async-start(), calls=%async_computation.24 | async-start | bytes 9732096 | tf_op jit(solution)/shard_map/reduce_scatter | solution.py:783
  1117.1 57.5 %collective-permute-start.24 = (bf16[4,352,256]{2,1,0:T(8,128)(2,1)}, bf16[4,352,256]{2,1,0:T(8,128)(2,1)S(1)}, u32[]{:S(2)}, u32[]{:S(2)}) collective-permute-start(bf16[4,352,256]{2,1,0:T(8,128)(2,1)} %get-tuple-element.312), channel_id=1, source_target_pairs={{0,1},{1,0},{2,3},{3,2},{4,5},{5,4},{6,7},{7,6},{8,9},{9,8},{10,11... | collective-permute-start | bytes 2162696 | tf_op jit(solution)/shard_map/ppermute | solution.py:68
  1119.3 55.3 %collective-permute-start.25 = (bf16[4,352,256]{2,1,0:T(8,128)(2,1)}, bf16[4,352,256]{2,1,0:T(8,128)(2,1)}, u32[]{:S(2)}, u32[]{:S(2)}) collective-permute-start(bf16[4,352,256]{2,1,0:T(8,128)(2,1)} %get-tuple-element.311), channel_id=1, source_target_pairs={{0,2},{1,3},{2,0},{3,1},{4,6},{5,7},{6,4},{7,5},{8,10},{9,11},{10,... | collective-permute-start | bytes 2162696 | tf_op jit(solution)/shard_map/ppermute | solution.py:68
  1119.9 55.0 %collective-permute-start.26 = (bf16[4,352,256]{2,1,0:T(8,128)(2,1)}, bf16[4,352,256]{2,1,0:T(8,128)(2,1)}, u32[]{:S(2)}, u32[]{:S(2)}) collective-permute-start(bf16[4,352,256]{2,1,0:T(8,128)(2,1)} %get-tuple-element.310), channel_id=1, source_target_pairs={{0,3},{1,2},{2,1},{3,0},{4,7},{5,6},{6,5},{7,4},{8,11},{9,10},{10,... | collective-permute-start | bytes 2162696 | tf_op jit(solution)/shard_map/ppermute | solution.py:68
  1175.7 113.6 %all-to-all-start.10 = ((bf16[4,4,352,256]{3,2,1,0:T(8,128)(2,1)}), bf16[4,4,352,256]{3,2,1,0:T(8,128)(2,1)}, u32[]{:S(2)}, u32[]{:S(2)}) async-start(bf16[4,4,352,256]{3,2,1,0:T(8,128)(2,1)} %bitcast.429), calls=%async_computation.14 | async-start | bytes 5767168 | tf_op jit(solution)/shard_map/all_to_all | solution.py:434
  1183.4 253.4 %reduce-scatter.15.cloned.1.call-start = ((), (), s32[]{:S(2)}) async-start(), calls=%async_computation.23 | async-start | bytes 9879552 | tf_op jit(solution)/shard_map/reduce_scatter | solution.py:783
  1211.7 26.5 %collective-permute-start.27 = (bf16[1024,512]{1,0:T(8,128)(2,1)}, bf16[1024,512]{1,0:T(8,128)(2,1)}, u32[]{:S(2)}, u32[]{:S(2)}) collective-permute-start(bf16[1024,512]{1,0:T(8,128)(2,1)} %get-tuple-element.293), channel_id=1, source_target_pairs={{0,1},{1,0},{2,3},{3,2},{4,5},{5,4},{6,7},{7,6},{8,9},{9,8},{10,11... | collective-permute-start | bytes 3145736 | tf_op jit(solution)/shard_map/ppermute | solution.py:68
  1217.5 43.9 %collective-permute-start.29 = (bf16[1024,512]{1,0:T(8,128)(2,1)}, bf16[1024,512]{1,0:T(8,128)(2,1)S(1)}, u32[]{:S(2)}, u32[]{:S(2)}) collective-permute-start(bf16[1024,512]{1,0:T(8,128)(2,1)} %get-tuple-element.294), channel_id=1, source_target_pairs={{0,3},{1,2},{2,1},{3,0},{4,7},{5,6},{6,5},{7,4},{8,11},{9,10},{10,... | collective-permute-start | bytes 3145736 | tf_op jit(solution)/shard_map/ppermute | solution.py:68
  1218.4 48.8 %collective-permute-start.28 = (bf16[1024,512]{1,0:T(8,128)(2,1)}, bf16[1024,512]{1,0:T(8,128)(2,1)S(1)}, u32[]{:S(2)}, u32[]{:S(2)}) collective-permute-start(bf16[1024,512]{1,0:T(8,128)(2,1)} %get-tuple-element.295), channel_id=1, source_target_pairs={{0,2},{1,3},{2,0},{3,1},{4,6},{5,7},{6,4},{7,5},{8,10},{9,11},{10,... | collective-permute-start | bytes 3145736 | tf_op jit(solution)/shard_map/ppermute | solution.py:68
  1228.2 61.1 %collective-permute-start.30 = (bf16[4,352,256]{2,1,0:T(8,128)(2,1)}, bf16[4,352,256]{2,1,0:T(8,128)(2,1)}, u32[]{:S(2)}, u32[]{:S(2)}) collective-permute-start(bf16[4,352,256]{2,1,0:T(8,128)(2,1)} %get-tuple-element.308), channel_id=1, source_target_pairs={{0,1},{1,0},{2,3},{3,2},{4,5},{5,4},{6,7},{7,6},{8,9},{9,8},{10,11... | collective-permute-start | bytes 2162696 | tf_op jit(solution)/shard_map/ppermute | solution.py:68
  1230.2 64.9 %collective-permute-start.31 = (bf16[4,352,256]{2,1,0:T(8,128)(2,1)}, bf16[4,352,256]{2,1,0:T(8,128)(2,1)}, u32[]{:S(2)}, u32[]{:S(2)}) collective-permute-start(bf16[4,352,256]{2,1,0:T(8,128)(2,1)} %get-tuple-element.307), channel_id=1, source_target_pairs={{0,2},{1,3},{2,0},{3,1},{4,6},{5,7},{6,4},{7,5},{8,10},{9,11},{10,... | collective-permute-start | bytes 2162696 | tf_op jit(solution)/shard_map/ppermute | solution.py:68
  1238.2 56.9 %collective-permute-start.32 = (bf16[4,352,256]{2,1,0:T(8,128)(2,1)}, bf16[4,352,256]{2,1,0:T(8,128)(2,1)}, u32[]{:S(2)}, u32[]{:S(2)}) collective-permute-start(bf16[4,352,256]{2,1,0:T(8,128)(2,1)} %get-tuple-element.306), channel_id=1, source_target_pairs={{0,3},{1,2},{2,1},{3,0},{4,7},{5,6},{6,5},{7,4},{8,11},{9,10},{10,... | collective-permute-start | bytes 2162696 | tf_op jit(solution)/shard_map/ppermute | solution.py:68
  1336.0 19.1 %collective-permute-start.39 = (bf16[4,352,256]{2,1,0:T(8,128)(2,1)S(1)}, bf16[4,352,256]{2,1,0:T(8,128)(2,1)S(1)}, u32[]{:S(2)}, u32[]{:S(2)}) collective-permute-start(bf16[4,352,256]{2,1,0:T(8,128)(2,1)S(1)} %get-tuple-element.304), channel_id=1, source_target_pairs={{0,1},{1,0},{2,3},{3,2},{4,5},{5,4},{6,7},{7,6},{8,9},{9,8},{10,11... | collective-permute-start | bytes 2162696 | tf_op jit(solution)/shard_map/ppermute | solution.py:68
  1337.2 88.0 %collective-permute-start.33 = (bf16[1024,512]{1,0:T(8,128)(2,1)S(1)}, bf16[1024,512]{1,0:T(8,128)(2,1)S(1)}, u32[]{:S(2)}, u32[]{:S(2)}) collective-permute-start(bf16[1024,512]{1,0:T(8,128)(2,1)S(1)} %fusion.38.refs_0_), channel_id=1, source_target_pairs={{0,1},{1,0},{2,3},{3,2},{4,5},{5,4},{6,7},{7,6},{8,9},{9,8},{10,11... | collective-permute-start | bytes 3145736 | tf_op jit(solution)/shard_map/ppermute | solution.py:68
  1338.1 87.2 %collective-permute-start.34 = (bf16[1024,512]{1,0:T(8,128)(2,1)S(1)}, bf16[1024,512]{1,0:T(8,128)(2,1)S(1)}, u32[]{:S(2)}, u32[]{:S(2)}) collective-permute-start(bf16[1024,512]{1,0:T(8,128)(2,1)S(1)} %fusion.38.refs_0_), channel_id=1, source_target_pairs={{0,2},{1,3},{2,0},{3,1},{4,6},{5,7},{6,4},{7,5},{8,10},{9,11},{10,... | collective-permute-start | bytes 3145736 | tf_op jit(solution)/shard_map/ppermute | solution.py:68
  1339.5 87.7 %collective-permute-start.35 = (bf16[1024,512]{1,0:T(8,128)(2,1)S(1)}, bf16[1024,512]{1,0:T(8,128)(2,1)}, u32[]{:S(2)}, u32[]{:S(2)}) collective-permute-start(bf16[1024,512]{1,0:T(8,128)(2,1)S(1)} %fusion.38.refs_0_), channel_id=1, source_target_pairs={{0,3},{1,2},{2,1},{3,0},{4,7},{5,6},{6,5},{7,4},{8,11},{9,10},{10,... | collective-permute-start | bytes 3145736 | tf_op jit(solution)/shard_map/ppermute | solution.py:68
  1340.7 70.8 %collective-permute-start.40 = (bf16[4,352,256]{2,1,0:T(8,128)(2,1)S(1)}, bf16[4,352,256]{2,1,0:T(8,128)(2,1)S(1)}, u32[]{:S(2)}, u32[]{:S(2)}) collective-permute-start(bf16[4,352,256]{2,1,0:T(8,128)(2,1)S(1)} %get-tuple-element.303), channel_id=1, source_target_pairs={{0,2},{1,3},{2,0},{3,1},{4,6},{5,7},{6,4},{7,5},{8,10},{9,11},{10,... | collective-permute-start | bytes 2162696 | tf_op jit(solution)/shard_map/ppermute | solution.py:68
  1355.2 56.3 %collective-permute-start.41 = (bf16[4,352,256]{2,1,0:T(8,128)(2,1)S(1)}, bf16[4,352,256]{2,1,0:T(8,128)(2,1)S(1)}, u32[]{:S(2)}, u32[]{:S(2)}) collective-permute-start(bf16[4,352,256]{2,1,0:T(8,128)(2,1)S(1)} %get-tuple-element.302), channel_id=1, source_target_pairs={{0,3},{1,2},{2,1},{3,0},{4,7},{5,6},{6,5},{7,4},{8,11},{9,10},{10,... | collective-permute-start | bytes 2162696 | tf_op jit(solution)/shard_map/ppermute | solution.py:68
  1439.1 9.0 collective-permute-start.38
  1440.8 9.6 collective-permute-start.37
  1442.3 8.1 collective-permute-start.36
  (112 other events, 1878.5 us)
Sparse Core Ops, SparseCore 0:
  20.3 86.0 all-gather.14
  212.2 52.5 reduce-scatter.6
  282.8 79.3 all-gather.16
  363.7 79.2 all-gather.18
  511.3 83.6 all-gather.20
  756.4 54.1 reduce-scatter.8
  830.0 105.9 reduce-scatter.10
  938.4 77.2 reduce-scatter.12
  1039.4 53.0 all-gather.10
  1104.1 77.6 all-gather.12
  1184.0 140.2 reduce-scatter.16
  1326.5 94.2 reduce-scatter.14

commit v13 on v12

--- a/solution.py
+++ b/solution.py
@@ -706,8 +706,8 @@
     grad_parts = send_back(rows_grad)
     rows_grad, shared_late = lax.optimization_barrier((rows_grad, shared_pre_grad))
     shared_grad_full = dot(shared_late, shared_in)
-    routed, pre_low, gated_active, shared_part = lax.optimization_barrier(
-        (combine(out_parts), pre_low, gated_active, scatter_t(shared_full))
+    routed, pre_low, gated_active = lax.optimization_barrier(
+        (combine(out_parts), pre_low, gated_active)
     )
     routed = scatter_z(routed).astype(F32)
     token_grad = jnp.sum(jnp.where(own_place, gate_grad[:, :, None], 0.0), axis=1)
@@ -742,6 +742,8 @@
     )
     shared_grad = jnp.sum(swap_t(shared_ready).astype(F32), axis=0)
     grad_pieces = take_apart(lay, ids, grad_in_own, grad_out_own, f_loc, d_loc, width)
+    grad_pieces, shared_full = lax.optimization_barrier((grad_pieces, shared_full))
+    shared_part = scatter_t(shared_full)
     routed_grad = scatter_z(combine(grad_parts)).astype(F32)
     grad_class = [
         sum(lay.over_c(grad_pieces[3 * k + g], k).astype(F32) for k in range(nq)).astype(BF16)
@@ -777,7 +779,10 @@
     residual_grad = cot_part.astype(F32) + ffn_inverse * (
         scaled - ffn_hat * row_mean(ffn_hat * scaled)
     )
-    residual_low = gather_t(residual_grad.astype(BF16))
+    residual_ready, shared_part = lax.optimization_barrier(
+        (residual_grad.astype(BF16), shared_part)
+    )
+    residual_low = gather_t(residual_ready)
 
     def sum_dp(values):
         return lax.psum_scatter(values, "dp", scatter_dimension=0, tiled=False).astype(F32)

time: 1480 us -> 1500 us (1.014)
  waiting for transfers between devices: 551 us -> 578 us
    reduce_scatter x2, waiting for transfers between devices: 52.6 us -> 0.02 us  [scatter_z(): lax.psum_scatter(values, 'dp', scatter_dimension=0, tiled=False, axis_ind...]
    reduce_scatter x2, waiting for transfers between devices: 43.2 us -> 85.3 us  [scatter_t(): lax.psum_scatter(values.astype(BF16), 'tensor', scatter_dimension=1, tile...]
    all_to_all x6, waiting for transfers between devices: 62.1 us -> 88 us  [swap_t(): lax.all_to_all(values, 'tensor', split_axis=0, concat_axis=0, tiled=True)]
    unnamed x247 -> x253, local copies, waits for them, and re-layouts: 48.2 us -> 49.7 us
  transfers between devices with their start and end apart: 65 -> 65, of which waited for: 34 -> 32; matrix products, arithmetic and copies ran while one was open for 39% -> 36% of each run, Pallas kernels for 7% -> 7%
where the time goes in v13:
time: 1500 us; the launch traced here: 1490 us
  waiting for transfers between devices  578 us (39%)
  matrix products  318 us (21%)
  local copies, waits for them, and re-layouts  209 us (14%)
  other arithmetic  121 us (8%)
  starting transfers between devices  120 us (8%)
  Pallas kernels  98 us (7%)
  blocking collectives  25.1 us (2%)
  between operations  17 us (1%)
    ppermute x24, waiting for transfers between devices, over_t(): return lax.ppermute(values, 'tensor', [(i, i ^ k) for i in range(self.t)])  158 us
    dot_general x9, matrix products, dot_nt(): lax.dot_general(a, b, (((1,), (1,)), ((), ())), preferred_element_type=F32)  96.6 us
    all_to_all x5, waiting for transfers between devices, swap_z(): lax.all_to_all(values, 'dp', split_axis=0, concat_axis=0, axis_index_grou...  88.6 us
    all_to_all x6, waiting for transfers between devices, swap_t(): lax.all_to_all(values, 'tensor', split_axis=0, concat_axis=0, tiled=True)  88 us
    reduce_scatter x2, waiting for transfers between devices, scatter_t(): lax.psum_scatter(values.astype(BF16), 'tensor', scatter_dimension=1, tile...  85.3 us
    dot_general x8, matrix products, dot_tn(): lax.dot_general(a, b, (((0,), (0,)), ((), ())), preferred_element_type=F32)  81.3 us
    dot_general x9, matrix products, dot(): return jnp.dot(a, b, preferred_element_type=F32)  78.2 us
    all_gather x2, waiting for transfers between devices, gather_z(): lax.all_gather(values, 'dp', axis=0, tiled=False, axis_index_groups=lay.z...  59.9 us
  transfers between devices with their start and end apart: 65, of which 32 were waited for; matrix products, arithmetic and copies ran while one was open for 36% of the time, Pallas kernels for 7%

profile of v13, /device:TPU:10, one launch (start us, length us, event | category | flops | bytes accessed | tf_op | source)
XLA Modules:
  0.0 1485.3 jit_solution(4984581999877089057)
XLA Ops:
  20.2 6.9 maximum_bitcast_fusion
  27.1 8.3 copy.295
  35.4 6.4 all-to-all-start
  51.4 55.1 %all-gather.15.cloned.1.call-done = bf16[17152,256]{1,0:T(8,128)(2,1)} async-done(((bf16[2144,256]{1,0:T(8,128)(2,1)}), bf16[17152,256]{1,0:T(8,128)(2,1)}) %all-gather.15.cloned.1.call-update) | async-done | bytes 8781840 | tf_op jit(solution)/shard_map/all_gather | solution.py:495
  117.2 19.4 %all-to-all-done = bf16[4,4,3,352,256]{4,3,1,2,0:T(8,128)(2,1)} async-done(((bf16[4,4,3,352,256]{4,3,1,2,0:T(8,128)(2,1)}), bf16[4,4,3,352,256]{4,3,1,2,0:T(8,128)(2,1)}, u32[]{:S(2)}, u32[]{:S(2)}) %all-to-all-start) | async-done | bytes 8650784 | tf_op jit(solution)/shard_map/all_to_all | solution.py:431
  166.0 6.4 fusion.111
  190.8 14.6 attend.1
  221.5 43.4 %reduce-scatter.7.cloned.1.call-done = bf16[1024,512]{1,0:T(8,128)(2,1)} async-done(((bf16[1024,2048]{1,0:T(8,128)(2,1)}), bf16[1024,512]{1,0:T(8,128)(2,1)}) %reduce-scatter.7.cloned.1.call-update) | async-done | bytes 1048592 | tf_op jit(solution)/shard_map/reduce_scatter | solution.py:426
  266.9 8.1 psum.21
  292.4 17.3 %collective-permute-done.3.refs_1_ = bf16[1024,512]{1,0:T(8,128)(2,1)} collective-permute-done((bf16[1024,512]{1,0:T(8,128)(2,1)}, bf16[1024,512]{1,0:T(8,128)(2,1)}, u32[]{:S(2)}, u32[]{:S(2)}) %collective-permute-start.3) | collective-permute-done | bytes 1048608 | tf_op jit(solution)/shard_map/ppermute | solution.py:68
  309.6 19.9 %collective-permute-done.4.refs_2_ = bf16[1024,512]{1,0:T(8,128)(2,1)} collective-permute-done((bf16[1024,512]{1,0:T(8,128)(2,1)}, bf16[1024,512]{1,0:T(8,128)(2,1)}, u32[]{:S(2)}, u32[]{:S(2)}) %collective-permute-start.4) | collective-permute-done | bytes 1048608 | tf_op jit(solution)/shard_map/ppermute | solution.py:68
  329.6 6.2 join_columns.2
  335.7 26.5 %all-gather.17.cloned.1.call-done = bf16[4096,512]{1,0:T(8,128)(2,1)} async-done(((bf16[1024,512]{1,0:T(8,128)(2,1)}), bf16[4096,512]{1,0:T(8,128)(2,1)}) %all-gather.17.cloned.1.call-update) | async-done | bytes 4194320 | tf_op jit(solution)/shard_map/all_gather | solution.py:415
  363.0 16.3 %convert_bitcast_fusion.1 = bf16[4,4,512,512]{3,2,0,1:T(8,128)(2,1)} fusion(s32[4,4,1024]{2,1,0:T(4,128)S(1)} %fusion.45, bf16[4,1024,512]{2,1,0:T(8,128)(2,1)} %bitcast.534), kind=kOutput, calls=%fused_computation.39 | convolution fusion | flops 8602517504 | bytes 12648448 | tf_op jit(solution)/shard_map/sepk,skd->espd/dot_general | solution.py:528
  379.3 7.5 copy.300
  396.5 13.1 lay_out_weights.2
  409.7 33.4 %all-gather.19.cloned.1.call-done = bf16[4096,512]{1,0:T(8,128)(2,1)} async-done(((bf16[1024,512]{1,0:T(8,128)(2,1)}), bf16[4096,512]{1,0:T(8,128)(2,1)}) %all-gather.19.cloned.1.call-update) | async-done | bytes 4194320 | tf_op jit(solution)/shard_map/all_gather | solution.py:415
  450.6 14.3 convert_bitcast_fusion
  465.0 7.5 copy.303
  472.5 23.1 %collective-permute-done.10 = bf16[4,352,256]{2,1,0:T(8,128)(2,1)S(1)} collective-permute-done((bf16[4,352,256]{2,1,0:T(8,128)(2,1)S(1)}, bf16[4,352,256]{2,1,0:T(8,128)(2,1)S(1)}, u32[]{:S(2)}, u32[]{:S(2)}) %collective-permute-start.10) | collective-permute-done | bytes 720928 | tf_op jit(solution)/shard_map/ppermute | solution.py:73
  495.6 13.9 collective-permute-done.9
  526.1 11.5 copy.301
  539.7 6.4 all-to-all-start.4
  546.1 32.4 %fusion.120 = f32[2048,2816]{1,0:T(8,128)} fusion(bf16[2048,2048]{0,1:T(8,128)(2,1)} %bitcast.442, bf16[2816,2048]{1,0:T(8,128)(2,1)} %bitcast.426), kind=kOutput, calls=%fused_computation.300 | convolution fusion | flops 23622320128 | bytes 42991616 | tf_op jit(solution)/shard_map/dot_general | solution.py:30
  578.5 12.3 fusion.8
  590.8 9.3 lay_out_weights.3
  602.7 15.0 %multiply_convert_fusion = bf16[2048,2048]{1,0:T(8,128)(2,1)} fusion(bf16[2048,1408]{1,0:T(8,128)(2,1)S(1)} %get-tuple-element.296, f32[2048]{0:T(1024)S(1)} %bitcast.504, bf16[1,1408,2048]{2,1,0:T(8,128)(2,1)S(1)} %lay_out_weights.3), kind=kOutput, calls=%fused_computation.5 | convolution fusion | flops 11819548672 | bytes 19931136 | tf_op jit(solution)/shard_map/dot_general | solution.py:26
  617.7 21.1 %all-to-all-done.4 = bf16[4,2048,512]{2,1,0:T(8,128)(2,1)} async-done(((bf16[4,2048,512]{2,1,0:T(8,128)(2,1)}), bf16[4,2048,512]{2,1,0:T(8,128)(2,1)}, u32[]{:S(2)}, u32[]{:S(2)}) %all-to-all-start.4) | async-done | bytes 8388640 | tf_op jit(solution)/shard_map/all_to_all | solution.py:431
  638.8 11.5 copy.310
  657.8 7.4 copy.389
  665.3 6.5 all-to-all-start.5
  671.7 27.9 %multiply_convert_fusion.2 = (bf16[2048,1408]{1,0:T(8,128)(2,1)}, bf16[2048,1408]{1,0:T(8,128)(2,1)}, f32[2048]{0:T(1024)S(1)}) fusion(f32[2048,2816]{1,0:T(8,128)} %fusion.120, f32[2048]{0:T(1024)S(1)} %bitcast.505, bf16[2048,1408]{1,0:T(8,128)(2,1)} %copy-done.37, bf16[2048,2048]{0,1:T(8,128)(2,1)} %bitcast.444, bf16[1,1408,2048]{2,1,0:T(8,128)(2,1)} %copy-done), kind=kOutput, calls=%fused_computation.16 | convolution fusion | flops 11860178944 | bytes 54542336 | tf_op jit(solution)/shard_map/dot_general | solution.py:30
  699.6 8.2 copy.313
  715.1 11.6 pad_maximum_fusion
  726.7 6.7 fusion.121
  733.4 6.1 multiply_convert_fusion.5
  752.0 12.1 collective-permute-done.20
  765.1 31.2 %convolution_convert_fusion.3 = bf16[2048,2048]{1,0:T(8,128)(2,1)} fusion(bf16[2048,2816]{1,0:T(8,128)(2,1)} %pad_maximum_fusion, bf16[2816,2048]{1,0:T(8,128)(2,1)} %bitcast.427), kind=kOutput, calls=%fused_computation.42 | convolution fusion | flops 23626514432 | bytes 31457280 | tf_op jit(solution)/shard_map/dot_general | solution.py:26
  796.4 7.4 copy.388
  803.8 7.1 all-to-all-start.6
  810.9 12.3 bitcast_convert_fusion.1
  823.2 17.9 %convolution_convert_fusion.2.out_ref = bf16[1408,2048]{1,0:T(8,128)(2,1)} fusion(bf16[2048,1408]{1,0:T(8,128)(2,1)} %get-tuple-element.141, bf16[2048,2048]{0,1:T(8,128)(2,1)} %bitcast.445), kind=kOutput, calls=%fused_computation.41 | convolution fusion | flops 11814043648 | bytes 19922944 | tf_op jit(solution)/shard_map/dot_general | solution.py:34
  841.2 11.3 fusion.123
  852.4 31.5 %convolution_convert_fusion = bf16[2816,2048]{1,0:T(8,128)(2,1)} fusion(bf16[2048,2816]{1,0:T(8,128)(2,1)} %pad_maximum_fusion, bf16[2048,2048]{0,1:T(8,128)(2,1)} %bitcast.443), kind=kOutput, calls=%fused_computation.20 | convolution fusion | flops 23628087296 | bytes 31457280 | tf_op jit(solution)/shard_map/dot_general | solution.py:34
  884.0 17.5 %all-to-all-done.6 = bf16[4,2048,512]{2,1,0:T(8,128)(2,1)} async-done(((bf16[4,2048,512]{2,1,0:T(8,128)(2,1)}), bf16[4,2048,512]{2,1,0:T(8,128)(2,1)}, u32[]{:S(2)}, u32[]{:S(2)}) %all-to-all-start.6) | async-done | bytes 8388640 | tf_op jit(solution)/shard_map/all_to_all | solution.py:431
  901.5 12.2 bitcast_convert_fusion
  913.7 13.3 take_apart.1
  964.9 29.9 %all-to-all-done.7 = bf16[4,1024,512]{2,1,0:T(8,128)(2,1)} async-done(((bf16[4,1024,512]{2,1,0:T(8,128)(2,1)}), bf16[4,1024,512]{2,1,0:T(8,128)(2,1)}, u32[]{:S(2)}, u32[]{:S(2)}) %all-to-all-start.7) | async-done | bytes 4194336 | tf_op jit(solution)/shard_map/all_to_all | solution.py:431
  1004.1 8.2 psum.22
  1012.3 41.9 %reduce-scatter.13.cloned.1.call-done = bf16[1024,512]{1,0:T(8,128)(2,1)} async-done(((bf16[1024,2048]{1,0:T(8,128)(2,1)}), bf16[1024,512]{1,0:T(8,128)(2,1)}) %reduce-scatter.13.cloned.1.call-update) | async-done | bytes 1048592 | tf_op jit(solution)/shard_map/reduce_scatter | solution.py:426
  1074.4 6.5 convolution_convert_fusion.1
  1088.5 39.9 %all-to-all-done.8 = bf16[4,4,352,256]{3,2,1,0:T(8,128)(2,1)} async-done(((bf16[4,4,352,256]{3,2,1,0:T(8,128)(2,1)}), bf16[4,4,352,256]{3,2,1,0:T(8,128)(2,1)}, u32[]{:S(2)}, u32[]{:S(2)}) %all-to-all-start.8) | async-done | bytes 2883616 | tf_op jit(solution)/shard_map/all_to_all | solution.py:434
  1128.5 7.9 all-to-all-start.9
  1148.8 21.6 %attend_back.1 = (bf16[1024,512]{1,0:T(8,128)(2,1)S(1)}, f32[1024,256]{1,0:T(8,128)S(1)}, bf16[1024,1024]{1,0:T(8,128)(2,1)S(1)}, f32[1024,256]{1,0:T(8,128)S(1)}) custom-call(s32[1]{0:T(128)} %copy.411.len_ref, bf16[1024,512]{1,0:T(8,128)(2,1)S(1)} %copy-done.5, bf16[1024,256]{1,0:T(8,128)(2,1)S(1)} %copy-done.10, bf16[1024,1024]{1,0:T(8,128)(2,1)S(1)} %copy-done.16, ...), custom_call_target="tpu_custom_call" | custom-call | flops 6710886400 | bytes 33554432 | tf_op jit(solution)/shard_map/attend_back/pallas_call | solution.py:330
  1172.6 25.1 %all-to-all-done.9 = bf16[4,4,352,256]{3,2,1,0:T(8,128)(2,1)} async-done(((bf16[4,4,352,256]{3,2,1,0:T(8,128)(2,1)}), bf16[4,4,352,256]{3,2,1,0:T(8,128)(2,1)}, u32[]{:S(2)}, u32[]{:S(2)}) %all-to-all-start.9) | async-done | bytes 2883616 | tf_op jit(solution)/shard_map/all_to_all | solution.py:434
  1198.5 7.9 all-to-all-start.10
  1252.9 8.0 collective-permute-done.27
  1264.8 18.7 %collective-permute-done.29 = bf16[1024,512]{1,0:T(8,128)(2,1)S(1)} collective-permute-done((bf16[1024,512]{1,0:T(8,128)(2,1)}, bf16[1024,512]{1,0:T(8,128)(2,1)S(1)}, u32[]{:S(2)}, u32[]{:S(2)}) %collective-permute-start.29) | collective-permute-done | bytes 1048608 | tf_op jit(solution)/shard_map/ppermute | solution.py:68
  1293.1 18.9 %all-to-all-done.10 = bf16[4,4,352,256]{3,2,1,0:T(8,128)(2,1)} async-done(((bf16[4,4,352,256]{3,2,1,0:T(8,128)(2,1)}), bf16[4,4,352,256]{3,2,1,0:T(8,128)(2,1)}, u32[]{:S(2)}, u32[]{:S(2)}) %all-to-all-start.10) | async-done | bytes 2883616 | tf_op jit(solution)/shard_map/all_to_all | solution.py:434
  1344.0 8.8 psum.23
  1363.9 13.4 collective-permute-done.39.refs_9_
  1378.9 54.9 %collective-permute-done.40.refs_10_ = bf16[4,352,256]{2,1,0:T(8,128)(2,1)S(1)} collective-permute-done((bf16[4,352,256]{2,1,0:T(8,128)(2,1)S(1)}, bf16[4,352,256]{2,1,0:T(8,128)(2,1)S(1)}, u32[]{:S(2)}, u32[]{:S(2)}) %collective-permute-start.40) | collective-permute-done | bytes 720928 | tf_op jit(solution)/shard_map/ppermute | solution.py:68
  1433.8 13.7 home_gradients.1
  1449.6 6.1 join_columns.3
  (519 shorter events, 401.4 us)
Async XLA Ops:
  7.2 99.3 %all-gather.15.cloned.1.call-start = ((), (), s32[]{:S(2)}) async-start(), calls=%async_computation.25 | async-start | bytes 9879552 | tf_op jit(solution)/shard_map/all_gather | solution.py:495
  35.4 101.2 %all-to-all-start = ((bf16[4,4,3,352,256]{4,3,1,2,0:T(8,128)(2,1)}), bf16[4,4,3,352,256]{4,3,1,2,0:T(8,128)(2,1)}, u32[]{:S(2)}, u32[]{:S(2)}) async-start(bf16[4,4,3,352,256]{4,3,1,2,0:T(8,128)(2,1)} %copy.295), calls=%async_computation | async-start | bytes 17301504 | tf_op jit(solution)/shard_map/all_to_all | solution.py:431
  41.9 9.0 collective-permute-start
  43.5 7.4 collective-permute-start.1
  44.7 6.6 collective-permute-start.2
  143.9 68.3 %all-to-all-start.1 = ((bf16[4,4,352,256]{3,2,1,0:T(8,128)(2,1)}), bf16[4,4,352,256]{3,2,1,0:T(8,128)(2,1)S(1)}, u32[]{:S(2)}, u32[]{:S(2)}) async-start(bf16[4,4,352,256]{3,2,1,0:T(8,128)(2,1)} %copy.297), calls=%async_computation.1 | async-start | bytes 5767168 | tf_op jit(solution)/shard_map/all_to_all | solution.py:434
  149.2 115.7 %reduce-scatter.7.cloned.1.call-start = ((), (), s32[]{:S(2)}) async-start(), calls=%async_computation.17 | async-start | bytes 5242880 | tf_op jit(solution)/shard_map/reduce_scatter | solution.py:426
  215.8 66.9 %all-to-all-start.2 = ((bf16[4,4,352,256]{3,2,1,0:T(8,128)(2,1)}), bf16[4,4,352,256]{3,2,1,0:T(8,128)(2,1)}, u32[]{:S(2)}, u32[]{:S(2)}) async-start(bf16[4,4,352,256]{3,2,1,0:T(8,128)(2,1)} %copy.298), calls=%async_computation.3 | async-start | bytes 5767168 | tf_op jit(solution)/shard_map/all_to_all | solution.py:434
  221.4 140.8 %all-gather.17.cloned.1.call-start = ((), (), s32[]{:S(2)}) async-start(), calls=%async_computation.26 | async-start | bytes 5242880 | tf_op jit(solution)/shard_map/all_gather | solution.py:415
  282.7 160.4 %all-gather.19.cloned.1.call-start = ((), (), s32[]{:S(2)}) async-start(), calls=%async_computation.27 | async-start | bytes 5242880 | tf_op jit(solution)/shard_map/all_gather | solution.py:415
  283.1 26.5 %collective-permute-start.3 = (bf16[1024,512]{1,0:T(8,128)(2,1)}, bf16[1024,512]{1,0:T(8,128)(2,1)}, u32[]{:S(2)}, u32[]{:S(2)}) collective-permute-start(bf16[1024,512]{1,0:T(8,128)(2,1)} %multiply_convert_fusion.8.refs_0_), channel_id=1, source_target_pairs={{0,1},{1,0},{2,3},{3,2},{4,5},{5,4},{6,7},{7,6},{8,9},{9,8},{10,11... | collective-permute-start | bytes 3145736 | tf_op jit(solution)/shard_map/ppermute | solution.py:68
  284.1 45.5 %collective-permute-start.4 = (bf16[1024,512]{1,0:T(8,128)(2,1)}, bf16[1024,512]{1,0:T(8,128)(2,1)}, u32[]{:S(2)}, u32[]{:S(2)}) collective-permute-start(bf16[1024,512]{1,0:T(8,128)(2,1)} %multiply_convert_fusion.8.refs_0_), channel_id=1, source_target_pairs={{0,2},{1,3},{2,0},{3,1},{4,6},{5,7},{6,4},{7,5},{8,10},{9,11},{10,... | collective-permute-start | bytes 3145736 | tf_op jit(solution)/shard_map/ppermute | solution.py:68
  285.3 44.2 %collective-permute-start.5 = (bf16[1024,512]{1,0:T(8,128)(2,1)}, bf16[1024,512]{1,0:T(8,128)(2,1)}, u32[]{:S(2)}, u32[]{:S(2)}) collective-permute-start(bf16[1024,512]{1,0:T(8,128)(2,1)} %multiply_convert_fusion.8.refs_0_), channel_id=1, source_target_pairs={{0,3},{1,2},{2,1},{3,0},{4,7},{5,6},{6,5},{7,4},{8,11},{9,10},{10,... | collective-permute-start | bytes 3145736 | tf_op jit(solution)/shard_map/ppermute | solution.py:68
  386.8 9.5 collective-permute-start.6
  386.8 9.7 collective-permute-start.7
  389.5 136.6 %all-to-all-start.3 = ((bf16[4,2048,512]{2,1,0:T(8,128)(2,1)}), bf16[4,2048,512]{2,1,0:T(8,128)(2,1)}, u32[]{:S(2)}, u32[]{:S(2)}) async-start(bf16[4,2048,512]{2,1,0:T(8,128)(2,1)} %bitcast.420), calls=%async_computation.4 | async-start | bytes 16777216 | tf_op jit(solution)/shard_map/all_to_all | solution.py:431
  395.6 254.7 %all-gather.21.cloned.1.call-start = ((), (), s32[]{:S(2)}) async-start(), calls=%async_computation.28 | async-start | bytes 9732096 | tf_op jit(solution)/shard_map/all_gather | solution.py:644
  445.2 50.4 %collective-permute-start.10 = (bf16[4,352,256]{2,1,0:T(8,128)(2,1)S(1)}, bf16[4,352,256]{2,1,0:T(8,128)(2,1)S(1)}, u32[]{:S(2)}, u32[]{:S(2)}) collective-permute-start(bf16[4,352,256]{2,1,0:T(8,128)(2,1)S(1)} %get-tuple-element.330), channel_id=1, source_target_pairs={{0,24},{4,28},{8,16},{12,20},{16,8},{20,12},{24,0},{28,4},{1,25},{... | collective-permute-start | bytes 2162696 | tf_op jit(solution)/shard_map/ppermute | solution.py:73
  447.7 61.7 %collective-permute-start.9 = (bf16[4,352,256]{2,1,0:T(8,128)(2,1)S(1)}, bf16[4,352,256]{2,1,0:T(8,128)(2,1)S(1)}, u32[]{:S(2)}, u32[]{:S(2)}) collective-permute-start(bf16[4,352,256]{2,1,0:T(8,128)(2,1)S(1)} %get-tuple-element.331), channel_id=1, source_target_pairs={{0,16},{4,20},{8,24},{12,28},{16,0},{20,4},{24,8},{28,12},{1,17},{... | collective-permute-start | bytes 2162696 | tf_op jit(solution)/shard_map/ppermute | solution.py:73
  450.6 58.8 %collective-permute-start.8 = (bf16[4,352,256]{2,1,0:T(8,128)(2,1)S(1)}, bf16[4,352,256]{2,1,0:T(8,128)(2,1)S(1)}, u32[]{:S(2)}, u32[]{:S(2)}) collective-permute-start(bf16[4,352,256]{2,1,0:T(8,128)(2,1)S(1)} %get-tuple-element.332), channel_id=1, source_target_pairs={{0,8},{4,12},{8,0},{12,4},{16,24},{20,28},{24,16},{28,20},{1,9},{5... | collective-permute-start | bytes 2162696 | tf_op jit(solution)/shard_map/ppermute | solution.py:73
  516.8 5.0 collective-permute-start.12
  517.1 5.9 collective-permute-start.13
  539.6 51.2 %collective-permute-start.11 = (bf16[16,352,256]{2,1,0:T(8,128)(2,1)S(1)}, bf16[16,352,256]{2,1,0:T(8,128)(2,1)}, u32[]{:S(2)}, u32[]{:S(2)}) collective-permute-start(bf16[16,352,256]{2,1,0:T(8,128)(2,1)S(1)} %bitcast.418), channel_id=1, source_target_pairs={{0,4},{4,0},{8,12},{12,8},{16,20},{20,16},{24,28},{28,24},{1,5},{5... | collective-permute-start | bytes 8650760 | tf_op jit(solution)/shard_map/ppermute | solution.py:78
  539.7 99.1 %all-to-all-start.4 = ((bf16[4,2048,512]{2,1,0:T(8,128)(2,1)}), bf16[4,2048,512]{2,1,0:T(8,128)(2,1)}, u32[]{:S(2)}, u32[]{:S(2)}) async-start(bf16[4,2048,512]{2,1,0:T(8,128)(2,1)} %bitcast.421), calls=%async_computation.5 | async-start | bytes 16777216 | tf_op jit(solution)/shard_map/all_to_all | solution.py:431
  665.3 99.8 %all-to-all-start.5 = ((bf16[4,2048,512]{2,1,0:T(8,128)(2,1)}), bf16[4,2048,512]{2,1,0:T(8,128)(2,1)}, u32[]{:S(2)}, u32[]{:S(2)}) async-start(bf16[4,2048,512]{2,1,0:T(8,128)(2,1)} %bitcast.422), calls=%async_computation.6 | async-start | bytes 16777216 | tf_op jit(solution)/shard_map/all_to_all | solution.py:431
  711.3 34.4 %collective-permute-start.17 = (f32[8,128]{1,0:T(8,128)S(1)}, f32[8,128]{1,0:T(8,128)S(1)}, u32[]{:S(2)}, u32[]{:S(2)}) collective-permute-start(f32[8,128]{1,0:T(8,128)S(1)} %get-tuple-element.356), channel_id=1, source_target_pairs={{0,24},{4,28},{8,16},{12,20},{16,8},{20,12},{24,0},{28,4},{1,25},{... | collective-permute-start | bytes 12296 | tf_op jit(solution)/shard_map/ppermute | solution.py:73
  713.1 32.6 %collective-permute-start.16 = (f32[8,128]{1,0:T(8,128)S(1)}, f32[8,128]{1,0:T(8,128)S(1)}, u32[]{:S(2)}, u32[]{:S(2)}) collective-permute-start(f32[8,128]{1,0:T(8,128)S(1)} %get-tuple-element.357), channel_id=1, source_target_pairs={{0,16},{4,20},{8,24},{12,28},{16,0},{20,4},{24,8},{28,12},{1,17},{... | collective-permute-start | bytes 12296 | tf_op jit(solution)/shard_map/ppermute | solution.py:73
  715.1 30.6 %collective-permute-start.15 = (f32[8,128]{1,0:T(8,128)S(1)}, f32[8,128]{1,0:T(8,128)S(1)}, u32[]{:S(2)}, u32[]{:S(2)}) collective-permute-start(f32[8,128]{1,0:T(8,128)S(1)} %get-tuple-element.358), channel_id=1, source_target_pairs={{0,8},{4,12},{8,0},{12,4},{16,24},{20,28},{24,16},{28,20},{1,9},{5... | collective-permute-start | bytes 12296 | tf_op jit(solution)/shard_map/ppermute | solution.py:73
  745.7 18.4 %collective-permute-start.20 = (f32[4,8,128]{2,1,0:T(8,128)S(1)}, f32[4,8,128]{2,1,0:T(8,128)S(1)}, u32[]{:S(2)}, u32[]{:S(2)}) collective-permute-start(f32[4,8,128]{2,1,0:T(8,128)S(1)} %get-tuple-element.354), channel_id=1, source_target_pairs={{0,3},{1,2},{2,1},{3,0},{4,7},{5,6},{6,5},{7,4},{8,11},{9,10},{10,... | collective-permute-start | bytes 49160 | tf_op jit(solution)/shard_map/ppermute | solution.py:68
  747.3 17.0 %collective-permute-start.19 = (f32[4,8,128]{2,1,0:T(8,128)S(1)}, f32[4,8,128]{2,1,0:T(8,128)S(1)}, u32[]{:S(2)}, u32[]{:S(2)}) collective-permute-start(f32[4,8,128]{2,1,0:T(8,128)S(1)} %get-tuple-element.354), channel_id=1, source_target_pairs={{0,2},{1,3},{2,0},{3,1},{4,6},{5,7},{6,4},{7,5},{8,10},{9,11},{10,... | collective-permute-start | bytes 49160 | tf_op jit(solution)/shard_map/ppermute | solution.py:68
  747.4 16.9 %collective-permute-start.18 = (f32[4,8,128]{2,1,0:T(8,128)S(1)}, f32[4,8,128]{2,1,0:T(8,128)S(1)}, u32[]{:S(2)}, u32[]{:S(2)}) collective-permute-start(f32[4,8,128]{2,1,0:T(8,128)S(1)} %get-tuple-element.354), channel_id=1, source_target_pairs={{0,1},{1,0},{2,3},{3,2},{4,5},{5,4},{6,7},{7,6},{8,9},{9,8},{10,11... | collective-permute-start | bytes 49160 | tf_op jit(solution)/shard_map/ppermute | solution.py:68
  803.8 97.7 %all-to-all-start.6 = ((bf16[4,2048,512]{2,1,0:T(8,128)(2,1)}), bf16[4,2048,512]{2,1,0:T(8,128)(2,1)}, u32[]{:S(2)}, u32[]{:S(2)}) async-start(bf16[4,2048,512]{2,1,0:T(8,128)(2,1)} %bitcast.423), calls=%async_computation.8 | async-start | bytes 16777216 | tf_op jit(solution)/shard_map/all_to_all | solution.py:431
  810.9 127.8 %reduce-scatter.9.cloned.1.call-start = ((), (), s32[]{:S(2)}) async-start(), calls=%async_computation.18 | async-start | bytes 5242880 | tf_op jit(solution)/shard_map/reduce_scatter | solution.py:418
  841.1 156.8 %reduce-scatter.11.cloned.1.call-start = ((), (), s32[]{:S(2)}) async-start(), calls=%async_computation.19 | async-start | bytes 5242880 | tf_op jit(solution)/shard_map/reduce_scatter | solution.py:418
  913.6 140.6 %reduce-scatter.13.cloned.1.call-start = ((), (), s32[]{:S(2)}) async-start(), calls=%async_computation.20 | async-start | bytes 5242880 | tf_op jit(solution)/shard_map/reduce_scatter | solution.py:426
  933.4 17.4 %collective-permute-start.21 = (bf16[16,352,256]{2,1,0:T(8,128)(2,1)}, bf16[16,352,256]{2,1,0:T(8,128)(2,1)}, u32[]{:S(2)}, u32[]{:S(2)}) collective-permute-start(bf16[16,352,256]{2,1,0:T(8,128)(2,1)} %copy-done.14), channel_id=1, source_target_pairs={{0,4},{4,0},{8,12},{12,8},{16,20},{20,16},{24,28},{28,24},{1,5},{5... | collective-permute-start | bytes 8650760 | tf_op jit(solution)/shard_map/ppermute | solution.py:78
  933.5 22.6 %collective-permute-start.22 = (bf16[16,352,256]{2,1,0:T(8,128)(2,1)}, bf16[16,352,256]{2,1,0:T(8,128)(2,1)}, u32[]{:S(2)}, u32[]{:S(2)}) collective-permute-start(bf16[16,352,256]{2,1,0:T(8,128)(2,1)} %copy-done.13), channel_id=1, source_target_pairs={{0,4},{4,0},{8,12},{12,8},{16,20},{20,16},{24,28},{28,24},{1,5},{5... | collective-permute-start | bytes 8650760 | tf_op jit(solution)/shard_map/ppermute | solution.py:78
  938.6 21.8 %collective-permute-start.23 = (bf16[16,352,256]{2,1,0:T(8,128)(2,1)}, bf16[16,352,256]{2,1,0:T(8,128)(2,1)}, u32[]{:S(2)}, u32[]{:S(2)}) collective-permute-start(bf16[16,352,256]{2,1,0:T(8,128)(2,1)} %get-tuple-element.160), channel_id=1, source_target_pairs={{0,4},{4,0},{8,12},{12,8},{16,20},{20,16},{24,28},{28,24},{1,5},{5... | collective-permute-start | bytes 8650760 | tf_op jit(solution)/shard_map/ppermute | solution.py:78
  941.6 53.3 %all-to-all-start.7 = ((bf16[4,1024,512]{2,1,0:T(8,128)(2,1)}), bf16[4,1024,512]{2,1,0:T(8,128)(2,1)}, u32[]{:S(2)}, u32[]{:S(2)}) async-start(bf16[4,1024,512]{2,1,0:T(8,128)(2,1)} %bitcast.425), calls=%async_computation.9 | async-start | bytes 8388608 | tf_op jit(solution)/shard_map/all_to_all | solution.py:431
  947.1 181.3 %all-gather.11.cloned.1.call-start = ((), (), s32[]{:S(2)}) async-start(), calls=%async_computation.21 | async-start | bytes 5242880 | tf_op jit(solution)/shard_map/all_gather | solution.py:423
  1061.1 67.4 %all-to-all-start.8 = ((bf16[4,4,352,256]{3,2,1,0:T(8,128)(2,1)}), bf16[4,4,352,256]{3,2,1,0:T(8,128)(2,1)}, u32[]{:S(2)}, u32[]{:S(2)}) async-start(bf16[4,4,352,256]{3,2,1,0:T(8,128)(2,1)} %bitcast.431), calls=%async_computation.12 | async-start | bytes 5767168 | tf_op jit(solution)/shard_map/all_to_all | solution.py:434
  1066.4 163.2 %all-gather.13.cloned.1.call-start = ((), (), s32[]{:S(2)}) async-start(), calls=%async_computation.22 | async-start | bytes 5242880 | tf_op jit(solution)/shard_map/all_gather | solution.py:423
  1128.5 69.3 %all-to-all-start.9 = ((bf16[4,4,352,256]{3,2,1,0:T(8,128)(2,1)}), bf16[4,4,352,256]{3,2,1,0:T(8,128)(2,1)}, u32[]{:S(2)}, u32[]{:S(2)}) async-start(bf16[4,4,352,256]{3,2,1,0:T(8,128)(2,1)} %bitcast.430), calls=%async_computation.13 | async-start | bytes 5767168 | tf_op jit(solution)/shard_map/all_to_all | solution.py:434
  1136.4 319.3 %reduce-scatter.17.cloned.1.call-start = ((), (), s32[]{:S(2)}) async-start(), calls=%async_computation.24 | async-start | bytes 9732096 | tf_op jit(solution)/shard_map/reduce_scatter | solution.py:788
  1140.3 57.4 %collective-permute-start.24 = (bf16[4,352,256]{2,1,0:T(8,128)(2,1)}, bf16[4,352,256]{2,1,0:T(8,128)(2,1)S(1)}, u32[]{:S(2)}, u32[]{:S(2)}) collective-permute-start(bf16[4,352,256]{2,1,0:T(8,128)(2,1)} %get-tuple-element.327), channel_id=1, source_target_pairs={{0,1},{1,0},{2,3},{3,2},{4,5},{5,4},{6,7},{7,6},{8,9},{9,8},{10,11... | collective-permute-start | bytes 2162696 | tf_op jit(solution)/shard_map/ppermute | solution.py:68
  1141.0 56.8 %collective-permute-start.25 = (bf16[4,352,256]{2,1,0:T(8,128)(2,1)}, bf16[4,352,256]{2,1,0:T(8,128)(2,1)}, u32[]{:S(2)}, u32[]{:S(2)}) collective-permute-start(bf16[4,352,256]{2,1,0:T(8,128)(2,1)} %get-tuple-element.326), channel_id=1, source_target_pairs={{0,2},{1,3},{2,0},{3,1},{4,6},{5,7},{6,4},{7,5},{8,10},{9,11},{10,... | collective-permute-start | bytes 2162696 | tf_op jit(solution)/shard_map/ppermute | solution.py:68
  1142.4 55.4 %collective-permute-start.26 = (bf16[4,352,256]{2,1,0:T(8,128)(2,1)}, bf16[4,352,256]{2,1,0:T(8,128)(2,1)}, u32[]{:S(2)}, u32[]{:S(2)}) collective-permute-start(bf16[4,352,256]{2,1,0:T(8,128)(2,1)} %get-tuple-element.325), channel_id=1, source_target_pairs={{0,3},{1,2},{2,1},{3,0},{4,7},{5,6},{6,5},{7,4},{8,11},{9,10},{10,... | collective-permute-start | bytes 2162696 | tf_op jit(solution)/shard_map/ppermute | solution.py:68
  1198.5 113.4 %all-to-all-start.10 = ((bf16[4,4,352,256]{3,2,1,0:T(8,128)(2,1)}), bf16[4,4,352,256]{3,2,1,0:T(8,128)(2,1)}, u32[]{:S(2)}, u32[]{:S(2)}) async-start(bf16[4,4,352,256]{3,2,1,0:T(8,128)(2,1)} %bitcast.429), calls=%async_computation.14 | async-start | bytes 5767168 | tf_op jit(solution)/shard_map/all_to_all | solution.py:434
  1206.5 252.7 %reduce-scatter.15.cloned.1.call-start = ((), (), s32[]{:S(2)}) async-start(), calls=%async_computation.23 | async-start | bytes 9879552 | tf_op jit(solution)/shard_map/reduce_scatter | solution.py:788
  1234.5 26.4 %collective-permute-start.27 = (bf16[1024,512]{1,0:T(8,128)(2,1)}, bf16[1024,512]{1,0:T(8,128)(2,1)}, u32[]{:S(2)}, u32[]{:S(2)}) collective-permute-start(bf16[1024,512]{1,0:T(8,128)(2,1)} %get-tuple-element.309), channel_id=1, source_target_pairs={{0,1},{1,0},{2,3},{3,2},{4,5},{5,4},{6,7},{7,6},{8,9},{9,8},{10,11... | collective-permute-start | bytes 3145736 | tf_op jit(solution)/shard_map/ppermute | solution.py:68
  1238.9 44.6 %collective-permute-start.29 = (bf16[1024,512]{1,0:T(8,128)(2,1)}, bf16[1024,512]{1,0:T(8,128)(2,1)S(1)}, u32[]{:S(2)}, u32[]{:S(2)}) collective-permute-start(bf16[1024,512]{1,0:T(8,128)(2,1)} %get-tuple-element.310), channel_id=1, source_target_pairs={{0,3},{1,2},{2,1},{3,0},{4,7},{5,6},{6,5},{7,4},{8,11},{9,10},{10,... | collective-permute-start | bytes 3145736 | tf_op jit(solution)/shard_map/ppermute | solution.py:68
  1240.4 48.8 %collective-permute-start.28 = (bf16[1024,512]{1,0:T(8,128)(2,1)}, bf16[1024,512]{1,0:T(8,128)(2,1)S(1)}, u32[]{:S(2)}, u32[]{:S(2)}) collective-permute-start(bf16[1024,512]{1,0:T(8,128)(2,1)} %get-tuple-element.311), channel_id=1, source_target_pairs={{0,2},{1,3},{2,0},{3,1},{4,6},{5,7},{6,4},{7,5},{8,10},{9,11},{10,... | collective-permute-start | bytes 3145736 | tf_op jit(solution)/shard_map/ppermute | solution.py:68
  1250.9 61.1 %collective-permute-start.30 = (bf16[4,352,256]{2,1,0:T(8,128)(2,1)}, bf16[4,352,256]{2,1,0:T(8,128)(2,1)}, u32[]{:S(2)}, u32[]{:S(2)}) collective-permute-start(bf16[4,352,256]{2,1,0:T(8,128)(2,1)} %get-tuple-element.323), channel_id=1, source_target_pairs={{0,1},{1,0},{2,3},{3,2},{4,5},{5,4},{6,7},{7,6},{8,9},{9,8},{10,11... | collective-permute-start | bytes 2162696 | tf_op jit(solution)/shard_map/ppermute | solution.py:68
  1251.6 65.8 %collective-permute-start.31 = (bf16[4,352,256]{2,1,0:T(8,128)(2,1)}, bf16[4,352,256]{2,1,0:T(8,128)(2,1)}, u32[]{:S(2)}, u32[]{:S(2)}) collective-permute-start(bf16[4,352,256]{2,1,0:T(8,128)(2,1)} %get-tuple-element.322), channel_id=1, source_target_pairs={{0,2},{1,3},{2,0},{3,1},{4,6},{5,7},{6,4},{7,5},{8,10},{9,11},{10,... | collective-permute-start | bytes 2162696 | tf_op jit(solution)/shard_map/ppermute | solution.py:68
  1260.9 56.5 %collective-permute-start.32 = (bf16[4,352,256]{2,1,0:T(8,128)(2,1)}, bf16[4,352,256]{2,1,0:T(8,128)(2,1)}, u32[]{:S(2)}, u32[]{:S(2)}) collective-permute-start(bf16[4,352,256]{2,1,0:T(8,128)(2,1)} %get-tuple-element.321), channel_id=1, source_target_pairs={{0,3},{1,2},{2,1},{3,0},{4,7},{5,6},{6,5},{7,4},{8,11},{9,10},{10,... | collective-permute-start | bytes 2162696 | tf_op jit(solution)/shard_map/ppermute | solution.py:68
  1358.2 19.1 %collective-permute-start.39 = (bf16[4,352,256]{2,1,0:T(8,128)(2,1)S(1)}, bf16[4,352,256]{2,1,0:T(8,128)(2,1)S(1)}, u32[]{:S(2)}, u32[]{:S(2)}) collective-permute-start(bf16[4,352,256]{2,1,0:T(8,128)(2,1)S(1)} %get-tuple-element.319), channel_id=1, source_target_pairs={{0,1},{1,0},{2,3},{3,2},{4,5},{5,4},{6,7},{7,6},{8,9},{9,8},{10,11... | collective-permute-start | bytes 2162696 | tf_op jit(solution)/shard_map/ppermute | solution.py:68
  1360.0 87.6 %collective-permute-start.33 = (bf16[1024,512]{1,0:T(8,128)(2,1)S(1)}, bf16[1024,512]{1,0:T(8,128)(2,1)S(1)}, u32[]{:S(2)}, u32[]{:S(2)}) collective-permute-start(bf16[1024,512]{1,0:T(8,128)(2,1)S(1)} %fusion.38.refs_0_), channel_id=1, source_target_pairs={{0,1},{1,0},{2,3},{3,2},{4,5},{5,4},{6,7},{7,6},{8,9},{9,8},{10,11... | collective-permute-start | bytes 3145736 | tf_op jit(solution)/shard_map/ppermute | solution.py:68
  1360.3 87.3 %collective-permute-start.34 = (bf16[1024,512]{1,0:T(8,128)(2,1)S(1)}, bf16[1024,512]{1,0:T(8,128)(2,1)S(1)}, u32[]{:S(2)}, u32[]{:S(2)}) collective-permute-start(bf16[1024,512]{1,0:T(8,128)(2,1)S(1)} %fusion.38.refs_0_), channel_id=1, source_target_pairs={{0,2},{1,3},{2,0},{3,1},{4,6},{5,7},{6,4},{7,5},{8,10},{9,11},{10,... | collective-permute-start | bytes 3145736 | tf_op jit(solution)/shard_map/ppermute | solution.py:68
  1361.0 88.6 %collective-permute-start.35 = (bf16[1024,512]{1,0:T(8,128)(2,1)S(1)}, bf16[1024,512]{1,0:T(8,128)(2,1)}, u32[]{:S(2)}, u32[]{:S(2)}) collective-permute-start(bf16[1024,512]{1,0:T(8,128)(2,1)S(1)} %fusion.38.refs_0_), channel_id=1, source_target_pairs={{0,3},{1,2},{2,1},{3,0},{4,7},{5,6},{6,5},{7,4},{8,11},{9,10},{10,... | collective-permute-start | bytes 3145736 | tf_op jit(solution)/shard_map/ppermute | solution.py:68
  1363.5 70.4 %collective-permute-start.40 = (bf16[4,352,256]{2,1,0:T(8,128)(2,1)S(1)}, bf16[4,352,256]{2,1,0:T(8,128)(2,1)S(1)}, u32[]{:S(2)}, u32[]{:S(2)}) collective-permute-start(bf16[4,352,256]{2,1,0:T(8,128)(2,1)S(1)} %get-tuple-element.318), channel_id=1, source_target_pairs={{0,2},{1,3},{2,0},{3,1},{4,6},{5,7},{6,4},{7,5},{8,10},{9,11},{10,... | collective-permute-start | bytes 2162696 | tf_op jit(solution)/shard_map/ppermute | solution.py:68
  1377.4 56.5 %collective-permute-start.41 = (bf16[4,352,256]{2,1,0:T(8,128)(2,1)S(1)}, bf16[4,352,256]{2,1,0:T(8,128)(2,1)S(1)}, u32[]{:S(2)}, u32[]{:S(2)}) collective-permute-start(bf16[4,352,256]{2,1,0:T(8,128)(2,1)S(1)} %get-tuple-element.317), channel_id=1, source_target_pairs={{0,3},{1,2},{2,1},{3,0},{4,7},{5,6},{6,5},{7,4},{8,11},{9,10},{10,... | collective-permute-start | bytes 2162696 | tf_op jit(solution)/shard_map/ppermute | solution.py:68
  1461.5 9.0 collective-permute-start.38
  1463.2 9.6 collective-permute-start.37
  1464.6 8.1 collective-permute-start.36
  (115 other events, 1936.4 us)
Sparse Core Ops, SparseCore 0:
  20.3 86.0 all-gather.14
  212.3 52.5 reduce-scatter.6
  282.8 79.3 all-gather.16
  363.7 79.2 all-gather.18
  511.3 83.6 all-gather.20
  841.2 76.9 reduce-scatter.8
  920.6 77.2 reduce-scatter.10
  1001.1 53.1 reduce-scatter.12
  1061.2 52.6 all-gather.10
  1128.6 76.8 all-gather.12
  1207.8 139.4 reduce-scatter.16
  1349.5 93.4 reduce-scatter.14
